TPU v7x, 32 devices: a whole 2x2x4 slice. The times are simulated.
32 devices in a mesh: seq: 16 (over z, x, core), head: 2 (over y).
Axes of the slice: x: 2, y: 2, z: 4, core: 2. Of those that a mesh axis runs over, the one named last changes fastest.
Arguments:
- qkv: bfloat16 [3, 8192, 4096], P(None, ('seq', 'head')), may hold values from -6 to 6
- send_rows: int32 [16, 16, 40], P('seq'), may hold values from -1 to 511, as said below
- recv_pos: int32 [16, 16, 40], P('seq'), may hold values from -1 to 511, as said below
- req_lengths: int32 [4], replicated, may hold values from 1 to 4096, 8192 in all
- norm_gain: float32 [4096], P('head'), may hold values from 0.5 to 1.5
Outputs:
- attn_out: bfloat16 [8192, 4096], P('seq', 'head')
Inputs may be any that keep to these rules, and one draw needn't show every extreme that they name: send_rows[l, o, c] is a row of loader group l (rows l * 512 to l * 512 + 511 of qkv, counted from the group's first) sent to owner o in slot c, or -1 for an empty slot; used slots come first. Every row of a group is sent exactly once. At most 40 rows go from one group to one owner, and in every draw some pairs carry exactly 40, so that every group sends and every owner receives 40 rows from one pair. The number of rows from group l to owner o depends only on (o - l) modulo the number of groups. recv_pos[o, l, c] is the position within owner o's block of 512 packed positions where slot c from group l lands, and -1 exactly where send_rows[l, o, c] is -1; every position of a block is filled exactly once.
All inputs are finite; a program needn't handle non-finite values.
Results may differ from a plain program's by a relative error of at most 0.003.
Values may be sent and summed in bfloat16 or wider, within the bound.
No kernel may reach another device: no remote copies, remote signals or barrier semaphores. Data moves between devices by JAX's collectives and lax.ppermute only.
A program may use at most 128 MiB of HBM per device.

v0:
```python
import jax
import jax.numpy as jnp
from jax import lax
from jax.sharding import PartitionSpec as P

HEAD_DIM = 128


norm_eps = 1e-06


def prefix(shard, axis, combine, identity):
    length, position = (lax.axis_size(axis), lax.axis_index(axis))
    everything = jax.tree.map(lambda part: lax.all_gather(part, axis), shard)
    start = jax.tree.map(
        lambda part, zero: jnp.broadcast_to(jnp.asarray(zero, part.dtype), part.shape),
        shard,
        identity,
    )

    def lap(k, before):
        reached = k < position
        new = combine(before, jax.tree.map(lambda part: part[k], everything))
        return jax.tree.map(lambda a, b: jnp.where(reached, a, b), new, before)

    return lax.fori_loop(0, length, lap, start)


def place_rows(incoming, land_rows, tok_rows):
    row_width = incoming.shape[-1]
    planes = incoming.shape[0]
    flat_rows = incoming.reshape(planes, -1, row_width)
    land_index = jnp.where(land_rows < 0, tok_rows, land_rows).reshape(-1)
    blank_rows = jnp.zeros((planes, tok_rows, row_width), incoming.dtype)
    return blank_rows.at[:, land_index].set(flat_rows, mode="drop")


def carry_combine(earlier, later):
    return (later[0] + (1.0 - later[1]) * earlier[0], jnp.maximum(earlier[1], later[1]))


def on_device(qkv, send_rows, recv_pos, req_lengths, norm_gain):
    seq_count = lax.axis_size("seq")
    slot_count = send_rows.shape[2]
    pick_rows = jnp.maximum(send_rows[0], 0).reshape(-1)
    land_rows = recv_pos[0]
    grouped = lax.all_to_all(qkv, "head", split_axis=2, concat_axis=1, tiled=True)
    outgoing = jnp.take(grouped, pick_rows, axis=1).reshape(
        3, seq_count, slot_count, grouped.shape[2]
    )
    arrived = lax.all_to_all(outgoing, "seq", split_axis=1, concat_axis=1, tiled=True)
    packed = place_rows(arrived, land_rows, grouped.shape[1])
    query, keys, values = (packed[0], packed[1], packed[2])
    tok_rows = keys.shape[0]
    head_count = keys.shape[1] // HEAD_DIM
    first_row = lax.axis_index("seq") * tok_rows
    req_ends = jnp.cumsum(req_lengths)
    req_starts = req_ends - req_lengths
    positions = first_row + jnp.arange(tok_rows, dtype=jnp.int32)
    segment = jnp.sum((req_starts[None, :] <= positions[:, None]).astype(jnp.int32), axis=1) - 1
    prev_segment = jnp.sum((req_starts < first_row).astype(jnp.int32)) - 1
    inside = jnp.any((req_starts >= first_row) & (req_starts < first_row + tok_rows))
    has_start = jnp.where(inside, 1.0, 0.0).astype(jnp.float32)
    carried_mask = segment == prev_segment
    tail_mask = segment == segment[tok_rows - 1]
    causal = (positions[None, :] <= positions[:, None]) & (segment[None, :] == segment[:, None])
    tail_keys = jnp.where(tail_mask[:, None], keys, jnp.zeros_like(keys))
    update = jnp.einsum(
        "shd,she->hde",
        tail_keys.reshape(tok_rows, head_count, HEAD_DIM),
        values.reshape(tok_rows, head_count, HEAD_DIM),
        preferred_element_type=jnp.float32,
    )
    identity = (jnp.zeros_like(update), jnp.zeros((), jnp.float32))
    carried_pair = prefix((update, has_start), "seq", carry_combine, identity)
    carried = carried_pair[0]
    outputs = []
    for number in range(head_count):
        columns = slice(number * HEAD_DIM, (number + 1) * HEAD_DIM)
        query_head = query[:, columns]
        key_head = keys[:, columns]
        value_head = values[:, columns]
        scores = lax.dot_general(
            query_head, key_head, (((1,), (1,)), ((), ())), preferred_element_type=jnp.float32
        )
        weights = jnp.where(causal, scores, 0.0).astype(jnp.bfloat16)
        local_term = jnp.dot(weights, value_head, preferred_element_type=jnp.float32)
        carried_term = jnp.dot(
            query_head.astype(jnp.float32),
            carried[number],
            precision=lax.Precision.HIGHEST,
            preferred_element_type=jnp.float32,
        )
        raw_out = local_term + jnp.where(carried_mask[:, None], carried_term, 0.0)
        inv_rms = lax.rsqrt(jnp.mean(raw_out * raw_out, axis=1, keepdims=True) + norm_eps)
        outputs.append((raw_out * inv_rms * norm_gain[columns][None, :]).astype(jnp.bfloat16))
    return jnp.concatenate(outputs, axis=1)


def solution(mesh):
    return jax.shard_map(
        on_device,
        mesh=mesh,
        in_specs=(
            P(None, ("seq", "head"), None),
            P("seq", None, None),
            P("seq", None, None),
            P(),
            P("head"),
        ),
        out_specs=P("seq", "head"),
        check_vma=False,
    )
```

profile of v0, /device:TPU:11, one launch (start us, length us, event | category | flops | bytes accessed | tf_op | source)
XLA Modules:
  0.0 777.8 jit_solution(8094631923778563405)
XLA Ops:
  6.5 13.1 %copy.40 = bf16[3,256,4096]{1,0,2:T(4,128)(2,1)} copy(bf16[3,256,4096]{2,1,0:T(8,128)(2,1)} %param.7) | data formatting | bytes 12582912 | tf_op args[0]
  19.6 7.1 all-to-all-start
  26.8 91.6 %all-to-all-done = bf16[3,256,4096]{1,0,2:T(4,128)(2,1)} async-done(((bf16[3,256,4096]{1,0,2:T(4,128)(2,1)}), bf16[3,256,4096]{1,0,2:T(4,128)(2,1)}, u32[]{:S(2)}, u32[]{:S(2)}) %all-to-all-start) | async-done | bytes 6291488 | tf_op jit(solution)/shard_map/all_to_all | solution.py:47
  118.4 7.0 copy.41
  125.4 8.7 %copy.42 = bf16[3,2,256,2048]{3,2,1,0:T(8,128)(2,1)} copy(bf16[3,2,256,2048]{2,3,1,0:T(8,128)(2,1)} %bitcast.90) | data formatting | bytes 12582912 | tf_op jit(solution)/shard_map/all_to_all | solution.py:47
  134.1 11.5 %copy.43 = bf16[3,512,2048]{2,0,1:T(4,128)(2,1)} copy(bf16[3,512,2048]{2,1,0:T(8,128)(2,1)} %bitcast.91) | data formatting | bytes 12582912 | tf_op jit(solution)/shard_map/all_to_all | solution.py:47
  145.6 24.5 %gather_fusion = bf16[640,3,2048]{2,1,0:T(4,128)(2,1)} fusion(bf16[3,512,2048]{2,0,1:T(4,128)(2,1)} %copy.43, s32[1024]{0:T(1024)S(1)} %pad_clamp_fusion), kind=kCustom, calls=%fused_computation | custom fusion | bytes 15731200 | tf_op jit(solution)/shard_map/jit(_take)/gather | solution.py:48
  170.1 16.3 %copy_select_fusion = bf16[3,16,40,2048]{3,2,0,1:T(8,128)(2,1)} fusion(bf16[3,16,40,2048]{3,0,2,1:T(4,128)(2,1)} %bitcast.88, pred[16,40]{1,0:T(8,128)(4,1)S(1)} %compare_bitcast_fusion), kind=kLoop, calls=%fused_computation.4 | loop fusion | flops 3932160 | bytes 15729280 | tf_op jit(solution)/shard_map/jit(_take)/select_n | solution.py:48
  186.3 7.6 all-to-all-start.1
  197.6 167.4 %all-to-all-done.1 = bf16[3,16,40,2048]{3,2,0,1:T(8,128)(2,1)} async-done(((bf16[3,16,40,2048]{3,2,0,1:T(8,128)(2,1)}), bf16[3,16,40,2048]{3,2,0,1:T(8,128)(2,1)}, u32[]{:S(2)}, u32[]{:S(2)}) %all-to-all-start.1) | async-done | bytes 7864352 | tf_op jit(solution)/shard_map/all_to_all | solution.py:51
  365.0 4.2 copy.45
  369.2 25.7 %copy.46 = bf16[640,3,2048]{2,1,0:T(4,128)(2,1)} copy(bf16[640,3,2048]{2,0,1:T(8,128)(2,1)S(1)} %bitcast.89) | data formatting | bytes 15728640 | tf_op jit(solution)/shard_map/reshape | solution.py:32
  395.0 7.6 broadcast_in_dim.178
  402.6 85.2 %scatter_fusion = bf16[3,512,2048]{2,0,1:T(4,128)(2,1)} fusion(bf16[3,512,2048]{2,0,1:T(4,128)(2,1)} %broadcast_in_dim.178, s32[640]{0:T(1024)S(1)} %fusion.213, bf16[640,3,2048]{2,1,0:T(4,128)(2,1)} %copy.46), kind=kCustom, calls=%fused_computation.1 | custom fusion | bytes 23595520 | tf_op jit(solution)/shard_map/scatter | solution.py:35
  487.8 20.8 %fusion.232 = (bf16[1,512,2048]{2,0,1:T(2,128)(2,1)}, bf16[1,512,2048]{2,0,1:T(2,128)(2,1)}, bf16[1,512,2048]{2,0,1:T(2,128)(2,1)}) fusion(bf16[3,512,2048]{2,0,1:T(4,128)(2,1)} %scatter_fusion), kind=kLoop, calls=%fused_computation.301 | loop fusion | bytes 12582912 | tf_op jit(solution)/shard_map/slice | solution.py:53
  508.7 9.0 %copy.47 = bf16[1,512,2048]{1,2,0:T(8,128)(2,1)S(1)} copy(bf16[1,512,2048]{2,0,1:T(2,128)(2,1)} %get-tuple-element.130) | data formatting | bytes 4194304 | tf_op jit(solution)/shard_map/slice | solution.py:53
  517.6 10.5 %copy.48 = bf16[1,512,2048]{1,2,0:T(8,128)(2,1)} copy(bf16[1,512,2048]{2,0,1:T(2,128)(2,1)} %get-tuple-element.131) | data formatting | bytes 4194304 | tf_op jit(solution)/shard_map/slice | solution.py:53
  528.1 3.3 fusion.1
  533.4 23.5 %all-reduce = f32[16]{0:T(128)S(1)} all-reduce(f32[16]{0:T(128)S(1)} %dynamic-update-slice), channel_id=1, replica_groups=mesh['seq'=16,'head'=2] {'seq'}, use_global_device_ids=true, to_apply=%add | all-reduce | flops 16 | bytes 128
  556.9 3.6 copy.59
  560.5 6.9 copy_bitcast_fusion
  567.4 87.3 %all-gather.3.cloned.1.call-done = f32[256,128,128]{2,1,0:T(8,128)} async-done(((f32[16,128,128]{2,1,0:T(8,128)}), f32[256,128,128]{2,1,0:T(8,128)}) %all-gather.3.cloned.1.call-update) | async-done | bytes 16777232 | tf_op jit(solution)/shard_map/all_gather | solution.py:14
  654.7 54.5 %while.14 = (s32[]{:T(128)}, f32[16,128,128]{2,1,0:T(8,128)S(1)}, s32[]{:T(128)}, f32[16,16,128,128]{3,2,1,0:T(8,128)}, f32[16]{0:T(128)S(1)}, /*index=5*/s32[]{:T(128)}, f32[1]{0:T(128)}, s32[]{:T(128)}) while((s32[]{:T(128)}, f32[16,128,128]{2,1,0:T(8,128)S(1)}, s32[]{:T(128)}, f32[16,16,128,128]{3,2,1,0:T(8,128)}, ...), condition=%wide.region_6.7_spmd.clone, body=%wide.region_5.6_spmd.clone.sunk | while | flops 1048581 | bytes 3145873 | solution.py:26
  655.9 2.1 fusion.300
  659.3 2.1 fusion.300
  662.7 2.1 fusion.300
  666.1 2.1 fusion.300
  669.5 2.1 fusion.300
  672.9 2.1 fusion.300
  689.9 2.1 fusion.300
  693.3 2.1 fusion.300
  696.7 2.1 fusion.300
  727.3 2.4 multiply_reduce_fusion.4
  729.7 2.3 multiply_reduce_fusion.5
  732.0 2.3 multiply_reduce_fusion.6
  734.3 2.3 multiply_reduce_fusion.7
  736.6 2.3 multiply_reduce_fusion.8
  738.9 2.3 multiply_reduce_fusion.9
  741.2 2.3 multiply_reduce_fusion.10
  743.5 2.3 multiply_reduce_fusion.11
  745.8 2.3 multiply_reduce_fusion.12
  748.1 2.3 multiply_reduce_fusion.13
  750.4 2.3 multiply_reduce_fusion.14
  752.7 2.3 multiply_reduce_fusion.15
  755.0 2.3 multiply_reduce_fusion
  757.3 2.2 multiply_reduce_fusion.2
  759.5 2.2 multiply_reduce_fusion.1
  768.4 2.4 copy.50
  (153 shorter events, 53.9 us)
Async XLA Ops:
  19.6 7.1 copy-start.25
  19.6 98.8 %all-to-all-start = ((bf16[3,256,4096]{1,0,2:T(4,128)(2,1)}), bf16[3,256,4096]{1,0,2:T(4,128)(2,1)}, u32[]{:S(2)}, u32[]{:S(2)}) async-start(bf16[3,256,4096]{1,0,2:T(4,128)(2,1)} %copy.40), calls=%async_computation | async-start | bytes 16777216 | tf_op jit(solution)/shard_map/all_to_all | solution.py:47
  186.3 7.6 copy-start.28
  186.3 9.1 %copy-start.26 = (s32[1,16,40]{2,1,0:T(8,128)S(1)}, s32[1,16,40]{2,1,0:T(8,128)}, u32[]{:S(2)}) copy-start(s32[1,16,40]{2,1,0:T(8,128)} %param.9) | copy-start | bytes 7684
  186.3 178.7 %all-to-all-start.1 = ((bf16[3,16,40,2048]{3,2,0,1:T(8,128)(2,1)}), bf16[3,16,40,2048]{3,2,0,1:T(8,128)(2,1)}, u32[]{:S(2)}, u32[]{:S(2)}) async-start(bf16[3,16,40,2048]{3,2,0,1:T(8,128)(2,1)} %copy_select_fusion), calls=%async_computation.1 | async-start | bytes 15728640 | tf_op jit(solution)/shard_map/all_to_all | solution.py:51
  193.9 460.8 %all-gather.3.cloned.1.call-start = ((), (), s32[]{:S(2)}) async-start(), calls=%async_computation.2 | async-start | bytes 17825792 | tf_op jit(solution)/shard_map/all_gather | solution.py:14
  528.1 3.3 copy-start.29
  528.1 28.7 %copy-start.27 = (f32[2048]{0:T(1024)S(1)}, f32[2048]{0:T(1024)}, u32[]{:S(2)}) copy-start(f32[2048]{0:T(1024)} %param.11) | copy-start | bytes 24580
  556.9 3.6 copy-start
  725.6 4.1 copy-start.24
  727.3 4.7 copy-start.23
  729.7 4.6 copy-start.22
  732.0 4.6 copy-start.21
  734.3 4.6 copy-start.20
  736.6 4.6 copy-start.19
  738.9 4.6 copy-start.18
  741.2 4.6 copy-start.17
  743.5 4.6 copy-start.16
  745.8 4.6 copy-start.15
  748.1 4.6 copy-start.14
  750.3 4.6 copy-start.13
  752.7 4.6 copy-start.12
  755.0 4.5 copy-start.11
  761.7 5.5 copy-start.10
  761.7 5.6 copy-start.7
  761.7 5.7 copy-start.6
  761.8 5.8 copy-start.4
  761.8 5.9 copy-start.3
  761.8 6.0 copy-start.2
  763.0 5.0 copy-start.1
  765.1 3.0 copy-start.9
  766.2 2.0 copy-start.8
  767.3 1.0 copy-start.5
Sparse Core Ops, SparseCore 0:
  531.6 123.0 all-gather.2
where the time goes:
time: 793 us; the launch traced here: 778 us
  waiting for transfers between devices  346 us (44%)
  local copies, waits for them, and re-layouts  253 us (32%)
  other arithmetic  59.2 us (7%)
  matrix products  55.6 us (7%)
  blocking collectives  23.5 us (3%)
  between operations  15.4 us (2%)
  starting transfers between devices  14.7 us (2%)
  loops' own time  10.4 us (1%)
    all_to_all x1, waiting for transfers between devices, on_device(): lax.all_to_all(outgoing, 'seq', split_axis=1, concat_axis=1, tiled=True)  167 us
    all_to_all x1, waiting for transfers between devices, on_device(): lax.all_to_all(qkv, 'head', split_axis=2, concat_axis=1, tiled=True)  91.6 us
    all_gather x1, waiting for transfers between devices, prefix(): everything = jax.tree.map(lambda part: lax.all_gather(part, axis), shard)  87.3 us
    scatter x1, local copies, waits for them, and re-layouts, place_rows(): return blank_rows.at[:, land_index].set(flat_rows, mode='drop')  85.2 us
    slice x3, local copies, waits for them, and re-layouts, on_device(): query, keys, values = (packed[0], packed[1], packed[2])  40.3 us
    dot_general x16, matrix products, on_device(): jnp.dot(weights, value_head, preferred_element_type=jnp.float32)  35.8 us
    select_n x16, other arithmetic, lap(): return jax.tree.map(lambda a, b: jnp.where(reached, a, b), new, before)  34.2 us
    all_to_all x3, local copies, waits for them, and re-layouts, on_device(): lax.all_to_all(qkv, 'head', split_axis=2, concat_axis=1, tiled=True)  27.2 us
  transfers between devices with their start and end apart: 3, of which 3 were waited for; matrix products, arithmetic and copies ran while one was open for 2% of the time, Pallas kernels for 0%

commit v1 on v0

v1 whole, which is shorter than its diff:
```python
import functools

import jax
import jax.numpy as jnp
from jax import lax
from jax.experimental import pallas as pl
from jax.experimental.pallas import tpu as pltpu
from jax.sharding import PartitionSpec as P

HEAD_DIM = 128

norm_eps = 1e-06

QUERY, KEYS, VALUES = 0, 1, 2


def pack_kernel(place_ref, *refs):
    count = (len(refs) - 1) // 3
    picks, sources = refs[:count], refs[count : 2 * count]
    out_ref, chosen = refs[2 * count], refs[2 * count + 1 :]

    @pl.when((pl.program_id(0) == 0) & (pl.program_id(1) == 0))
    def _():
        for pick, onehot in zip(picks, chosen):
            rows = lax.broadcasted_iota(jnp.int32, onehot.shape, 1)
            onehot[...] = jnp.where(pick[...] == rows, 1.0, 0.0).astype(onehot.dtype)

    total = None
    for source, onehot in zip(sources, chosen):
        part = jnp.dot(onehot[...], source[0], preferred_element_type=jnp.float32)
        total = part if total is None else total + part
    out_ref[...] = total.astype(out_ref.dtype)


def pack_rows(place, picks, sources, planes, columns):
    slots = picks[0].shape[0]
    width = min(columns, 512)
    blocks = columns // width
    lens = [array.shape[1] for array, _, _ in sources]

    def source_spec(array, plane_start, first):
        return pl.BlockSpec(
            (1, array.shape[1], width),
            lambda p, j, place_ref: (plane_start + p, 0, first(place_ref[0], width) + j),
        )

    return pl.pallas_call(
        pack_kernel,
        out_shape=jax.ShapeDtypeStruct((slots, planes * columns), jnp.bfloat16),
        grid_spec=pltpu.PrefetchScalarGridSpec(
            num_scalar_prefetch=1,
            grid=(planes, blocks),
            in_specs=[pl.BlockSpec((slots, 1), lambda p, j, place_ref: (0, 0)) for _ in picks]
            + [source_spec(*source) for source in sources],
            out_specs=pl.BlockSpec((slots, width), lambda p, j, place_ref: (0, p * blocks + j)),
            scratch_shapes=[pltpu.VMEM((slots, length), jnp.bfloat16) for length in lens],
        ),
        cost_estimate=pl.CostEstimate(
            flops=2 * slots * sum(lens) * planes * columns,
            bytes_accessed=2 * planes * columns * (slots + sum(lens)),
            transcendentals=0,
        ),
        name="pack_rows",
    )(place, *picks, *[array for array, _, _ in sources])


def unpack_kernel(land_ref, tail_ref, keys_ref, values_ref, keys_out, values_out, update_ref, order):
    @pl.when(pl.program_id(0) == 0)
    def _():
        rows = lax.broadcasted_iota(jnp.int32, order.shape, 0)
        order[...] = jnp.where(land_ref[...] == rows, 1.0, 0.0).astype(order.dtype)

    keys = jnp.dot(order[...], keys_ref[...], preferred_element_type=jnp.float32)
    keys_out[...] = keys.astype(keys_out.dtype)
    values = jnp.dot(order[...], values_ref[...], preferred_element_type=jnp.float32).astype(
        values_out.dtype
    )
    values_out[...] = values
    tail_keys = jnp.where(tail_ref[...] != 0, keys, 0.0).astype(values.dtype)
    for part in range(keys.shape[1] // HEAD_DIM):
        columns = slice(part * HEAD_DIM, (part + 1) * HEAD_DIM)
        update_ref[columns, :] = lax.dot_general(
            tail_keys[:, columns],
            values[:, columns],
            (((0,), (0,)), ((), ())),
            preferred_element_type=jnp.float32,
        ).astype(update_ref.dtype)


def unpack_keys_values(arrived, land_row, tail, tok_rows):
    slots, columns = arrived.shape[0], arrived.shape[1] // 2
    width = min(columns, 2 * HEAD_DIM)
    blocks = columns // width
    packed = jax.ShapeDtypeStruct((tok_rows, columns), arrived.dtype)
    column_spec = pl.BlockSpec((tok_rows, width), lambda j: (0, j))
    return pl.pallas_call(
        unpack_kernel,
        out_shape=(packed, packed, jax.ShapeDtypeStruct((columns, HEAD_DIM), jnp.bfloat16)),
        grid=(blocks,),
        in_specs=[
            pl.BlockSpec((1, slots), lambda j: (0, 0)),
            pl.BlockSpec((tok_rows, 1), lambda j: (0, 0)),
            pl.BlockSpec((slots, width), lambda j: (0, j)),
            pl.BlockSpec((slots, width), lambda j: (0, blocks + j)),
        ],
        out_specs=(column_spec, column_spec, pl.BlockSpec((width, HEAD_DIM), lambda j: (j, 0))),
        scratch_shapes=[pltpu.VMEM((tok_rows, slots), jnp.bfloat16)],
        cost_estimate=pl.CostEstimate(
            flops=2 * tok_rows * columns * (2 * slots + HEAD_DIM),
            bytes_accessed=4 * columns * (slots + tok_rows),
            transcendentals=0,
        ),
        name="unpack_keys_values",
    )(land_row, tail, arrived, arrived)


def carry_kernel(keep_ref, updates_ref, carried_ref):
    count = updates_ref.shape[0]
    state = jnp.zeros(updates_ref.shape[1:], jnp.float32)
    carried_ref[0] = state.astype(carried_ref.dtype)
    for block in range(1, count):
        state = jnp.where(keep_ref[block] != 0, state, 0.0) + updates_ref[block - 1].astype(jnp.float32)
        carried_ref[block] = state.astype(carried_ref.dtype)


def carry_states(update, keep):
    seq_count = lax.axis_size("seq")
    share = update.shape[0] // seq_count
    updates = lax.all_to_all(update, "seq", split_axis=0, concat_axis=0, tiled=True)
    states = pl.pallas_call(
        carry_kernel,
        out_shape=jax.ShapeDtypeStruct((seq_count, share, HEAD_DIM), update.dtype),
        grid_spec=pltpu.PrefetchScalarGridSpec(
            num_scalar_prefetch=1,
            grid=(1,),
            in_specs=[pl.BlockSpec((seq_count, share, HEAD_DIM), lambda i, keep_ref: (0, 0, 0))],
            out_specs=pl.BlockSpec((seq_count, share, HEAD_DIM), lambda i, keep_ref: (0, 0, 0)),
        ),
        cost_estimate=pl.CostEstimate(
            flops=2 * update.size, bytes_accessed=4 * update.size, transcendentals=0
        ),
        name="carry_states",
    )(keep, updates.reshape(seq_count, share, HEAD_DIM))
    return lax.all_to_all(
        states.reshape(seq_count * share, HEAD_DIM), "seq", split_axis=0, concat_axis=0, tiled=True
    )


def attend_kernel(
    land_ref, seg_col_ref, seg_row_ref, carried_mask_ref, gain_ref, query_ref, keys_ref, values_ref,
    states_ref, out_ref, order, causal,
):
    tok_rows = order.shape[0]

    @pl.when(pl.program_id(0) == 0)
    def _():
        rows = lax.broadcasted_iota(jnp.int32, order.shape, 0)
        order[...] = jnp.where(land_ref[...] == rows, 1.0, 0.0).astype(order.dtype)
        later = lax.broadcasted_iota(jnp.int32, causal.shape, 0)
        earlier = lax.broadcasted_iota(jnp.int32, causal.shape, 1)
        open_pair = (earlier <= later) & (seg_col_ref[...] == seg_row_ref[...])
        causal[...] = jnp.where(open_pair, 1.0, 0.0)

    query = jnp.dot(order[...], query_ref[...], preferred_element_type=jnp.float32).astype(
        keys_ref.dtype
    )
    half = tok_rows // 2
    for part in range(query.shape[1] // HEAD_DIM):
        columns = slice(part * HEAD_DIM, (part + 1) * HEAD_DIM)
        for rows, reach in ((slice(0, half), half), (slice(half, tok_rows), tok_rows)):
            queries = query[rows, columns]
            scores = lax.dot_general(
                queries,
                keys_ref[:reach, columns],
                (((1,), (1,)), ((), ())),
                preferred_element_type=jnp.float32,
            )
            weights = jnp.where(causal[rows, :reach] != 0.0, scores, 0.0).astype(keys_ref.dtype)
            local_term = jnp.dot(
                weights, values_ref[:reach, columns], preferred_element_type=jnp.float32
            )
            carried_term = jnp.dot(
                queries, states_ref[columns, :], preferred_element_type=jnp.float32
            )
            raw_out = local_term + jnp.where(carried_mask_ref[rows, :] != 0, carried_term, 0.0)
            inv_rms = lax.rsqrt(jnp.mean(raw_out * raw_out, axis=1, keepdims=True) + norm_eps)
            out_ref[rows, columns] = (raw_out * inv_rms * gain_ref[:, columns]).astype(out_ref.dtype)


def attend(arrived, keys, values, states, land_row, seg_col, seg_row, carried_mask, gain):
    slots, columns = arrived.shape
    tok_rows = keys.shape[0]
    width = min(columns, 2 * HEAD_DIM)
    column_spec = pl.BlockSpec((tok_rows, width), lambda j: (0, j))
    return pl.pallas_call(
        attend_kernel,
        out_shape=jax.ShapeDtypeStruct((tok_rows, columns), jnp.bfloat16),
        grid=(columns // width,),
        in_specs=[
            pl.BlockSpec((1, slots), lambda j: (0, 0)),
            pl.BlockSpec((tok_rows, 1), lambda j: (0, 0)),
            pl.BlockSpec((1, tok_rows), lambda j: (0, 0)),
            pl.BlockSpec((tok_rows, 1), lambda j: (0, 0)),
            pl.BlockSpec((1, width), lambda j: (0, j)),
            pl.BlockSpec((slots, width), lambda j: (0, j)),
            column_spec,
            column_spec,
            pl.BlockSpec((width, HEAD_DIM), lambda j: (j, 0)),
        ],
        out_specs=column_spec,
        scratch_shapes=[
            pltpu.VMEM((tok_rows, slots), jnp.bfloat16),
            pltpu.VMEM((tok_rows, tok_rows), jnp.float32),
        ],
        cost_estimate=pl.CostEstimate(
            flops=2 * tok_rows * columns * (slots + 2 * tok_rows + HEAD_DIM),
            bytes_accessed=2 * columns * (slots + 3 * tok_rows),
            transcendentals=0,
        ),
        name="attend",
    )(land_row, seg_col, seg_row, carried_mask, gain, arrived, keys, values, states)


def send_packed(qkv, send_rows, plane_start, planes, start, columns):
    head_count = lax.axis_size("head")
    place = lax.axis_index("head")
    rows = qkv.shape[1]
    mine = qkv.shape[2] // head_count
    slots = send_rows.reshape(-1, 1)
    part = lax.slice_in_dim(qkv, plane_start, plane_start + planes, axis=0)
    if head_count == 2:
        low = part[:, :, start : start + columns]
        high = part[:, :, mine + start : mine + start + columns]
        outgoing = jnp.where(place == 0, high, low)
        incoming = lax.ppermute(outgoing, "head", [(0, 1), (1, 0)])
        picks = (slots - place * rows, slots - (1 - place) * rows)
        sources = (
            (qkv, plane_start, lambda at, width: at * (mine // width) + start // width),
            (incoming, 0, lambda at, width: 0),
        )
    else:
        split = part.reshape(planes, rows, head_count, mine)[..., start : start + columns]
        incoming = lax.all_to_all(
            jnp.moveaxis(split, 2, 0), "head", split_axis=0, concat_axis=0, tiled=False
        )
        incoming = jnp.moveaxis(incoming, 0, 1).reshape(planes, head_count * rows, columns)
        picks = (slots,)
        sources = ((incoming, 0, lambda at, width: 0),)
    outgoing = pack_rows(
        jnp.reshape(place, (1,)).astype(jnp.int32), picks, sources, planes, columns
    )
    return lax.all_to_all(outgoing, "seq", split_axis=0, concat_axis=0, tiled=True)


def on_device(qkv, send_rows, recv_pos, req_lengths, norm_gain):
    seq_count, head_count = lax.axis_size("seq"), lax.axis_size("head")
    block = lax.axis_index("seq")
    tok_rows = qkv.shape[1] * head_count
    columns = qkv.shape[2] // head_count
    half = columns // 2

    req_ends = jnp.cumsum(req_lengths)
    req_starts = req_ends - req_lengths
    first_row = block * tok_rows
    positions = first_row + jnp.arange(tok_rows, dtype=jnp.int32)
    segment = jnp.sum((req_starts[None, :] <= positions[:, None]).astype(jnp.int32), axis=1) - 1
    last_rows = (jnp.arange(seq_count, dtype=jnp.int32) + 1) * tok_rows - 1
    last_segment = jnp.sum((req_starts[None, :] <= last_rows[:, None]).astype(jnp.int32), axis=1) - 1
    prev_segment = jnp.sum((req_starts < first_row).astype(jnp.int32)) - 1
    keep = jnp.concatenate(
        [jnp.zeros((2,), jnp.int32), (last_segment[1:-1] == last_segment[:-2]).astype(jnp.int32)]
    )
    carried_mask = (segment == prev_segment).astype(jnp.int32)[:, None]
    tail = (segment == segment[tok_rows - 1]).astype(jnp.int32)[:, None]
    land_row = recv_pos[0].reshape(1, -1)
    gain = norm_gain.reshape(1, -1)

    arrived = [send_packed(qkv, send_rows[0], KEYS, 2, start, half) for start in (0, half)]
    query = send_packed(qkv, send_rows[0], QUERY, 1, 0, columns)
    keys, values, updates = zip(*[unpack_keys_values(part, land_row, tail, tok_rows) for part in arrived])
    states = carry_states(jnp.concatenate(updates, axis=0), keep)
    return attend(
        query,
        jnp.concatenate(keys, axis=1),
        jnp.concatenate(values, axis=1),
        states,
        land_row,
        segment[:, None],
        segment[None, :],
        carried_mask,
        gain,
    )


def solution(mesh):
    return jax.shard_map(
        on_device,
        mesh=mesh,
        in_specs=(
            P(None, ("seq", "head"), None),
            P("seq", None, None),
            P("seq", None, None),
            P(),
            P("head"),
        ),
        out_specs=P("seq", "head"),
        check_vma=False,
    )
```

time: 793 us -> 292 us (0.37); the launches traced: 778 us -> 289 us
  local copies, waits for them, and re-layouts: 253 us -> 8.17 us
  waiting for transfers between devices: 346 us -> 190 us
  matrix products: 55.6 us -> 0 us
  other arithmetic: 59.2 us -> 14.6 us
  Pallas kernels: 0 us -> 44 us
  blocking collectives: 23.5 us -> 0 us
  starting transfers between devices: 14.7 us -> 30.9 us
  between operations: 15.4 us -> 0.74 us
  loops' own time: 10.4 us -> 0 us
    all_to_all x2 -> x5, waiting for transfers between devices: 259 us -> 146 us  [the longest x3 130 us: send_packed(): lax.all_to_all(outgoing, 'seq', split_axis=0, concat_axis=0, tiled=True)]
    all_gather x1 -> x0, waiting for transfers between devices: 87.3 us -> none  [prefix(): everything = jax.tree.map(lambda part: lax.all_gather(part, axis), shard)]
    scatter x1 -> x0, local copies, waits for them, and re-layouts: 85.2 us -> none  [place_rows(): return blank_rows.at[:, land_index].set(flat_rows, mode='drop')]
    dot_general x33 -> x0, matrix products: 55.6 us -> none  [the longest x16 35.8 us: on_device(): jnp.dot(weights, value_head, preferred_element_type=jnp.float32)]
    select_n x18 -> x2, other arithmetic: 50.5 us -> 5.03 us  [send_packed(): outgoing = jnp.where(place == 0, high, low)]
    ppermute x0 -> x3, waiting for transfers between devices: none -> 44.5 us  [send_packed(): incoming = lax.ppermute(outgoing, 'head', [(0, 1), (1, 0)])]
    pallas_call x0 -> x7, Pallas kernels: none -> 44 us  [the longest x3 16 us: pack_rows(): pl.pallas_call(pack_kernel, out_shape=jax.ShapeDtypeStruct((slots, planes...]
    slice x5 -> x1, local copies, waits for them, and re-layouts: 40.9 us -> 0.58 us  [on_device(): tail = (segment == segment[tok_rows - 1]).astype(jnp.int32)[:, None]]
  transfers between devices with their start and end apart: 3 -> 8, of which waited for: 3 -> 7; matrix products, arithmetic and copies ran while one was open for 2% -> 5% of each run, Pallas kernels for 0% -> 8%
where the time goes in v1:
time: 292 us; the launch traced here: 289 us
  waiting for transfers between devices  190 us (65%)
  Pallas kernels  44 us (15%)
  starting transfers between devices  30.9 us (11%)
  other arithmetic  14.6 us (5%)
  local copies, waits for them, and re-layouts  8.17 us (3%)
    all_to_all x3, waiting for transfers between devices, send_packed(): lax.all_to_all(outgoing, 'seq', split_axis=0, concat_axis=0, tiled=True)  130 us
    ppermute x3, waiting for transfers between devices, send_packed(): incoming = lax.ppermute(outgoing, 'head', [(0, 1), (1, 0)])  44.5 us
    all_to_all x3, starting transfers between devices, send_packed(): lax.all_to_all(outgoing, 'seq', split_axis=0, concat_axis=0, tiled=True)  17.3 us
    pallas_call x3, Pallas kernels, pack_rows(): pl.pallas_call(pack_kernel, out_shape=jax.ShapeDtypeStruct((slots, planes...  16 us
    pallas_call x1, Pallas kernels, attend(): pl.pallas_call(attend_kernel, out_shape=jax.ShapeDtypeStruct((tok_rows, c...  14.2 us
    pallas_call x2, Pallas kernels, unpack_keys_values(): pl.pallas_call(unpack_kernel, out_shape=(packed, packed, jax.ShapeDtypeSt...  11.2 us
    all_to_all x1, waiting for transfers between devices, carry_states(): lax.all_to_all(states.reshape(seq_count * share, HEAD_DIM), 'seq', split_...  8.85 us
    all_to_all x1, waiting for transfers between devices, carry_states(): lax.all_to_all(update, 'seq', split_axis=0, concat_axis=0, tiled=True)  7.29 us
  transfers between devices with their start and end apart: 8, of which 7 were waited for; matrix products, arithmetic and copies ran while one was open for 5% of the time, Pallas kernels for 8%

profile of v1, /device:TPU:11, one launch (start us, length us, event | category | flops | bytes accessed | tf_op | source)
XLA Modules:
  0.0 288.8 jit_solution(17105907046113999369)
XLA Ops:
  0.0 3.4 %slice_select_fusion.1 = (bf16[2,256,1024]{2,1,0:T(8,128)(2,1)S(1)}, bf16[2,256,1024]{2,1,0:T(8,128)(2,1)}) fusion(bf16[3,256,4096]{2,1,0:T(8,128)(2,1)} %refs_2_.5, pred[]{:T(512)S(6)} %eq.36), kind=kLoop, calls=%fused_computation.3 | loop fusion | flops 1048576 | bytes 6291457 | tf_op jit(solution)/shard_map/jit(_where)/select_n | solution.py:234
  3.4 1.2 collective-permute-start.1
  4.6 0.0 copy-done.9
  4.6 0.9 sub.63.refs_0_
  5.5 0.9 sub.64.refs_1_
  6.4 21.0 %collective-permute-done.1.refs_3_ = bf16[2,256,1024]{2,1,0:T(8,128)(2,1)S(1)} collective-permute-done((bf16[2,256,1024]{2,1,0:T(8,128)(2,1)S(1)}, bf16[2,256,1024]{2,1,0:T(8,128)(2,1)S(1)}, u32[]{:S(2)}, u32[]{:S(2)}) %collective-permute-start.1) | collective-permute-done | bytes 1048608 | tf_op jit(solution)/shard_map/ppermute | solution.py:235
  27.4 1.0 copy-done.5
  28.4 5.3 %pack_rows.4 = bf16[640,2048]{1,0:T(8,128)(2,1)} custom-call(s32[1]{0:T(128)} %bitcast.5.place_ref, s32[640,1]{1,0:T(8,128)} %sub.63.refs_0_, s32[640,1]{1,0:T(8,128)} %sub.64.refs_1_, bf16[3,256,4096]{2,1,0:T(8,128)(2,1)} %refs_2_.5, bf16[2,256,1024]{2,1,0:T(8,128)(2,1)} %copy-done.5), custom_call_target="tpu_custom_call" | custom-call | flops 1342177280 | bytes 4718592 | tf_op jit(solution)/shard_map/pack_rows/pallas_call | solution.py:47
  33.7 7.4 %all-to-all-start.1 = ((bf16[16,40,2048]{2,1,0:T(8,128)(2,1)}), bf16[16,40,2048]{2,1,0:T(8,128)(2,1)S(1)}, u32[]{:S(2)}, u32[]{:S(2)}) async-start(bf16[16,40,2048]{2,1,0:T(8,128)(2,1)} %bitcast.21), calls=%async_computation.1 | async-start | bytes 5242880 | tf_op jit(solution)/shard_map/all_to_all | solution.py:252
  41.1 1.2 collective-permute-start.2
  42.4 23.5 %collective-permute-done.2.refs_3_ = bf16[2,256,1024]{2,1,0:T(8,128)(2,1)} collective-permute-done((bf16[2,256,1024]{2,1,0:T(8,128)(2,1)}, bf16[2,256,1024]{2,1,0:T(8,128)(2,1)}, u32[]{:S(2)}, u32[]{:S(2)}) %collective-permute-start.2) | collective-permute-done | bytes 1048608 | tf_op jit(solution)/shard_map/ppermute | solution.py:235
  65.8 5.4 %pack_rows.5 = bf16[640,2048]{1,0:T(8,128)(2,1)} custom-call(s32[1]{0:T(128)} %bitcast.5.place_ref, s32[640,1]{1,0:T(8,128)} %sub.63.refs_0_, s32[640,1]{1,0:T(8,128)} %sub.64.refs_1_, bf16[3,256,4096]{2,1,0:T(8,128)(2,1)} %refs_2_.5, bf16[2,256,1024]{2,1,0:T(8,128)(2,1)} %collective-permute-done.2.refs_3_), custom_call_target="tpu_custom_call" | custom-call | flops 1342177280 | bytes 4718592 | tf_op jit(solution)/shard_map/pack_rows/pallas_call | solution.py:47
  71.2 28.6 %all-to-all-done.1 = bf16[16,40,2048]{2,1,0:T(8,128)(2,1)S(1)} async-done(((bf16[16,40,2048]{2,1,0:T(8,128)(2,1)}), bf16[16,40,2048]{2,1,0:T(8,128)(2,1)S(1)}, u32[]{:S(2)}, u32[]{:S(2)}) %all-to-all-start.1) | async-done | bytes 2621472 | tf_op jit(solution)/shard_map/all_to_all | solution.py:252
  99.8 1.5 copy-done
  101.2 4.9 %all-to-all-start.2 = ((bf16[16,40,2048]{2,1,0:T(8,128)(2,1)}), bf16[16,40,2048]{2,1,0:T(8,128)(2,1)}, u32[]{:S(2)}, u32[]{:S(2)}) async-start(bf16[16,40,2048]{2,1,0:T(8,128)(2,1)} %bitcast.19), calls=%async_computation.2 | async-start | bytes 5242880 | tf_op jit(solution)/shard_map/all_to_all | solution.py:252
  106.2 0.0 copy-start.10
  106.2 1.7 slice_select_fusion.2
  107.8 1.3 collective-permute-start
  109.1 0.0 copy-done.11
  109.1 0.2 reduce-window.9
  109.3 0.6 fusion
  110.0 0.1 convert_reduce_fusion
  110.0 0.6 slice.38
  110.6 0.1 copy.34.seg_col_ref
  110.8 0.7 reshape_squeeze.2.land_ref
  112.1 1.4 compare_convert_fusion
  113.5 5.6 %unpack_keys_values.2 = (bf16[512,1024]{1,0:T(8,128)(2,1)}, bf16[512,1024]{1,0:T(8,128)(2,1)}, bf16[1024,128]{1,0:T(8,128)(2,1)}) custom-call(s32[1,640]{1,0:T(1,128)} %reshape_squeeze.2.land_ref, s32[512,1]{1,0:T(8,128)} %get-tuple-element.21.tail_ref, bf16[640,2048]{1,0:T(8,128)(2,1)} %bitcast.17, bf16[640,2048]{1,0:T(8,128)(2,1)} %bitcast.18), custom_call_target="tpu_custom_call" | custom-call | flops 1476395008 | bytes 4718592 | tf_op jit(solution)/shard_map/unpack_keys_values/pallas_call | solution.py:96
  119.1 45.8 %all-to-all-done.2 = bf16[16,40,2048]{2,1,0:T(8,128)(2,1)} async-done(((bf16[16,40,2048]{2,1,0:T(8,128)(2,1)}), bf16[16,40,2048]{2,1,0:T(8,128)(2,1)}, u32[]{:S(2)}, u32[]{:S(2)}) %all-to-all-start.2) | async-done | bytes 2621472 | tf_op jit(solution)/shard_map/all_to_all | solution.py:252
  164.9 5.6 %unpack_keys_values.3 = (bf16[512,1024]{1,0:T(8,128)(2,1)}, bf16[512,1024]{1,0:T(8,128)(2,1)}, bf16[1024,128]{1,0:T(8,128)(2,1)}) custom-call(s32[1,640]{1,0:T(1,128)} %reshape_squeeze.2.land_ref, s32[512,1]{1,0:T(8,128)} %get-tuple-element.21.tail_ref, bf16[640,2048]{1,0:T(8,128)(2,1)} %bitcast.12.keys_ref.values_ref, ...), custom_call_target="tpu_custom_call" | custom-call | flops 1476395008 | bytes 4718592 | tf_op jit(solution)/shard_map/unpack_keys_values/pallas_call | solution.py:96
  170.5 1.8 pad_maximum_fusion.2
  172.3 4.9 %all-to-all-start.3 = ((bf16[16,128,128]{2,1,0:T(8,128)(2,1)}), bf16[16,128,128]{2,1,0:T(8,128)(2,1)S(1)}, u32[]{:S(2)}, u32[]{:S(2)}) async-start(bf16[16,128,128]{2,1,0:T(8,128)(2,1)} %bitcast.13), calls=%async_computation.3 | async-start | bytes 1048576 | tf_op jit(solution)/shard_map/all_to_all | solution.py:129
  177.2 0.0 collective-permute-done.refs_3_
  177.2 0.0 copy-start.4
  177.2 1.0 copy-done.4
  178.2 5.3 %pack_rows.3 = bf16[640,2048]{1,0:T(8,128)(2,1)} custom-call(s32[1]{0:T(128)} %bitcast.5.place_ref, s32[640,1]{1,0:T(8,128)} %sub.63.refs_0_, s32[640,1]{1,0:T(8,128)} %sub.64.refs_1_, bf16[3,256,4096]{2,1,0:T(8,128)(2,1)} %refs_2_.5, bf16[1,256,2048]{2,1,0:T(8,128)(2,1)} %copy-done.4), custom_call_target="tpu_custom_call" | custom-call | flops 1342177280 | bytes 4718592 | tf_op jit(solution)/shard_map/pack_rows/pallas_call | solution.py:47
  183.5 7.3 %all-to-all-done.3.updates_ref = bf16[16,128,128]{2,1,0:T(8,128)(2,1)S(1)} async-done(((bf16[16,128,128]{2,1,0:T(8,128)(2,1)}), bf16[16,128,128]{2,1,0:T(8,128)(2,1)S(1)}, u32[]{:S(2)}, u32[]{:S(2)}) %all-to-all-start.3) | async-done | bytes 524320 | tf_op jit(solution)/shard_map/all_to_all | solution.py:129
  190.8 0.8 copy-done.2
  191.6 5.0 %all-to-all-start = ((bf16[16,40,2048]{2,1,0:T(8,128)(2,1)}), bf16[16,40,2048]{2,1,0:T(8,128)(2,1)S(1)}, u32[]{:S(2)}, u32[]{:S(2)}) async-start(bf16[16,40,2048]{2,1,0:T(8,128)(2,1)} %bitcast.20), calls=%async_computation | async-start | bytes 5242880 | tf_op jit(solution)/shard_map/all_to_all | solution.py:252
  196.6 0.1 convert_reduce_fusion.1
  196.7 0.1 slice_compare_fusion
  196.8 0.6 pad_convert_fusion.keep_ref
  197.4 2.6 carry_states.1
  200.0 55.3 %all-to-all-done = bf16[16,40,2048]{2,1,0:T(8,128)(2,1)S(1)} async-done(((bf16[16,40,2048]{2,1,0:T(8,128)(2,1)}), bf16[16,40,2048]{2,1,0:T(8,128)(2,1)S(1)}, u32[]{:S(2)}, u32[]{:S(2)}) %all-to-all-start) | async-done | bytes 2621472 | tf_op jit(solution)/shard_map/all_to_all | solution.py:252
  255.3 4.9 %all-to-all-start.4 = ((bf16[16,128,128]{2,1,0:T(8,128)(2,1)}), bf16[16,128,128]{2,1,0:T(8,128)(2,1)S(1)}, u32[]{:S(2)}, u32[]{:S(2)}) async-start(bf16[16,128,128]{2,1,0:T(8,128)(2,1)} %carry_states.1), calls=%async_computation.4 | async-start | bytes 1048576 | tf_op jit(solution)/shard_map/all_to_all | solution.py:144
  260.2 4.7 %pad_maximum_fusion = (bf16[512,2048]{1,0:T(8,128)(2,1)}, bf16[512,2048]{1,0:T(8,128)(2,1)}) fusion(bf16[512,1024]{1,0:T(8,128)(2,1)} %get-tuple-element.12, bf16[512,1024]{1,0:T(8,128)(2,1)} %get-tuple-element.11, bf16[512,1024]{1,0:T(8,128)(2,1)} %get-tuple-element.14, bf16[512,1024]{1,0:T(8,128)(2,1)} %get-tuple-element.13), kind=kLoop, calls=%fused_computation | loop fusion | flops 8388608 | bytes 8388608 | tf_op jit(solution)/shard_map/concatenate | solution.py:284
  264.9 8.8 %all-to-all-done.4 = bf16[16,128,128]{2,1,0:T(8,128)(2,1)S(1)} async-done(((bf16[16,128,128]{2,1,0:T(8,128)(2,1)}), bf16[16,128,128]{2,1,0:T(8,128)(2,1)S(1)}, u32[]{:S(2)}, u32[]{:S(2)}) %all-to-all-start.4) | async-done | bytes 524320 | tf_op jit(solution)/shard_map/all_to_all | solution.py:144
  273.8 0.8 copy-done.6
  274.6 14.2 %attend.1 = bf16[512,2048]{1,0:T(8,128)(2,1)} custom-call(s32[1,640]{1,0:T(1,128)} %reshape_squeeze.2.land_ref, s32[512,1]{1,0:T(8,128)} %copy-done.3, s32[1,512]{1,0:T(1,128)} %bitcast.25, s32[512,1]{1,0:T(8,128)} %get-tuple-element.22.carried_mask_ref, f32[1,2048]{1,0:T(1,128)} %bitcast.27, bf16[640,2048]{1,0:T(8,128)(2,1)} %bitcast.22, ...), custom_call_target="tpu_custom_call" | custom-call | flops 3758096384 | bytes 8912896 | tf_op jit(solution)/shard_map/attend/pallas_call | solution.py:195
  (20 shorter events, 0.1 us)
Async XLA Ops:
  0.0 4.6 %copy-start.9 = (s32[1,16,40]{2,1,0:T(8,128)S(1)}, s32[1,16,40]{2,1,0:T(8,128)}, u32[]{:S(2)}) copy-start(s32[1,16,40]{2,1,0:T(8,128)} %param.6) | copy-start | bytes 7684
  3.4 24.0 %collective-permute-start.1 = (bf16[2,256,1024]{2,1,0:T(8,128)(2,1)S(1)}, bf16[2,256,1024]{2,1,0:T(8,128)(2,1)S(1)}, u32[]{:S(2)}, u32[]{:S(2)}) collective-permute-start(bf16[2,256,1024]{2,1,0:T(8,128)(2,1)S(1)} %get-tuple-element.19), channel_id=1, source_target_pairs={{0,1},{1,0},{2,3},{3,2},{4,5},{5,4},{6,7},{7,6},{8,9},{9,8},{10,11... | collective-permute-start | bytes 3145736 | tf_op jit(solution)/shard_map/ppermute | solution.py:235
  27.4 1.0 copy-start.5
  33.7 66.1 %all-to-all-start.1 = ((bf16[16,40,2048]{2,1,0:T(8,128)(2,1)}), bf16[16,40,2048]{2,1,0:T(8,128)(2,1)S(1)}, u32[]{:S(2)}, u32[]{:S(2)}) async-start(bf16[16,40,2048]{2,1,0:T(8,128)(2,1)} %bitcast.21), calls=%async_computation.1 | async-start | bytes 5242880 | tf_op jit(solution)/shard_map/all_to_all | solution.py:252
  41.1 24.7 %collective-permute-start.2 = (bf16[2,256,1024]{2,1,0:T(8,128)(2,1)}, bf16[2,256,1024]{2,1,0:T(8,128)(2,1)}, u32[]{:S(2)}, u32[]{:S(2)}) collective-permute-start(bf16[2,256,1024]{2,1,0:T(8,128)(2,1)} %get-tuple-element.20), channel_id=1, source_target_pairs={{0,1},{1,0},{2,3},{3,2},{4,5},{5,4},{6,7},{7,6},{8,9},{9,8},{10,11... | collective-permute-start | bytes 3145736 | tf_op jit(solution)/shard_map/ppermute | solution.py:235
  99.8 1.5 copy-start
  101.2 63.7 %all-to-all-start.2 = ((bf16[16,40,2048]{2,1,0:T(8,128)(2,1)}), bf16[16,40,2048]{2,1,0:T(8,128)(2,1)}, u32[]{:S(2)}, u32[]{:S(2)}) async-start(bf16[16,40,2048]{2,1,0:T(8,128)(2,1)} %bitcast.19), calls=%async_computation.2 | async-start | bytes 5242880 | tf_op jit(solution)/shard_map/all_to_all | solution.py:252
  106.1 3.0 %copy-start.11 = (s32[4]{0:T(128)S(1)}, s32[4]{0:T(128)}, u32[]{:S(2)}) copy-start(s32[4]{0:T(128)} %param.8) | copy-start | bytes 52
  106.2 4.6 %copy-start.10 = (s32[1,16,40]{2,1,0:T(8,128)S(1)}, s32[1,16,40]{2,1,0:T(8,128)}, u32[]{:S(2)}) copy-start(s32[1,16,40]{2,1,0:T(8,128)} %param.7) | copy-start | bytes 7684
  107.8 69.4 %collective-permute-start = (bf16[1,256,2048]{2,1,0:T(8,128)(2,1)S(1)}, bf16[1,256,2048]{2,1,0:T(8,128)(2,1)S(1)}, u32[]{:S(2)}, u32[]{:S(2)}) collective-permute-start(bf16[1,256,2048]{2,1,0:T(8,128)(2,1)S(1)} %slice_select_fusion.2), channel_id=1, source_target_pairs={{0,1},{1,0},{2,3},{3,2},{4,5},{5,4},{6,7},{7,6},{8,9},{9,8},{10,11... | collective-permute-start | bytes 3145736 | tf_op jit(solution)/shard_map/ppermute | solution.py:235
  110.0 9.0 %copy-start.8 = (s32[512]{0:T(512)}, s32[512]{0:T(512)S(1)}, u32[]{:S(2)}) copy-start(s32[512]{0:T(512)S(1)} %broadcast_add_fusion) | copy-start | bytes 6148
  110.8 8.3 %copy-start.3 = (s32[512,1]{1,0:T(8,128)}, s32[512,1]{1,0:T(8,128)S(1)}, u32[]{:S(2)}) copy-start(s32[512,1]{1,0:T(8,128)S(1)} %copy.34.seg_col_ref) | copy-start | bytes 6148
  164.9 5.6 %copy-start.7 = (bf16[1024,128]{1,0:T(8,128)(2,1)S(1)}, bf16[1024,128]{1,0:T(8,128)(2,1)}, u32[]{:S(2)}) copy-start(bf16[1024,128]{1,0:T(8,128)(2,1)} %get-tuple-element.15) | copy-start | bytes 786436
  172.3 18.5 %all-to-all-start.3 = ((bf16[16,128,128]{2,1,0:T(8,128)(2,1)}), bf16[16,128,128]{2,1,0:T(8,128)(2,1)S(1)}, u32[]{:S(2)}, u32[]{:S(2)}) async-start(bf16[16,128,128]{2,1,0:T(8,128)(2,1)} %bitcast.13), calls=%async_computation.3 | async-start | bytes 1048576 | tf_op jit(solution)/shard_map/all_to_all | solution.py:129
  177.2 1.0 copy-start.4
  190.8 0.8 copy-start.2
  191.6 63.6 %all-to-all-start = ((bf16[16,40,2048]{2,1,0:T(8,128)(2,1)}), bf16[16,40,2048]{2,1,0:T(8,128)(2,1)S(1)}, u32[]{:S(2)}, u32[]{:S(2)}) async-start(bf16[16,40,2048]{2,1,0:T(8,128)(2,1)} %bitcast.20), calls=%async_computation | async-start | bytes 5242880 | tf_op jit(solution)/shard_map/all_to_all | solution.py:252
  255.3 9.7 %copy-start.1 = (bf16[16,40,2048]{2,1,0:T(8,128)(2,1)}, bf16[16,40,2048]{2,1,0:T(8,128)(2,1)S(1)}, u32[]{:S(2)}) copy-start(bf16[16,40,2048]{2,1,0:T(8,128)(2,1)S(1)} %all-to-all-done) | copy-start | bytes 7864324
  255.3 18.5 %all-to-all-start.4 = ((bf16[16,128,128]{2,1,0:T(8,128)(2,1)}), bf16[16,128,128]{2,1,0:T(8,128)(2,1)S(1)}, u32[]{:S(2)}, u32[]{:S(2)}) async-start(bf16[16,128,128]{2,1,0:T(8,128)(2,1)} %carry_states.1), calls=%async_computation.4 | async-start | bytes 1048576 | tf_op jit(solution)/shard_map/all_to_all | solution.py:144
  273.8 0.8 copy-start.6

commit v2 on v1

--- a/solution.py
+++ b/solution.py
@@ -1,4 +1,4 @@
-import functools
+import math
 
 import jax
 import jax.numpy as jnp
@@ -32,9 +32,8 @@
     out_ref[...] = total.astype(out_ref.dtype)
 
 
-def pack_rows(place, picks, sources, planes, columns):
+def pack_rows(place, picks, sources, planes, columns, width):
     slots = picks[0].shape[0]
-    width = min(columns, 512)
     blocks = columns // width
     lens = [array.shape[1] for array, _, _ in sources]
 
@@ -64,7 +63,9 @@
     )(place, *picks, *[array for array, _, _ in sources])
 
 
-def unpack_kernel(land_ref, tail_ref, keys_ref, values_ref, keys_out, values_out, update_ref, order):
+def unpack_kernel(land_ref, tail_ref, keys_ref, values_ref, *refs):
+    keys_out, values_out, update_ref, order = refs[-4:]
+
     @pl.when(pl.program_id(0) == 0)
     def _():
         rows = lax.broadcasted_iota(jnp.int32, order.shape, 0)
@@ -84,66 +85,129 @@
             values[:, columns],
             (((0,), (0,)), ((), ())),
             preferred_element_type=jnp.float32,
-        ).astype(update_ref.dtype)
-
-
-def unpack_keys_values(arrived, land_row, tail, tok_rows):
+        )
+
+
+def unpack_keys_values(arrived, land_row, tail, tok_rows, start, mine, filled):
     slots, columns = arrived.shape[0], arrived.shape[1] // 2
     width = min(columns, 2 * HEAD_DIM)
-    blocks = columns // width
-    packed = jax.ShapeDtypeStruct((tok_rows, columns), arrived.dtype)
-    column_spec = pl.BlockSpec((tok_rows, width), lambda j: (0, j))
+    blocks, first = columns // width, start // width
+    packed = jax.ShapeDtypeStruct((tok_rows, mine), arrived.dtype)
+    column_spec = pl.BlockSpec((tok_rows, width), lambda j: (0, first + j))
     return pl.pallas_call(
         unpack_kernel,
-        out_shape=(packed, packed, jax.ShapeDtypeStruct((columns, HEAD_DIM), jnp.bfloat16)),
+        out_shape=(packed, packed, jax.ShapeDtypeStruct((mine, HEAD_DIM), jnp.float32)),
         grid=(blocks,),
         in_specs=[
             pl.BlockSpec((1, slots), lambda j: (0, 0)),
             pl.BlockSpec((tok_rows, 1), lambda j: (0, 0)),
             pl.BlockSpec((slots, width), lambda j: (0, j)),
             pl.BlockSpec((slots, width), lambda j: (0, blocks + j)),
-        ],
-        out_specs=(column_spec, column_spec, pl.BlockSpec((width, HEAD_DIM), lambda j: (j, 0))),
+        ]
+        + [pl.BlockSpec(memory_space=pl.ANY) for _ in filled],
+        out_specs=(
+            column_spec,
+            column_spec,
+            pl.BlockSpec((width, HEAD_DIM), lambda j: (first + j, 0)),
+        ),
         scratch_shapes=[pltpu.VMEM((tok_rows, slots), jnp.bfloat16)],
+        input_output_aliases={4 + number: number for number in range(len(filled))},
         cost_estimate=pl.CostEstimate(
             flops=2 * tok_rows * columns * (2 * slots + HEAD_DIM),
             bytes_accessed=4 * columns * (slots + tok_rows),
             transcendentals=0,
         ),
         name="unpack_keys_values",
-    )(land_row, tail, arrived, arrived)
-
-
-def carry_kernel(keep_ref, updates_ref, carried_ref):
-    count = updates_ref.shape[0]
-    state = jnp.zeros(updates_ref.shape[1:], jnp.float32)
-    carried_ref[0] = state.astype(carried_ref.dtype)
-    for block in range(1, count):
-        state = jnp.where(keep_ref[block] != 0, state, 0.0) + updates_ref[block - 1].astype(jnp.float32)
-        carried_ref[block] = state.astype(carried_ref.dtype)
-
-
-def carry_states(update, keep):
-    seq_count = lax.axis_size("seq")
-    share = update.shape[0] // seq_count
-    updates = lax.all_to_all(update, "seq", split_axis=0, concat_axis=0, tiled=True)
-    states = pl.pallas_call(
-        carry_kernel,
-        out_shape=jax.ShapeDtypeStruct((seq_count, share, HEAD_DIM), update.dtype),
+    )(land_row, tail, arrived, arrived, *filled)
+
+
+def sum_kernel(take_ref, *refs):
+    count = take_ref.shape[1]
+    pieces, outs = refs[:count], refs[count:]
+    number = 0
+    for out in outs:
+        for part in range(out.shape[0]):
+            total = jnp.zeros(out.shape[1:], jnp.float32)
+            for piece in range(count):
+                wanted = take_ref[number, piece] != 0
+                total = total + jnp.where(wanted, pieces[piece][...], 0.0)
+            out[part] = total
+            number += 1
+
+
+def sum_pieces(take, pieces, counts):
+    rows = pieces[0].shape[0]
+    step = math.gcd(rows, 128)
+    return pl.pallas_call(
+        sum_kernel,
+        out_shape=tuple(jax.ShapeDtypeStruct((n, rows, HEAD_DIM), jnp.float32) for n in counts),
         grid_spec=pltpu.PrefetchScalarGridSpec(
             num_scalar_prefetch=1,
-            grid=(1,),
-            in_specs=[pl.BlockSpec((seq_count, share, HEAD_DIM), lambda i, keep_ref: (0, 0, 0))],
-            out_specs=pl.BlockSpec((seq_count, share, HEAD_DIM), lambda i, keep_ref: (0, 0, 0)),
+            grid=(rows // step,),
+            in_specs=[pl.BlockSpec((step, HEAD_DIM), lambda i, take_ref: (i, 0)) for _ in pieces],
+            out_specs=tuple(
+                pl.BlockSpec((n, step, HEAD_DIM), lambda i, take_ref: (0, i, 0)) for n in counts
+            ),
         ),
         cost_estimate=pl.CostEstimate(
-            flops=2 * update.size, bytes_accessed=4 * update.size, transcendentals=0
-        ),
-        name="carry_states",
-    )(keep, updates.reshape(seq_count, share, HEAD_DIM))
-    return lax.all_to_all(
-        states.reshape(seq_count * share, HEAD_DIM), "seq", split_axis=0, concat_axis=0, tiled=True
-    )
+            flops=sum(counts) * len(pieces) * rows * HEAD_DIM,
+            bytes_accessed=4 * (len(pieces) + sum(counts)) * rows * HEAD_DIM,
+            transcendentals=0,
+        ),
+        name="sum_pieces",
+    )(take.astype(jnp.int32), *pieces)
+
+
+def carry_states(update, last_segment):
+    seq_count, block = lax.axis_size("seq"), lax.axis_index("seq")
+    near = math.gcd(seq_count, 4)
+    far = seq_count // near
+    share = update.shape[0] // near
+    place, run = block % near, block // near
+    base = run * near
+
+    def swap(value, k):
+        return lax.ppermute(value, "seq", [(i, i ^ k) for i in range(seq_count)])
+
+    pieces = [lax.dynamic_slice_in_dim(update, place * share, share, axis=0)]
+    for k in range(1, near):
+        mine = lax.dynamic_slice_in_dim(update, (place ^ k) * share, share, axis=0)
+        pieces.append(swap(mine, k))
+    source = base + (place ^ jnp.arange(near))
+    before = jnp.maximum(source - 1, 0)
+    inside = (source[None, :] < source[:, None]) & (
+        last_segment[source][None, :] == last_segment[before][:, None]
+    )
+    whole = last_segment[source] == last_segment[base + near - 1]
+    inner, total = sum_pieces(jnp.concatenate([inside, whole[None]]), pieces, (near, 1))
+    total = total[0]
+
+    def ends(run_number):
+        return last_segment[jnp.maximum(run_number, 0) * near + near - 1]
+
+    entering, window, reach = None, total, 1
+    while reach < far:
+        shifted = lax.ppermute(
+            window, "seq", [(i, i + reach * near) for i in range(seq_count - reach * near)]
+        )
+        same_start = (run >= reach) & (ends(run - reach) == ends(run - 1))
+        same_end = (run >= reach) & (ends(run - reach) == ends(run))
+        shifted_in = jnp.where(same_start, shifted, 0.0)
+        entering = shifted_in if entering is None else entering + shifted_in
+        window = window + jnp.where(same_end, shifted, 0.0)
+        reach *= 2
+    handed = []
+    for k in range(near):
+        state = inner[k]
+        if entering is not None:
+            same = (run >= 1) & (last_segment[before[k]] == ends(run - 1))
+            state = state + jnp.where(same, entering, 0.0)
+        handed.append(state if k == 0 else swap(state, k))
+    stacked = jnp.stack(handed)
+    return [
+        lax.dynamic_index_in_dim(stacked, place ^ number, axis=0, keepdims=False)
+        for number in range(near)
+    ]
 
 
 def attend_kernel(
@@ -164,6 +228,8 @@
     query = jnp.dot(order[...], query_ref[...], preferred_element_type=jnp.float32).astype(
         keys_ref.dtype
     )
+    state_high = states_ref[...].astype(query.dtype)
+    state_low = (states_ref[...] - state_high.astype(jnp.float32)).astype(query.dtype)
     half = tok_rows // 2
     for part in range(query.shape[1] // HEAD_DIM):
         columns = slice(part * HEAD_DIM, (part + 1) * HEAD_DIM)
@@ -180,8 +246,8 @@
                 weights, values_ref[:reach, columns], preferred_element_type=jnp.float32
             )
             carried_term = jnp.dot(
-                queries, states_ref[columns, :], preferred_element_type=jnp.float32
-            )
+                queries, state_high[columns], preferred_element_type=jnp.float32
+            ) + jnp.dot(queries, state_low[columns], preferred_element_type=jnp.float32)
             raw_out = local_term + jnp.where(carried_mask_ref[rows, :] != 0, carried_term, 0.0)
             inv_rms = lax.rsqrt(jnp.mean(raw_out * raw_out, axis=1, keepdims=True) + norm_eps)
             out_ref[rows, columns] = (raw_out * inv_rms * gain_ref[:, columns]).astype(out_ref.dtype)
@@ -227,6 +293,7 @@
     rows = qkv.shape[1]
     mine = qkv.shape[2] // head_count
     slots = send_rows.reshape(-1, 1)
+    width = math.gcd(math.gcd(columns, start), math.gcd(mine, 512))
     part = lax.slice_in_dim(qkv, plane_start, plane_start + planes, axis=0)
     if head_count == 2:
         low = part[:, :, start : start + columns]
@@ -247,7 +314,7 @@
         picks = (slots,)
         sources = ((incoming, 0, lambda at, width: 0),)
     outgoing = pack_rows(
-        jnp.reshape(place, (1,)).astype(jnp.int32), picks, sources, planes, columns
+        jnp.reshape(place, (1,)).astype(jnp.int32), picks, sources, planes, columns, width
     )
     return lax.all_to_all(outgoing, "seq", split_axis=0, concat_axis=0, tiled=True)
 
@@ -257,7 +324,6 @@
     block = lax.axis_index("seq")
     tok_rows = qkv.shape[1] * head_count
     columns = qkv.shape[2] // head_count
-    half = columns // 2
 
     req_ends = jnp.cumsum(req_lengths)
     req_starts = req_ends - req_lengths
@@ -267,28 +333,24 @@
     last_rows = (jnp.arange(seq_count, dtype=jnp.int32) + 1) * tok_rows - 1
     last_segment = jnp.sum((req_starts[None, :] <= last_rows[:, None]).astype(jnp.int32), axis=1) - 1
     prev_segment = jnp.sum((req_starts < first_row).astype(jnp.int32)) - 1
-    keep = jnp.concatenate(
-        [jnp.zeros((2,), jnp.int32), (last_segment[1:-1] == last_segment[:-2]).astype(jnp.int32)]
-    )
     carried_mask = (segment == prev_segment).astype(jnp.int32)[:, None]
     tail = (segment == segment[tok_rows - 1]).astype(jnp.int32)[:, None]
     land_row = recv_pos[0].reshape(1, -1)
     gain = norm_gain.reshape(1, -1)
 
-    arrived = [send_packed(qkv, send_rows[0], KEYS, 2, start, half) for start in (0, half)]
+    head_share = columns // HEAD_DIM
+    first = max(1, 3 * head_share // 16) * 2 * HEAD_DIM
+    arrived = []
+    for start, size in ((0, first), (first, columns - first)):
+        arrived.append((start, send_packed(qkv, send_rows[0], KEYS, 2, start, size)))
     query = send_packed(qkv, send_rows[0], QUERY, 1, 0, columns)
-    keys, values, updates = zip(*[unpack_keys_values(part, land_row, tail, tok_rows) for part in arrived])
-    states = carry_states(jnp.concatenate(updates, axis=0), keep)
+    filled = ()
+    for start, part in arrived:
+        filled = unpack_keys_values(part, land_row, tail, tok_rows, start, columns, filled)
+    keys, values, update = filled
+    states = jnp.concatenate(carry_states(update, last_segment), axis=0)
     return attend(
-        query,
-        jnp.concatenate(keys, axis=1),
-        jnp.concatenate(values, axis=1),
-        states,
-        land_row,
-        segment[:, None],
-        segment[None, :],
-        carried_mask,
-        gain,
+        query, keys, values, states, land_row, segment[:, None], segment[None, :], carried_mask, gain
     )
 
 

time: 292 us -> 281 us (0.962)
  waiting for transfers between devices: 190 us -> 148 us
  between operations: 0.74 us -> 16.5 us
  starting transfers between devices: 30.9 us -> 37.2 us
  Pallas kernels: 44 us -> 50.2 us
  local copies, waits for them, and re-layouts: 8.17 us -> 13.5 us
    all_to_all x3, waiting for transfers between devices: 130 us -> 42.5 us  [send_packed(): lax.all_to_all(outgoing, 'seq', split_axis=0, concat_axis=0, tiled=True)]
    ppermute x0 -> x8, waiting for transfers between devices: none -> 38.1 us  [the longest x6 29.6 us: swap(): return lax.ppermute(value, 'seq', [(i, i ^ k) for i in range(seq_count)])]
    ppermute x3, waiting for transfers between devices: 44.5 us -> 67.7 us  [send_packed(): incoming = lax.ppermute(outgoing, 'head', [(0, 1), (1, 0)])]
    all_to_all x2 -> x0, waiting for transfers between devices: 16.1 us -> none  [the longest x1 8.85 us: carry_states(): lax.all_to_all(states.reshape(seq_count * share, HEAD_DIM), 'seq', split_...]
    ppermute x0 -> x8, starting transfers between devices: none -> 16.1 us  [the longest x2 10.7 us: carry_states(): lax.ppermute(window, 'seq', [(i, i + reach * near) for i in range(seq_cou...]
    all_to_all x2 -> x0, starting transfers between devices: 9.81 us -> none  [the longest x1 4.91 us: carry_states(): lax.all_to_all(states.reshape(seq_count * share, HEAD_DIM), 'seq', split_...]
    concatenate x3 -> x1, other arithmetic: 7.1 us -> 1.05 us  [on_device(): states = jnp.concatenate(carry_states(update, last_segment), axis=0)]
    pallas_call x3, Pallas kernels: 16 us -> 20.5 us  [pack_rows(): pl.pallas_call(pack_kernel, out_shape=jax.ShapeDtypeStruct((slots, planes...]
  transfers between devices with their start and end apart: 8 -> 14, of which waited for: 7 -> 11; matrix products, arithmetic and copies ran while one was open for 5% -> 7% of each run, Pallas kernels for 8% -> 11%
where the time goes in v2:
time: 281 us; the launch traced here: 279 us
  waiting for transfers between devices  148 us (53%)
  Pallas kernels  50.2 us (18%)
  starting transfers between devices  37.2 us (13%)
  between operations  16.5 us (6%)
  local copies, waits for them, and re-layouts  13.5 us (5%)
  other arithmetic  13 us (5%)
    ppermute x3, waiting for transfers between devices, send_packed(): incoming = lax.ppermute(outgoing, 'head', [(0, 1), (1, 0)])  67.7 us
    all_to_all x3, waiting for transfers between devices, send_packed(): lax.all_to_all(outgoing, 'seq', split_axis=0, concat_axis=0, tiled=True)  42.5 us
    ppermute x6, waiting for transfers between devices, swap(): return lax.ppermute(value, 'seq', [(i, i ^ k) for i in range(seq_count)])  29.6 us
    pallas_call x3, Pallas kernels, pack_rows(): pl.pallas_call(pack_kernel, out_shape=jax.ShapeDtypeStruct((slots, planes...  20.5 us
    all_to_all x3, starting transfers between devices, send_packed(): lax.all_to_all(outgoing, 'seq', split_axis=0, concat_axis=0, tiled=True)  17.2 us
    pallas_call x1, Pallas kernels, attend(): pl.pallas_call(attend_kernel, out_shape=jax.ShapeDtypeStruct((tok_rows, c...  14 us
    pallas_call x2, Pallas kernels, unpack_keys_values(): pl.pallas_call(unpack_kernel, out_shape=(packed, packed, jax.ShapeDtypeSt...  11.4 us
    ppermute x2, starting transfers between devices, carry_states(): lax.ppermute(window, 'seq', [(i, i + reach * near) for i in range(seq_cou...  10.7 us
  transfers between devices with their start and end apart: 14, of which 11 were waited for; matrix products, arithmetic and copies ran while one was open for 7% of the time, Pallas kernels for 11%

profile of v2, /device:TPU:11, one launch (start us, length us, event | category | flops | bytes accessed | tf_op | source)
XLA Modules:
  0.0 278.5 jit_solution(8141166309478954061)
XLA Ops:
  0.0 1.5 slice_select_fusion.2
  1.5 1.3 collective-permute-start.2
  2.8 0.9 sub.113.refs_0_
  3.6 0.9 sub.114.refs_1_
  4.5 15.4 %collective-permute-done.2.refs_3_ = bf16[2,256,768]{2,1,0:T(8,128)(2,1)S(1)} collective-permute-done((bf16[2,256,768]{2,1,0:T(8,128)(2,1)S(1)}, bf16[2,256,768]{2,1,0:T(8,128)(2,1)S(1)}, u32[]{:S(2)}, u32[]{:S(2)}) %collective-permute-start.2) | collective-permute-done | bytes 786464 | tf_op jit(solution)/shard_map/ppermute | solution.py:302
  20.0 0.9 copy-done.5
  20.8 6.0 %pack_rows.5 = bf16[640,1536]{1,0:T(8,128)(2,1)} custom-call(s32[1]{0:T(128)} %bitcast.5.place_ref, s32[640,1]{1,0:T(8,128)} %sub.113.refs_0_, s32[640,1]{1,0:T(8,128)} %sub.114.refs_1_, bf16[3,256,4096]{2,1,0:T(8,128)(2,1)} %refs_2_.5, bf16[2,256,768]{2,1,0:T(8,128)(2,1)} %copy-done.5), custom_call_target="tpu_custom_call" | custom-call | flops 1006632960 | bytes 3538944 | tf_op jit(solution)/shard_map/pack_rows/pallas_call | solution.py:46
  26.9 7.4 %all-to-all-start.2 = ((bf16[16,40,1536]{2,1,0:T(8,128)(2,1)}), bf16[16,40,1536]{2,1,0:T(8,128)(2,1)S(1)}, u32[]{:S(2)}, u32[]{:S(2)}) async-start(bf16[16,40,1536]{2,1,0:T(8,128)(2,1)} %bitcast.63), calls=%async_computation.2 | async-start | bytes 3932160 | tf_op jit(solution)/shard_map/all_to_all | solution.py:319
  34.3 1.9 slice_select_fusion
  36.2 1.3 collective-permute-start.1
  37.5 28.8 %collective-permute-done.1.refs_3_ = bf16[2,256,1280]{2,1,0:T(8,128)(2,1)S(1)} collective-permute-done((bf16[2,256,1280]{2,1,0:T(8,128)(2,1)S(1)}, bf16[2,256,1280]{2,1,0:T(8,128)(2,1)S(1)}, u32[]{:S(2)}, u32[]{:S(2)}) %collective-permute-start.1) | collective-permute-done | bytes 1310752 | tf_op jit(solution)/shard_map/ppermute | solution.py:302
  66.2 1.1 copy-done.2
  67.3 9.1 %pack_rows.4 = bf16[640,2560]{1,0:T(8,128)(2,1)} custom-call(s32[1]{0:T(128)} %bitcast.5.place_ref, s32[640,1]{1,0:T(8,128)} %sub.113.refs_0_, s32[640,1]{1,0:T(8,128)} %sub.114.refs_1_, bf16[3,256,4096]{2,1,0:T(8,128)(2,1)} %refs_2_.5, bf16[2,256,1280]{2,1,0:T(8,128)(2,1)} %copy-done.2), custom_call_target="tpu_custom_call" | custom-call | flops 1677721600 | bytes 5898240 | tf_op jit(solution)/shard_map/pack_rows/pallas_call | solution.py:46
  76.4 2.5 all-to-all-done.2
  78.9 1.3 copy-done.1
  80.2 4.9 %all-to-all-start.1 = ((bf16[16,40,2560]{2,1,0:T(8,128)(2,1)}), bf16[16,40,2560]{2,1,0:T(8,128)(2,1)S(1)}, u32[]{:S(2)}, u32[]{:S(2)}) async-start(bf16[16,40,2560]{2,1,0:T(8,128)(2,1)} %bitcast.61), calls=%async_computation.1 | async-start | bytes 6553600 | tf_op jit(solution)/shard_map/all_to_all | solution.py:319
  85.1 2.7 slice_select_fusion.1
  87.8 1.2 collective-permute-start
  89.0 23.5 %collective-permute-done.refs_3_ = bf16[1,256,2048]{2,1,0:T(8,128)(2,1)} collective-permute-done((bf16[1,256,2048]{2,1,0:T(8,128)(2,1)}, bf16[1,256,2048]{2,1,0:T(8,128)(2,1)}, u32[]{:S(2)}, u32[]{:S(2)}) %collective-permute-start) | collective-permute-done | bytes 1048608 | tf_op jit(solution)/shard_map/ppermute | solution.py:302
  112.5 5.4 %pack_rows.3 = bf16[640,2048]{1,0:T(8,128)(2,1)} custom-call(s32[1]{0:T(128)} %bitcast.5.place_ref, s32[640,1]{1,0:T(8,128)} %sub.113.refs_0_, s32[640,1]{1,0:T(8,128)} %sub.114.refs_1_, bf16[3,256,4096]{2,1,0:T(8,128)(2,1)} %refs_2_.5, bf16[1,256,2048]{2,1,0:T(8,128)(2,1)} %collective-permute-done.refs_3_), custom_call_target="tpu_custom_call" | custom-call | flops 1342177280 | bytes 4718592 | tf_op jit(solution)/shard_map/pack_rows/pallas_call | solution.py:46
  117.8 40.0 %all-to-all-done.1 = bf16[16,40,2560]{2,1,0:T(8,128)(2,1)S(1)} async-done(((bf16[16,40,2560]{2,1,0:T(8,128)(2,1)}), bf16[16,40,2560]{2,1,0:T(8,128)(2,1)S(1)}, u32[]{:S(2)}, u32[]{:S(2)}) %all-to-all-start.1) | async-done | bytes 3276832 | tf_op jit(solution)/shard_map/all_to_all | solution.py:319
  157.8 1.7 copy-done
  159.5 4.9 %all-to-all-start = ((bf16[16,40,2048]{2,1,0:T(8,128)(2,1)}), bf16[16,40,2048]{2,1,0:T(8,128)(2,1)}, u32[]{:S(2)}, u32[]{:S(2)}) async-start(bf16[16,40,2048]{2,1,0:T(8,128)(2,1)} %bitcast.62), calls=%async_computation | async-start | bytes 5242880 | tf_op jit(solution)/shard_map/all_to_all | solution.py:319
  164.4 0.7 fusion.4
  170.3 0.7 fusion.1
  172.6 0.7 reshape_squeeze.2.land_ref
  177.2 0.7 fusion.3
  178.0 1.4 compare_convert_fusion
  179.4 4.7 %unpack_keys_values.2 = (bf16[512,2048]{1,0:T(8,128)(2,1)}, bf16[512,2048]{1,0:T(8,128)(2,1)}, f32[2048,128]{1,0:T(8,128)}) custom-call(s32[1,640]{1,0:T(1,128)} %reshape_squeeze.2.land_ref, s32[512,1]{1,0:T(8,128)} %get-tuple-element.38.tail_ref, bf16[640,1536]{1,0:T(8,128)(2,1)} %bitcast.59, bf16[640,1536]{1,0:T(8,128)(2,1)} %bitcast.60), custom_call_target="tpu_custom_call" | custom-call | flops 1107296256 | bytes 3538944 | tf_op jit(solution)/shard_map/unpack_keys_values/pallas_call | solution.py:97
  184.1 6.7 %unpack_keys_values.3 = (bf16[512,2048]{1,0:T(8,128)(2,1)}, bf16[512,2048]{1,0:T(8,128)(2,1)}, f32[2048,128]{1,0:T(8,128)}) custom-call(s32[1,640]{1,0:T(1,128)} %reshape_squeeze.2.land_ref, s32[512,1]{1,0:T(8,128)} %get-tuple-element.38.tail_ref, bf16[640,2560]{1,0:T(8,128)(2,1)} %bitcast.57, ...), custom_call_target="tpu_custom_call", output_to_operand_aliasing={{0}: (4, {}), {1}: (5, {}), {2}: (6, {})} | custom-call | flops 1845493760 | bytes 5898240 | tf_op jit(solution)/shard_map/unpack_keys_values/pallas_call | solution.py:97
  190.8 1.9 constant_dynamic-slice_fusion
  193.4 1.5 collective-permute-start.5
  196.2 8.3 %collective-permute-done.4.refs_2_ = f32[512,128]{1,0:T(8,128)S(1)} collective-permute-done((f32[512,128]{1,0:T(8,128)S(1)}, f32[512,128]{1,0:T(8,128)S(1)}, u32[]{:S(2)}, u32[]{:S(2)}) %collective-permute-start.4) | collective-permute-done | bytes 262176 | tf_op jit(solution)/shard_map/ppermute | solution.py:170
  204.5 9.3 %collective-permute-done.5.refs_3_ = f32[512,128]{1,0:T(8,128)S(1)} collective-permute-done((f32[512,128]{1,0:T(8,128)S(1)}, f32[512,128]{1,0:T(8,128)S(1)}, u32[]{:S(2)}, u32[]{:S(2)}) %collective-permute-start.5) | collective-permute-done | bytes 262176 | tf_op jit(solution)/shard_map/ppermute | solution.py:170
  213.8 0.7 copy-done.8
  214.5 4.2 %sum_pieces.1 = (f32[4,512,128]{2,1,0:T(8,128)}, f32[1,512,128]{2,1,0:T(8,128)}) custom-call(s32[5,4]{1,0:T(8,128)} %add_convert_fusion.take_ref, f32[512,128]{1,0:T(8,128)} %get-tuple-element.37.refs_0_, f32[512,128]{1,0:T(8,128)} %copy-done.6, f32[512,128]{1,0:T(8,128)} %copy-done.7, f32[512,128]{1,0:T(8,128)} %copy-done.8), custom_call_target="tpu_custom_call" | custom-call | flops 1310720 | bytes 2359296 | tf_op jit(solution)/shard_map/sum_pieces/pallas_call | solution.py:141
  218.8 6.7 %collective-permute-start.6 = (f32[512,128]{1,0:T(8,128)}, f32[512,128]{1,0:T(8,128)S(1)}, u32[]{:S(2)}, u32[]{:S(2)}) collective-permute-start(f32[512,128]{1,0:T(8,128)} %bitcast.64), channel_id=1, source_target_pairs={{0,8},{2,10},{4,12},{6,14},{8,16},{10,18},{12,20},{14,22},{16,24},... | collective-permute-start | bytes 786440 | tf_op jit(solution)/shard_map/ppermute | solution.py:190
  226.9 4.5 %collective-permute-done.6 = f32[512,128]{1,0:T(8,128)S(1)} collective-permute-done((f32[512,128]{1,0:T(8,128)}, f32[512,128]{1,0:T(8,128)S(1)}, u32[]{:S(2)}, u32[]{:S(2)}) %collective-permute-start.6) | collective-permute-done | bytes 262176 | tf_op jit(solution)/shard_map/ppermute | solution.py:190
  231.4 1.0 select_add_fusion.1
  232.4 4.0 %collective-permute-start.7 = (f32[512,128]{1,0:T(8,128)S(1)}, f32[512,128]{1,0:T(8,128)S(1)}, u32[]{:S(2)}, u32[]{:S(2)}) collective-permute-start(f32[512,128]{1,0:T(8,128)S(1)} %select_add_fusion.1), channel_id=1, source_target_pairs={{0,16},{2,18},{4,20},{6,22},{8,24},{10,26},{12,28},{14,30},{1,17},... | collective-permute-start | bytes 786440 | tf_op jit(solution)/shard_map/ppermute | solution.py:190
  243.0 4.0 %collective-permute-done.7 = f32[512,128]{1,0:T(8,128)S(1)} collective-permute-done((f32[512,128]{1,0:T(8,128)S(1)}, f32[512,128]{1,0:T(8,128)S(1)}, u32[]{:S(2)}, u32[]{:S(2)}) %collective-permute-start.7) | collective-permute-done | bytes 262176 | tf_op jit(solution)/shard_map/ppermute | solution.py:190
  247.0 1.0 fusion
  248.1 1.5 collective-permute-start.8
  249.6 1.7 collective-permute-start.10
  251.3 6.2 %collective-permute-done.9 = f32[512,128]{1,0:T(8,128)S(1)} collective-permute-done((f32[512,128]{1,0:T(8,128)S(1)}, f32[512,128]{1,0:T(8,128)S(1)}, u32[]{:S(2)}, u32[]{:S(2)}) %collective-permute-start.9) | collective-permute-done | bytes 262176 | tf_op jit(solution)/shard_map/ppermute | solution.py:170
  257.5 5.8 %collective-permute-done.10 = f32[512,128]{1,0:T(8,128)S(1)} collective-permute-done((f32[512,128]{1,0:T(8,128)S(1)}, f32[512,128]{1,0:T(8,128)S(1)}, u32[]{:S(2)}, u32[]{:S(2)}) %collective-permute-start.10) | collective-permute-done | bytes 262176 | tf_op jit(solution)/shard_map/ppermute | solution.py:170
  263.4 1.0 pad_maximum_fusion.1.states_ref
  264.5 14.0 %attend.1 = bf16[512,2048]{1,0:T(8,128)(2,1)} custom-call(s32[1,640]{1,0:T(1,128)} %reshape_squeeze.2.land_ref, s32[512,1]{1,0:T(8,128)} %copy-done.3, s32[1,512]{1,0:T(1,128)} %bitcast.69, s32[512,1]{1,0:T(8,128)} %get-tuple-element.39.carried_mask_ref, f32[1,2048]{1,0:T(1,128)} %bitcast.71, bf16[640,2048]{1,0:T(8,128)(2,1)} %bitcast.7.query_ref, ...), custom_call_target="tpu_custom_call" | custom-call | flops 3758096384 | bytes 8912896 | tf_op jit(solution)/shard_map/attend/pallas_call | solution.py:261
  (49 shorter events, 4.6 us)
Async XLA Ops:
  0.0 2.8 copy-start.10
  1.5 18.5 %collective-permute-start.2 = (bf16[2,256,768]{2,1,0:T(8,128)(2,1)S(1)}, bf16[2,256,768]{2,1,0:T(8,128)(2,1)S(1)}, u32[]{:S(2)}, u32[]{:S(2)}) collective-permute-start(bf16[2,256,768]{2,1,0:T(8,128)(2,1)S(1)} %slice_select_fusion.2), channel_id=1, source_target_pairs={{0,1},{1,0},{2,3},{3,2},{4,5},{5,4},{6,7},{7,6},{8,9},{9,8},{10,11... | collective-permute-start | bytes 2359304 | tf_op jit(solution)/shard_map/ppermute | solution.py:302
  20.0 0.9 copy-start.5
  26.9 52.0 %all-to-all-start.2 = ((bf16[16,40,1536]{2,1,0:T(8,128)(2,1)}), bf16[16,40,1536]{2,1,0:T(8,128)(2,1)S(1)}, u32[]{:S(2)}, u32[]{:S(2)}) async-start(bf16[16,40,1536]{2,1,0:T(8,128)(2,1)} %bitcast.63), calls=%async_computation.2 | async-start | bytes 3932160 | tf_op jit(solution)/shard_map/all_to_all | solution.py:319
  36.2 30.1 %collective-permute-start.1 = (bf16[2,256,1280]{2,1,0:T(8,128)(2,1)S(1)}, bf16[2,256,1280]{2,1,0:T(8,128)(2,1)S(1)}, u32[]{:S(2)}, u32[]{:S(2)}) collective-permute-start(bf16[2,256,1280]{2,1,0:T(8,128)(2,1)S(1)} %slice_select_fusion), channel_id=1, source_target_pairs={{0,1},{1,0},{2,3},{3,2},{4,5},{5,4},{6,7},{7,6},{8,9},{9,8},{10,11... | collective-permute-start | bytes 3932168 | tf_op jit(solution)/shard_map/ppermute | solution.py:302
  66.2 1.1 copy-start.2
  78.9 1.3 copy-start.1
  80.2 77.6 %all-to-all-start.1 = ((bf16[16,40,2560]{2,1,0:T(8,128)(2,1)}), bf16[16,40,2560]{2,1,0:T(8,128)(2,1)S(1)}, u32[]{:S(2)}, u32[]{:S(2)}) async-start(bf16[16,40,2560]{2,1,0:T(8,128)(2,1)} %bitcast.61), calls=%async_computation.1 | async-start | bytes 6553600 | tf_op jit(solution)/shard_map/all_to_all | solution.py:319
  87.8 24.7 %collective-permute-start = (bf16[1,256,2048]{2,1,0:T(8,128)(2,1)}, bf16[1,256,2048]{2,1,0:T(8,128)(2,1)}, u32[]{:S(2)}, u32[]{:S(2)}) collective-permute-start(bf16[1,256,2048]{2,1,0:T(8,128)(2,1)} %slice_select_fusion.1), channel_id=1, source_target_pairs={{0,1},{1,0},{2,3},{3,2},{4,5},{5,4},{6,7},{7,6},{8,9},{9,8},{10,11... | collective-permute-start | bytes 3145736 | tf_op jit(solution)/shard_map/ppermute | solution.py:302
  157.8 1.7 copy-start
  157.8 12.3 %copy-start.12 = (s32[4]{0:T(128)S(1)}, s32[4]{0:T(128)}, u32[]{:S(2)}) copy-start(s32[4]{0:T(128)} %param.8) | copy-start | bytes 52
  157.8 14.8 %copy-start.11 = (s32[1,16,40]{2,1,0:T(8,128)S(1)}, s32[1,16,40]{2,1,0:T(8,128)}, u32[]{:S(2)}) copy-start(s32[1,16,40]{2,1,0:T(8,128)} %param.7) | copy-start | bytes 7684
  159.5 105.0 %all-to-all-start = ((bf16[16,40,2048]{2,1,0:T(8,128)(2,1)}), bf16[16,40,2048]{2,1,0:T(8,128)(2,1)}, u32[]{:S(2)}, u32[]{:S(2)}) async-start(bf16[16,40,2048]{2,1,0:T(8,128)(2,1)} %bitcast.62), calls=%async_computation | async-start | bytes 5242880 | tf_op jit(solution)/shard_map/all_to_all | solution.py:319
  171.1 13.0 %copy-start.9 = (s32[512]{0:T(512)}, s32[512]{0:T(512)S(1)}, u32[]{:S(2)}) copy-start(s32[512]{0:T(512)S(1)} %broadcast_add_fusion) | copy-start | bytes 6148
  171.9 12.2 %copy-start.3 = (s32[512,1]{1,0:T(8,128)}, s32[512,1]{1,0:T(8,128)S(1)}, u32[]{:S(2)}) copy-start(s32[512,1]{1,0:T(8,128)S(1)} %copy.37.seg_col_ref) | copy-start | bytes 6148
  192.8 3.4 %collective-permute-start.3 = (f32[512,128]{1,0:T(8,128)S(1)}, f32[512,128]{1,0:T(8,128)S(1)}, u32[]{:S(2)}, u32[]{:S(2)}) collective-permute-start(f32[512,128]{1,0:T(8,128)S(1)} %get-tuple-element.36), channel_id=1, source_target_pairs={{0,2},{2,0},{4,6},{6,4},{8,10},{10,8},{12,14},{14,12},{16,18},{18,... | collective-permute-start | bytes 786440 | tf_op jit(solution)/shard_map/ppermute | solution.py:170
  193.2 11.4 %collective-permute-start.4 = (f32[512,128]{1,0:T(8,128)S(1)}, f32[512,128]{1,0:T(8,128)S(1)}, u32[]{:S(2)}, u32[]{:S(2)}) collective-permute-start(f32[512,128]{1,0:T(8,128)S(1)} %get-tuple-element.35), channel_id=1, source_target_pairs={{0,4},{2,6},{4,0},{6,2},{8,12},{10,14},{12,8},{14,10},{16,20},{18,... | collective-permute-start | bytes 786440 | tf_op jit(solution)/shard_map/ppermute | solution.py:170
  193.4 20.4 %collective-permute-start.5 = (f32[512,128]{1,0:T(8,128)S(1)}, f32[512,128]{1,0:T(8,128)S(1)}, u32[]{:S(2)}, u32[]{:S(2)}) collective-permute-start(f32[512,128]{1,0:T(8,128)S(1)} %get-tuple-element.34), channel_id=1, source_target_pairs={{0,6},{2,4},{4,2},{6,0},{8,14},{10,12},{12,10},{14,8},{16,22},{18,... | collective-permute-start | bytes 786440 | tf_op jit(solution)/shard_map/ppermute | solution.py:170
  196.2 17.6 %copy-start.6 = (f32[512,128]{1,0:T(8,128)}, f32[512,128]{1,0:T(8,128)S(1)}, u32[]{:S(2)}) copy-start(f32[512,128]{1,0:T(8,128)S(1)} %collective-permute-done.3.refs_1_) | copy-start | bytes 786436
  204.5 9.3 %copy-start.7 = (f32[512,128]{1,0:T(8,128)}, f32[512,128]{1,0:T(8,128)S(1)}, u32[]{:S(2)}) copy-start(f32[512,128]{1,0:T(8,128)S(1)} %collective-permute-done.4.refs_2_) | copy-start | bytes 786436
  213.8 0.7 copy-start.8
  218.8 29.3 %copy-start.4 = (f32[4,512,128]{2,1,0:T(8,128)S(1)}, f32[4,512,128]{2,1,0:T(8,128)}, u32[]{:S(2)}) copy-start(f32[4,512,128]{2,1,0:T(8,128)} %get-tuple-element.19) | copy-start | bytes 3145732
  218.8 12.6 %collective-permute-start.6 = (f32[512,128]{1,0:T(8,128)}, f32[512,128]{1,0:T(8,128)S(1)}, u32[]{:S(2)}, u32[]{:S(2)}) collective-permute-start(f32[512,128]{1,0:T(8,128)} %bitcast.64), channel_id=1, source_target_pairs={{0,8},{2,10},{4,12},{6,14},{8,16},{10,18},{12,20},{14,22},{16,24},... | collective-permute-start | bytes 786440 | tf_op jit(solution)/shard_map/ppermute | solution.py:190
  232.4 14.7 %collective-permute-start.7 = (f32[512,128]{1,0:T(8,128)S(1)}, f32[512,128]{1,0:T(8,128)S(1)}, u32[]{:S(2)}, u32[]{:S(2)}) collective-permute-start(f32[512,128]{1,0:T(8,128)S(1)} %select_add_fusion.1), channel_id=1, source_target_pairs={{0,16},{2,18},{4,20},{6,22},{8,24},{10,26},{12,28},{14,30},{1,17},... | collective-permute-start | bytes 786440 | tf_op jit(solution)/shard_map/ppermute | solution.py:190
  248.1 3.2 %collective-permute-start.8 = (f32[512,128]{1,0:T(8,128)S(1)}, f32[512,128]{1,0:T(8,128)S(1)}, u32[]{:S(2)}, u32[]{:S(2)}) collective-permute-start(f32[512,128]{1,0:T(8,128)S(1)} %get-tuple-element.27), channel_id=1, source_target_pairs={{0,2},{2,0},{4,6},{6,4},{8,10},{10,8},{12,14},{14,12},{16,18},{18,... | collective-permute-start | bytes 786440 | tf_op jit(solution)/shard_map/ppermute | solution.py:170
  249.6 7.9 %collective-permute-start.9 = (f32[512,128]{1,0:T(8,128)S(1)}, f32[512,128]{1,0:T(8,128)S(1)}, u32[]{:S(2)}, u32[]{:S(2)}) collective-permute-start(f32[512,128]{1,0:T(8,128)S(1)} %get-tuple-element.28), channel_id=1, source_target_pairs={{0,4},{2,6},{4,0},{6,2},{8,12},{10,14},{12,8},{14,10},{16,20},{18,... | collective-permute-start | bytes 786440 | tf_op jit(solution)/shard_map/ppermute | solution.py:170
  249.6 13.7 %collective-permute-start.10 = (f32[512,128]{1,0:T(8,128)S(1)}, f32[512,128]{1,0:T(8,128)S(1)}, u32[]{:S(2)}, u32[]{:S(2)}) collective-permute-start(f32[512,128]{1,0:T(8,128)S(1)} %get-tuple-element.29), channel_id=1, source_target_pairs={{0,6},{2,4},{4,2},{6,0},{8,14},{10,12},{12,10},{14,8},{16,22},{18,... | collective-permute-start | bytes 786440 | tf_op jit(solution)/shard_map/ppermute | solution.py:170

commit v3 on v2

--- a/solution.py
+++ b/solution.py
@@ -63,32 +63,57 @@
     )(place, *picks, *[array for array, _, _ in sources])
 
 
-def unpack_kernel(land_ref, tail_ref, keys_ref, values_ref, *refs):
-    keys_out, values_out, update_ref, order = refs[-4:]
+def update_kernel(tail_ref, keys_ref, values_ref, update_ref):
+    tail = tail_ref[...] != 0
+    for part in range(keys_ref.shape[1] // HEAD_DIM):
+        columns = slice(part * HEAD_DIM, (part + 1) * HEAD_DIM)
+        keys = keys_ref[:, columns]
+        update_ref[columns, :] = lax.dot_general(
+            jnp.where(tail, keys, jnp.zeros_like(keys)),
+            values_ref[:, columns],
+            (((0,), (0,)), ((), ())),
+            preferred_element_type=jnp.float32,
+        )
+
+
+def block_update(arrived, tail_slots):
+    slots, columns = arrived.shape[0], arrived.shape[1] // 2
+    width = min(columns, 2 * HEAD_DIM)
+    blocks = columns // width
+    return pl.pallas_call(
+        update_kernel,
+        out_shape=jax.ShapeDtypeStruct((columns, HEAD_DIM), jnp.float32),
+        grid=(blocks,),
+        in_specs=[
+            pl.BlockSpec((slots, 1), lambda j: (0, 0)),
+            pl.BlockSpec((slots, width), lambda j: (0, j)),
+            pl.BlockSpec((slots, width), lambda j: (0, blocks + j)),
+        ],
+        out_specs=pl.BlockSpec((width, HEAD_DIM), lambda j: (j, 0)),
+        cost_estimate=pl.CostEstimate(
+            flops=2 * slots * columns * HEAD_DIM,
+            bytes_accessed=4 * columns * (slots + HEAD_DIM),
+            transcendentals=0,
+        ),
+        name="block_update",
+    )(tail_slots, arrived, arrived)
+
+
+def unpack_kernel(land_ref, keys_ref, values_ref, *refs):
+    keys_out, values_out, order = refs[-3:]
 
     @pl.when(pl.program_id(0) == 0)
     def _():
         rows = lax.broadcasted_iota(jnp.int32, order.shape, 0)
         order[...] = jnp.where(land_ref[...] == rows, 1.0, 0.0).astype(order.dtype)
 
-    keys = jnp.dot(order[...], keys_ref[...], preferred_element_type=jnp.float32)
-    keys_out[...] = keys.astype(keys_out.dtype)
-    values = jnp.dot(order[...], values_ref[...], preferred_element_type=jnp.float32).astype(
-        values_out.dtype
-    )
-    values_out[...] = values
-    tail_keys = jnp.where(tail_ref[...] != 0, keys, 0.0).astype(values.dtype)
-    for part in range(keys.shape[1] // HEAD_DIM):
-        columns = slice(part * HEAD_DIM, (part + 1) * HEAD_DIM)
-        update_ref[columns, :] = lax.dot_general(
-            tail_keys[:, columns],
-            values[:, columns],
-            (((0,), (0,)), ((), ())),
-            preferred_element_type=jnp.float32,
-        )
-
-
-def unpack_keys_values(arrived, land_row, tail, tok_rows, start, mine, filled):
+    for source, out in ((keys_ref, keys_out), (values_ref, values_out)):
+        out[...] = jnp.dot(
+            order[...], source[...], preferred_element_type=jnp.float32
+        ).astype(out.dtype)
+
+
+def unpack_keys_values(arrived, land_row, tok_rows, start, mine, filled):
     slots, columns = arrived.shape[0], arrived.shape[1] // 2
     width = min(columns, 2 * HEAD_DIM)
     blocks, first = columns // width, start // width
@@ -96,29 +121,24 @@
     column_spec = pl.BlockSpec((tok_rows, width), lambda j: (0, first + j))
     return pl.pallas_call(
         unpack_kernel,
-        out_shape=(packed, packed, jax.ShapeDtypeStruct((mine, HEAD_DIM), jnp.float32)),
+        out_shape=(packed, packed),
         grid=(blocks,),
         in_specs=[
             pl.BlockSpec((1, slots), lambda j: (0, 0)),
-            pl.BlockSpec((tok_rows, 1), lambda j: (0, 0)),
             pl.BlockSpec((slots, width), lambda j: (0, j)),
             pl.BlockSpec((slots, width), lambda j: (0, blocks + j)),
         ]
         + [pl.BlockSpec(memory_space=pl.ANY) for _ in filled],
-        out_specs=(
-            column_spec,
-            column_spec,
-            pl.BlockSpec((width, HEAD_DIM), lambda j: (first + j, 0)),
-        ),
+        out_specs=(column_spec, column_spec),
         scratch_shapes=[pltpu.VMEM((tok_rows, slots), jnp.bfloat16)],
-        input_output_aliases={4 + number: number for number in range(len(filled))},
+        input_output_aliases={3 + number: number for number in range(len(filled))},
         cost_estimate=pl.CostEstimate(
-            flops=2 * tok_rows * columns * (2 * slots + HEAD_DIM),
+            flops=4 * tok_rows * columns * slots,
             bytes_accessed=4 * columns * (slots + tok_rows),
             transcendentals=0,
         ),
         name="unpack_keys_values",
-    )(land_row, tail, arrived, arrived, *filled)
+    )(land_row, arrived, arrived, *filled)
 
 
 def sum_kernel(take_ref, *refs):
@@ -137,7 +157,7 @@
 
 def sum_pieces(take, pieces, counts):
     rows = pieces[0].shape[0]
-    step = math.gcd(rows, 128)
+    step = rows // 2
     return pl.pallas_call(
         sum_kernel,
         out_shape=tuple(jax.ShapeDtypeStruct((n, rows, HEAD_DIM), jnp.float32) for n in counts),
@@ -287,32 +307,36 @@
     )(land_row, seg_col, seg_row, carried_mask, gain, arrived, keys, values, states)
 
 
-def send_packed(qkv, send_rows, plane_start, planes, start, columns):
+def swap_heads(qkv, plane_start, planes, start, columns):
+    head_count = lax.axis_size("head")
+    rows = qkv.shape[1]
+    mine = qkv.shape[2] // head_count
+    part = lax.slice_in_dim(qkv, plane_start, plane_start + planes, axis=0)
+    if head_count == 2:
+        low = part[:, :, start : start + columns]
+        high = part[:, :, mine + start : mine + start + columns]
+        outgoing = jnp.where(lax.axis_index("head") == 0, high, low)
+        return lax.ppermute(outgoing, "head", [(0, 1), (1, 0)])
+    split = part.reshape(planes, rows, head_count, mine)[..., start : start + columns]
+    incoming = lax.all_to_all(
+        jnp.moveaxis(split, 2, 0), "head", split_axis=0, concat_axis=0, tiled=False
+    )
+    return jnp.moveaxis(incoming, 0, 1).reshape(planes, head_count * rows, columns)
+
+
+def send_packed(qkv, incoming, send_rows, plane_start, planes, start, columns):
     head_count = lax.axis_size("head")
     place = lax.axis_index("head")
     rows = qkv.shape[1]
     mine = qkv.shape[2] // head_count
     slots = send_rows.reshape(-1, 1)
     width = math.gcd(math.gcd(columns, start), math.gcd(mine, 512))
-    part = lax.slice_in_dim(qkv, plane_start, plane_start + planes, axis=0)
+    picks, sources = (slots,), ((incoming, 0, lambda at, width: 0),)
     if head_count == 2:
-        low = part[:, :, start : start + columns]
-        high = part[:, :, mine + start : mine + start + columns]
-        outgoing = jnp.where(place == 0, high, low)
-        incoming = lax.ppermute(outgoing, "head", [(0, 1), (1, 0)])
         picks = (slots - place * rows, slots - (1 - place) * rows)
         sources = (
             (qkv, plane_start, lambda at, width: at * (mine // width) + start // width),
-            (incoming, 0, lambda at, width: 0),
-        )
-    else:
-        split = part.reshape(planes, rows, head_count, mine)[..., start : start + columns]
-        incoming = lax.all_to_all(
-            jnp.moveaxis(split, 2, 0), "head", split_axis=0, concat_axis=0, tiled=False
-        )
-        incoming = jnp.moveaxis(incoming, 0, 1).reshape(planes, head_count * rows, columns)
-        picks = (slots,)
-        sources = ((incoming, 0, lambda at, width: 0),)
+        ) + sources
     outgoing = pack_rows(
         jnp.reshape(place, (1,)).astype(jnp.int32), picks, sources, planes, columns, width
     )
@@ -334,23 +358,42 @@
     last_segment = jnp.sum((req_starts[None, :] <= last_rows[:, None]).astype(jnp.int32), axis=1) - 1
     prev_segment = jnp.sum((req_starts < first_row).astype(jnp.int32)) - 1
     carried_mask = (segment == prev_segment).astype(jnp.int32)[:, None]
-    tail = (segment == segment[tok_rows - 1]).astype(jnp.int32)[:, None]
     land_row = recv_pos[0].reshape(1, -1)
+    landing = first_row + land_row.reshape(-1, 1)
+    landing_segment = jnp.sum((req_starts[None, :] <= landing).astype(jnp.int32), axis=1, keepdims=True) - 1
+    in_tail = (land_row.reshape(-1, 1) >= 0) & (landing_segment == last_segment[block])
+    tail_slots = in_tail.astype(jnp.int32)
     gain = norm_gain.reshape(1, -1)
 
+    rows = send_rows[0]
     head_share = columns // HEAD_DIM
     first = max(1, 3 * head_share // 16) * 2 * HEAD_DIM
-    arrived = []
-    for start, size in ((0, first), (first, columns - first)):
-        arrived.append((start, send_packed(qkv, send_rows[0], KEYS, 2, start, size)))
-    query = send_packed(qkv, send_rows[0], QUERY, 1, 0, columns)
-    filled = ()
-    for start, part in arrived:
-        filled = unpack_keys_values(part, land_row, tail, tok_rows, start, columns, filled)
-    keys, values, update = filled
-    states = jnp.concatenate(carry_states(update, last_segment), axis=0)
+    second = columns - first
+    arrived = send_packed(
+        qkv, swap_heads(qkv, KEYS, 2, 0, first), rows, KEYS, 2, 0, first
+    )
+    arrived_next = send_packed(
+        qkv, swap_heads(qkv, KEYS, 2, first, second), rows, KEYS, 2, first, second
+    )
+    states = carry_states(block_update(arrived, tail_slots), last_segment)
+    filled = unpack_keys_values(arrived, land_row, tok_rows, 0, columns, ())
+    incoming = swap_heads(qkv, QUERY, 1, 0, columns)
+    incoming, states, filled, tail_slots, last_segment, segment, carried_mask = lax.optimization_barrier(
+        (incoming, states, filled, tail_slots, last_segment, segment, carried_mask)
+    )
+    query = send_packed(qkv, incoming, rows, QUERY, 1, 0, columns)
+    states += carry_states(block_update(arrived_next, tail_slots), last_segment)
+    keys, values = unpack_keys_values(arrived_next, land_row, tok_rows, first, columns, filled)
     return attend(
-        query, keys, values, states, land_row, segment[:, None], segment[None, :], carried_mask, gain
+        query,
+        keys,
+        values,
+        jnp.concatenate(states, axis=0),
+        land_row,
+        segment[:, None],
+        segment[None, :],
+        carried_mask,
+        gain,
     )
 
 

time: 281 us -> 299 us (1.064)
  the two profiles are of different devices: /device:TPU:11 before, /device:TPU:0 now
where the time goes in v3:
time: 299 us; the launch traced here: 297 us
  waiting for transfers between devices  98.1 us (33%)
  starting transfers between devices  76.7 us (26%)
  Pallas kernels  59.8 us (20%)
  between operations  23.8 us (8%)
  local copies, waits for them, and re-layouts  20.3 us (7%)
  other arithmetic  18.5 us (6%)
    ppermute x3, waiting for transfers between devices, swap_heads(): return lax.ppermute(outgoing, 'head', [(0, 1), (1, 0)])  45.4 us
    ppermute x4, starting transfers between devices, carry_states(): lax.ppermute(window, 'seq', [(i, i + reach * near) for i in range(seq_cou...  44.9 us
    ppermute x4, waiting for transfers between devices, carry_states(): lax.ppermute(window, 'seq', [(i, i + reach * near) for i in range(seq_cou...  26.5 us
    ppermute x12, waiting for transfers between devices, swap(): return lax.ppermute(value, 'seq', [(i, i ^ k) for i in range(seq_count)])  26.2 us
    pallas_call x3, Pallas kernels, pack_rows(): pl.pallas_call(pack_kernel, out_shape=jax.ShapeDtypeStruct((slots, planes...  20.5 us
    all_to_all x3, starting transfers between devices, send_packed(): lax.all_to_all(outgoing, 'seq', split_axis=0, concat_axis=0, tiled=True)  17.9 us
    pallas_call x1, Pallas kernels, attend(): pl.pallas_call(attend_kernel, out_shape=jax.ShapeDtypeStruct((tok_rows, c...  14 us
    pallas_call x2, Pallas kernels, unpack_keys_values(): pl.pallas_call(unpack_kernel, out_shape=(packed, packed), grid=(blocks,),...  10.8 us
  transfers between devices with their start and end apart: 22, of which 9 were waited for; matrix products, arithmetic and copies ran while one was open for 10% of the time, Pallas kernels for 13%

profile of v3, /device:TPU:0, one launch (start us, length us, event | category | flops | bytes accessed | tf_op | source)
XLA Modules:
  0.0 297.2 jit_solution(13824319818896040982)
XLA Ops:
  0.0 1.5 slice_select_fusion.2
  1.5 3.0 %collective-permute-start.1 = (bf16[2,256,768]{2,1,0:T(8,128)(2,1)S(1)}, bf16[2,256,768]{2,1,0:T(8,128)(2,1)S(1)}, u32[]{:S(2)}, u32[]{:S(2)}) collective-permute-start(bf16[2,256,768]{2,1,0:T(8,128)(2,1)S(1)} %slice_select_fusion.2), channel_id=1, source_target_pairs={{0,1},{1,0},{2,3},{3,2},{4,5},{5,4},{6,7},{7,6},{8,9},{9,8},{10,11... | collective-permute-start | bytes 2359304 | tf_op jit(solution)/shard_map/ppermute | solution.py:319
  4.5 0.9 sub.134.refs_0_
  5.4 0.9 sub.135.refs_1_
  6.3 15.7 %collective-permute-done.1.refs_3_ = bf16[2,256,768]{2,1,0:T(8,128)(2,1)S(1)} collective-permute-done((bf16[2,256,768]{2,1,0:T(8,128)(2,1)S(1)}, bf16[2,256,768]{2,1,0:T(8,128)(2,1)S(1)}, u32[]{:S(2)}, u32[]{:S(2)}) %collective-permute-start.1) | collective-permute-done | bytes 786464 | tf_op jit(solution)/shard_map/ppermute | solution.py:319
  22.9 6.0 %pack_rows.3 = bf16[640,1536]{1,0:T(8,128)(2,1)} custom-call(s32[1]{0:T(128)} %bitcast.7.place_ref, s32[640,1]{1,0:T(8,128)} %sub.134.refs_0_, s32[640,1]{1,0:T(8,128)} %sub.135.refs_1_, bf16[3,256,4096]{2,1,0:T(8,128)(2,1)} %refs_2_.5, bf16[2,256,768]{2,1,0:T(8,128)(2,1)} %copy-done.2), custom_call_target="tpu_custom_call" | custom-call | flops 1006632960 | bytes 3538944 | tf_op jit(solution)/shard_map/pack_rows/pallas_call | solution.py:46
  29.0 6.1 %all-to-all-start = ((bf16[16,40,1536]{2,1,0:T(8,128)(2,1)}), bf16[16,40,1536]{2,1,0:T(8,128)(2,1)S(1)}, u32[]{:S(2)}, u32[]{:S(2)}) async-start(bf16[16,40,1536]{2,1,0:T(8,128)(2,1)} %bitcast.102), calls=%async_computation | async-start | bytes 3932160 | tf_op jit(solution)/shard_map/all_to_all | solution.py:343
  35.1 1.9 slice_select_fusion
  37.0 1.6 collective-permute-start.10
  38.6 29.7 %collective-permute-done.10.refs_3_ = bf16[2,256,1280]{2,1,0:T(8,128)(2,1)} collective-permute-done((bf16[2,256,1280]{2,1,0:T(8,128)(2,1)S(1)}, bf16[2,256,1280]{2,1,0:T(8,128)(2,1)}, u32[]{:S(2)}, u32[]{:S(2)}) %collective-permute-start.10) | collective-permute-done | bytes 1310752 | tf_op jit(solution)/shard_map/ppermute | solution.py:319
  68.3 9.1 %pack_rows.5 = bf16[640,2560]{1,0:T(8,128)(2,1)} custom-call(s32[1]{0:T(128)} %bitcast.7.place_ref, s32[640,1]{1,0:T(8,128)} %sub.134.refs_0_, s32[640,1]{1,0:T(8,128)} %sub.135.refs_1_, bf16[3,256,4096]{2,1,0:T(8,128)(2,1)} %refs_2_.5, bf16[2,256,1280]{2,1,0:T(8,128)(2,1)} %collective-permute-done.10.refs_3_), custom_call_target="tpu_custom_call" | custom-call | flops 1677721600 | bytes 5898240 | tf_op jit(solution)/shard_map/pack_rows/pallas_call | solution.py:46
  77.4 1.3 copy-done.1
  78.6 7.3 %all-to-all-start.2 = ((bf16[16,40,2560]{2,1,0:T(8,128)(2,1)}), bf16[16,40,2560]{2,1,0:T(8,128)(2,1)S(1)}, u32[]{:S(2)}, u32[]{:S(2)}) async-start(bf16[16,40,2560]{2,1,0:T(8,128)(2,1)} %bitcast.100), calls=%async_computation.2 | async-start | bytes 6553600 | tf_op jit(solution)/shard_map/all_to_all | solution.py:343
  85.9 2.7 slice_select_fusion.1
  88.6 1.5 collective-permute-start
  105.7 3.8 %block_update.2 = f32[768,128]{1,0:T(8,128)} custom-call(s32[640,1]{1,0:T(8,128)} %fusion.tail_ref, bf16[640,1536]{1,0:T(8,128)(2,1)} %bitcast.96, bf16[640,1536]{1,0:T(8,128)(2,1)} %bitcast.97), custom_call_target="tpu_custom_call" | custom-call | flops 125829120 | bytes 2359296 | tf_op jit(solution)/shard_map/block_update/pallas_call | solution.py:83
  109.4 1.7 constant_dynamic-slice_fusion.4
  111.3 1.8 collective-permute-start.3
  113.2 7.3 %collective-permute-done.3.refs_2_ = f32[192,128]{1,0:T(8,128)S(1)} collective-permute-done((f32[192,128]{1,0:T(8,128)S(1)}, f32[192,128]{1,0:T(8,128)S(1)}, u32[]{:S(2)}, u32[]{:S(2)}) %collective-permute-start.3) | collective-permute-done | bytes 98336 | tf_op jit(solution)/shard_map/ppermute | solution.py:190
  120.5 2.2 collective-permute-done.4.refs_3_
  123.3 2.5 sum_pieces.2
  125.8 1.3 collective-permute-start.5
  127.3 14.8 %collective-permute-done.5 = f32[192,128]{1,0:T(8,128)S(1)} collective-permute-done((f32[192,128]{1,0:T(8,128)}, f32[192,128]{1,0:T(8,128)S(1)}, u32[]{:S(2)}, u32[]{:S(2)}) %collective-permute-start.5) | collective-permute-done | bytes 98336 | tf_op jit(solution)/shard_map/ppermute | solution.py:210
  142.0 1.5 select_add_fusion.3
  143.6 22.8 %collective-permute-start.6 = (f32[192,128]{1,0:T(8,128)}, f32[192,128]{1,0:T(8,128)S(1)}, u32[]{:S(2)}, u32[]{:S(2)}) collective-permute-start(f32[192,128]{1,0:T(8,128)} %select_add_fusion.3), channel_id=1, source_target_pairs={{0,16},{2,18},{4,20},{6,22},{8,24},{10,26},{12,28},{14,30},{1,17},... | collective-permute-start | bytes 294920 | tf_op jit(solution)/shard_map/ppermute | solution.py:210
  173.8 0.9 fusion.2
  174.7 1.7 bitcast_add_fusion.6
  176.5 1.4 collective-permute-start.8
  179.0 4.5 %unpack_keys_values.2 = (bf16[512,2048]{1,0:T(8,128)(2,1)}, bf16[512,2048]{1,0:T(8,128)(2,1)}) custom-call(s32[1,640]{1,0:T(1,128)} %reshape_squeeze.2.land_ref, bf16[640,1536]{1,0:T(8,128)(2,1)} %bitcast.98, bf16[640,1536]{1,0:T(8,128)(2,1)} %bitcast.99), custom_call_target="tpu_custom_call" | custom-call | flops 1006632960 | bytes 3538944 | tf_op jit(solution)/shard_map/unpack_keys_values/pallas_call | solution.py:122
  183.7 1.0 pad_maximum_fusion.1
  185.5 5.4 %pack_rows.4 = bf16[640,2048]{1,0:T(8,128)(2,1)} custom-call(s32[1]{0:T(128)} %bitcast.7.place_ref, s32[640,1]{1,0:T(8,128)} %sub.134.refs_0_, s32[640,1]{1,0:T(8,128)} %sub.135.refs_1_, bf16[3,256,4096]{2,1,0:T(8,128)(2,1)} %refs_2_.5, bf16[1,256,2048]{2,1,0:T(8,128)(2,1)} %collective-permute-done.refs_3_), custom_call_target="tpu_custom_call" | custom-call | flops 1342177280 | bytes 4718592 | tf_op jit(solution)/shard_map/pack_rows/pallas_call | solution.py:46
  190.9 1.7 copy-done
  192.5 4.5 %all-to-all-start.1 = ((bf16[16,40,2048]{2,1,0:T(8,128)(2,1)}), bf16[16,40,2048]{2,1,0:T(8,128)(2,1)}, u32[]{:S(2)}, u32[]{:S(2)}) async-start(bf16[16,40,2048]{2,1,0:T(8,128)(2,1)} %bitcast.101), calls=%async_computation.1 | async-start | bytes 5242880 | tf_op jit(solution)/shard_map/all_to_all | solution.py:343
  199.1 5.4 %block_update.3 = f32[1280,128]{1,0:T(8,128)} custom-call(s32[640,1]{1,0:T(8,128)} %fusion.tail_ref, bf16[640,2560]{1,0:T(8,128)(2,1)} %bitcast.92, bf16[640,2560]{1,0:T(8,128)(2,1)} %bitcast.93), custom_call_target="tpu_custom_call" | custom-call | flops 209715200 | bytes 3932160 | tf_op jit(solution)/shard_map/block_update/pallas_call | solution.py:83
  204.5 1.9 constant_dynamic-slice_fusion
  206.6 1.7 collective-permute-start.12
  209.6 9.4 %collective-permute-done.12.refs_2_ = f32[320,128]{1,0:T(8,128)S(1)} collective-permute-done((f32[320,128]{1,0:T(8,128)S(1)}, f32[320,128]{1,0:T(8,128)S(1)}, u32[]{:S(2)}, u32[]{:S(2)}) %collective-permute-start.12) | collective-permute-done | bytes 163872 | tf_op jit(solution)/shard_map/ppermute | solution.py:190
  219.0 7.0 %collective-permute-done.13.refs_3_ = f32[320,128]{1,0:T(8,128)S(1)} collective-permute-done((f32[320,128]{1,0:T(8,128)S(1)}, f32[320,128]{1,0:T(8,128)S(1)}, u32[]{:S(2)}, u32[]{:S(2)}) %collective-permute-start.13) | collective-permute-done | bytes 163872 | tf_op jit(solution)/shard_map/ppermute | solution.py:190
  226.7 2.8 sum_pieces.3
  229.5 1.4 collective-permute-start.14
  232.2 11.7 %collective-permute-done.14 = f32[320,128]{1,0:T(8,128)S(1)} collective-permute-done((f32[320,128]{1,0:T(8,128)}, f32[320,128]{1,0:T(8,128)S(1)}, u32[]{:S(2)}, u32[]{:S(2)}) %collective-permute-start.14) | collective-permute-done | bytes 163872 | tf_op jit(solution)/shard_map/ppermute | solution.py:210
  243.9 0.9 select_add_fusion.1
  244.9 19.3 %collective-permute-start.15 = (f32[320,128]{1,0:T(8,128)S(1)}, f32[320,128]{1,0:T(8,128)S(1)}, u32[]{:S(2)}, u32[]{:S(2)}) collective-permute-start(f32[320,128]{1,0:T(8,128)S(1)} %select_add_fusion.1), channel_id=1, source_target_pairs={{0,16},{2,18},{4,20},{6,22},{8,24},{10,26},{12,28},{14,30},{1,17},... | collective-permute-start | bytes 491528 | tf_op jit(solution)/shard_map/ppermute | solution.py:210
  270.9 1.0 fusion.1
  272.0 1.4 collective-permute-start.17
  275.6 6.4 %unpack_keys_values.3 = (bf16[512,2048]{1,0:T(8,128)(2,1)}, bf16[512,2048]{1,0:T(8,128)(2,1)}) custom-call(s32[1,640]{1,0:T(1,128)} %reshape_squeeze.2.land_ref, bf16[640,2560]{1,0:T(8,128)(2,1)} %bitcast.94, bf16[640,2560]{1,0:T(8,128)(2,1)} %bitcast.95, bf16[512,2048]{1,0:T(8,128)(2,1)} %get-tuple-element.31.refs_0_, ...), custom_call_target="tpu_custom_call", output_to_operand_aliasing={{0}: (3, {}), {1}: (4, {})} | custom-call | flops 1677721600 | bytes 5898240 | tf_op jit(solution)/shard_map/unpack_keys_values/pallas_call | solution.py:122
  282.1 1.0 copy-done.14
  283.1 14.0 %attend.1 = bf16[512,2048]{1,0:T(8,128)(2,1)} custom-call(s32[1,640]{1,0:T(1,128)} %reshape_squeeze.2.land_ref, s32[512,1]{1,0:T(8,128)} %copy.26.seg_col_ref, s32[1,512]{1,0:T(1,128)} %bitcast.109, s32[512,1]{1,0:T(8,128)} %copy.27.carried_mask_ref, f32[1,2048]{1,0:T(1,128)} %bitcast.112, bf16[640,2048]{1,0:T(8,128)(2,1)} %bitcast.38.query_ref, ...), custom_call_target="tpu_custom_call" | custom-call | flops 3758096384 | bytes 8912896 | tf_op jit(solution)/shard_map/attend/pallas_call | solution.py:281
  (103 shorter events, 18.1 us)
Async XLA Ops:
  0.0 4.5 %copy-start.16 = (s32[1,16,40]{2,1,0:T(8,128)S(1)}, s32[1,16,40]{2,1,0:T(8,128)}, u32[]{:S(2)}) copy-start(s32[1,16,40]{2,1,0:T(8,128)} %param.6) | copy-start | bytes 7684
  1.5 20.6 %collective-permute-start.1 = (bf16[2,256,768]{2,1,0:T(8,128)(2,1)S(1)}, bf16[2,256,768]{2,1,0:T(8,128)(2,1)S(1)}, u32[]{:S(2)}, u32[]{:S(2)}) collective-permute-start(bf16[2,256,768]{2,1,0:T(8,128)(2,1)S(1)} %slice_select_fusion.2), channel_id=1, source_target_pairs={{0,1},{1,0},{2,3},{3,2},{4,5},{5,4},{6,7},{7,6},{8,9},{9,8},{10,11... | collective-permute-start | bytes 2359304 | tf_op jit(solution)/shard_map/ppermute | solution.py:319
  22.0 0.9 copy-start.2
  29.0 48.4 %all-to-all-start = ((bf16[16,40,1536]{2,1,0:T(8,128)(2,1)}), bf16[16,40,1536]{2,1,0:T(8,128)(2,1)S(1)}, u32[]{:S(2)}, u32[]{:S(2)}) async-start(bf16[16,40,1536]{2,1,0:T(8,128)(2,1)} %bitcast.102), calls=%async_computation | async-start | bytes 3932160 | tf_op jit(solution)/shard_map/all_to_all | solution.py:343
  37.0 31.3 %collective-permute-start.10 = (bf16[2,256,1280]{2,1,0:T(8,128)(2,1)S(1)}, bf16[2,256,1280]{2,1,0:T(8,128)(2,1)}, u32[]{:S(2)}, u32[]{:S(2)}) collective-permute-start(bf16[2,256,1280]{2,1,0:T(8,128)(2,1)S(1)} %slice_select_fusion), channel_id=1, source_target_pairs={{0,1},{1,0},{2,3},{3,2},{4,5},{5,4},{6,7},{7,6},{8,9},{9,8},{10,11... | collective-permute-start | bytes 3932168 | tf_op jit(solution)/shard_map/ppermute | solution.py:319
  77.4 1.3 copy-start.1
  78.6 112.2 %all-to-all-start.2 = ((bf16[16,40,2560]{2,1,0:T(8,128)(2,1)}), bf16[16,40,2560]{2,1,0:T(8,128)(2,1)S(1)}, u32[]{:S(2)}, u32[]{:S(2)}) async-start(bf16[16,40,2560]{2,1,0:T(8,128)(2,1)} %bitcast.100), calls=%async_computation.2 | async-start | bytes 6553600 | tf_op jit(solution)/shard_map/all_to_all | solution.py:343
  85.9 9.9 %copy-start.17 = (s32[4]{0:T(128)S(1)}, s32[4]{0:T(128)}, u32[]{:S(2)}) copy-start(s32[4]{0:T(128)} %param.8) | copy-start | bytes 52
  85.9 10.0 %copy-start.13 = (s32[1,16,40]{2,1,0:T(8,128)S(1)}, s32[1,16,40]{2,1,0:T(8,128)}, u32[]{:S(2)}) copy-start(s32[1,16,40]{2,1,0:T(8,128)} %param.7) | copy-start | bytes 7684
  88.6 96.8 %collective-permute-start = (bf16[1,256,2048]{2,1,0:T(8,128)(2,1)}, bf16[1,256,2048]{2,1,0:T(8,128)(2,1)}, u32[]{:S(2)}, u32[]{:S(2)}) collective-permute-start(bf16[1,256,2048]{2,1,0:T(8,128)(2,1)} %slice_select_fusion.1), channel_id=1, source_target_pairs={{0,1},{1,0},{2,3},{3,2},{4,5},{5,4},{6,7},{7,6},{8,9},{9,8},{10,11... | collective-permute-start | bytes 3145736 | tf_op jit(solution)/shard_map/ppermute | solution.py:319
  111.1 2.1 collective-permute-start.2
  111.3 9.2 %collective-permute-start.3 = (f32[192,128]{1,0:T(8,128)S(1)}, f32[192,128]{1,0:T(8,128)S(1)}, u32[]{:S(2)}, u32[]{:S(2)}) collective-permute-start(f32[192,128]{1,0:T(8,128)S(1)} %get-tuple-element.66), channel_id=1, source_target_pairs={{0,4},{2,6},{4,0},{6,2},{8,12},{10,14},{12,8},{14,10},{16,20},{18,... | collective-permute-start | bytes 294920 | tf_op jit(solution)/shard_map/ppermute | solution.py:190
  113.1 9.6 %collective-permute-start.4 = (f32[192,128]{1,0:T(8,128)S(1)}, f32[192,128]{1,0:T(8,128)S(1)}, u32[]{:S(2)}, u32[]{:S(2)}) collective-permute-start(f32[192,128]{1,0:T(8,128)S(1)} %get-tuple-element.65), channel_id=1, source_target_pairs={{0,6},{2,4},{4,2},{6,0},{8,14},{10,12},{12,10},{14,8},{16,22},{18,... | collective-permute-start | bytes 294920 | tf_op jit(solution)/shard_map/ppermute | solution.py:190
  113.2 10.1 %copy-start.10 = (f32[192,128]{1,0:T(8,128)}, f32[192,128]{1,0:T(8,128)S(1)}, u32[]{:S(2)}) copy-start(f32[192,128]{1,0:T(8,128)S(1)} %collective-permute-done.2.refs_1_) | copy-start | bytes 294916
  120.5 2.8 copy-start.11
  122.7 0.6 copy-start.12
  125.8 16.2 %collective-permute-start.5 = (f32[192,128]{1,0:T(8,128)}, f32[192,128]{1,0:T(8,128)S(1)}, u32[]{:S(2)}, u32[]{:S(2)}) collective-permute-start(f32[192,128]{1,0:T(8,128)} %bitcast.107), channel_id=1, source_target_pairs={{0,8},{2,10},{4,12},{6,14},{8,16},{10,18},{12,20},{14,22},{16,24},... | collective-permute-start | bytes 294920 | tf_op jit(solution)/shard_map/ppermute | solution.py:210
  143.6 29.6 %collective-permute-start.6 = (f32[192,128]{1,0:T(8,128)}, f32[192,128]{1,0:T(8,128)S(1)}, u32[]{:S(2)}, u32[]{:S(2)}) collective-permute-start(f32[192,128]{1,0:T(8,128)} %select_add_fusion.3), channel_id=1, source_target_pairs={{0,16},{2,18},{4,20},{6,22},{8,24},{10,26},{12,28},{14,30},{1,17},... | collective-permute-start | bytes 294920 | tf_op jit(solution)/shard_map/ppermute | solution.py:210
  166.4 107.5 %copy-start.15 = (s32[512]{0:T(512)}, s32[512]{0:T(512)S(1)}, u32[]{:S(2)}) copy-start(s32[512]{0:T(512)S(1)} %broadcast_add_fusion.1) | copy-start | bytes 6148
  173.2 0.6 copy-start.9
  176.5 7.0 %collective-permute-start.7 = (f32[192,128]{1,0:T(8,128)}, f32[192,128]{1,0:T(8,128)}, u32[]{:S(2)}, u32[]{:S(2)}) collective-permute-start(f32[192,128]{1,0:T(8,128)} %get-tuple-element.58), channel_id=1, source_target_pairs={{0,2},{2,0},{4,6},{6,4},{8,10},{10,8},{12,14},{14,12},{16,18},{18,... | collective-permute-start | bytes 294920 | tf_op jit(solution)/shard_map/ppermute | solution.py:190
  176.5 7.0 %collective-permute-start.8 = (f32[192,128]{1,0:T(8,128)}, f32[192,128]{1,0:T(8,128)}, u32[]{:S(2)}, u32[]{:S(2)}) collective-permute-start(f32[192,128]{1,0:T(8,128)} %get-tuple-element.59), channel_id=1, source_target_pairs={{0,4},{2,6},{4,0},{6,2},{8,12},{10,14},{12,8},{14,10},{16,20},{18,... | collective-permute-start | bytes 294920 | tf_op jit(solution)/shard_map/ppermute | solution.py:190
  177.9 5.8 %collective-permute-start.9 = (f32[192,128]{1,0:T(8,128)S(1)}, f32[192,128]{1,0:T(8,128)}, u32[]{:S(2)}, u32[]{:S(2)}) collective-permute-start(f32[192,128]{1,0:T(8,128)S(1)} %get-tuple-element.60), channel_id=1, source_target_pairs={{0,6},{2,4},{4,2},{6,0},{8,14},{10,12},{12,10},{14,8},{16,22},{18,... | collective-permute-start | bytes 294920 | tf_op jit(solution)/shard_map/ppermute | solution.py:190
  190.9 1.7 copy-start
  192.5 89.6 %all-to-all-start.1 = ((bf16[16,40,2048]{2,1,0:T(8,128)(2,1)}), bf16[16,40,2048]{2,1,0:T(8,128)(2,1)}, u32[]{:S(2)}, u32[]{:S(2)}) async-start(bf16[16,40,2048]{2,1,0:T(8,128)(2,1)} %bitcast.101), calls=%async_computation.1 | async-start | bytes 5242880 | tf_op jit(solution)/shard_map/all_to_all | solution.py:343
  199.1 33.1 %copy-start.5 = (f32[192,128]{1,0:T(8,128)S(1)}, f32[192,128]{1,0:T(8,128)}, u32[]{:S(2)}) copy-start(f32[192,128]{1,0:T(8,128)} %get-tuple-element.35) | copy-start | bytes 294916
  204.5 59.7 %copy-start.4 = (f32[192,128]{1,0:T(8,128)S(1)}, f32[192,128]{1,0:T(8,128)}, u32[]{:S(2)}) copy-start(f32[192,128]{1,0:T(8,128)} %get-tuple-element.36) | copy-start | bytes 294916
  206.4 3.2 %collective-permute-start.11 = (f32[320,128]{1,0:T(8,128)S(1)}, f32[320,128]{1,0:T(8,128)S(1)}, u32[]{:S(2)}, u32[]{:S(2)}) collective-permute-start(f32[320,128]{1,0:T(8,128)S(1)} %get-tuple-element.56), channel_id=1, source_target_pairs={{0,2},{2,0},{4,6},{6,4},{8,10},{10,8},{12,14},{14,12},{16,18},{18,... | collective-permute-start | bytes 491528 | tf_op jit(solution)/shard_map/ppermute | solution.py:190
  206.6 12.4 %collective-permute-start.12 = (f32[320,128]{1,0:T(8,128)S(1)}, f32[320,128]{1,0:T(8,128)S(1)}, u32[]{:S(2)}, u32[]{:S(2)}) collective-permute-start(f32[320,128]{1,0:T(8,128)S(1)} %get-tuple-element.55), channel_id=1, source_target_pairs={{0,4},{2,6},{4,0},{6,2},{8,12},{10,14},{12,8},{14,10},{16,20},{18,... | collective-permute-start | bytes 491528 | tf_op jit(solution)/shard_map/ppermute | solution.py:190
  208.3 17.8 %collective-permute-start.13 = (f32[320,128]{1,0:T(8,128)S(1)}, f32[320,128]{1,0:T(8,128)S(1)}, u32[]{:S(2)}, u32[]{:S(2)}) collective-permute-start(f32[320,128]{1,0:T(8,128)S(1)} %get-tuple-element.54), channel_id=1, source_target_pairs={{0,6},{2,4},{4,2},{6,0},{8,14},{10,12},{12,10},{14,8},{16,22},{18,... | collective-permute-start | bytes 491528 | tf_op jit(solution)/shard_map/ppermute | solution.py:190
  209.6 16.5 %copy-start.6 = (f32[320,128]{1,0:T(8,128)}, f32[320,128]{1,0:T(8,128)S(1)}, u32[]{:S(2)}) copy-start(f32[320,128]{1,0:T(8,128)S(1)} %collective-permute-done.11.refs_1_) | copy-start | bytes 491524
  219.0 7.1 %copy-start.7 = (f32[320,128]{1,0:T(8,128)}, f32[320,128]{1,0:T(8,128)S(1)}, u32[]{:S(2)}) copy-start(f32[320,128]{1,0:T(8,128)S(1)} %collective-permute-done.12.refs_2_) | copy-start | bytes 491524
  226.1 0.7 copy-start.8
  229.5 42.3 %copy-start.3 = (f32[4,320,128]{2,1,0:T(8,128)S(1)}, f32[4,320,128]{2,1,0:T(8,128)}, u32[]{:S(2)}) copy-start(f32[4,320,128]{2,1,0:T(8,128)} %get-tuple-element.41) | copy-start | bytes 1966084
  229.5 14.4 %collective-permute-start.14 = (f32[320,128]{1,0:T(8,128)}, f32[320,128]{1,0:T(8,128)S(1)}, u32[]{:S(2)}, u32[]{:S(2)}) collective-permute-start(f32[320,128]{1,0:T(8,128)} %bitcast.106), channel_id=1, source_target_pairs={{0,8},{2,10},{4,12},{6,14},{8,16},{10,18},{12,20},{14,22},{16,24},... | collective-permute-start | bytes 491528 | tf_op jit(solution)/shard_map/ppermute | solution.py:210
  244.9 26.0 %collective-permute-start.15 = (f32[320,128]{1,0:T(8,128)S(1)}, f32[320,128]{1,0:T(8,128)S(1)}, u32[]{:S(2)}, u32[]{:S(2)}) collective-permute-start(f32[320,128]{1,0:T(8,128)S(1)} %select_add_fusion.1), channel_id=1, source_target_pairs={{0,16},{2,18},{4,20},{6,22},{8,24},{10,26},{12,28},{14,30},{1,17},... | collective-permute-start | bytes 491528 | tf_op jit(solution)/shard_map/ppermute | solution.py:210
  271.9 10.0 %collective-permute-start.16 = (f32[320,128]{1,0:T(8,128)S(1)}, f32[320,128]{1,0:T(8,128)S(1)}, u32[]{:S(2)}, u32[]{:S(2)}) collective-permute-start(f32[320,128]{1,0:T(8,128)S(1)} %get-tuple-element.51), channel_id=1, source_target_pairs={{0,2},{2,0},{4,6},{6,4},{8,10},{10,8},{12,14},{14,12},{16,18},{18,... | collective-permute-start | bytes 491528 | tf_op jit(solution)/shard_map/ppermute | solution.py:190
  272.0 10.0 %collective-permute-start.17 = (f32[320,128]{1,0:T(8,128)S(1)}, f32[320,128]{1,0:T(8,128)S(1)}, u32[]{:S(2)}, u32[]{:S(2)}) collective-permute-start(f32[320,128]{1,0:T(8,128)S(1)} %get-tuple-element.52), channel_id=1, source_target_pairs={{0,4},{2,6},{4,0},{6,2},{8,12},{10,14},{12,8},{14,10},{16,20},{18,... | collective-permute-start | bytes 491528 | tf_op jit(solution)/shard_map/ppermute | solution.py:190
  273.4 8.6 %collective-permute-start.18 = (f32[320,128]{1,0:T(8,128)S(1)}, f32[320,128]{1,0:T(8,128)S(1)}, u32[]{:S(2)}, u32[]{:S(2)}) collective-permute-start(f32[320,128]{1,0:T(8,128)S(1)} %get-tuple-element.53), channel_id=1, source_target_pairs={{0,6},{2,4},{4,2},{6,0},{8,14},{10,12},{12,10},{14,8},{16,22},{18,... | collective-permute-start | bytes 491528 | tf_op jit(solution)/shard_map/ppermute | solution.py:190
  282.1 1.0 copy-start.14

commit v4 on v3

--- a/solution.py
+++ b/solution.py
@@ -144,95 +144,98 @@
 def sum_kernel(take_ref, *refs):
     count = take_ref.shape[1]
     pieces, outs = refs[:count], refs[count:]
-    number = 0
-    for out in outs:
-        for part in range(out.shape[0]):
-            total = jnp.zeros(out.shape[1:], jnp.float32)
-            for piece in range(count):
-                wanted = take_ref[number, piece] != 0
-                total = total + jnp.where(wanted, pieces[piece][...], 0.0)
-            out[part] = total
-            number += 1
-
-
-def sum_pieces(take, pieces, counts):
+    for number, out in enumerate(outs):
+        total = jnp.zeros(out.shape, jnp.float32)
+        for piece in range(count):
+            total = total + jnp.where(take_ref[number, piece] != 0, pieces[piece][...], 0.0)
+        out[...] = total
+
+
+def sum_pieces(take, pieces):
     rows = pieces[0].shape[0]
     step = rows // 2
+    spec = pl.BlockSpec((step, HEAD_DIM), lambda i, take_ref: (i, 0))
+    count = take.shape[0]
     return pl.pallas_call(
         sum_kernel,
-        out_shape=tuple(jax.ShapeDtypeStruct((n, rows, HEAD_DIM), jnp.float32) for n in counts),
+        out_shape=(jax.ShapeDtypeStruct((rows, HEAD_DIM), jnp.float32),) * count,
         grid_spec=pltpu.PrefetchScalarGridSpec(
             num_scalar_prefetch=1,
             grid=(rows // step,),
-            in_specs=[pl.BlockSpec((step, HEAD_DIM), lambda i, take_ref: (i, 0)) for _ in pieces],
-            out_specs=tuple(
-                pl.BlockSpec((n, step, HEAD_DIM), lambda i, take_ref: (0, i, 0)) for n in counts
-            ),
-        ),
-        cost_estimate=pl.CostEstimate(
-            flops=sum(counts) * len(pieces) * rows * HEAD_DIM,
-            bytes_accessed=4 * (len(pieces) + sum(counts)) * rows * HEAD_DIM,
+            in_specs=[spec] * len(pieces),
+            out_specs=(spec,) * count,
+        ),
+        cost_estimate=pl.CostEstimate(
+            flops=count * len(pieces) * rows * HEAD_DIM,
+            bytes_accessed=4 * (len(pieces) + count) * rows * HEAD_DIM,
             transcendentals=0,
         ),
         name="sum_pieces",
     )(take.astype(jnp.int32), *pieces)
 
 
-def carry_states(update, last_segment):
+def run_of_blocks():
     seq_count, block = lax.axis_size("seq"), lax.axis_index("seq")
     near = math.gcd(seq_count, 4)
-    far = seq_count // near
+    return near, seq_count // near, block % near, block // near
+
+
+def swap_places(value, k):
+    seq_count = lax.axis_size("seq")
+    return lax.ppermute(value, "seq", [(i, i ^ k) for i in range(seq_count)])
+
+
+def carry_tables(last_segment):
+    near, far, place, run = run_of_blocks()
+    base = run * near
+    source = base + (place ^ jnp.arange(near))
+    before = last_segment[jnp.maximum(source - 1, 0)]
+    of_source = last_segment[source]
+    inside = (source[None, :] < source[:, None]) & (of_source[None, :] == before[:, None])
+    whole = of_source == last_segment[base + near - 1]
+    within = jnp.concatenate([inside, whole[None]])
+    shifts = jnp.arange(1, far // 2 + 1)
+    ends = last_segment[jnp.maximum(run - shifts, 0) * near + near - 1]
+    across = (run >= shifts)[None, :] & (ends[None, :] == before[:, None])
+    own = jnp.arange(near)[:, None] == jnp.arange(near)[None, :]
+    return within, jnp.concatenate([own, across], axis=1)
+
+
+def carry_within(update, within):
+    near, _, place, _ = run_of_blocks()
     share = update.shape[0] // near
-    place, run = block % near, block // near
-    base = run * near
-
-    def swap(value, k):
-        return lax.ppermute(value, "seq", [(i, i ^ k) for i in range(seq_count)])
-
-    pieces = [lax.dynamic_slice_in_dim(update, place * share, share, axis=0)]
-    for k in range(1, near):
+    pieces = []
+    for k in range(near):
         mine = lax.dynamic_slice_in_dim(update, (place ^ k) * share, share, axis=0)
-        pieces.append(swap(mine, k))
-    source = base + (place ^ jnp.arange(near))
-    before = jnp.maximum(source - 1, 0)
-    inside = (source[None, :] < source[:, None]) & (
-        last_segment[source][None, :] == last_segment[before][:, None]
-    )
-    whole = last_segment[source] == last_segment[base + near - 1]
-    inner, total = sum_pieces(jnp.concatenate([inside, whole[None]]), pieces, (near, 1))
-    total = total[0]
-
-    def ends(run_number):
-        return last_segment[jnp.maximum(run_number, 0) * near + near - 1]
-
-    entering, window, reach = None, total, 1
-    while reach < far:
-        shifted = lax.ppermute(
-            window, "seq", [(i, i + reach * near) for i in range(seq_count - reach * near)]
+        pieces.append(mine if k == 0 else swap_places(mine, k))
+    return sum_pieces(within, pieces)
+
+
+def pass_totals(sums):
+    seq_count = lax.axis_size("seq")
+    near, far, _, _ = run_of_blocks()
+    pieces = list(sums[:near])
+    for shift in range(1, far // 2 + 1):
+        step = shift * near
+        pieces.append(
+            lax.ppermute(sums[near], "seq", [(i, i + step) for i in range(seq_count - step)])
         )
-        same_start = (run >= reach) & (ends(run - reach) == ends(run - 1))
-        same_end = (run >= reach) & (ends(run - reach) == ends(run))
-        shifted_in = jnp.where(same_start, shifted, 0.0)
-        entering = shifted_in if entering is None else entering + shifted_in
-        window = window + jnp.where(same_end, shifted, 0.0)
-        reach *= 2
-    handed = []
-    for k in range(near):
-        state = inner[k]
-        if entering is not None:
-            same = (run >= 1) & (last_segment[before[k]] == ends(run - 1))
-            state = state + jnp.where(same, entering, 0.0)
-        handed.append(state if k == 0 else swap(state, k))
-    stacked = jnp.stack(handed)
+    return pieces
+
+
+def hand_back(pieces, across):
+    near, _, place, _ = run_of_blocks()
+    handed = sum_pieces(across, pieces)
+    stacked = jnp.stack([handed[0]] + [swap_places(handed[k], k) for k in range(1, near)])
     return [
         lax.dynamic_index_in_dim(stacked, place ^ number, axis=0, keepdims=False)
         for number in range(near)
     ]
 
 
-def attend_kernel(
-    land_ref, seg_col_ref, seg_row_ref, carried_mask_ref, gain_ref, query_ref, keys_ref, values_ref,
-    states_ref, out_ref, order, causal,
+def local_kernel(
+    land_ref, seg_col_ref, seg_row_ref, arrived_ref, keys_ref, values_ref, query_out, local_out,
+    order, causal,
 ):
     tok_rows = order.shape[0]
 
@@ -245,66 +248,98 @@
         open_pair = (earlier <= later) & (seg_col_ref[...] == seg_row_ref[...])
         causal[...] = jnp.where(open_pair, 1.0, 0.0)
 
-    query = jnp.dot(order[...], query_ref[...], preferred_element_type=jnp.float32).astype(
+    query = jnp.dot(order[...], arrived_ref[...], preferred_element_type=jnp.float32).astype(
         keys_ref.dtype
     )
-    state_high = states_ref[...].astype(query.dtype)
-    state_low = (states_ref[...] - state_high.astype(jnp.float32)).astype(query.dtype)
+    query_out[...] = query
     half = tok_rows // 2
     for part in range(query.shape[1] // HEAD_DIM):
         columns = slice(part * HEAD_DIM, (part + 1) * HEAD_DIM)
         for rows, reach in ((slice(0, half), half), (slice(half, tok_rows), tok_rows)):
-            queries = query[rows, columns]
             scores = lax.dot_general(
-                queries,
+                query[rows, columns],
                 keys_ref[:reach, columns],
                 (((1,), (1,)), ((), ())),
                 preferred_element_type=jnp.float32,
             )
             weights = jnp.where(causal[rows, :reach] != 0.0, scores, 0.0).astype(keys_ref.dtype)
-            local_term = jnp.dot(
+            local_out[rows, columns] = jnp.dot(
                 weights, values_ref[:reach, columns], preferred_element_type=jnp.float32
             )
-            carried_term = jnp.dot(
-                queries, state_high[columns], preferred_element_type=jnp.float32
-            ) + jnp.dot(queries, state_low[columns], preferred_element_type=jnp.float32)
-            raw_out = local_term + jnp.where(carried_mask_ref[rows, :] != 0, carried_term, 0.0)
-            inv_rms = lax.rsqrt(jnp.mean(raw_out * raw_out, axis=1, keepdims=True) + norm_eps)
-            out_ref[rows, columns] = (raw_out * inv_rms * gain_ref[:, columns]).astype(out_ref.dtype)
-
-
-def attend(arrived, keys, values, states, land_row, seg_col, seg_row, carried_mask, gain):
+
+
+def attend_locally(arrived, keys, values, land_row, seg_col, seg_row):
     slots, columns = arrived.shape
     tok_rows = keys.shape[0]
     width = min(columns, 2 * HEAD_DIM)
     column_spec = pl.BlockSpec((tok_rows, width), lambda j: (0, j))
     return pl.pallas_call(
-        attend_kernel,
-        out_shape=jax.ShapeDtypeStruct((tok_rows, columns), jnp.bfloat16),
+        local_kernel,
+        out_shape=(
+            jax.ShapeDtypeStruct((tok_rows, columns), jnp.bfloat16),
+            jax.ShapeDtypeStruct((tok_rows, columns), jnp.float32),
+        ),
         grid=(columns // width,),
         in_specs=[
             pl.BlockSpec((1, slots), lambda j: (0, 0)),
             pl.BlockSpec((tok_rows, 1), lambda j: (0, 0)),
             pl.BlockSpec((1, tok_rows), lambda j: (0, 0)),
+            pl.BlockSpec((slots, width), lambda j: (0, j)),
+            column_spec,
+            column_spec,
+        ],
+        out_specs=(column_spec, column_spec),
+        scratch_shapes=[
+            pltpu.VMEM((tok_rows, slots), jnp.bfloat16),
+            pltpu.VMEM((tok_rows, tok_rows), jnp.float32),
+        ],
+        cost_estimate=pl.CostEstimate(
+            flops=2 * tok_rows * columns * (slots + 2 * tok_rows),
+            bytes_accessed=2 * columns * (slots + 5 * tok_rows),
+            transcendentals=0,
+        ),
+        name="attend_locally",
+    )(land_row, seg_col, seg_row, arrived, keys, values)
+
+
+def finish_kernel(mask_ref, gain_ref, query_ref, local_ref, states_ref, out_ref):
+    states = states_ref[...]
+    high = states.astype(query_ref.dtype)
+    low = (states - high.astype(jnp.float32)).astype(query_ref.dtype)
+    for part in range(out_ref.shape[1] // HEAD_DIM):
+        columns = slice(part * HEAD_DIM, (part + 1) * HEAD_DIM)
+        query = query_ref[:, columns]
+        carried_term = jnp.dot(
+            query, high[columns], preferred_element_type=jnp.float32
+        ) + jnp.dot(query, low[columns], preferred_element_type=jnp.float32)
+        raw_out = local_ref[:, columns] + jnp.where(mask_ref[...] != 0, carried_term, 0.0)
+        inv_rms = lax.rsqrt(jnp.mean(raw_out * raw_out, axis=1, keepdims=True) + norm_eps)
+        out_ref[:, columns] = (raw_out * inv_rms * gain_ref[:, columns]).astype(out_ref.dtype)
+
+
+def finish(query, local_term, states, carried_mask, gain):
+    tok_rows, columns = query.shape
+    width = min(columns, 4 * HEAD_DIM)
+    column_spec = pl.BlockSpec((tok_rows, width), lambda j: (0, j))
+    return pl.pallas_call(
+        finish_kernel,
+        out_shape=jax.ShapeDtypeStruct((tok_rows, columns), jnp.bfloat16),
+        grid=(columns // width,),
+        in_specs=[
             pl.BlockSpec((tok_rows, 1), lambda j: (0, 0)),
             pl.BlockSpec((1, width), lambda j: (0, j)),
-            pl.BlockSpec((slots, width), lambda j: (0, j)),
             column_spec,
             column_spec,
             pl.BlockSpec((width, HEAD_DIM), lambda j: (j, 0)),
         ],
         out_specs=column_spec,
-        scratch_shapes=[
-            pltpu.VMEM((tok_rows, slots), jnp.bfloat16),
-            pltpu.VMEM((tok_rows, tok_rows), jnp.float32),
-        ],
-        cost_estimate=pl.CostEstimate(
-            flops=2 * tok_rows * columns * (slots + 2 * tok_rows + HEAD_DIM),
-            bytes_accessed=2 * columns * (slots + 3 * tok_rows),
-            transcendentals=0,
-        ),
-        name="attend",
-    )(land_row, seg_col, seg_row, carried_mask, gain, arrived, keys, values, states)
+        cost_estimate=pl.CostEstimate(
+            flops=4 * tok_rows * columns * HEAD_DIM,
+            bytes_accessed=8 * columns * tok_rows,
+            transcendentals=0,
+        ),
+        name="finish",
+    )(carried_mask, gain, query, local_term, states)
 
 
 def swap_heads(qkv, plane_start, planes, start, columns):
@@ -324,7 +359,7 @@
     return jnp.moveaxis(incoming, 0, 1).reshape(planes, head_count * rows, columns)
 
 
-def send_packed(qkv, incoming, send_rows, plane_start, planes, start, columns):
+def pack_chunk(qkv, incoming, send_rows, plane_start, planes, start, columns):
     head_count = lax.axis_size("head")
     place = lax.axis_index("head")
     rows = qkv.shape[1]
@@ -337,9 +372,12 @@
         sources = (
             (qkv, plane_start, lambda at, width: at * (mine // width) + start // width),
         ) + sources
-    outgoing = pack_rows(
+    return pack_rows(
         jnp.reshape(place, (1,)).astype(jnp.int32), picks, sources, planes, columns, width
     )
+
+
+def to_owners(outgoing):
     return lax.all_to_all(outgoing, "seq", split_axis=0, concat_axis=0, tiled=True)
 
 
@@ -369,32 +407,32 @@
     head_share = columns // HEAD_DIM
     first = max(1, 3 * head_share // 16) * 2 * HEAD_DIM
     second = columns - first
-    arrived = send_packed(
-        qkv, swap_heads(qkv, KEYS, 2, 0, first), rows, KEYS, 2, 0, first
-    )
-    arrived_next = send_packed(
+    outgoing = pack_chunk(qkv, swap_heads(qkv, KEYS, 2, 0, first), rows, KEYS, 2, 0, first)
+    arrived = to_owners(outgoing)
+    outgoing = pack_chunk(
         qkv, swap_heads(qkv, KEYS, 2, first, second), rows, KEYS, 2, first, second
     )
-    states = carry_states(block_update(arrived, tail_slots), last_segment)
+    arrived_next = to_owners(outgoing)
+    within, across = carry_tables(last_segment)
+    sums = carry_within(block_update(arrived, tail_slots), within)
     filled = unpack_keys_values(arrived, land_row, tok_rows, 0, columns, ())
     incoming = swap_heads(qkv, QUERY, 1, 0, columns)
-    incoming, states, filled, tail_slots, last_segment, segment, carried_mask = lax.optimization_barrier(
-        (incoming, states, filled, tail_slots, last_segment, segment, carried_mask)
-    )
-    query = send_packed(qkv, incoming, rows, QUERY, 1, 0, columns)
-    states += carry_states(block_update(arrived_next, tail_slots), last_segment)
-    keys, values = unpack_keys_values(arrived_next, land_row, tok_rows, first, columns, filled)
-    return attend(
-        query,
-        keys,
-        values,
-        jnp.concatenate(states, axis=0),
-        land_row,
-        segment[:, None],
-        segment[None, :],
-        carried_mask,
-        gain,
-    )
+    incoming, sums, filled, tables = lax.optimization_barrier(
+        (incoming, sums, filled, (tail_slots, within, across, segment, carried_mask))
+    )
+    tail_slots, within, across, segment, carried_mask = tables
+    outgoing = pack_chunk(qkv, incoming, rows, QUERY, 1, 0, columns)
+    outgoing, pieces = lax.optimization_barrier((outgoing, pass_totals(sums)))
+    query = to_owners(outgoing)
+    sums = carry_within(block_update(arrived_next, tail_slots), within)
+    states = hand_back(pieces, across)
+    filled = unpack_keys_values(arrived_next, land_row, tok_rows, first, columns, filled)
+    pieces, (keys, values) = lax.optimization_barrier((pass_totals(sums), filled))
+    states += hand_back(pieces, across)
+    query, local_term = attend_locally(
+        query, keys, values, land_row, segment[:, None], segment[None, :]
+    )
+    return finish(query, local_term, jnp.concatenate(states, axis=0), carried_mask, gain)
 
 
 def solution(mesh):

time: 299 us -> 276 us (0.923)
  the two profiles are of different devices: /device:TPU:0 before, /device:TPU:11 now
where the time goes in v4:
time: 276 us; the launch traced here: 274 us
  waiting for transfers between devices  122 us (44%)
  Pallas kernels  71.2 us (26%)
  starting transfers between devices  50.2 us (18%)
  local copies, waits for them, and re-layouts  17.2 us (6%)
  other arithmetic  12.3 us (4%)
    ppermute x4, waiting for transfers between devices, pass_totals(): lax.ppermute(sums[near], 'seq', [(i, i + step) for i in range(seq_count -...  53 us
    ppermute x3, waiting for transfers between devices, swap_heads(): return lax.ppermute(outgoing, 'head', [(0, 1), (1, 0)])  44.2 us
    ppermute x12, waiting for transfers between devices, swap_places(): return lax.ppermute(value, 'seq', [(i, i ^ k) for i in range(seq_count)])  22.1 us
    pallas_call x3, Pallas kernels, pack_rows(): pl.pallas_call(pack_kernel, out_shape=jax.ShapeDtypeStruct((slots, planes...  20.5 us
    all_to_all x3, starting transfers between devices, to_owners(): lax.all_to_all(outgoing, 'seq', split_axis=0, concat_axis=0, tiled=True)  19.8 us
    ppermute x4, starting transfers between devices, pass_totals(): lax.ppermute(sums[near], 'seq', [(i, i + step) for i in range(seq_count -...  17.7 us
    pallas_call x1, Pallas kernels, attend_locally(): pl.pallas_call(local_kernel, out_shape=(jax.ShapeDtypeStruct((tok_rows, c...  13 us
    pallas_call x2, Pallas kernels, unpack_keys_values(): pl.pallas_call(unpack_kernel, out_shape=(packed, packed), grid=(blocks,),...  10.8 us
  transfers between devices with their start and end apart: 22, of which 13 were waited for; matrix products, arithmetic and copies ran while one was open for 8% of the time, Pallas kernels for 16%

profile of v4, /device:TPU:11, one launch (start us, length us, event | category | flops | bytes accessed | tf_op | source)
XLA Modules:
  0.0 273.6 jit_solution(13723157905290762372)
XLA Ops:
  0.0 1.5 slice_select_fusion.2
  1.5 1.3 collective-permute-start.1
  4.6 15.4 %collective-permute-done.1.refs_3_ = bf16[2,256,768]{2,1,0:T(8,128)(2,1)S(1)} collective-permute-done((bf16[2,256,768]{2,1,0:T(8,128)(2,1)S(1)}, bf16[2,256,768]{2,1,0:T(8,128)(2,1)S(1)}, u32[]{:S(2)}, u32[]{:S(2)}) %collective-permute-start.1) | collective-permute-done | bytes 786464 | tf_op jit(solution)/shard_map/ppermute | solution.py:354
  20.8 6.0 %pack_rows.3 = bf16[640,1536]{1,0:T(8,128)(2,1)} custom-call(s32[1]{0:T(128)} %bitcast.7.place_ref, s32[640,1]{1,0:T(8,128)} %sub.94.refs_0_, s32[640,1]{1,0:T(8,128)} %sub.95.refs_1_, bf16[3,256,4096]{2,1,0:T(8,128)(2,1)} %refs_2_.5, bf16[2,256,768]{2,1,0:T(8,128)(2,1)} %copy-done.4), custom_call_target="tpu_custom_call" | custom-call | flops 1006632960 | bytes 3538944 | tf_op jit(solution)/shard_map/pack_rows/pallas_call | solution.py:46
  26.9 7.4 %all-to-all-start = ((bf16[16,40,1536]{2,1,0:T(8,128)(2,1)}), bf16[16,40,1536]{2,1,0:T(8,128)(2,1)S(1)}, u32[]{:S(2)}, u32[]{:S(2)}) async-start(bf16[16,40,1536]{2,1,0:T(8,128)(2,1)} %bitcast.59), calls=%async_computation | async-start | bytes 3932160 | tf_op jit(solution)/shard_map/all_to_all | solution.py:381
  34.3 1.9 slice_select_fusion
  36.2 1.3 collective-permute-start.7
  37.5 28.8 %collective-permute-done.7.refs_3_ = bf16[2,256,1280]{2,1,0:T(8,128)(2,1)S(1)} collective-permute-done((bf16[2,256,1280]{2,1,0:T(8,128)(2,1)S(1)}, bf16[2,256,1280]{2,1,0:T(8,128)(2,1)S(1)}, u32[]{:S(2)}, u32[]{:S(2)}) %collective-permute-start.7) | collective-permute-done | bytes 1310752 | tf_op jit(solution)/shard_map/ppermute | solution.py:354
  66.2 1.1 copy-done.2
  67.3 9.1 %pack_rows.5 = bf16[640,2560]{1,0:T(8,128)(2,1)} custom-call(s32[1]{0:T(128)} %bitcast.7.place_ref, s32[640,1]{1,0:T(8,128)} %sub.94.refs_0_, s32[640,1]{1,0:T(8,128)} %sub.95.refs_1_, bf16[3,256,4096]{2,1,0:T(8,128)(2,1)} %refs_2_.5, bf16[2,256,1280]{2,1,0:T(8,128)(2,1)} %copy-done.2), custom_call_target="tpu_custom_call" | custom-call | flops 1677721600 | bytes 5898240 | tf_op jit(solution)/shard_map/pack_rows/pallas_call | solution.py:46
  76.4 2.5 all-to-all-done
  78.9 1.3 copy-done.1
  80.2 4.9 %all-to-all-start.2 = ((bf16[16,40,2560]{2,1,0:T(8,128)(2,1)}), bf16[16,40,2560]{2,1,0:T(8,128)(2,1)S(1)}, u32[]{:S(2)}, u32[]{:S(2)}) async-start(bf16[16,40,2560]{2,1,0:T(8,128)(2,1)} %bitcast.57), calls=%async_computation.2 | async-start | bytes 6553600 | tf_op jit(solution)/shard_map/all_to_all | solution.py:381
  85.1 2.6 slice_select_fusion.1
  87.8 1.2 collective-permute-start
  96.7 3.8 %block_update.2 = f32[768,128]{1,0:T(8,128)} custom-call(s32[640,1]{1,0:T(8,128)} %fusion.tail_ref, bf16[640,1536]{1,0:T(8,128)(2,1)} %bitcast.53, bf16[640,1536]{1,0:T(8,128)(2,1)} %bitcast.54), custom_call_target="tpu_custom_call" | custom-call | flops 125829120 | bytes 2359296 | tf_op jit(solution)/shard_map/block_update/pallas_call | solution.py:83
  100.5 1.8 constant_dynamic-slice_fusion.4
  103.1 1.4 collective-permute-start.4
  105.3 4.5 %unpack_keys_values.2 = (bf16[512,2048]{1,0:T(8,128)(2,1)}, bf16[512,2048]{1,0:T(8,128)(2,1)}) custom-call(s32[1,640]{1,0:T(1,128)} %reshape_squeeze.2.land_ref, bf16[640,1536]{1,0:T(8,128)(2,1)} %bitcast.55, bf16[640,1536]{1,0:T(8,128)(2,1)} %bitcast.56), custom_call_target="tpu_custom_call" | custom-call | flops 1006632960 | bytes 3538944 | tf_op jit(solution)/shard_map/unpack_keys_values/pallas_call | solution.py:122
  109.7 1.0 collective-permute-done.4.refs_3_
  110.7 2.5 sum_pieces.4
  113.2 2.7 collective-permute-start.5
  115.9 6.3 %collective-permute-start.6 = (f32[192,128]{1,0:T(8,128)}, f32[192,128]{1,0:T(8,128)S(1)}, u32[]{:S(2)}, u32[]{:S(2)}) collective-permute-start(f32[192,128]{1,0:T(8,128)} %get-tuple-element.71), channel_id=1, source_target_pairs={{0,16},{2,18},{4,20},{6,22},{8,24},{10,26},{12,28},{14,30},{1,17},... | collective-permute-start | bytes 294920 | tf_op jit(solution)/shard_map/ppermute | solution.py:221
  122.2 5.4 %pack_rows.4 = bf16[640,2048]{1,0:T(8,128)(2,1)} custom-call(s32[1]{0:T(128)} %bitcast.7.place_ref, s32[640,1]{1,0:T(8,128)} %sub.94.refs_0_, s32[640,1]{1,0:T(8,128)} %sub.95.refs_1_, bf16[3,256,4096]{2,1,0:T(8,128)(2,1)} %refs_2_.5, bf16[1,256,2048]{2,1,0:T(8,128)(2,1)} %collective-permute-done.refs_3_), custom_call_target="tpu_custom_call" | custom-call | flops 1342177280 | bytes 4718592 | tf_op jit(solution)/shard_map/pack_rows/pallas_call | solution.py:46
  127.6 32.3 %collective-permute-done.5.refs_4_ = f32[192,128]{1,0:T(8,128)S(1)} collective-permute-done((f32[192,128]{1,0:T(8,128)}, f32[192,128]{1,0:T(8,128)S(1)}, u32[]{:S(2)}, u32[]{:S(2)}) %collective-permute-start.5) | collective-permute-done | bytes 98336 | tf_op jit(solution)/shard_map/ppermute | solution.py:221
  159.9 2.1 collective-permute-done.6.refs_5_
  162.7 1.1 copy-done
  163.8 7.4 %all-to-all-start.1 = ((bf16[16,40,2048]{2,1,0:T(8,128)(2,1)}), bf16[16,40,2048]{2,1,0:T(8,128)(2,1)}, u32[]{:S(2)}, u32[]{:S(2)}) async-start(bf16[16,40,2048]{2,1,0:T(8,128)(2,1)} %bitcast.58), calls=%async_computation.1 | async-start | bytes 5242880 | tf_op jit(solution)/shard_map/all_to_all | solution.py:381
  174.1 2.6 sum_pieces.6
  177.4 1.5 collective-permute-start.15
  178.9 5.4 %block_update.3 = f32[1280,128]{1,0:T(8,128)} custom-call(s32[640,1]{1,0:T(8,128)} %fusion.tail_ref, bf16[640,2560]{1,0:T(8,128)(2,1)} %bitcast.49, bf16[640,2560]{1,0:T(8,128)(2,1)} %bitcast.50), custom_call_target="tpu_custom_call" | custom-call | flops 209715200 | bytes 3932160 | tf_op jit(solution)/shard_map/block_update/pallas_call | solution.py:83
  184.3 1.9 constant_dynamic-slice_fusion
  186.8 1.2 collective-permute-start.9
  188.0 3.7 %collective-permute-done.15 = f32[192,128]{1,0:T(8,128)S(1)} collective-permute-done((f32[192,128]{1,0:T(8,128)}, f32[192,128]{1,0:T(8,128)S(1)}, u32[]{:S(2)}, u32[]{:S(2)}) %collective-permute-start.15) | collective-permute-done | bytes 98336 | tf_op jit(solution)/shard_map/ppermute | solution.py:185
  191.7 3.6 %collective-permute-done.10.refs_3_ = f32[320,128]{1,0:T(8,128)S(1)} collective-permute-done((f32[320,128]{1,0:T(8,128)S(1)}, f32[320,128]{1,0:T(8,128)S(1)}, u32[]{:S(2)}, u32[]{:S(2)}) %collective-permute-start.10) | collective-permute-done | bytes 163872 | tf_op jit(solution)/shard_map/ppermute | solution.py:185
  195.3 5.9 %collective-permute-done.9.refs_2_ = f32[320,128]{1,0:T(8,128)S(1)} collective-permute-done((f32[320,128]{1,0:T(8,128)S(1)}, f32[320,128]{1,0:T(8,128)S(1)}, u32[]{:S(2)}, u32[]{:S(2)}) %collective-permute-start.9) | collective-permute-done | bytes 163872 | tf_op jit(solution)/shard_map/ppermute | solution.py:185
  201.9 2.8 %sum_pieces.5 = (f32[320,128]{1,0:T(8,128)}, f32[320,128]{1,0:T(8,128)}, f32[320,128]{1,0:T(8,128)}, f32[320,128]{1,0:T(8,128)}, f32[320,128]{1,0:T(8,128)}) custom-call(s32[5,4]{1,0:T(8,128)} %convert_element_type.46.take_ref, f32[320,128]{1,0:T(8,128)} %get-tuple-element.114.refs_0_, f32[320,128]{1,0:T(8,128)} %copy-done.6, f32[320,128]{1,0:T(8,128)} %copy-done.7, ...), custom_call_target="tpu_custom_call" | custom-call | flops 819200 | bytes 1474560 | tf_op jit(solution)/shard_map/sum_pieces/pallas_call | solution.py:159
  204.7 3.1 %collective-permute-start.11 = (f32[320,128]{1,0:T(8,128)}, f32[320,128]{1,0:T(8,128)S(1)}, u32[]{:S(2)}, u32[]{:S(2)}) collective-permute-start(f32[320,128]{1,0:T(8,128)} %get-tuple-element.79), channel_id=1, source_target_pairs={{0,8},{2,10},{4,12},{6,14},{8,16},{10,18},{12,20},{14,22},{16,24},... | collective-permute-start | bytes 491528 | tf_op jit(solution)/shard_map/ppermute | solution.py:221
  207.8 5.6 %collective-permute-start.12 = (f32[320,128]{1,0:T(8,128)}, f32[320,128]{1,0:T(8,128)S(1)}, u32[]{:S(2)}, u32[]{:S(2)}) collective-permute-start(f32[320,128]{1,0:T(8,128)} %get-tuple-element.79), channel_id=1, source_target_pairs={{0,16},{2,18},{4,20},{6,22},{8,24},{10,26},{12,28},{14,30},{1,17},... | collective-permute-start | bytes 491528 | tf_op jit(solution)/shard_map/ppermute | solution.py:221
  213.4 6.4 %unpack_keys_values.3 = (bf16[512,2048]{1,0:T(8,128)(2,1)}, bf16[512,2048]{1,0:T(8,128)(2,1)}) custom-call(s32[1,640]{1,0:T(1,128)} %reshape_squeeze.2.land_ref, bf16[640,2560]{1,0:T(8,128)(2,1)} %bitcast.51, bf16[640,2560]{1,0:T(8,128)(2,1)} %bitcast.52, bf16[512,2048]{1,0:T(8,128)(2,1)} %get-tuple-element.80.refs_0_, ...), custom_call_target="tpu_custom_call", output_to_operand_aliasing={{0}: (3, {}), {1}: (4, {})} | custom-call | flops 1677721600 | bytes 5898240 | tf_op jit(solution)/shard_map/unpack_keys_values/pallas_call | solution.py:122
  219.8 15.0 %collective-permute-done.11.refs_4_ = f32[320,128]{1,0:T(8,128)S(1)} collective-permute-done((f32[320,128]{1,0:T(8,128)}, f32[320,128]{1,0:T(8,128)S(1)}, u32[]{:S(2)}, u32[]{:S(2)}) %collective-permute-start.11) | collective-permute-done | bytes 163872 | tf_op jit(solution)/shard_map/ppermute | solution.py:221
  234.8 3.5 %collective-permute-done.12.refs_5_ = f32[320,128]{1,0:T(8,128)S(1)} collective-permute-done((f32[320,128]{1,0:T(8,128)}, f32[320,128]{1,0:T(8,128)S(1)}, u32[]{:S(2)}, u32[]{:S(2)}) %collective-permute-start.12) | collective-permute-done | bytes 163872 | tf_op jit(solution)/shard_map/ppermute | solution.py:221
  239.0 2.8 %sum_pieces.7 = (f32[320,128]{1,0:T(8,128)}, f32[320,128]{1,0:T(8,128)}, f32[320,128]{1,0:T(8,128)}, f32[320,128]{1,0:T(8,128)}) custom-call(s32[4,6]{1,0:T(4,128)} %convert_element_type.47.take_ref, f32[320,128]{1,0:T(8,128)} %get-tuple-element.99.refs_0_, f32[320,128]{1,0:T(8,128)} %get-tuple-element.100.refs_1_, f32[320,128]{1,0:T(8,128)} %get-tuple-element.101.refs_2_, ...), custom_call_target="tpu_custom_call" | custom-call | flops 983040 | bytes 1638400 | tf_op jit(solution)/shard_map/sum_pieces/pallas_call | solution.py:159
  243.1 1.3 collective-permute-start.18
  244.4 4.2 %collective-permute-done.17 = f32[320,128]{1,0:T(8,128)S(1)} collective-permute-done((f32[320,128]{1,0:T(8,128)}, f32[320,128]{1,0:T(8,128)S(1)}, u32[]{:S(2)}, u32[]{:S(2)}) %collective-permute-start.17) | collective-permute-done | bytes 163872 | tf_op jit(solution)/shard_map/ppermute | solution.py:185
  248.7 3.7 %collective-permute-done.18 = f32[320,128]{1,0:T(8,128)S(1)} collective-permute-done((f32[320,128]{1,0:T(8,128)}, f32[320,128]{1,0:T(8,128)S(1)}, u32[]{:S(2)}, u32[]{:S(2)}) %collective-permute-start.18) | collective-permute-done | bytes 163872 | tf_op jit(solution)/shard_map/ppermute | solution.py:185
  253.5 13.0 %attend_locally.1 = (bf16[512,2048]{1,0:T(8,128)(2,1)}, f32[512,2048]{1,0:T(8,128)}) custom-call(s32[1,640]{1,0:T(1,128)} %reshape_squeeze.2.land_ref, s32[512,1]{1,0:T(8,128)} %copy.26.seg_col_ref, s32[1,512]{1,0:T(1,128)} %bitcast.69, bf16[640,2048]{1,0:T(8,128)(2,1)} %bitcast.16.arrived_ref, bf16[512,2048]{1,0:T(8,128)(2,1)} %get-tuple-element.84.keys_ref, ...), custom_call_target="tpu_custom_call" | custom-call | flops 3489660928 | bytes 13107200 | tf_op jit(solution)/shard_map/attend_locally/pallas_call | solution.py:276
  266.5 7.1 %finish.1 = bf16[512,2048]{1,0:T(8,128)(2,1)} custom-call(s32[512,1]{1,0:T(8,128)} %copy.27.mask_ref, f32[1,2048]{1,0:T(1,128)} %bitcast.71, bf16[512,2048]{1,0:T(8,128)(2,1)} %get-tuple-element.86.query_ref, f32[512,2048]{1,0:T(8,128)} %get-tuple-element.87.local_ref, f32[2048,128]{1,0:T(8,128)} %copy-done.3), custom_call_target="tpu_custom_call" | custom-call | flops 536870912 | bytes 8388608 | tf_op jit(solution)/shard_map/finish/pallas_call | solution.py:324
  (99 shorter events, 20.0 us)
Async XLA Ops:
  0.0 2.8 %copy-start.15 = (s32[1,16,40]{2,1,0:T(8,128)S(1)}, s32[1,16,40]{2,1,0:T(8,128)}, u32[]{:S(2)}) copy-start(s32[1,16,40]{2,1,0:T(8,128)} %param.6) | copy-start | bytes 7684
  1.5 18.5 %collective-permute-start.1 = (bf16[2,256,768]{2,1,0:T(8,128)(2,1)S(1)}, bf16[2,256,768]{2,1,0:T(8,128)(2,1)S(1)}, u32[]{:S(2)}, u32[]{:S(2)}) collective-permute-start(bf16[2,256,768]{2,1,0:T(8,128)(2,1)S(1)} %slice_select_fusion.2), channel_id=1, source_target_pairs={{0,1},{1,0},{2,3},{3,2},{4,5},{5,4},{6,7},{7,6},{8,9},{9,8},{10,11... | collective-permute-start | bytes 2359304 | tf_op jit(solution)/shard_map/ppermute | solution.py:354
  20.0 0.9 copy-start.4
  26.9 52.0 %all-to-all-start = ((bf16[16,40,1536]{2,1,0:T(8,128)(2,1)}), bf16[16,40,1536]{2,1,0:T(8,128)(2,1)S(1)}, u32[]{:S(2)}, u32[]{:S(2)}) async-start(bf16[16,40,1536]{2,1,0:T(8,128)(2,1)} %bitcast.59), calls=%async_computation | async-start | bytes 3932160 | tf_op jit(solution)/shard_map/all_to_all | solution.py:381
  36.2 30.1 %collective-permute-start.7 = (bf16[2,256,1280]{2,1,0:T(8,128)(2,1)S(1)}, bf16[2,256,1280]{2,1,0:T(8,128)(2,1)S(1)}, u32[]{:S(2)}, u32[]{:S(2)}) collective-permute-start(bf16[2,256,1280]{2,1,0:T(8,128)(2,1)S(1)} %slice_select_fusion), channel_id=1, source_target_pairs={{0,1},{1,0},{2,3},{3,2},{4,5},{5,4},{6,7},{7,6},{8,9},{9,8},{10,11... | collective-permute-start | bytes 3932168 | tf_op jit(solution)/shard_map/ppermute | solution.py:354
  66.2 1.1 copy-start.2
  78.9 1.3 copy-start.1
  80.2 81.8 %all-to-all-start.2 = ((bf16[16,40,2560]{2,1,0:T(8,128)(2,1)}), bf16[16,40,2560]{2,1,0:T(8,128)(2,1)S(1)}, u32[]{:S(2)}, u32[]{:S(2)}) async-start(bf16[16,40,2560]{2,1,0:T(8,128)(2,1)} %bitcast.57), calls=%async_computation.2 | async-start | bytes 6553600 | tf_op jit(solution)/shard_map/all_to_all | solution.py:381
  85.1 3.9 %copy-start.16 = (s32[4]{0:T(128)S(1)}, s32[4]{0:T(128)}, u32[]{:S(2)}) copy-start(s32[4]{0:T(128)} %param.8) | copy-start | bytes 52
  85.1 4.1 %copy-start.13 = (s32[1,16,40]{2,1,0:T(8,128)S(1)}, s32[1,16,40]{2,1,0:T(8,128)}, u32[]{:S(2)}) copy-start(s32[1,16,40]{2,1,0:T(8,128)} %param.7) | copy-start | bytes 7684
  87.8 25.4 %collective-permute-start = (bf16[1,256,2048]{2,1,0:T(8,128)(2,1)}, bf16[1,256,2048]{2,1,0:T(8,128)(2,1)}, u32[]{:S(2)}, u32[]{:S(2)}) collective-permute-start(bf16[1,256,2048]{2,1,0:T(8,128)(2,1)} %slice_select_fusion.1), channel_id=1, source_target_pairs={{0,1},{1,0},{2,3},{3,2},{4,5},{5,4},{6,7},{7,6},{8,9},{9,8},{10,11... | collective-permute-start | bytes 3145736 | tf_op jit(solution)/shard_map/ppermute | solution.py:354
  94.2 78.1 %copy-start.14 = (s32[512]{0:T(512)}, s32[512]{0:T(512)S(1)}, u32[]{:S(2)}) copy-start(s32[512]{0:T(512)S(1)} %broadcast_add_fusion.1) | copy-start | bytes 6148
  102.2 7.5 %collective-permute-start.2 = (f32[192,128]{1,0:T(8,128)}, f32[192,128]{1,0:T(8,128)}, u32[]{:S(2)}, u32[]{:S(2)}) collective-permute-start(f32[192,128]{1,0:T(8,128)} %get-tuple-element.117), channel_id=1, source_target_pairs={{0,2},{2,0},{4,6},{6,4},{8,10},{10,8},{12,14},{14,12},{16,18},{18,... | collective-permute-start | bytes 294920 | tf_op jit(solution)/shard_map/ppermute | solution.py:185
  102.9 6.9 %collective-permute-start.3 = (f32[192,128]{1,0:T(8,128)S(1)}, f32[192,128]{1,0:T(8,128)}, u32[]{:S(2)}, u32[]{:S(2)}) collective-permute-start(f32[192,128]{1,0:T(8,128)S(1)} %get-tuple-element.116), channel_id=1, source_target_pairs={{0,4},{2,6},{4,0},{6,2},{8,12},{10,14},{12,8},{14,10},{16,20},{18,... | collective-permute-start | bytes 294920 | tf_op jit(solution)/shard_map/ppermute | solution.py:185
  103.1 7.6 %collective-permute-start.4 = (f32[192,128]{1,0:T(8,128)S(1)}, f32[192,128]{1,0:T(8,128)}, u32[]{:S(2)}, u32[]{:S(2)}) collective-permute-start(f32[192,128]{1,0:T(8,128)S(1)} %get-tuple-element.115), channel_id=1, source_target_pairs={{0,6},{2,4},{4,2},{6,0},{8,14},{10,12},{12,10},{14,8},{16,22},{18,... | collective-permute-start | bytes 294920 | tf_op jit(solution)/shard_map/ppermute | solution.py:185
  113.2 46.7 %collective-permute-start.5 = (f32[192,128]{1,0:T(8,128)}, f32[192,128]{1,0:T(8,128)S(1)}, u32[]{:S(2)}, u32[]{:S(2)}) collective-permute-start(f32[192,128]{1,0:T(8,128)} %get-tuple-element.71), channel_id=1, source_target_pairs={{0,8},{2,10},{4,12},{6,14},{8,16},{10,18},{12,20},{14,22},{16,24},... | collective-permute-start | bytes 294920 | tf_op jit(solution)/shard_map/ppermute | solution.py:221
  115.9 46.1 %collective-permute-start.6 = (f32[192,128]{1,0:T(8,128)}, f32[192,128]{1,0:T(8,128)S(1)}, u32[]{:S(2)}, u32[]{:S(2)}) collective-permute-start(f32[192,128]{1,0:T(8,128)} %get-tuple-element.71), channel_id=1, source_target_pairs={{0,16},{2,18},{4,20},{6,22},{8,24},{10,26},{12,28},{14,30},{1,17},... | collective-permute-start | bytes 294920 | tf_op jit(solution)/shard_map/ppermute | solution.py:221
  159.9 2.1 copy-start.10
  162.0 0.6 copy-start.11
  162.0 1.7 copy-start
  163.8 89.7 %all-to-all-start.1 = ((bf16[16,40,2048]{2,1,0:T(8,128)(2,1)}), bf16[16,40,2048]{2,1,0:T(8,128)(2,1)}, u32[]{:S(2)}, u32[]{:S(2)}) async-start(bf16[16,40,2048]{2,1,0:T(8,128)(2,1)} %bitcast.58), calls=%async_computation.1 | async-start | bytes 5242880 | tf_op jit(solution)/shard_map/all_to_all | solution.py:381
  176.7 10.1 %collective-permute-start.13 = (f32[192,128]{1,0:T(8,128)}, f32[192,128]{1,0:T(8,128)S(1)}, u32[]{:S(2)}, u32[]{:S(2)}) collective-permute-start(f32[192,128]{1,0:T(8,128)} %get-tuple-element.96), channel_id=1, source_target_pairs={{0,2},{2,0},{4,6},{6,4},{8,10},{10,8},{12,14},{14,12},{16,18},{18,... | collective-permute-start | bytes 294920 | tf_op jit(solution)/shard_map/ppermute | solution.py:185
  177.1 10.9 %collective-permute-start.14 = (f32[192,128]{1,0:T(8,128)}, f32[192,128]{1,0:T(8,128)S(1)}, u32[]{:S(2)}, u32[]{:S(2)}) collective-permute-start(f32[192,128]{1,0:T(8,128)} %get-tuple-element.97), channel_id=1, source_target_pairs={{0,4},{2,6},{4,0},{6,2},{8,12},{10,14},{12,8},{14,10},{16,20},{18,... | collective-permute-start | bytes 294920 | tf_op jit(solution)/shard_map/ppermute | solution.py:185
  177.4 14.3 %collective-permute-start.15 = (f32[192,128]{1,0:T(8,128)}, f32[192,128]{1,0:T(8,128)S(1)}, u32[]{:S(2)}, u32[]{:S(2)}) collective-permute-start(f32[192,128]{1,0:T(8,128)} %get-tuple-element.98), channel_id=1, source_target_pairs={{0,6},{2,4},{4,2},{6,0},{8,14},{10,12},{12,10},{14,8},{16,22},{18,... | collective-permute-start | bytes 294920 | tf_op jit(solution)/shard_map/ppermute | solution.py:185
  178.9 12.8 %copy-start.12 = (f32[192,128]{1,0:T(8,128)S(1)}, f32[192,128]{1,0:T(8,128)}, u32[]{:S(2)}) copy-start(f32[192,128]{1,0:T(8,128)} %get-tuple-element.95) | copy-start | bytes 294916
  186.1 9.2 %collective-permute-start.10 = (f32[320,128]{1,0:T(8,128)S(1)}, f32[320,128]{1,0:T(8,128)S(1)}, u32[]{:S(2)}, u32[]{:S(2)}) collective-permute-start(f32[320,128]{1,0:T(8,128)S(1)} %get-tuple-element.111), channel_id=1, source_target_pairs={{0,6},{2,4},{4,2},{6,0},{8,14},{10,12},{12,10},{14,8},{16,22},{18,... | collective-permute-start | bytes 491528 | tf_op jit(solution)/shard_map/ppermute | solution.py:185
  186.3 8.9 %collective-permute-start.8 = (f32[320,128]{1,0:T(8,128)S(1)}, f32[320,128]{1,0:T(8,128)S(1)}, u32[]{:S(2)}, u32[]{:S(2)}) collective-permute-start(f32[320,128]{1,0:T(8,128)S(1)} %get-tuple-element.113), channel_id=1, source_target_pairs={{0,2},{2,0},{4,6},{6,4},{8,10},{10,8},{12,14},{14,12},{16,18},{18,... | collective-permute-start | bytes 491528 | tf_op jit(solution)/shard_map/ppermute | solution.py:185
  186.8 14.4 %collective-permute-start.9 = (f32[320,128]{1,0:T(8,128)S(1)}, f32[320,128]{1,0:T(8,128)S(1)}, u32[]{:S(2)}, u32[]{:S(2)}) collective-permute-start(f32[320,128]{1,0:T(8,128)S(1)} %get-tuple-element.112), channel_id=1, source_target_pairs={{0,4},{2,6},{4,0},{6,2},{8,12},{10,14},{12,8},{14,10},{16,20},{18,... | collective-permute-start | bytes 491528 | tf_op jit(solution)/shard_map/ppermute | solution.py:185
  195.3 5.9 %copy-start.5 = (f32[320,128]{1,0:T(8,128)}, f32[320,128]{1,0:T(8,128)S(1)}, u32[]{:S(2)}) copy-start(f32[320,128]{1,0:T(8,128)S(1)} %collective-permute-done.10.refs_3_) | copy-start | bytes 491524
  195.3 5.9 %copy-start.6 = (f32[320,128]{1,0:T(8,128)}, f32[320,128]{1,0:T(8,128)S(1)}, u32[]{:S(2)}) copy-start(f32[320,128]{1,0:T(8,128)S(1)} %collective-permute-done.8.refs_1_) | copy-start | bytes 491524
  201.2 0.7 copy-start.7
  204.7 30.1 %collective-permute-start.11 = (f32[320,128]{1,0:T(8,128)}, f32[320,128]{1,0:T(8,128)S(1)}, u32[]{:S(2)}, u32[]{:S(2)}) collective-permute-start(f32[320,128]{1,0:T(8,128)} %get-tuple-element.79), channel_id=1, source_target_pairs={{0,8},{2,10},{4,12},{6,14},{8,16},{10,18},{12,20},{14,22},{16,24},... | collective-permute-start | bytes 491528 | tf_op jit(solution)/shard_map/ppermute | solution.py:221
  207.8 30.5 %collective-permute-start.12 = (f32[320,128]{1,0:T(8,128)}, f32[320,128]{1,0:T(8,128)S(1)}, u32[]{:S(2)}, u32[]{:S(2)}) collective-permute-start(f32[320,128]{1,0:T(8,128)} %get-tuple-element.79), channel_id=1, source_target_pairs={{0,16},{2,18},{4,20},{6,22},{8,24},{10,26},{12,28},{14,30},{1,17},... | collective-permute-start | bytes 491528 | tf_op jit(solution)/shard_map/ppermute | solution.py:221
  234.8 3.5 %copy-start.8 = (f32[320,128]{1,0:T(8,128)}, f32[320,128]{1,0:T(8,128)S(1)}, u32[]{:S(2)}) copy-start(f32[320,128]{1,0:T(8,128)S(1)} %collective-permute-done.11.refs_4_) | copy-start | bytes 491524
  238.3 0.7 copy-start.9
  241.8 2.7 collective-permute-start.16
  242.7 6.0 %collective-permute-start.17 = (f32[320,128]{1,0:T(8,128)}, f32[320,128]{1,0:T(8,128)S(1)}, u32[]{:S(2)}, u32[]{:S(2)}) collective-permute-start(f32[320,128]{1,0:T(8,128)} %get-tuple-element.107), channel_id=1, source_target_pairs={{0,4},{2,6},{4,0},{6,2},{8,12},{10,14},{12,8},{14,10},{16,20},{18,... | collective-permute-start | bytes 491528 | tf_op jit(solution)/shard_map/ppermute | solution.py:185
  243.1 9.3 %collective-permute-start.18 = (f32[320,128]{1,0:T(8,128)}, f32[320,128]{1,0:T(8,128)S(1)}, u32[]{:S(2)}, u32[]{:S(2)}) collective-permute-start(f32[320,128]{1,0:T(8,128)} %get-tuple-element.108), channel_id=1, source_target_pairs={{0,6},{2,4},{4,2},{6,0},{8,14},{10,12},{12,10},{14,8},{16,22},{18,... | collective-permute-start | bytes 491528 | tf_op jit(solution)/shard_map/ppermute | solution.py:185
  253.4 13.0 %copy-start.3 = (f32[2048,128]{1,0:T(8,128)}, f32[2048,128]{1,0:T(8,128)S(1)}, u32[]{:S(2)}) copy-start(f32[2048,128]{1,0:T(8,128)S(1)} %bitcast_dynamic-update-slice_fusion.states_ref) | copy-start | bytes 3145732

commit v5 on v4

--- a/solution.py
+++ b/solution.py
@@ -78,7 +78,7 @@
 
 def block_update(arrived, tail_slots):
     slots, columns = arrived.shape[0], arrived.shape[1] // 2
-    width = min(columns, 2 * HEAD_DIM)
+    width = math.gcd(columns, 4 * HEAD_DIM)
     blocks = columns // width
     return pl.pallas_call(
         update_kernel,
@@ -115,7 +115,7 @@
 
 def unpack_keys_values(arrived, land_row, tok_rows, start, mine, filled):
     slots, columns = arrived.shape[0], arrived.shape[1] // 2
-    width = min(columns, 2 * HEAD_DIM)
+    width = math.gcd(math.gcd(columns, start), 4 * HEAD_DIM)
     blocks, first = columns // width, start // width
     packed = jax.ShapeDtypeStruct((tok_rows, mine), arrived.dtype)
     column_spec = pl.BlockSpec((tok_rows, width), lambda j: (0, first + j))
@@ -234,8 +234,8 @@
 
 
 def local_kernel(
-    land_ref, seg_col_ref, seg_row_ref, arrived_ref, keys_ref, values_ref, query_out, local_out,
-    order, causal,
+    land_ref, seg_col_ref, seg_row_ref, mask_ref, arrived_ref, keys_ref, values_ref, query_out,
+    local_out, order, causal, carried,
 ):
     tok_rows = order.shape[0]
 
@@ -246,15 +246,18 @@
         later = lax.broadcasted_iota(jnp.int32, causal.shape, 0)
         earlier = lax.broadcasted_iota(jnp.int32, causal.shape, 1)
         open_pair = (earlier <= later) & (seg_col_ref[...] == seg_row_ref[...])
-        causal[...] = jnp.where(open_pair, 1.0, 0.0)
+        causal[...] = jnp.where(open_pair, 1.0, 0.0).astype(causal.dtype)
+        carried[...] = jnp.broadcast_to(
+            jnp.where(mask_ref[...] != 0, 1.0, 0.0).astype(carried.dtype), carried.shape
+        )
 
     query = jnp.dot(order[...], arrived_ref[...], preferred_element_type=jnp.float32).astype(
         keys_ref.dtype
     )
-    query_out[...] = query
     half = tok_rows // 2
     for part in range(query.shape[1] // HEAD_DIM):
         columns = slice(part * HEAD_DIM, (part + 1) * HEAD_DIM)
+        query_out[:, columns] = query[:, columns] * carried[...]
         for rows, reach in ((slice(0, half), half), (slice(half, tok_rows), tok_rows)):
             scores = lax.dot_general(
                 query[rows, columns],
@@ -262,16 +265,16 @@
                 (((1,), (1,)), ((), ())),
                 preferred_element_type=jnp.float32,
             )
-            weights = jnp.where(causal[rows, :reach] != 0.0, scores, 0.0).astype(keys_ref.dtype)
+            weights = scores.astype(keys_ref.dtype) * causal[rows, :reach]
             local_out[rows, columns] = jnp.dot(
                 weights, values_ref[:reach, columns], preferred_element_type=jnp.float32
             )
 
 
-def attend_locally(arrived, keys, values, land_row, seg_col, seg_row):
+def attend_locally(arrived, keys, values, land_row, seg_col, seg_row, carried_mask):
     slots, columns = arrived.shape
     tok_rows = keys.shape[0]
-    width = min(columns, 2 * HEAD_DIM)
+    width = math.gcd(columns, 4 * HEAD_DIM)
     column_spec = pl.BlockSpec((tok_rows, width), lambda j: (0, j))
     return pl.pallas_call(
         local_kernel,
@@ -284,6 +287,7 @@
             pl.BlockSpec((1, slots), lambda j: (0, 0)),
             pl.BlockSpec((tok_rows, 1), lambda j: (0, 0)),
             pl.BlockSpec((1, tok_rows), lambda j: (0, 0)),
+            pl.BlockSpec((tok_rows, 1), lambda j: (0, 0)),
             pl.BlockSpec((slots, width), lambda j: (0, j)),
             column_spec,
             column_spec,
@@ -291,7 +295,8 @@
         out_specs=(column_spec, column_spec),
         scratch_shapes=[
             pltpu.VMEM((tok_rows, slots), jnp.bfloat16),
-            pltpu.VMEM((tok_rows, tok_rows), jnp.float32),
+            pltpu.VMEM((tok_rows, tok_rows), jnp.bfloat16),
+            pltpu.VMEM((tok_rows, HEAD_DIM), jnp.bfloat16),
         ],
         cost_estimate=pl.CostEstimate(
             flops=2 * tok_rows * columns * (slots + 2 * tok_rows),
@@ -299,34 +304,41 @@
             transcendentals=0,
         ),
         name="attend_locally",
-    )(land_row, seg_col, seg_row, arrived, keys, values)
-
-
-def finish_kernel(mask_ref, gain_ref, query_ref, local_ref, states_ref, out_ref):
-    states = states_ref[...]
-    high = states.astype(query_ref.dtype)
-    low = (states - high.astype(jnp.float32)).astype(query_ref.dtype)
+    )(land_row, seg_col, seg_row, carried_mask, arrived, keys, values)
+
+
+def two_terms(value):
+    high = value.astype(jnp.bfloat16)
+    return high, (value - high.astype(jnp.float32)).astype(jnp.bfloat16)
+
+
+def finish_kernel(gain_ref, query_ref, local_ref, states_ref, out_ref):
+    ones = jnp.full((HEAD_DIM, HEAD_DIM), 1.0, jnp.bfloat16)
+
+    def product(left, right):
+        return jnp.dot(left, right, preferred_element_type=jnp.float32)
+
     for part in range(out_ref.shape[1] // HEAD_DIM):
         columns = slice(part * HEAD_DIM, (part + 1) * HEAD_DIM)
+        high, low = two_terms(states_ref[columns, :])
         query = query_ref[:, columns]
-        carried_term = jnp.dot(
-            query, high[columns], preferred_element_type=jnp.float32
-        ) + jnp.dot(query, low[columns], preferred_element_type=jnp.float32)
-        raw_out = local_ref[:, columns] + jnp.where(mask_ref[...] != 0, carried_term, 0.0)
-        inv_rms = lax.rsqrt(jnp.mean(raw_out * raw_out, axis=1, keepdims=True) + norm_eps)
-        out_ref[:, columns] = (raw_out * inv_rms * gain_ref[:, columns]).astype(out_ref.dtype)
-
-
-def finish(query, local_term, states, carried_mask, gain):
+        raw_out = local_ref[:, columns] + (product(query, high) + product(query, low))
+        high, low = two_terms(raw_out * raw_out)
+        mean = (product(high, ones) + product(low, ones)) * (1.0 / HEAD_DIM)
+        out_ref[:, columns] = (raw_out * lax.rsqrt(mean + norm_eps) * gain_ref[:, columns]).astype(
+            out_ref.dtype
+        )
+
+
+def finish(query, local_term, states, gain):
     tok_rows, columns = query.shape
-    width = min(columns, 4 * HEAD_DIM)
+    width = math.gcd(columns, 4 * HEAD_DIM)
     column_spec = pl.BlockSpec((tok_rows, width), lambda j: (0, j))
     return pl.pallas_call(
         finish_kernel,
         out_shape=jax.ShapeDtypeStruct((tok_rows, columns), jnp.bfloat16),
         grid=(columns // width,),
         in_specs=[
-            pl.BlockSpec((tok_rows, 1), lambda j: (0, 0)),
             pl.BlockSpec((1, width), lambda j: (0, j)),
             column_spec,
             column_spec,
@@ -334,12 +346,12 @@
         ],
         out_specs=column_spec,
         cost_estimate=pl.CostEstimate(
-            flops=4 * tok_rows * columns * HEAD_DIM,
+            flops=8 * tok_rows * columns * HEAD_DIM,
             bytes_accessed=8 * columns * tok_rows,
             transcendentals=0,
         ),
         name="finish",
-    )(carried_mask, gain, query, local_term, states)
+    )(gain, query, local_term, states)
 
 
 def swap_heads(qkv, plane_start, planes, start, columns):
@@ -405,7 +417,7 @@
 
     rows = send_rows[0]
     head_share = columns // HEAD_DIM
-    first = max(1, 3 * head_share // 16) * 2 * HEAD_DIM
+    first = max(2, head_share // 4) * HEAD_DIM
     second = columns - first
     outgoing = pack_chunk(qkv, swap_heads(qkv, KEYS, 2, 0, first), rows, KEYS, 2, 0, first)
     arrived = to_owners(outgoing)
@@ -425,14 +437,15 @@
     outgoing, pieces = lax.optimization_barrier((outgoing, pass_totals(sums)))
     query = to_owners(outgoing)
     sums = carry_within(block_update(arrived_next, tail_slots), within)
+    pieces, sums = lax.optimization_barrier((pieces, sums))
     states = hand_back(pieces, across)
     filled = unpack_keys_values(arrived_next, land_row, tok_rows, first, columns, filled)
-    pieces, (keys, values) = lax.optimization_barrier((pass_totals(sums), filled))
+    local = attend_locally(
+        query, *filled, land_row, segment[:, None], segment[None, :], carried_mask
+    )
+    pieces, (query, local_term) = lax.optimization_barrier((pass_totals(sums), local))
     states += hand_back(pieces, across)
-    query, local_term = attend_locally(
-        query, keys, values, land_row, segment[:, None], segment[None, :]
-    )
-    return finish(query, local_term, jnp.concatenate(states, axis=0), carried_mask, gain)
+    return finish(query, local_term, jnp.concatenate(states, axis=0), gain)
 
 
 def solution(mesh):

time: 276 us -> 288 us (1.043)
  waiting for transfers between devices: 122 us -> 150 us
  Pallas kernels: 71.2 us -> 59.4 us
  starting transfers between devices: 50.2 us -> 44.9 us
    all_to_all x3, waiting for transfers between devices: 2.5 us -> 26.4 us  [to_owners(): lax.all_to_all(outgoing, 'seq', split_axis=0, concat_axis=0, tiled=True)]
    ppermute x4, starting transfers between devices: 17.7 us -> 10.4 us  [pass_totals(): lax.ppermute(sums[near], 'seq', [(i, i + step) for i in range(seq_count -...]
    ppermute x4, waiting for transfers between devices: 53 us -> 59 us  [pass_totals(): lax.ppermute(sums[near], 'seq', [(i, i + step) for i in range(seq_count -...]
    pallas_call x3, Pallas kernels: 20.5 us -> 16 us  [pack_rows(): pl.pallas_call(pack_kernel, out_shape=jax.ShapeDtypeStruct((slots, planes...]
    unnamed x41 -> x45, local copies, waits for them, and re-layouts: 6.49 us -> 7.66 us
  transfers between devices with their start and end apart: 22 -> 22, of which waited for: 13 -> 12; matrix products, arithmetic and copies ran while one was open for 8% -> 7% of each run, Pallas kernels for 16% -> 16%
where the time goes in v5:
time: 288 us; the launch traced here: 286 us
  waiting for transfers between devices  150 us (52%)
  Pallas kernels  59.4 us (21%)
  starting transfers between devices  44.9 us (16%)
  local copies, waits for them, and re-layouts  18.2 us (6%)
  other arithmetic  11.9 us (4%)
    ppermute x4, waiting for transfers between devices, pass_totals(): lax.ppermute(sums[near], 'seq', [(i, i + step) for i in range(seq_count -...  59 us
    ppermute x3, waiting for transfers between devices, swap_heads(): return lax.ppermute(outgoing, 'head', [(0, 1), (1, 0)])  43.5 us
    all_to_all x3, waiting for transfers between devices, to_owners(): lax.all_to_all(outgoing, 'seq', split_axis=0, concat_axis=0, tiled=True)  26.4 us
    ppermute x12, waiting for transfers between devices, swap_places(): return lax.ppermute(value, 'seq', [(i, i ^ k) for i in range(seq_count)])  21.3 us
    all_to_all x3, starting transfers between devices, to_owners(): lax.all_to_all(outgoing, 'seq', split_axis=0, concat_axis=0, tiled=True)  20.8 us
    pallas_call x3, Pallas kernels, pack_rows(): pl.pallas_call(pack_kernel, out_shape=jax.ShapeDtypeStruct((slots, planes...  16 us
    pallas_call x4, Pallas kernels, sum_pieces(): pl.pallas_call(sum_kernel, out_shape=(jax.ShapeDtypeStruct((rows, HEAD_DI...  10.5 us
    ppermute x4, starting transfers between devices, pass_totals(): lax.ppermute(sums[near], 'seq', [(i, i + step) for i in range(seq_count -...  10.4 us
  transfers between devices with their start and end apart: 22, of which 12 were waited for; matrix products, arithmetic and copies ran while one was open for 7% of the time, Pallas kernels for 16%

profile of v5, /device:TPU:11, one launch (start us, length us, event | category | flops | bytes accessed | tf_op | source)
XLA Modules:
  0.0 285.6 jit_solution(17107562254104790447)
XLA Ops:
  0.0 1.3 slice_select_fusion.2
  1.3 1.3 collective-permute-start.1
  5.0 9.1 %collective-permute-done.1.refs_3_ = bf16[2,256,512]{2,1,0:T(8,128)(2,1)S(1)} collective-permute-done((bf16[2,256,512]{2,1,0:T(8,128)(2,1)S(1)}, bf16[2,256,512]{2,1,0:T(8,128)(2,1)S(1)}, u32[]{:S(2)}, u32[]{:S(2)}) %collective-permute-start.1) | collective-permute-done | bytes 524320 | tf_op jit(solution)/shard_map/ppermute | solution.py:366
  14.9 3.4 %pack_rows.3 = bf16[640,1024]{1,0:T(8,128)(2,1)} custom-call(s32[1]{0:T(128)} %bitcast.1.place_ref, s32[640,1]{1,0:T(8,128)} %sub.94.refs_0_, s32[640,1]{1,0:T(8,128)} %sub.95.refs_1_, bf16[3,256,4096]{2,1,0:T(8,128)(2,1)} %refs_2_.5, bf16[2,256,512]{2,1,0:T(8,128)(2,1)} %copy-done.5), custom_call_target="tpu_custom_call" | custom-call | flops 671088640 | bytes 2359296 | tf_op jit(solution)/shard_map/pack_rows/pallas_call | solution.py:46
  18.3 7.4 %all-to-all-start = ((bf16[16,40,1024]{2,1,0:T(8,128)(2,1)}), bf16[16,40,1024]{2,1,0:T(8,128)(2,1)S(1)}, u32[]{:S(2)}, u32[]{:S(2)}) async-start(bf16[16,40,1024]{2,1,0:T(8,128)(2,1)} %bitcast.55), calls=%async_computation | async-start | bytes 2621440 | tf_op jit(solution)/shard_map/all_to_all | solution.py:393
  25.8 2.0 slice_select_fusion
  27.8 1.3 collective-permute-start.7
  29.1 34.4 %collective-permute-done.7.refs_3_ = bf16[2,256,1536]{2,1,0:T(8,128)(2,1)S(1)} collective-permute-done((bf16[2,256,1536]{2,1,0:T(8,128)(2,1)S(1)}, bf16[2,256,1536]{2,1,0:T(8,128)(2,1)S(1)}, u32[]{:S(2)}, u32[]{:S(2)}) %collective-permute-start.7) | collective-permute-done | bytes 1572896 | tf_op jit(solution)/shard_map/ppermute | solution.py:366
  63.5 1.1 copy-done.2
  64.6 7.2 %pack_rows.5 = bf16[640,3072]{1,0:T(8,128)(2,1)} custom-call(s32[1]{0:T(128)} %bitcast.1.place_ref, s32[640,1]{1,0:T(8,128)} %sub.94.refs_0_, s32[640,1]{1,0:T(8,128)} %sub.95.refs_1_, bf16[3,256,4096]{2,1,0:T(8,128)(2,1)} %refs_2_.5, bf16[2,256,1536]{2,1,0:T(8,128)(2,1)} %copy-done.2), custom_call_target="tpu_custom_call" | custom-call | flops 2013265920 | bytes 7077888 | tf_op jit(solution)/shard_map/pack_rows/pallas_call | solution.py:46
  71.8 1.1 copy-done
  73.0 6.8 %all-to-all-start.1 = ((bf16[16,40,3072]{2,1,0:T(8,128)(2,1)}), bf16[16,40,3072]{2,1,0:T(8,128)(2,1)}, u32[]{:S(2)}, u32[]{:S(2)}) async-start(bf16[16,40,3072]{2,1,0:T(8,128)(2,1)} %bitcast.53), calls=%async_computation.1 | async-start | bytes 7864320 | tf_op jit(solution)/shard_map/all_to_all | solution.py:393
  79.9 1.7 slice_select_fusion.1
  81.5 1.3 collective-permute-start
  90.5 2.6 block_update.2
  93.1 1.6 constant_dynamic-slice_fusion.4
  95.4 1.2 collective-permute-start.3
  97.5 3.1 %unpack_keys_values.2 = (bf16[512,2048]{1,0:T(8,128)(2,1)}, bf16[512,2048]{1,0:T(8,128)(2,1)}) custom-call(s32[1,640]{1,0:T(1,128)} %reshape_squeeze.2.land_ref, bf16[640,1024]{1,0:T(8,128)(2,1)} %bitcast.51, bf16[640,1024]{1,0:T(8,128)(2,1)} %bitcast.52), custom_call_target="tpu_custom_call" | custom-call | flops 671088640 | bytes 2359296 | tf_op jit(solution)/shard_map/unpack_keys_values/pallas_call | solution.py:122
  100.6 5.2 %collective-permute-done.3.refs_2_ = f32[128,128]{1,0:T(8,128)S(1)} collective-permute-done((f32[128,128]{1,0:T(8,128)S(1)}, f32[128,128]{1,0:T(8,128)S(1)}, u32[]{:S(2)}, u32[]{:S(2)}) %collective-permute-start.3) | collective-permute-done | bytes 65568 | tf_op jit(solution)/shard_map/ppermute | solution.py:185
  106.5 2.3 sum_pieces.4
  108.9 3.6 %collective-permute-start.6 = (f32[128,128]{1,0:T(8,128)}, f32[128,128]{1,0:T(8,128)S(1)}, u32[]{:S(2)}, u32[]{:S(2)}) collective-permute-start(f32[128,128]{1,0:T(8,128)} %get-tuple-element.80), channel_id=1, source_target_pairs={{0,16},{2,18},{4,20},{6,22},{8,24},{10,26},{12,28},{14,30},{1,17},... | collective-permute-start | bytes 196616 | tf_op jit(solution)/shard_map/ppermute | solution.py:221
  112.5 1.9 collective-permute-start.5
  114.4 5.4 %pack_rows.4 = bf16[640,2048]{1,0:T(8,128)(2,1)} custom-call(s32[1]{0:T(128)} %bitcast.1.place_ref, s32[640,1]{1,0:T(8,128)} %sub.94.refs_0_, s32[640,1]{1,0:T(8,128)} %sub.95.refs_1_, bf16[3,256,4096]{2,1,0:T(8,128)(2,1)} %refs_2_.5, bf16[1,256,2048]{2,1,0:T(8,128)(2,1)} %copy-done.4), custom_call_target="tpu_custom_call" | custom-call | flops 1342177280 | bytes 4718592 | tf_op jit(solution)/shard_map/pack_rows/pallas_call | solution.py:46
  119.8 47.5 %collective-permute-done.6.refs_5_ = f32[128,128]{1,0:T(8,128)S(1)} collective-permute-done((f32[128,128]{1,0:T(8,128)}, f32[128,128]{1,0:T(8,128)S(1)}, u32[]{:S(2)}, u32[]{:S(2)}) %collective-permute-start.6) | collective-permute-done | bytes 65568 | tf_op jit(solution)/shard_map/ppermute | solution.py:221
  167.3 1.4 collective-permute-done.5.refs_4_
  169.3 6.5 %all-to-all-start.2 = ((bf16[16,40,2048]{2,1,0:T(8,128)(2,1)}), bf16[16,40,2048]{2,1,0:T(8,128)(2,1)S(1)}, u32[]{:S(2)}, u32[]{:S(2)}) async-start(bf16[16,40,2048]{2,1,0:T(8,128)(2,1)} %bitcast.54), calls=%async_computation.2 | async-start | bytes 5242880 | tf_op jit(solution)/shard_map/all_to_all | solution.py:393
  175.9 4.5 %block_update.3 = f32[1536,128]{1,0:T(8,128)} custom-call(s32[640,1]{1,0:T(8,128)} %fusion.tail_ref, bf16[640,3072]{1,0:T(8,128)(2,1)} %bitcast.14.keys_ref.values_ref, bf16[640,3072]{1,0:T(8,128)(2,1)} %bitcast.14.keys_ref.values_ref), custom_call_target="tpu_custom_call" | custom-call | flops 251658240 | bytes 4718592 | tf_op jit(solution)/shard_map/block_update/pallas_call | solution.py:83
  180.3 2.0 constant_dynamic-slice_fusion
  182.8 1.2 collective-permute-start.9
  187.3 5.7 %unpack_keys_values.3 = (bf16[512,2048]{1,0:T(8,128)(2,1)}, bf16[512,2048]{1,0:T(8,128)(2,1)}) custom-call(s32[1,640]{1,0:T(1,128)} %reshape_squeeze.2.land_ref, bf16[640,3072]{1,0:T(8,128)(2,1)} %bitcast.14.keys_ref.values_ref, bf16[640,3072]{1,0:T(8,128)(2,1)} %bitcast.14.keys_ref.values_ref, ...), custom_call_target="tpu_custom_call", output_to_operand_aliasing={{0}: (3, {}), {1}: (4, {})} | custom-call | flops 2013265920 | bytes 7077888 | tf_op jit(solution)/shard_map/unpack_keys_values/pallas_call | solution.py:122
  193.0 3.0 %collective-permute-done.10.refs_3_ = f32[384,128]{1,0:T(8,128)S(1)} collective-permute-done((f32[384,128]{1,0:T(8,128)S(1)}, f32[384,128]{1,0:T(8,128)S(1)}, u32[]{:S(2)}, u32[]{:S(2)}) %collective-permute-start.10) | collective-permute-done | bytes 196640 | tf_op jit(solution)/shard_map/ppermute | solution.py:185
  196.0 3.7 %collective-permute-done.9.refs_2_ = f32[384,128]{1,0:T(8,128)} collective-permute-done((f32[384,128]{1,0:T(8,128)S(1)}, f32[384,128]{1,0:T(8,128)}, u32[]{:S(2)}, u32[]{:S(2)}) %collective-permute-start.9) | collective-permute-done | bytes 196640 | tf_op jit(solution)/shard_map/ppermute | solution.py:185
  199.7 2.9 %sum_pieces.5 = (f32[384,128]{1,0:T(8,128)}, f32[384,128]{1,0:T(8,128)}, f32[384,128]{1,0:T(8,128)}, f32[384,128]{1,0:T(8,128)}, f32[384,128]{1,0:T(8,128)}) custom-call(s32[5,4]{1,0:T(8,128)} %convert_element_type.46.take_ref, f32[384,128]{1,0:T(8,128)} %get-tuple-element.136.refs_0_, f32[384,128]{1,0:T(8,128)} %collective-permute-done.8.refs_1_, ...), custom_call_target="tpu_custom_call" | custom-call | flops 983040 | bytes 1769472 | tf_op jit(solution)/shard_map/sum_pieces/pallas_call | solution.py:159
  202.6 2.4 sum_pieces.6
  205.9 2.3 collective-permute-start.14
  208.2 26.4 %all-to-all-done.2 = bf16[16,40,2048]{2,1,0:T(8,128)(2,1)S(1)} async-done(((bf16[16,40,2048]{2,1,0:T(8,128)(2,1)}), bf16[16,40,2048]{2,1,0:T(8,128)(2,1)S(1)}, u32[]{:S(2)}, u32[]{:S(2)}) %all-to-all-start.2) | async-done | bytes 2621472 | tf_op jit(solution)/shard_map/all_to_all | solution.py:393
  234.6 1.5 copy-done.1
  236.1 10.4 %attend_locally.1 = (bf16[512,2048]{1,0:T(8,128)(2,1)}, f32[512,2048]{1,0:T(8,128)}) custom-call(s32[1,640]{1,0:T(1,128)} %reshape_squeeze.2.land_ref, s32[512,1]{1,0:T(8,128)} %copy.26.seg_col_ref, s32[1,512]{1,0:T(1,128)} %bitcast.66, s32[512,1]{1,0:T(8,128)} %copy.27.mask_ref, bf16[640,2048]{1,0:T(8,128)(2,1)} %bitcast.56, ...), custom_call_target="tpu_custom_call" | custom-call | flops 3489660928 | bytes 13107200 | tf_op jit(solution)/shard_map/attend_locally/pallas_call | solution.py:279
  246.5 3.0 %collective-permute-start.12 = (f32[384,128]{1,0:T(8,128)S(1)}, f32[384,128]{1,0:T(8,128)S(1)}, u32[]{:S(2)}, u32[]{:S(2)}) collective-permute-start(f32[384,128]{1,0:T(8,128)S(1)} %copy-done.18), channel_id=1, source_target_pairs={{0,16},{2,18},{4,20},{6,22},{8,24},{10,26},{12,28},{14,30},{1,17},... | collective-permute-start | bytes 589832 | tf_op jit(solution)/shard_map/ppermute | solution.py:221
  249.5 1.9 collective-permute-start.11
  251.6 5.8 %collective-permute-done.12.refs_5_ = f32[384,128]{1,0:T(8,128)S(1)} collective-permute-done((f32[384,128]{1,0:T(8,128)S(1)}, f32[384,128]{1,0:T(8,128)S(1)}, u32[]{:S(2)}, u32[]{:S(2)}) %collective-permute-start.12) | collective-permute-done | bytes 196640 | tf_op jit(solution)/shard_map/ppermute | solution.py:221
  257.4 4.2 %collective-permute-done.11.refs_4_ = f32[384,128]{1,0:T(8,128)S(1)} collective-permute-done((f32[384,128]{1,0:T(8,128)S(1)}, f32[384,128]{1,0:T(8,128)S(1)}, u32[]{:S(2)}, u32[]{:S(2)}) %collective-permute-start.11) | collective-permute-done | bytes 196640 | tf_op jit(solution)/shard_map/ppermute | solution.py:221
  262.3 2.9 %sum_pieces.7 = (f32[384,128]{1,0:T(8,128)}, f32[384,128]{1,0:T(8,128)}, f32[384,128]{1,0:T(8,128)}, f32[384,128]{1,0:T(8,128)}) custom-call(s32[4,6]{1,0:T(4,128)} %convert_element_type.47.take_ref, f32[384,128]{1,0:T(8,128)} %get-tuple-element.121.refs_0_, f32[384,128]{1,0:T(8,128)} %get-tuple-element.122.refs_1_, f32[384,128]{1,0:T(8,128)} %get-tuple-element.123.refs_2_, ...), custom_call_target="tpu_custom_call" | custom-call | flops 1179648 | bytes 1966080 | tf_op jit(solution)/shard_map/sum_pieces/pallas_call | solution.py:159
  265.7 1.7 collective-permute-start.18
  267.4 5.0 %collective-permute-done.17 = f32[384,128]{1,0:T(8,128)S(1)} collective-permute-done((f32[384,128]{1,0:T(8,128)}, f32[384,128]{1,0:T(8,128)S(1)}, u32[]{:S(2)}, u32[]{:S(2)}) %collective-permute-start.17) | collective-permute-done | bytes 196640 | tf_op jit(solution)/shard_map/ppermute | solution.py:185
  272.4 4.4 %collective-permute-done.18 = f32[384,128]{1,0:T(8,128)S(1)} collective-permute-done((f32[384,128]{1,0:T(8,128)}, f32[384,128]{1,0:T(8,128)S(1)}, u32[]{:S(2)}, u32[]{:S(2)}) %collective-permute-start.18) | collective-permute-done | bytes 196640 | tf_op jit(solution)/shard_map/ppermute | solution.py:185
  276.8 1.0 pad_maximum_fusion
  278.9 6.7 %finish.1 = bf16[512,2048]{1,0:T(8,128)(2,1)} custom-call(f32[1,2048]{1,0:T(1,128)} %bitcast.68, bf16[512,2048]{1,0:T(8,128)(2,1)} %get-tuple-element.108.query_ref, f32[512,2048]{1,0:T(8,128)} %get-tuple-element.109.local_ref, f32[2048,128]{1,0:T(8,128)} %copy-done.3), custom_call_target="tpu_custom_call" | custom-call | flops 1073741824 | bytes 8388608 | tf_op jit(solution)/shard_map/finish/pallas_call | solution.py:337
  (103 shorter events, 20.3 us)
Async XLA Ops:
  1.3 12.9 %collective-permute-start.1 = (bf16[2,256,512]{2,1,0:T(8,128)(2,1)S(1)}, bf16[2,256,512]{2,1,0:T(8,128)(2,1)S(1)}, u32[]{:S(2)}, u32[]{:S(2)}) collective-permute-start(bf16[2,256,512]{2,1,0:T(8,128)(2,1)S(1)} %slice_select_fusion.2), channel_id=1, source_target_pairs={{0,1},{1,0},{2,3},{3,2},{4,5},{5,4},{6,7},{7,6},{8,9},{9,8},{10,11... | collective-permute-start | bytes 1572872 | tf_op jit(solution)/shard_map/ppermute | solution.py:366
  14.1 0.8 copy-start.5
  18.3 53.5 %all-to-all-start = ((bf16[16,40,1024]{2,1,0:T(8,128)(2,1)}), bf16[16,40,1024]{2,1,0:T(8,128)(2,1)S(1)}, u32[]{:S(2)}, u32[]{:S(2)}) async-start(bf16[16,40,1024]{2,1,0:T(8,128)(2,1)} %bitcast.55), calls=%async_computation | async-start | bytes 2621440 | tf_op jit(solution)/shard_map/all_to_all | solution.py:393
  27.8 35.7 %collective-permute-start.7 = (bf16[2,256,1536]{2,1,0:T(8,128)(2,1)S(1)}, bf16[2,256,1536]{2,1,0:T(8,128)(2,1)S(1)}, u32[]{:S(2)}, u32[]{:S(2)}) collective-permute-start(bf16[2,256,1536]{2,1,0:T(8,128)(2,1)S(1)} %slice_select_fusion), channel_id=1, source_target_pairs={{0,1},{1,0},{2,3},{3,2},{4,5},{5,4},{6,7},{7,6},{8,9},{9,8},{10,11... | collective-permute-start | bytes 4718600 | tf_op jit(solution)/shard_map/ppermute | solution.py:366
  63.5 1.1 copy-start.2
  71.8 1.2 copy-start
  73.0 95.7 %all-to-all-start.1 = ((bf16[16,40,3072]{2,1,0:T(8,128)(2,1)}), bf16[16,40,3072]{2,1,0:T(8,128)(2,1)}, u32[]{:S(2)}, u32[]{:S(2)}) async-start(bf16[16,40,3072]{2,1,0:T(8,128)(2,1)} %bitcast.53), calls=%async_computation.1 | async-start | bytes 7864320 | tf_op jit(solution)/shard_map/all_to_all | solution.py:393
  79.8 3.0 %copy-start.17 = (s32[4]{0:T(128)S(1)}, s32[4]{0:T(128)}, u32[]{:S(2)}) copy-start(s32[4]{0:T(128)} %param.8) | copy-start | bytes 52
  79.8 6.5 %copy-start.9 = (s32[1,16,40]{2,1,0:T(8,128)S(1)}, s32[1,16,40]{2,1,0:T(8,128)}, u32[]{:S(2)}) copy-start(s32[1,16,40]{2,1,0:T(8,128)} %param.7) | copy-start | bytes 7684
  81.5 27.3 %collective-permute-start = (bf16[1,256,2048]{2,1,0:T(8,128)(2,1)S(1)}, bf16[1,256,2048]{2,1,0:T(8,128)(2,1)S(1)}, u32[]{:S(2)}, u32[]{:S(2)}) collective-permute-start(bf16[1,256,2048]{2,1,0:T(8,128)(2,1)S(1)} %slice_select_fusion.1), channel_id=1, source_target_pairs={{0,1},{1,0},{2,3},{3,2},{4,5},{5,4},{6,7},{7,6},{8,9},{9,8},{10,11... | collective-permute-start | bytes 3145736 | tf_op jit(solution)/shard_map/ppermute | solution.py:366
  88.9 97.5 %copy-start.16 = (s32[512]{0:T(512)}, s32[512]{0:T(512)S(1)}, u32[]{:S(2)}) copy-start(s32[512]{0:T(512)S(1)} %broadcast_add_fusion.1) | copy-start | bytes 6148
  94.6 6.0 %collective-permute-start.4 = (f32[128,128]{1,0:T(8,128)S(1)}, f32[128,128]{1,0:T(8,128)S(1)}, u32[]{:S(2)}, u32[]{:S(2)}) collective-permute-start(f32[128,128]{1,0:T(8,128)S(1)} %get-tuple-element.137), channel_id=1, source_target_pairs={{0,6},{2,4},{4,2},{6,0},{8,14},{10,12},{12,10},{14,8},{16,22},{18,... | collective-permute-start | bytes 196616 | tf_op jit(solution)/shard_map/ppermute | solution.py:185
  95.4 10.4 %collective-permute-start.3 = (f32[128,128]{1,0:T(8,128)S(1)}, f32[128,128]{1,0:T(8,128)S(1)}, u32[]{:S(2)}, u32[]{:S(2)}) collective-permute-start(f32[128,128]{1,0:T(8,128)S(1)} %get-tuple-element.138), channel_id=1, source_target_pairs={{0,4},{2,6},{4,0},{6,2},{8,12},{10,14},{12,8},{14,10},{16,20},{18,... | collective-permute-start | bytes 196616 | tf_op jit(solution)/shard_map/ppermute | solution.py:185
  96.6 9.3 %collective-permute-start.2 = (f32[128,128]{1,0:T(8,128)S(1)}, f32[128,128]{1,0:T(8,128)S(1)}, u32[]{:S(2)}, u32[]{:S(2)}) collective-permute-start(f32[128,128]{1,0:T(8,128)S(1)} %get-tuple-element.139), channel_id=1, source_target_pairs={{0,2},{2,0},{4,6},{6,4},{8,10},{10,8},{12,14},{14,12},{16,18},{18,... | collective-permute-start | bytes 196616 | tf_op jit(solution)/shard_map/ppermute | solution.py:185
  100.6 5.3 %copy-start.12 = (f32[128,128]{1,0:T(8,128)}, f32[128,128]{1,0:T(8,128)S(1)}, u32[]{:S(2)}) copy-start(f32[128,128]{1,0:T(8,128)S(1)} %collective-permute-done.4.refs_3_) | copy-start | bytes 196612
  105.9 0.6 copy-start.13
  105.9 0.6 copy-start.14
  108.9 5.5 %copy-start.4 = (bf16[1,256,2048]{2,1,0:T(8,128)(2,1)}, bf16[1,256,2048]{2,1,0:T(8,128)(2,1)S(1)}, u32[]{:S(2)}) copy-start(bf16[1,256,2048]{2,1,0:T(8,128)(2,1)S(1)} %collective-permute-done.refs_3_) | copy-start | bytes 3145732
  108.9 58.4 %collective-permute-start.6 = (f32[128,128]{1,0:T(8,128)}, f32[128,128]{1,0:T(8,128)S(1)}, u32[]{:S(2)}, u32[]{:S(2)}) collective-permute-start(f32[128,128]{1,0:T(8,128)} %get-tuple-element.80), channel_id=1, source_target_pairs={{0,16},{2,18},{4,20},{6,22},{8,24},{10,26},{12,28},{14,30},{1,17},... | collective-permute-start | bytes 196616 | tf_op jit(solution)/shard_map/ppermute | solution.py:221
  112.5 56.2 %collective-permute-start.5 = (f32[128,128]{1,0:T(8,128)}, f32[128,128]{1,0:T(8,128)S(1)}, u32[]{:S(2)}, u32[]{:S(2)}) collective-permute-start(f32[128,128]{1,0:T(8,128)} %get-tuple-element.80), channel_id=1, source_target_pairs={{0,8},{2,10},{4,12},{6,14},{8,16},{10,18},{12,20},{14,22},{16,24},... | collective-permute-start | bytes 196616 | tf_op jit(solution)/shard_map/ppermute | solution.py:221
  167.3 1.4 copy-start.10
  168.7 0.6 copy-start.11
  169.3 65.3 %all-to-all-start.2 = ((bf16[16,40,2048]{2,1,0:T(8,128)(2,1)}), bf16[16,40,2048]{2,1,0:T(8,128)(2,1)S(1)}, u32[]{:S(2)}, u32[]{:S(2)}) async-start(bf16[16,40,2048]{2,1,0:T(8,128)(2,1)} %bitcast.54), calls=%async_computation.2 | async-start | bytes 5242880 | tf_op jit(solution)/shard_map/all_to_all | solution.py:393
  182.3 13.7 %collective-permute-start.10 = (f32[384,128]{1,0:T(8,128)S(1)}, f32[384,128]{1,0:T(8,128)S(1)}, u32[]{:S(2)}, u32[]{:S(2)}) collective-permute-start(f32[384,128]{1,0:T(8,128)S(1)} %get-tuple-element.133), channel_id=1, source_target_pairs={{0,6},{2,4},{4,2},{6,0},{8,14},{10,12},{12,10},{14,8},{16,22},{18,... | collective-permute-start | bytes 589832 | tf_op jit(solution)/shard_map/ppermute | solution.py:185
  182.8 16.9 %collective-permute-start.9 = (f32[384,128]{1,0:T(8,128)S(1)}, f32[384,128]{1,0:T(8,128)}, u32[]{:S(2)}, u32[]{:S(2)}) collective-permute-start(f32[384,128]{1,0:T(8,128)S(1)} %get-tuple-element.134), channel_id=1, source_target_pairs={{0,4},{2,6},{4,0},{6,2},{8,12},{10,14},{12,8},{14,10},{16,20},{18,... | collective-permute-start | bytes 589832 | tf_op jit(solution)/shard_map/ppermute | solution.py:185
  184.0 15.7 %collective-permute-start.8 = (f32[384,128]{1,0:T(8,128)S(1)}, f32[384,128]{1,0:T(8,128)}, u32[]{:S(2)}, u32[]{:S(2)}) collective-permute-start(f32[384,128]{1,0:T(8,128)S(1)} %get-tuple-element.135), channel_id=1, source_target_pairs={{0,2},{2,0},{4,6},{6,4},{8,10},{10,8},{12,14},{14,12},{16,18},{18,... | collective-permute-start | bytes 589832 | tf_op jit(solution)/shard_map/ppermute | solution.py:185
  196.0 3.7 %copy-start.8 = (f32[384,128]{1,0:T(8,128)}, f32[384,128]{1,0:T(8,128)S(1)}, u32[]{:S(2)}) copy-start(f32[384,128]{1,0:T(8,128)S(1)} %collective-permute-done.10.refs_3_) | copy-start | bytes 589828
  204.9 46.5 %collective-permute-start.13 = (f32[128,128]{1,0:T(8,128)}, f32[128,128]{1,0:T(8,128)S(1)}, u32[]{:S(2)}, u32[]{:S(2)}) collective-permute-start(f32[128,128]{1,0:T(8,128)} %get-tuple-element.118), channel_id=1, source_target_pairs={{0,2},{2,0},{4,6},{6,4},{8,10},{10,8},{12,14},{14,12},{16,18},{18,... | collective-permute-start | bytes 196616 | tf_op jit(solution)/shard_map/ppermute | solution.py:185
  205.9 45.6 %collective-permute-start.14 = (f32[128,128]{1,0:T(8,128)}, f32[128,128]{1,0:T(8,128)S(1)}, u32[]{:S(2)}, u32[]{:S(2)}) collective-permute-start(f32[128,128]{1,0:T(8,128)} %get-tuple-element.119), channel_id=1, source_target_pairs={{0,4},{2,6},{4,0},{6,2},{8,12},{10,14},{12,8},{14,10},{16,20},{18,... | collective-permute-start | bytes 196616 | tf_op jit(solution)/shard_map/ppermute | solution.py:185
  208.1 43.4 %collective-permute-start.15 = (f32[128,128]{1,0:T(8,128)}, f32[128,128]{1,0:T(8,128)S(1)}, u32[]{:S(2)}, u32[]{:S(2)}) collective-permute-start(f32[128,128]{1,0:T(8,128)} %get-tuple-element.120), channel_id=1, source_target_pairs={{0,6},{2,4},{4,2},{6,0},{8,14},{10,12},{12,10},{14,8},{16,22},{18,... | collective-permute-start | bytes 196616 | tf_op jit(solution)/shard_map/ppermute | solution.py:185
  234.6 1.5 copy-start.1
  236.1 10.4 %copy-start.18 = (f32[384,128]{1,0:T(8,128)S(1)}, f32[384,128]{1,0:T(8,128)}, u32[]{:S(2)}) copy-start(f32[384,128]{1,0:T(8,128)} %get-tuple-element.98) | copy-start | bytes 589828
  236.1 15.4 %copy-start.15 = (f32[128,128]{1,0:T(8,128)S(1)}, f32[128,128]{1,0:T(8,128)}, u32[]{:S(2)}) copy-start(f32[128,128]{1,0:T(8,128)} %get-tuple-element.117) | copy-start | bytes 196612
  246.5 10.9 %collective-permute-start.12 = (f32[384,128]{1,0:T(8,128)S(1)}, f32[384,128]{1,0:T(8,128)S(1)}, u32[]{:S(2)}, u32[]{:S(2)}) collective-permute-start(f32[384,128]{1,0:T(8,128)S(1)} %copy-done.18), channel_id=1, source_target_pairs={{0,16},{2,18},{4,20},{6,22},{8,24},{10,26},{12,28},{14,30},{1,17},... | collective-permute-start | bytes 589832 | tf_op jit(solution)/shard_map/ppermute | solution.py:221
  249.5 12.1 %collective-permute-start.11 = (f32[384,128]{1,0:T(8,128)S(1)}, f32[384,128]{1,0:T(8,128)S(1)}, u32[]{:S(2)}, u32[]{:S(2)}) collective-permute-start(f32[384,128]{1,0:T(8,128)S(1)} %copy-done.18), channel_id=1, source_target_pairs={{0,8},{2,10},{4,12},{6,14},{8,16},{10,18},{12,20},{14,22},{16,24},... | collective-permute-start | bytes 589832 | tf_op jit(solution)/shard_map/ppermute | solution.py:221
  257.4 4.2 %copy-start.6 = (f32[384,128]{1,0:T(8,128)}, f32[384,128]{1,0:T(8,128)S(1)}, u32[]{:S(2)}) copy-start(f32[384,128]{1,0:T(8,128)S(1)} %collective-permute-done.12.refs_5_) | copy-start | bytes 589828
  261.6 0.7 copy-start.7
  265.2 2.2 collective-permute-start.16
  265.7 6.7 %collective-permute-start.17 = (f32[384,128]{1,0:T(8,128)}, f32[384,128]{1,0:T(8,128)S(1)}, u32[]{:S(2)}, u32[]{:S(2)}) collective-permute-start(f32[384,128]{1,0:T(8,128)} %get-tuple-element.129), channel_id=1, source_target_pairs={{0,4},{2,6},{4,0},{6,2},{8,12},{10,14},{12,8},{14,10},{16,20},{18,... | collective-permute-start | bytes 589832 | tf_op jit(solution)/shard_map/ppermute | solution.py:185
  265.7 11.1 %collective-permute-start.18 = (f32[384,128]{1,0:T(8,128)}, f32[384,128]{1,0:T(8,128)S(1)}, u32[]{:S(2)}, u32[]{:S(2)}) collective-permute-start(f32[384,128]{1,0:T(8,128)} %get-tuple-element.130), channel_id=1, source_target_pairs={{0,6},{2,4},{4,2},{6,0},{8,14},{10,12},{12,10},{14,8},{16,22},{18,... | collective-permute-start | bytes 589832 | tf_op jit(solution)/shard_map/ppermute | solution.py:185
  277.9 1.0 copy-start.3

commit v6 on v5

--- a/solution.py
+++ b/solution.py
@@ -12,6 +12,9 @@
 norm_eps = 1e-06
 
 QUERY, KEYS, VALUES = 0, 1, 2
+
+PACK_WEIGHT = 20
+ATTEND_WEIGHT = 7
 
 
 def pack_kernel(place_ref, *refs):
@@ -55,7 +58,7 @@
             scratch_shapes=[pltpu.VMEM((slots, length), jnp.bfloat16) for length in lens],
         ),
         cost_estimate=pl.CostEstimate(
-            flops=2 * slots * sum(lens) * planes * columns,
+            flops=PACK_WEIGHT * 2 * slots * sum(lens) * planes * columns,
             bytes_accessed=2 * planes * columns * (slots + sum(lens)),
             transcendentals=0,
         ),
@@ -233,10 +236,16 @@
     ]
 
 
-def local_kernel(
-    land_ref, seg_col_ref, seg_row_ref, mask_ref, arrived_ref, keys_ref, values_ref, query_out,
-    local_out, order, causal, carried,
+def two_terms(value):
+    high = value.astype(jnp.bfloat16)
+    return high, (value - high.astype(jnp.float32)).astype(jnp.bfloat16)
+
+
+def attend_kernel(
+    land_ref, seg_col_ref, seg_row_ref, mask_ref, gain_ref, arrived_ref, keys_ref, values_ref,
+    states_ref, *refs,
 ):
+    out_ref, order, causal, carried = refs[-4:]
     tok_rows = order.shape[0]
 
     @pl.when(pl.program_id(0) == 0)
@@ -251,107 +260,71 @@
             jnp.where(mask_ref[...] != 0, 1.0, 0.0).astype(carried.dtype), carried.shape
         )
 
-    query = jnp.dot(order[...], arrived_ref[...], preferred_element_type=jnp.float32).astype(
-        keys_ref.dtype
-    )
+    def product(left, right):
+        return jnp.dot(left, right, preferred_element_type=jnp.float32)
+
+    ones = jnp.full((HEAD_DIM, HEAD_DIM), 1.0, jnp.bfloat16)
+    query = product(order[...], arrived_ref[...]).astype(keys_ref.dtype)
     half = tok_rows // 2
     for part in range(query.shape[1] // HEAD_DIM):
         columns = slice(part * HEAD_DIM, (part + 1) * HEAD_DIM)
-        query_out[:, columns] = query[:, columns] * carried[...]
+        state_high, state_low = two_terms(states_ref[columns, :])
         for rows, reach in ((slice(0, half), half), (slice(half, tok_rows), tok_rows)):
+            queries = query[rows, columns]
             scores = lax.dot_general(
-                query[rows, columns],
+                queries,
                 keys_ref[:reach, columns],
                 (((1,), (1,)), ((), ())),
                 preferred_element_type=jnp.float32,
             )
             weights = scores.astype(keys_ref.dtype) * causal[rows, :reach]
-            local_out[rows, columns] = jnp.dot(
-                weights, values_ref[:reach, columns], preferred_element_type=jnp.float32
+            carrying = queries * carried[rows, :]
+            raw_out = product(weights, values_ref[:reach, columns]) + (
+                product(carrying, state_high) + product(carrying, state_low)
             )
-
-
-def attend_locally(arrived, keys, values, land_row, seg_col, seg_row, carried_mask):
+            square_high, square_low = two_terms(raw_out * raw_out)
+            mean = (product(square_high, ones) + product(square_low, ones)) * (1.0 / HEAD_DIM)
+            out_ref[rows, columns] = (
+                raw_out * lax.rsqrt(mean + norm_eps) * gain_ref[:, columns]
+            ).astype(out_ref.dtype)
+
+
+def attend(arrived, keys, values, states, tables, gain, start, filled):
     slots, columns = arrived.shape
-    tok_rows = keys.shape[0]
-    width = math.gcd(columns, 4 * HEAD_DIM)
-    column_spec = pl.BlockSpec((tok_rows, width), lambda j: (0, j))
+    tok_rows, mine = keys.shape
+    width = math.gcd(math.gcd(columns, start), 4 * HEAD_DIM)
+    first = start // width
+    column_spec = pl.BlockSpec((tok_rows, width), lambda j: (0, first + j))
     return pl.pallas_call(
-        local_kernel,
-        out_shape=(
-            jax.ShapeDtypeStruct((tok_rows, columns), jnp.bfloat16),
-            jax.ShapeDtypeStruct((tok_rows, columns), jnp.float32),
-        ),
+        attend_kernel,
+        out_shape=jax.ShapeDtypeStruct((tok_rows, mine), jnp.bfloat16),
         grid=(columns // width,),
         in_specs=[
             pl.BlockSpec((1, slots), lambda j: (0, 0)),
             pl.BlockSpec((tok_rows, 1), lambda j: (0, 0)),
             pl.BlockSpec((1, tok_rows), lambda j: (0, 0)),
             pl.BlockSpec((tok_rows, 1), lambda j: (0, 0)),
+            pl.BlockSpec((1, width), lambda j: (0, first + j)),
             pl.BlockSpec((slots, width), lambda j: (0, j)),
             column_spec,
             column_spec,
-        ],
-        out_specs=(column_spec, column_spec),
+            pl.BlockSpec((width, HEAD_DIM), lambda j: (first + j, 0)),
+        ]
+        + [pl.BlockSpec(memory_space=pl.ANY) for _ in filled],
+        out_specs=column_spec,
         scratch_shapes=[
             pltpu.VMEM((tok_rows, slots), jnp.bfloat16),
             pltpu.VMEM((tok_rows, tok_rows), jnp.bfloat16),
             pltpu.VMEM((tok_rows, HEAD_DIM), jnp.bfloat16),
         ],
+        input_output_aliases={9: 0} if filled else {},
         cost_estimate=pl.CostEstimate(
-            flops=2 * tok_rows * columns * (slots + 2 * tok_rows),
-            bytes_accessed=2 * columns * (slots + 5 * tok_rows),
+            flops=ATTEND_WEIGHT * 2 * tok_rows * columns * (slots + 2 * tok_rows + 4 * HEAD_DIM),
+            bytes_accessed=2 * columns * (slots + 4 * tok_rows),
             transcendentals=0,
         ),
-        name="attend_locally",
-    )(land_row, seg_col, seg_row, carried_mask, arrived, keys, values)
-
-
-def two_terms(value):
-    high = value.astype(jnp.bfloat16)
-    return high, (value - high.astype(jnp.float32)).astype(jnp.bfloat16)
-
-
-def finish_kernel(gain_ref, query_ref, local_ref, states_ref, out_ref):
-    ones = jnp.full((HEAD_DIM, HEAD_DIM), 1.0, jnp.bfloat16)
-
-    def product(left, right):
-        return jnp.dot(left, right, preferred_element_type=jnp.float32)
-
-    for part in range(out_ref.shape[1] // HEAD_DIM):
-        columns = slice(part * HEAD_DIM, (part + 1) * HEAD_DIM)
-        high, low = two_terms(states_ref[columns, :])
-        query = query_ref[:, columns]
-        raw_out = local_ref[:, columns] + (product(query, high) + product(query, low))
-        high, low = two_terms(raw_out * raw_out)
-        mean = (product(high, ones) + product(low, ones)) * (1.0 / HEAD_DIM)
-        out_ref[:, columns] = (raw_out * lax.rsqrt(mean + norm_eps) * gain_ref[:, columns]).astype(
-            out_ref.dtype
-        )
-
-
-def finish(query, local_term, states, gain):
-    tok_rows, columns = query.shape
-    width = math.gcd(columns, 4 * HEAD_DIM)
-    column_spec = pl.BlockSpec((tok_rows, width), lambda j: (0, j))
-    return pl.pallas_call(
-        finish_kernel,
-        out_shape=jax.ShapeDtypeStruct((tok_rows, columns), jnp.bfloat16),
-        grid=(columns // width,),
-        in_specs=[
-            pl.BlockSpec((1, width), lambda j: (0, j)),
-            column_spec,
-            column_spec,
-            pl.BlockSpec((width, HEAD_DIM), lambda j: (j, 0)),
-        ],
-        out_specs=column_spec,
-        cost_estimate=pl.CostEstimate(
-            flops=8 * tok_rows * columns * HEAD_DIM,
-            bytes_accessed=8 * columns * tok_rows,
-            transcendentals=0,
-        ),
-        name="finish",
-    )(gain, query, local_term, states)
+        name="attend",
+    )(*tables, gain, arrived, keys, values, states, *filled)
 
 
 def swap_heads(qkv, plane_start, planes, start, columns):
@@ -371,14 +344,14 @@
     return jnp.moveaxis(incoming, 0, 1).reshape(planes, head_count * rows, columns)
 
 
-def pack_chunk(qkv, incoming, send_rows, plane_start, planes, start, columns):
+def pack_chunk(qkv, incoming, send_rows, plane_start, planes, start, columns, offset=0):
     head_count = lax.axis_size("head")
     place = lax.axis_index("head")
     rows = qkv.shape[1]
     mine = qkv.shape[2] // head_count
     slots = send_rows.reshape(-1, 1)
     width = math.gcd(math.gcd(columns, start), math.gcd(mine, 512))
-    picks, sources = (slots,), ((incoming, 0, lambda at, width: 0),)
+    picks, sources = (slots,), ((incoming, 0, lambda at, width: offset // width),)
     if head_count == 2:
         picks = (slots - place * rows, slots - (1 - place) * rows)
         sources = (
@@ -433,19 +406,25 @@
         (incoming, sums, filled, (tail_slots, within, across, segment, carried_mask))
     )
     tail_slots, within, across, segment, carried_mask = tables
-    outgoing = pack_chunk(qkv, incoming, rows, QUERY, 1, 0, columns)
+    part = max(2, head_share // 2) * HEAD_DIM
+    outgoing, outgoing_next = (
+        pack_chunk(qkv, incoming, rows, QUERY, 1, start, size, start)
+        for start, size in ((0, part), (part, columns - part))
+    )
     outgoing, pieces = lax.optimization_barrier((outgoing, pass_totals(sums)))
     query = to_owners(outgoing)
     sums = carry_within(block_update(arrived_next, tail_slots), within)
-    pieces, sums = lax.optimization_barrier((pieces, sums))
     states = hand_back(pieces, across)
-    filled = unpack_keys_values(arrived_next, land_row, tok_rows, first, columns, filled)
-    local = attend_locally(
-        query, *filled, land_row, segment[:, None], segment[None, :], carried_mask
-    )
-    pieces, (query, local_term) = lax.optimization_barrier((pass_totals(sums), local))
-    states += hand_back(pieces, across)
-    return finish(query, local_term, jnp.concatenate(states, axis=0), gain)
+    keys, values = unpack_keys_values(arrived_next, land_row, tok_rows, first, columns, filled)
+    outgoing_next, sums, states, keys, values = lax.optimization_barrier(
+        (outgoing_next, sums, states, keys, values)
+    )
+    pieces = pass_totals(sums)
+    query_next = to_owners(outgoing_next)
+    states = jnp.concatenate(states + hand_back(pieces, across), axis=0)
+    tables = (land_row, segment[:, None], segment[None, :], carried_mask)
+    out = attend(query, keys, values, states, tables, gain, 0, ())
+    return attend(query_next, keys, values, states, tables, gain, part, (out,))
 
 
 def solution(mesh):

time: 288 us -> 264 us (0.917)
  waiting for transfers between devices: 150 us -> 118 us
  starting transfers between devices: 44.9 us -> 49.3 us
  Pallas kernels: 59.4 us -> 62.3 us
    all_to_all x3 -> x4, waiting for transfers between devices: 26.4 us -> 2.3 us  [to_owners(): lax.all_to_all(outgoing, 'seq', split_axis=0, concat_axis=0, tiled=True)]
    ppermute x3, waiting for transfers between devices: 43.5 us -> 28.6 us  [swap_heads(): return lax.ppermute(outgoing, 'head', [(0, 1), (1, 0)])]
    all_to_all x3 -> x4, starting transfers between devices: 20.8 us -> 26.6 us  [to_owners(): lax.all_to_all(outgoing, 'seq', split_axis=0, concat_axis=0, tiled=True)]
    ppermute x12, waiting for transfers between devices: 21.3 us -> 26.2 us  [swap_places(): return lax.ppermute(value, 'seq', [(i, i ^ k) for i in range(seq_count)])]
    unnamed x45 -> x47, local copies, waits for them, and re-layouts: 7.66 us -> 9.6 us
    pallas_call x3 -> x4, Pallas kernels: 16 us -> 17.4 us  [pack_rows(): pl.pallas_call(pack_kernel, out_shape=jax.ShapeDtypeStruct((slots, planes...]
  transfers between devices with their start and end apart: 22 -> 23, of which waited for: 12 -> 12; matrix products, arithmetic and copies ran while one was open for 7% -> 10% of each run, Pallas kernels for 16% -> 20%
where the time goes in v6:
time: 264 us; the launch traced here: 263 us
  waiting for transfers between devices  118 us (45%)
  Pallas kernels  62.3 us (24%)
  starting transfers between devices  49.3 us (19%)
  local copies, waits for them, and re-layouts  20.9 us (8%)
  other arithmetic  11.5 us (4%)
    ppermute x4, waiting for transfers between devices, pass_totals(): lax.ppermute(sums[near], 'seq', [(i, i + step) for i in range(seq_count -...  60.6 us
    ppermute x3, waiting for transfers between devices, swap_heads(): return lax.ppermute(outgoing, 'head', [(0, 1), (1, 0)])  28.6 us
    all_to_all x4, starting transfers between devices, to_owners(): lax.all_to_all(outgoing, 'seq', split_axis=0, concat_axis=0, tiled=True)  26.6 us
    ppermute x12, waiting for transfers between devices, swap_places(): return lax.ppermute(value, 'seq', [(i, i ^ k) for i in range(seq_count)])  26.2 us
    pallas_call x2, Pallas kernels, attend(): pl.pallas_call(attend_kernel, out_shape=jax.ShapeDtypeStruct((tok_rows, m...  18.4 us
    pallas_call x4, Pallas kernels, pack_rows(): pl.pallas_call(pack_kernel, out_shape=jax.ShapeDtypeStruct((slots, planes...  17.4 us
    ppermute x4, starting transfers between devices, pass_totals(): lax.ppermute(sums[near], 'seq', [(i, i + step) for i in range(seq_count -...  10.5 us
    pallas_call x4, Pallas kernels, sum_pieces(): pl.pallas_call(sum_kernel, out_shape=(jax.ShapeDtypeStruct((rows, HEAD_DI...  10.5 us
  transfers between devices with their start and end apart: 23, of which 12 were waited for; matrix products, arithmetic and copies ran while one was open for 10% of the time, Pallas kernels for 20%

profile of v6, /device:TPU:11, one launch (start us, length us, event | category | flops | bytes accessed | tf_op | source)
XLA Modules:
  0.0 262.5 jit_solution(17431365115052718905)
XLA Ops:
  0.0 1.3 slice_select_fusion.2
  1.3 1.3 collective-permute-start.1
  2.6 2.0 slice_select_fusion
  6.7 7.5 %collective-permute-done.1.refs_3_ = bf16[2,256,512]{2,1,0:T(8,128)(2,1)S(1)} collective-permute-done((bf16[2,256,512]{2,1,0:T(8,128)(2,1)S(1)}, bf16[2,256,512]{2,1,0:T(8,128)(2,1)S(1)}, u32[]{:S(2)}, u32[]{:S(2)}) %collective-permute-start.1) | collective-permute-done | bytes 524320 | tf_op jit(solution)/shard_map/ppermute | solution.py:339
  14.9 3.4 %pack_rows.4 = bf16[640,1024]{1,0:T(8,128)(2,1)} custom-call(s32[1]{0:T(128)} %bitcast.7.place_ref, s32[640,1]{1,0:T(8,128)} %sub.99.refs_0_, s32[640,1]{1,0:T(8,128)} %sub.100.refs_1_, bf16[3,256,4096]{2,1,0:T(8,128)(2,1)} %refs_2_.7, bf16[2,256,512]{2,1,0:T(8,128)(2,1)} %copy-done.19), custom_call_target="tpu_custom_call" | custom-call | flops 13421772800 | bytes 2359296 | tf_op jit(solution)/shard_map/pack_rows/pallas_call | solution.py:49
  18.3 8.6 %all-to-all-start = ((bf16[16,40,1024]{2,1,0:T(8,128)(2,1)}), bf16[16,40,1024]{2,1,0:T(8,128)(2,1)S(1)}, u32[]{:S(2)}, u32[]{:S(2)}) async-start(bf16[16,40,1024]{2,1,0:T(8,128)(2,1)} %bitcast.59), calls=%async_computation | async-start | bytes 2621440 | tf_op jit(solution)/shard_map/all_to_all | solution.py:366
  26.9 21.1 %collective-permute-done.5.refs_3_ = bf16[2,256,1536]{2,1,0:T(8,128)(2,1)} collective-permute-done((bf16[2,256,1536]{2,1,0:T(8,128)(2,1)S(1)}, bf16[2,256,1536]{2,1,0:T(8,128)(2,1)}, u32[]{:S(2)}, u32[]{:S(2)}) %collective-permute-start.5) | collective-permute-done | bytes 1572896 | tf_op jit(solution)/shard_map/ppermute | solution.py:339
  47.9 7.2 %pack_rows.6 = bf16[640,3072]{1,0:T(8,128)(2,1)} custom-call(s32[1]{0:T(128)} %bitcast.7.place_ref, s32[640,1]{1,0:T(8,128)} %sub.99.refs_0_, s32[640,1]{1,0:T(8,128)} %sub.100.refs_1_, bf16[3,256,4096]{2,1,0:T(8,128)(2,1)} %refs_2_.7, bf16[2,256,1536]{2,1,0:T(8,128)(2,1)} %collective-permute-done.5.refs_3_), custom_call_target="tpu_custom_call" | custom-call | flops 40265318400 | bytes 7077888 | tf_op jit(solution)/shard_map/pack_rows/pallas_call | solution.py:49
  55.1 2.3 all-to-all-done
  57.4 1.1 copy-done
  58.5 5.1 %all-to-all-start.1 = ((bf16[16,40,3072]{2,1,0:T(8,128)(2,1)}), bf16[16,40,3072]{2,1,0:T(8,128)(2,1)}, u32[]{:S(2)}, u32[]{:S(2)}) async-start(bf16[16,40,3072]{2,1,0:T(8,128)(2,1)} %bitcast.55), calls=%async_computation.1 | async-start | bytes 7864320 | tf_op jit(solution)/shard_map/all_to_all | solution.py:366
  63.6 1.7 slice_select_fusion.1
  65.3 1.3 collective-permute-start
  74.5 2.6 block_update.2
  77.1 1.6 constant_dynamic-slice_fusion.4
  79.6 1.4 collective-permute-start.4
  81.7 3.2 %unpack_keys_values.2 = (bf16[512,2048]{1,0:T(8,128)(2,1)}, bf16[512,2048]{1,0:T(8,128)(2,1)}) custom-call(s32[1,640]{1,0:T(1,128)} %reshape_squeeze.2.land_ref, bf16[640,1024]{1,0:T(8,128)(2,1)} %bitcast.53, bf16[640,1024]{1,0:T(8,128)(2,1)} %bitcast.54), custom_call_target="tpu_custom_call" | custom-call | flops 671088640 | bytes 2359296 | tf_op jit(solution)/shard_map/unpack_keys_values/pallas_call | solution.py:125
  84.9 5.2 %collective-permute-done.4.refs_3_ = f32[128,128]{1,0:T(8,128)S(1)} collective-permute-done((f32[128,128]{1,0:T(8,128)S(1)}, f32[128,128]{1,0:T(8,128)S(1)}, u32[]{:S(2)}, u32[]{:S(2)}) %collective-permute-start.4) | collective-permute-done | bytes 65568 | tf_op jit(solution)/shard_map/ppermute | solution.py:188
  90.7 2.3 sum_pieces.4
  93.1 3.3 %collective-permute-start.10 = (f32[128,128]{1,0:T(8,128)}, f32[128,128]{1,0:T(8,128)S(1)}, u32[]{:S(2)}, u32[]{:S(2)}) collective-permute-start(f32[128,128]{1,0:T(8,128)} %get-tuple-element.81), channel_id=1, source_target_pairs={{0,16},{2,18},{4,20},{6,22},{8,24},{10,26},{12,28},{14,30},{1,17},... | collective-permute-start | bytes 196616 | tf_op jit(solution)/shard_map/ppermute | solution.py:224
  96.4 1.9 collective-permute-start.9
  98.3 3.4 %pack_rows.7 = bf16[640,1024]{1,0:T(8,128)(2,1)} custom-call(s32[1]{0:T(128)} %bitcast.7.place_ref, s32[640,1]{1,0:T(8,128)} %sub.99.refs_0_, s32[640,1]{1,0:T(8,128)} %sub.100.refs_1_, bf16[3,256,4096]{2,1,0:T(8,128)(2,1)} %refs_2_.7, bf16[1,256,2048]{2,1,0:T(8,128)(2,1)} %copy-done.18), custom_call_target="tpu_custom_call" | custom-call | flops 13421772800 | bytes 2359296 | tf_op jit(solution)/shard_map/pack_rows/pallas_call | solution.py:49
  101.7 49.4 %collective-permute-done.10.refs_5_ = f32[128,128]{1,0:T(8,128)S(1)} collective-permute-done((f32[128,128]{1,0:T(8,128)}, f32[128,128]{1,0:T(8,128)S(1)}, u32[]{:S(2)}, u32[]{:S(2)}) %collective-permute-start.10) | collective-permute-done | bytes 65568 | tf_op jit(solution)/shard_map/ppermute | solution.py:224
  151.1 1.4 collective-permute-done.9.refs_4_
  152.5 6.5 %all-to-all-start.3 = ((bf16[16,40,1024]{2,1,0:T(8,128)(2,1)}), bf16[16,40,1024]{2,1,0:T(8,128)(2,1)S(1)}, u32[]{:S(2)}, u32[]{:S(2)}) async-start(bf16[16,40,1024]{2,1,0:T(8,128)(2,1)} %bitcast.57), calls=%async_computation.3 | async-start | bytes 2621440 | tf_op jit(solution)/shard_map/all_to_all | solution.py:366
  159.6 2.4 sum_pieces.6
  162.7 1.5 collective-permute-start.13
  164.2 3.5 %pack_rows.5 = bf16[640,1024]{1,0:T(8,128)(2,1)} custom-call(s32[1]{0:T(128)} %bitcast.7.place_ref, s32[640,1]{1,0:T(8,128)} %sub.99.refs_0_, s32[640,1]{1,0:T(8,128)} %sub.100.refs_1_, bf16[3,256,4096]{2,1,0:T(8,128)(2,1)} %refs_2_.7, bf16[1,256,2048]{2,1,0:T(8,128)(2,1)} %copy-done.18), custom_call_target="tpu_custom_call" | custom-call | flops 13421772800 | bytes 2359296 | tf_op jit(solution)/shard_map/pack_rows/pallas_call | solution.py:49
  170.3 4.5 %block_update.3 = f32[1536,128]{1,0:T(8,128)} custom-call(s32[640,1]{1,0:T(8,128)} %fusion.tail_ref, bf16[640,3072]{1,0:T(8,128)(2,1)} %bitcast.16.keys_ref.values_ref, bf16[640,3072]{1,0:T(8,128)(2,1)} %bitcast.16.keys_ref.values_ref), custom_call_target="tpu_custom_call" | custom-call | flops 251658240 | bytes 4718592 | tf_op jit(solution)/shard_map/block_update/pallas_call | solution.py:86
  174.8 2.0 constant_dynamic-slice_fusion
  176.9 2.0 collective-permute-start.8
  178.9 5.7 %unpack_keys_values.3 = (bf16[512,2048]{1,0:T(8,128)(2,1)}, bf16[512,2048]{1,0:T(8,128)(2,1)}) custom-call(s32[1,640]{1,0:T(1,128)} %reshape_squeeze.2.land_ref, bf16[640,3072]{1,0:T(8,128)(2,1)} %bitcast.16.keys_ref.values_ref, bf16[640,3072]{1,0:T(8,128)(2,1)} %bitcast.16.keys_ref.values_ref, ...), custom_call_target="tpu_custom_call", output_to_operand_aliasing={{0}: (3, {}), {1}: (4, {})} | custom-call | flops 2013265920 | bytes 7077888 | tf_op jit(solution)/shard_map/unpack_keys_values/pallas_call | solution.py:125
  184.7 1.3 collective-permute-done.7.refs_2_
  186.0 6.0 %collective-permute-done.8.refs_3_ = f32[384,128]{1,0:T(8,128)S(1)} collective-permute-done((f32[384,128]{1,0:T(8,128)S(1)}, f32[384,128]{1,0:T(8,128)S(1)}, u32[]{:S(2)}, u32[]{:S(2)}) %collective-permute-start.8) | collective-permute-done | bytes 196640 | tf_op jit(solution)/shard_map/ppermute | solution.py:188
  192.7 2.9 %sum_pieces.5 = (f32[384,128]{1,0:T(8,128)}, f32[384,128]{1,0:T(8,128)}, f32[384,128]{1,0:T(8,128)}, f32[384,128]{1,0:T(8,128)}, f32[384,128]{1,0:T(8,128)}) custom-call(s32[5,4]{1,0:T(8,128)} %convert_element_type.46.take_ref, f32[384,128]{1,0:T(8,128)} %get-tuple-element.118.refs_0_, f32[384,128]{1,0:T(8,128)} %copy-done.5, f32[384,128]{1,0:T(8,128)} %copy-done.6, ...), custom_call_target="tpu_custom_call" | custom-call | flops 983040 | bytes 1769472 | tf_op jit(solution)/shard_map/sum_pieces/pallas_call | solution.py:162
  195.5 2.5 collective-permute-start.14
  198.1 2.8 %collective-permute-start.15 = (f32[384,128]{1,0:T(8,128)}, f32[384,128]{1,0:T(8,128)S(1)}, u32[]{:S(2)}, u32[]{:S(2)}) collective-permute-start(f32[384,128]{1,0:T(8,128)} %get-tuple-element.107), channel_id=1, source_target_pairs={{0,16},{2,18},{4,20},{6,22},{8,24},{10,26},{12,28},{14,30},{1,17},... | collective-permute-start | bytes 589832 | tf_op jit(solution)/shard_map/ppermute | solution.py:224
  200.9 6.4 %all-to-all-start.2 = ((bf16[16,40,1024]{2,1,0:T(8,128)(2,1)}), bf16[16,40,1024]{2,1,0:T(8,128)(2,1)S(1)}, u32[]{:S(2)}, u32[]{:S(2)}) async-start(bf16[16,40,1024]{2,1,0:T(8,128)(2,1)} %bitcast.25), calls=%async_computation.2 | async-start | bytes 2621440 | tf_op jit(solution)/shard_map/all_to_all | solution.py:366
  208.5 9.8 %collective-permute-done.15.refs_5_ = f32[384,128]{1,0:T(8,128)S(1)} collective-permute-done((f32[384,128]{1,0:T(8,128)}, f32[384,128]{1,0:T(8,128)S(1)}, u32[]{:S(2)}, u32[]{:S(2)}) %collective-permute-start.15) | collective-permute-done | bytes 196640 | tf_op jit(solution)/shard_map/ppermute | solution.py:224
  219.0 2.9 %sum_pieces.7 = (f32[384,128]{1,0:T(8,128)}, f32[384,128]{1,0:T(8,128)}, f32[384,128]{1,0:T(8,128)}, f32[384,128]{1,0:T(8,128)}) custom-call(s32[4,6]{1,0:T(4,128)} %convert_element_type.47.take_ref, f32[384,128]{1,0:T(8,128)} %get-tuple-element.103.refs_0_, f32[384,128]{1,0:T(8,128)} %get-tuple-element.104.refs_1_, f32[384,128]{1,0:T(8,128)} %get-tuple-element.105.refs_2_, ...), custom_call_target="tpu_custom_call" | custom-call | flops 1179648 | bytes 1966080 | tf_op jit(solution)/shard_map/sum_pieces/pallas_call | solution.py:162
  221.9 0.9 collective-permute-start.16
  222.9 1.2 collective-permute-start.17
  225.8 7.2 %collective-permute-done.17 = f32[384,128]{1,0:T(8,128)S(1)} collective-permute-done((f32[384,128]{1,0:T(8,128)}, f32[384,128]{1,0:T(8,128)S(1)}, u32[]{:S(2)}, u32[]{:S(2)}) %collective-permute-start.17) | collective-permute-done | bytes 196640 | tf_op jit(solution)/shard_map/ppermute | solution.py:188
  233.1 6.1 %collective-permute-done.18 = f32[384,128]{1,0:T(8,128)S(1)} collective-permute-done((f32[384,128]{1,0:T(8,128)}, f32[384,128]{1,0:T(8,128)S(1)}, u32[]{:S(2)}, u32[]{:S(2)}) %collective-permute-start.18) | collective-permute-done | bytes 196640 | tf_op jit(solution)/shard_map/ppermute | solution.py:188
  239.2 1.0 pad_maximum_fusion
  243.0 9.2 %attend.2.refs_0_ = bf16[512,2048]{1,0:T(8,128)(2,1)} custom-call(s32[1,640]{1,0:T(1,128)} %reshape_squeeze.2.land_ref, s32[512,1]{1,0:T(8,128)} %copy.35.seg_col_ref, s32[1,512]{1,0:T(1,128)} %bitcast.69, s32[512,1]{1,0:T(8,128)} %copy.36.mask_ref, f32[1,2048]{1,0:T(1,128)} %bitcast.73, bf16[640,1024]{1,0:T(8,128)(2,1)} %bitcast.56, ...), custom_call_target="tpu_custom_call" | custom-call | flops 15971909632 | bytes 5505024 | tf_op jit(solution)/shard_map/attend/pallas_call | solution.py:298
  252.2 1.1 copy-done.2
  253.3 9.2 %attend.3 = bf16[512,2048]{1,0:T(8,128)(2,1)} custom-call(s32[1,640]{1,0:T(1,128)} %reshape_squeeze.2.land_ref, s32[512,1]{1,0:T(8,128)} %copy.35.seg_col_ref, s32[1,512]{1,0:T(1,128)} %bitcast.70, s32[512,1]{1,0:T(8,128)} %copy.36.mask_ref, f32[1,2048]{1,0:T(1,128)} %bitcast.74, bf16[640,1024]{1,0:T(8,128)(2,1)} %bitcast.58, ...), custom_call_target="tpu_custom_call", output_to_operand_aliasing={{}: (9, {})} | custom-call | flops 15971909632 | bytes 5505024 | tf_op jit(solution)/shard_map/attend/pallas_call | solution.py:298
  (109 shorter events, 23.6 us)
Async XLA Ops:
  1.3 3.7 %copy-start.16 = (s32[1,16,40]{2,1,0:T(8,128)S(1)}, s32[1,16,40]{2,1,0:T(8,128)}, u32[]{:S(2)}) copy-start(s32[1,16,40]{2,1,0:T(8,128)} %param.6) | copy-start | bytes 7684
  1.3 12.9 %collective-permute-start.1 = (bf16[2,256,512]{2,1,0:T(8,128)(2,1)S(1)}, bf16[2,256,512]{2,1,0:T(8,128)(2,1)S(1)}, u32[]{:S(2)}, u32[]{:S(2)}) collective-permute-start(bf16[2,256,512]{2,1,0:T(8,128)(2,1)S(1)} %slice_select_fusion.2), channel_id=1, source_target_pairs={{0,1},{1,0},{2,3},{3,2},{4,5},{5,4},{6,7},{7,6},{8,9},{9,8},{10,11... | collective-permute-start | bytes 1572872 | tf_op jit(solution)/shard_map/ppermute | solution.py:339
  4.6 43.3 %collective-permute-start.5 = (bf16[2,256,1536]{2,1,0:T(8,128)(2,1)S(1)}, bf16[2,256,1536]{2,1,0:T(8,128)(2,1)}, u32[]{:S(2)}, u32[]{:S(2)}) collective-permute-start(bf16[2,256,1536]{2,1,0:T(8,128)(2,1)S(1)} %slice_select_fusion), channel_id=1, source_target_pairs={{0,1},{1,0},{2,3},{3,2},{4,5},{5,4},{6,7},{7,6},{8,9},{9,8},{10,11... | collective-permute-start | bytes 4718600 | tf_op jit(solution)/shard_map/ppermute | solution.py:339
  14.1 0.8 copy-start.19
  18.3 39.1 %all-to-all-start = ((bf16[16,40,1024]{2,1,0:T(8,128)(2,1)}), bf16[16,40,1024]{2,1,0:T(8,128)(2,1)S(1)}, u32[]{:S(2)}, u32[]{:S(2)}) async-start(bf16[16,40,1024]{2,1,0:T(8,128)(2,1)} %bitcast.59), calls=%async_computation | async-start | bytes 2621440 | tf_op jit(solution)/shard_map/all_to_all | solution.py:366
  57.4 1.1 copy-start
  58.5 94.0 %all-to-all-start.1 = ((bf16[16,40,3072]{2,1,0:T(8,128)(2,1)}), bf16[16,40,3072]{2,1,0:T(8,128)(2,1)}, u32[]{:S(2)}, u32[]{:S(2)}) async-start(bf16[16,40,3072]{2,1,0:T(8,128)(2,1)} %bitcast.55), calls=%async_computation.1 | async-start | bytes 7864320 | tf_op jit(solution)/shard_map/all_to_all | solution.py:366
  63.6 3.0 %copy-start.17 = (s32[4]{0:T(128)S(1)}, s32[4]{0:T(128)}, u32[]{:S(2)}) copy-start(s32[4]{0:T(128)} %param.8) | copy-start | bytes 52
  63.6 3.2 %copy-start.8 = (s32[1,16,40]{2,1,0:T(8,128)S(1)}, s32[1,16,40]{2,1,0:T(8,128)}, u32[]{:S(2)}) copy-start(s32[1,16,40]{2,1,0:T(8,128)} %param.7) | copy-start | bytes 7684
  65.3 27.8 %collective-permute-start = (bf16[1,256,2048]{2,1,0:T(8,128)(2,1)S(1)}, bf16[1,256,2048]{2,1,0:T(8,128)(2,1)S(1)}, u32[]{:S(2)}, u32[]{:S(2)}) collective-permute-start(bf16[1,256,2048]{2,1,0:T(8,128)(2,1)S(1)} %slice_select_fusion.1), channel_id=1, source_target_pairs={{0,1},{1,0},{2,3},{3,2},{4,5},{5,4},{6,7},{7,6},{8,9},{9,8},{10,11... | collective-permute-start | bytes 3145736 | tf_op jit(solution)/shard_map/ppermute | solution.py:339
  72.9 95.4 %copy-start.15 = (s32[512]{0:T(512)}, s32[512]{0:T(512)S(1)}, u32[]{:S(2)}) copy-start(s32[512]{0:T(512)S(1)} %broadcast_add_fusion.1) | copy-start | bytes 6148
  78.7 6.2 %collective-permute-start.2 = (f32[128,128]{1,0:T(8,128)S(1)}, f32[128,128]{1,0:T(8,128)S(1)}, u32[]{:S(2)}, u32[]{:S(2)}) collective-permute-start(f32[128,128]{1,0:T(8,128)S(1)} %get-tuple-element.125), channel_id=1, source_target_pairs={{0,2},{2,0},{4,6},{6,4},{8,10},{10,8},{12,14},{14,12},{16,18},{18,... | collective-permute-start | bytes 196616 | tf_op jit(solution)/shard_map/ppermute | solution.py:188
  79.3 5.6 %collective-permute-start.3 = (f32[128,128]{1,0:T(8,128)S(1)}, f32[128,128]{1,0:T(8,128)S(1)}, u32[]{:S(2)}, u32[]{:S(2)}) collective-permute-start(f32[128,128]{1,0:T(8,128)S(1)} %get-tuple-element.124), channel_id=1, source_target_pairs={{0,4},{2,6},{4,0},{6,2},{8,12},{10,14},{12,8},{14,10},{16,20},{18,... | collective-permute-start | bytes 196616 | tf_op jit(solution)/shard_map/ppermute | solution.py:188
  79.6 10.5 %collective-permute-start.4 = (f32[128,128]{1,0:T(8,128)S(1)}, f32[128,128]{1,0:T(8,128)S(1)}, u32[]{:S(2)}, u32[]{:S(2)}) collective-permute-start(f32[128,128]{1,0:T(8,128)S(1)} %get-tuple-element.123), channel_id=1, source_target_pairs={{0,6},{2,4},{4,2},{6,0},{8,14},{10,12},{12,10},{14,8},{16,22},{18,... | collective-permute-start | bytes 196616 | tf_op jit(solution)/shard_map/ppermute | solution.py:188
  84.9 5.2 %copy-start.11 = (f32[128,128]{1,0:T(8,128)}, f32[128,128]{1,0:T(8,128)S(1)}, u32[]{:S(2)}) copy-start(f32[128,128]{1,0:T(8,128)S(1)} %collective-permute-done.2.refs_1_) | copy-start | bytes 196612
  84.9 5.2 %copy-start.12 = (f32[128,128]{1,0:T(8,128)}, f32[128,128]{1,0:T(8,128)S(1)}, u32[]{:S(2)}) copy-start(f32[128,128]{1,0:T(8,128)S(1)} %collective-permute-done.3.refs_2_) | copy-start | bytes 196612
  90.1 0.6 copy-start.13
  93.1 5.2 %copy-start.18 = (bf16[1,256,2048]{2,1,0:T(8,128)(2,1)}, bf16[1,256,2048]{2,1,0:T(8,128)(2,1)S(1)}, u32[]{:S(2)}) copy-start(bf16[1,256,2048]{2,1,0:T(8,128)(2,1)S(1)} %collective-permute-done.refs_3_) | copy-start | bytes 3145732
  93.1 58.0 %collective-permute-start.10 = (f32[128,128]{1,0:T(8,128)}, f32[128,128]{1,0:T(8,128)S(1)}, u32[]{:S(2)}, u32[]{:S(2)}) collective-permute-start(f32[128,128]{1,0:T(8,128)} %get-tuple-element.81), channel_id=1, source_target_pairs={{0,16},{2,18},{4,20},{6,22},{8,24},{10,26},{12,28},{14,30},{1,17},... | collective-permute-start | bytes 196616 | tf_op jit(solution)/shard_map/ppermute | solution.py:224
  96.4 56.1 %collective-permute-start.9 = (f32[128,128]{1,0:T(8,128)}, f32[128,128]{1,0:T(8,128)S(1)}, u32[]{:S(2)}, u32[]{:S(2)}) collective-permute-start(f32[128,128]{1,0:T(8,128)} %get-tuple-element.81), channel_id=1, source_target_pairs={{0,8},{2,10},{4,12},{6,14},{8,16},{10,18},{12,20},{14,22},{16,24},... | collective-permute-start | bytes 196616 | tf_op jit(solution)/shard_map/ppermute | solution.py:224
  151.1 8.5 %copy-start.9 = (f32[128,128]{1,0:T(8,128)}, f32[128,128]{1,0:T(8,128)S(1)}, u32[]{:S(2)}) copy-start(f32[128,128]{1,0:T(8,128)S(1)} %collective-permute-done.10.refs_5_) | copy-start | bytes 196612
  152.5 7.1 %copy-start.10 = (f32[128,128]{1,0:T(8,128)}, f32[128,128]{1,0:T(8,128)S(1)}, u32[]{:S(2)}) copy-start(f32[128,128]{1,0:T(8,128)S(1)} %collective-permute-done.9.refs_4_) | copy-start | bytes 196612
  152.5 48.4 %all-to-all-start.3 = ((bf16[16,40,1024]{2,1,0:T(8,128)(2,1)}), bf16[16,40,1024]{2,1,0:T(8,128)(2,1)S(1)}, u32[]{:S(2)}, u32[]{:S(2)}) async-start(bf16[16,40,1024]{2,1,0:T(8,128)(2,1)} %bitcast.57), calls=%async_computation.3 | async-start | bytes 2621440 | tf_op jit(solution)/shard_map/all_to_all | solution.py:366
  162.0 8.0 %collective-permute-start.11 = (f32[128,128]{1,0:T(8,128)}, f32[128,128]{1,0:T(8,128)S(1)}, u32[]{:S(2)}, u32[]{:S(2)}) collective-permute-start(f32[128,128]{1,0:T(8,128)} %get-tuple-element.89), channel_id=1, source_target_pairs={{0,2},{2,0},{4,6},{6,4},{8,10},{10,8},{12,14},{14,12},{16,18},{18,... | collective-permute-start | bytes 196616 | tf_op jit(solution)/shard_map/ppermute | solution.py:188
  162.4 7.6 %collective-permute-start.12 = (f32[128,128]{1,0:T(8,128)}, f32[128,128]{1,0:T(8,128)S(1)}, u32[]{:S(2)}, u32[]{:S(2)}) collective-permute-start(f32[128,128]{1,0:T(8,128)} %get-tuple-element.90), channel_id=1, source_target_pairs={{0,4},{2,6},{4,0},{6,2},{8,12},{10,14},{12,8},{14,10},{16,20},{18,... | collective-permute-start | bytes 196616 | tf_op jit(solution)/shard_map/ppermute | solution.py:188
  162.7 7.6 %copy-start.14 = (f32[128,128]{1,0:T(8,128)S(1)}, f32[128,128]{1,0:T(8,128)}, u32[]{:S(2)}) copy-start(f32[128,128]{1,0:T(8,128)} %get-tuple-element.88) | copy-start | bytes 196612
  162.7 7.6 %collective-permute-start.13 = (f32[128,128]{1,0:T(8,128)}, f32[128,128]{1,0:T(8,128)S(1)}, u32[]{:S(2)}, u32[]{:S(2)}) collective-permute-start(f32[128,128]{1,0:T(8,128)} %get-tuple-element.91), channel_id=1, source_target_pairs={{0,6},{2,4},{4,2},{6,0},{8,14},{10,12},{12,10},{14,8},{16,22},{18,... | collective-permute-start | bytes 196616 | tf_op jit(solution)/shard_map/ppermute | solution.py:188
  176.8 7.9 %collective-permute-start.6 = (f32[384,128]{1,0:T(8,128)S(1)}, f32[384,128]{1,0:T(8,128)S(1)}, u32[]{:S(2)}, u32[]{:S(2)}) collective-permute-start(f32[384,128]{1,0:T(8,128)S(1)} %get-tuple-element.117), channel_id=1, source_target_pairs={{0,2},{2,0},{4,6},{6,4},{8,10},{10,8},{12,14},{14,12},{16,18},{18,... | collective-permute-start | bytes 589832 | tf_op jit(solution)/shard_map/ppermute | solution.py:188
  176.9 9.1 %collective-permute-start.7 = (f32[384,128]{1,0:T(8,128)S(1)}, f32[384,128]{1,0:T(8,128)S(1)}, u32[]{:S(2)}, u32[]{:S(2)}) collective-permute-start(f32[384,128]{1,0:T(8,128)S(1)} %get-tuple-element.116), channel_id=1, source_target_pairs={{0,4},{2,6},{4,0},{6,2},{8,12},{10,14},{12,8},{14,10},{16,20},{18,... | collective-permute-start | bytes 589832 | tf_op jit(solution)/shard_map/ppermute | solution.py:188
  176.9 15.0 %collective-permute-start.8 = (f32[384,128]{1,0:T(8,128)S(1)}, f32[384,128]{1,0:T(8,128)S(1)}, u32[]{:S(2)}, u32[]{:S(2)}) collective-permute-start(f32[384,128]{1,0:T(8,128)S(1)} %get-tuple-element.115), channel_id=1, source_target_pairs={{0,6},{2,4},{4,2},{6,0},{8,14},{10,12},{12,10},{14,8},{16,22},{18,... | collective-permute-start | bytes 589832 | tf_op jit(solution)/shard_map/ppermute | solution.py:188
  184.7 7.3 %copy-start.5 = (f32[384,128]{1,0:T(8,128)}, f32[384,128]{1,0:T(8,128)S(1)}, u32[]{:S(2)}) copy-start(f32[384,128]{1,0:T(8,128)S(1)} %collective-permute-done.6.refs_1_) | copy-start | bytes 589828
  186.0 6.0 %copy-start.6 = (f32[384,128]{1,0:T(8,128)}, f32[384,128]{1,0:T(8,128)S(1)}, u32[]{:S(2)}) copy-start(f32[384,128]{1,0:T(8,128)S(1)} %collective-permute-done.7.refs_2_) | copy-start | bytes 589828
  192.0 0.7 copy-start.7
  195.5 13.0 %collective-permute-start.14 = (f32[384,128]{1,0:T(8,128)}, f32[384,128]{1,0:T(8,128)S(1)}, u32[]{:S(2)}, u32[]{:S(2)}) collective-permute-start(f32[384,128]{1,0:T(8,128)} %get-tuple-element.107), channel_id=1, source_target_pairs={{0,8},{2,10},{4,12},{6,14},{8,16},{10,18},{12,20},{14,22},{16,24},... | collective-permute-start | bytes 589832 | tf_op jit(solution)/shard_map/ppermute | solution.py:224
  198.1 20.3 %collective-permute-start.15 = (f32[384,128]{1,0:T(8,128)}, f32[384,128]{1,0:T(8,128)S(1)}, u32[]{:S(2)}, u32[]{:S(2)}) collective-permute-start(f32[384,128]{1,0:T(8,128)} %get-tuple-element.107), channel_id=1, source_target_pairs={{0,16},{2,18},{4,20},{6,22},{8,24},{10,26},{12,28},{14,30},{1,17},... | collective-permute-start | bytes 589832 | tf_op jit(solution)/shard_map/ppermute | solution.py:224
  200.9 24.3 %copy-start.1 = (bf16[16,40,1024]{2,1,0:T(8,128)(2,1)}, bf16[16,40,1024]{2,1,0:T(8,128)(2,1)S(1)}, u32[]{:S(2)}) copy-start(bf16[16,40,1024]{2,1,0:T(8,128)(2,1)S(1)} %all-to-all-done.3) | copy-start | bytes 3932164
  200.9 51.3 %all-to-all-start.2 = ((bf16[16,40,1024]{2,1,0:T(8,128)(2,1)}), bf16[16,40,1024]{2,1,0:T(8,128)(2,1)S(1)}, u32[]{:S(2)}, u32[]{:S(2)}) async-start(bf16[16,40,1024]{2,1,0:T(8,128)(2,1)} %bitcast.25), calls=%async_computation.2 | async-start | bytes 2621440 | tf_op jit(solution)/shard_map/all_to_all | solution.py:366
  208.5 9.8 %copy-start.3 = (f32[384,128]{1,0:T(8,128)}, f32[384,128]{1,0:T(8,128)S(1)}, u32[]{:S(2)}) copy-start(f32[384,128]{1,0:T(8,128)S(1)} %collective-permute-done.14.refs_4_) | copy-start | bytes 589828
  218.3 0.7 copy-start.4
  221.9 3.9 %collective-permute-start.16 = (f32[384,128]{1,0:T(8,128)}, f32[384,128]{1,0:T(8,128)S(1)}, u32[]{:S(2)}, u32[]{:S(2)}) collective-permute-start(f32[384,128]{1,0:T(8,128)} %get-tuple-element.109), channel_id=1, source_target_pairs={{0,2},{2,0},{4,6},{6,4},{8,10},{10,8},{12,14},{14,12},{16,18},{18,... | collective-permute-start | bytes 589832 | tf_op jit(solution)/shard_map/ppermute | solution.py:188
  222.9 10.2 %collective-permute-start.17 = (f32[384,128]{1,0:T(8,128)}, f32[384,128]{1,0:T(8,128)S(1)}, u32[]{:S(2)}, u32[]{:S(2)}) collective-permute-start(f32[384,128]{1,0:T(8,128)} %get-tuple-element.110), channel_id=1, source_target_pairs={{0,4},{2,6},{4,0},{6,2},{8,12},{10,14},{12,8},{14,10},{16,20},{18,... | collective-permute-start | bytes 589832 | tf_op jit(solution)/shard_map/ppermute | solution.py:188
  224.0 15.2 %collective-permute-start.18 = (f32[384,128]{1,0:T(8,128)}, f32[384,128]{1,0:T(8,128)S(1)}, u32[]{:S(2)}, u32[]{:S(2)}) collective-permute-start(f32[384,128]{1,0:T(8,128)} %get-tuple-element.111), channel_id=1, source_target_pairs={{0,6},{2,4},{4,2},{6,0},{8,14},{10,12},{12,10},{14,8},{16,22},{18,... | collective-permute-start | bytes 589832 | tf_op jit(solution)/shard_map/ppermute | solution.py:188
  252.2 1.1 copy-start.2

commit v7 on v6

--- a/solution.py
+++ b/solution.py
@@ -14,7 +14,7 @@
 QUERY, KEYS, VALUES = 0, 1, 2
 
 PACK_WEIGHT = 20
-ATTEND_WEIGHT = 7
+ATTEND_WEIGHT = 20
 
 
 def pack_kernel(place_ref, *refs):
@@ -66,58 +66,99 @@
     )(place, *picks, *[array for array, _, _ in sources])
 
 
-def update_kernel(tail_ref, keys_ref, values_ref, update_ref):
+def update_kernel(place_ref, tail_ref, keys_ref, values_ref, *outs):
     tail = tail_ref[...] != 0
-    for part in range(keys_ref.shape[1] // HEAD_DIM):
-        columns = slice(part * HEAD_DIM, (part + 1) * HEAD_DIM)
-        keys = keys_ref[:, columns]
-        update_ref[columns, :] = lax.dot_general(
-            jnp.where(tail, keys, jnp.zeros_like(keys)),
-            values_ref[:, columns],
-            (((0,), (0,)), ((), ())),
-            preferred_element_type=jnp.float32,
-        )
+    for number, out in enumerate(outs):
+
+        @pl.when(pl.program_id(0) == number)
+        def _():
+            for part in range(keys_ref.shape[1] // HEAD_DIM):
+                columns = slice(part * HEAD_DIM, (part + 1) * HEAD_DIM)
+                keys = keys_ref[:, columns]
+                out[columns, :] = lax.dot_general(
+                    jnp.where(tail, keys, jnp.zeros_like(keys)),
+                    values_ref[:, columns],
+                    (((0,), (0,)), ((), ())),
+                    preferred_element_type=jnp.float32,
+                )
 
 
 def block_update(arrived, tail_slots):
+    near, _, place, _ = run_of_blocks()
     slots, columns = arrived.shape[0], arrived.shape[1] // 2
-    width = math.gcd(columns, 4 * HEAD_DIM)
-    blocks = columns // width
-    return pl.pallas_call(
+    share = columns // near
+    direct = share % HEAD_DIM == 0
+    width, blocks = (share, near) if direct else (columns, 1)
+
+    def column_spec(first):
+        return pl.BlockSpec((slots, width), lambda j, place_ref: (0, first + (j ^ place_ref[0])))
+
+    updates = pl.pallas_call(
         update_kernel,
-        out_shape=jax.ShapeDtypeStruct((columns, HEAD_DIM), jnp.float32),
-        grid=(blocks,),
-        in_specs=[
-            pl.BlockSpec((slots, 1), lambda j: (0, 0)),
-            pl.BlockSpec((slots, width), lambda j: (0, j)),
-            pl.BlockSpec((slots, width), lambda j: (0, blocks + j)),
-        ],
-        out_specs=pl.BlockSpec((width, HEAD_DIM), lambda j: (j, 0)),
+        out_shape=(jax.ShapeDtypeStruct((width, HEAD_DIM), jnp.float32),) * blocks,
+        grid_spec=pltpu.PrefetchScalarGridSpec(
+            num_scalar_prefetch=1,
+            grid=(blocks,),
+            in_specs=[
+                pl.BlockSpec((slots, 1), lambda j, place_ref: (0, 0)),
+                column_spec(0),
+                column_spec(blocks),
+            ],
+            out_specs=(pl.BlockSpec((width, HEAD_DIM), lambda j, place_ref: (0, 0)),) * blocks,
+        ),
         cost_estimate=pl.CostEstimate(
             flops=2 * slots * columns * HEAD_DIM,
             bytes_accessed=4 * columns * (slots + HEAD_DIM),
             transcendentals=0,
         ),
         name="block_update",
-    )(tail_slots, arrived, arrived)
-
-
-def unpack_kernel(land_ref, keys_ref, values_ref, *refs):
-    keys_out, values_out, order = refs[-3:]
-
-    @pl.when(pl.program_id(0) == 0)
-    def _():
-        rows = lax.broadcasted_iota(jnp.int32, order.shape, 0)
-        order[...] = jnp.where(land_ref[...] == rows, 1.0, 0.0).astype(order.dtype)
-
-    for source, out in ((keys_ref, keys_out), (values_ref, values_out)):
+    )(jnp.reshape(place if direct else 0 * place, (1,)), tail_slots, arrived, arrived)
+    if direct:
+        return list(updates)
+    return [
+        lax.dynamic_slice_in_dim(updates[0], (place ^ k) * share, share, axis=0)
+        for k in range(near)
+    ]
+
+
+def tables_kernel(land_ref, seg_col_ref, seg_row_ref, mask_ref, order, causal, carried):
+    rows = lax.broadcasted_iota(jnp.int32, order.shape, 0)
+    order[...] = jnp.where(land_ref[...] == rows, 1.0, 0.0).astype(order.dtype)
+    later = lax.broadcasted_iota(jnp.int32, causal.shape, 0)
+    earlier = lax.broadcasted_iota(jnp.int32, causal.shape, 1)
+    open_pair = (earlier <= later) & (seg_col_ref[...] == seg_row_ref[...])
+    causal[...] = jnp.where(open_pair, 1.0, 0.0).astype(causal.dtype)
+    carried[...] = jnp.broadcast_to(
+        jnp.where(mask_ref[...] != 0, 1.0, 0.0).astype(carried.dtype), carried.shape
+    )
+
+
+def block_tables(land_row, segment, carried_mask):
+    slots, tok_rows = land_row.shape[1], segment.shape[0]
+    return pl.pallas_call(
+        tables_kernel,
+        out_shape=tuple(
+            jax.ShapeDtypeStruct((tok_rows, n), jnp.bfloat16) for n in (slots, tok_rows, HEAD_DIM)
+        ),
+        cost_estimate=pl.CostEstimate(
+            flops=8 * tok_rows * (slots + tok_rows),
+            bytes_accessed=2 * tok_rows * (slots + tok_rows),
+            transcendentals=0,
+        ),
+        name="block_tables",
+    )(land_row, segment[:, None], segment[None, :], carried_mask)
+
+
+def unpack_kernel(order_ref, keys_ref, values_ref, *refs):
+    for source, out in zip((keys_ref, values_ref), refs[-2:]):
         out[...] = jnp.dot(
-            order[...], source[...], preferred_element_type=jnp.float32
+            order_ref[...], source[...], preferred_element_type=jnp.float32
         ).astype(out.dtype)
 
 
-def unpack_keys_values(arrived, land_row, tok_rows, start, mine, filled):
+def unpack_keys_values(arrived, order, start, mine, filled):
     slots, columns = arrived.shape[0], arrived.shape[1] // 2
+    tok_rows = order.shape[0]
     width = math.gcd(math.gcd(columns, start), 4 * HEAD_DIM)
     blocks, first = columns // width, start // width
     packed = jax.ShapeDtypeStruct((tok_rows, mine), arrived.dtype)
@@ -127,13 +168,12 @@
         out_shape=(packed, packed),
         grid=(blocks,),
         in_specs=[
-            pl.BlockSpec((1, slots), lambda j: (0, 0)),
+            pl.BlockSpec((tok_rows, slots), lambda j: (0, 0)),
             pl.BlockSpec((slots, width), lambda j: (0, j)),
             pl.BlockSpec((slots, width), lambda j: (0, blocks + j)),
         ]
         + [pl.BlockSpec(memory_space=pl.ANY) for _ in filled],
         out_specs=(column_spec, column_spec),
-        scratch_shapes=[pltpu.VMEM((tok_rows, slots), jnp.bfloat16)],
         input_output_aliases={3 + number: number for number in range(len(filled))},
         cost_estimate=pl.CostEstimate(
             flops=4 * tok_rows * columns * slots,
@@ -141,7 +181,7 @@
             transcendentals=0,
         ),
         name="unpack_keys_values",
-    )(land_row, arrived, arrived, *filled)
+    )(order, arrived, arrived, *filled)
 
 
 def sum_kernel(take_ref, *refs):
@@ -156,18 +196,13 @@
 
 def sum_pieces(take, pieces):
     rows = pieces[0].shape[0]
-    step = rows // 2
-    spec = pl.BlockSpec((step, HEAD_DIM), lambda i, take_ref: (i, 0))
     count = take.shape[0]
+    whole = pl.BlockSpec(memory_space=pltpu.VMEM)
     return pl.pallas_call(
         sum_kernel,
         out_shape=(jax.ShapeDtypeStruct((rows, HEAD_DIM), jnp.float32),) * count,
-        grid_spec=pltpu.PrefetchScalarGridSpec(
-            num_scalar_prefetch=1,
-            grid=(rows // step,),
-            in_specs=[spec] * len(pieces),
-            out_specs=(spec,) * count,
-        ),
+        in_specs=[pl.BlockSpec(memory_space=pltpu.SMEM)] + [whole] * len(pieces),
+        out_specs=(whole,) * count,
         cost_estimate=pl.CostEstimate(
             flops=count * len(pieces) * rows * HEAD_DIM,
             bytes_accessed=4 * (len(pieces) + count) * rows * HEAD_DIM,
@@ -179,7 +214,7 @@
 
 def run_of_blocks():
     seq_count, block = lax.axis_size("seq"), lax.axis_index("seq")
-    near = math.gcd(seq_count, 4)
+    near = run_size()
     return near, seq_count // near, block % near, block // near
 
 
@@ -204,14 +239,8 @@
     return within, jnp.concatenate([own, across], axis=1)
 
 
-def carry_within(update, within):
-    near, _, place, _ = run_of_blocks()
-    share = update.shape[0] // near
-    pieces = []
-    for k in range(near):
-        mine = lax.dynamic_slice_in_dim(update, (place ^ k) * share, share, axis=0)
-        pieces.append(mine if k == 0 else swap_places(mine, k))
-    return sum_pieces(within, pieces)
+def carry_within(shares, within):
+    return sum_pieces(within, [shares[0]] + [swap_places(shares[k], k) for k in range(1, len(shares))])
 
 
 def pass_totals(sums):
@@ -227,13 +256,8 @@
 
 
 def hand_back(pieces, across):
-    near, _, place, _ = run_of_blocks()
     handed = sum_pieces(across, pieces)
-    stacked = jnp.stack([handed[0]] + [swap_places(handed[k], k) for k in range(1, near)])
-    return [
-        lax.dynamic_index_in_dim(stacked, place ^ number, axis=0, keepdims=False)
-        for number in range(near)
-    ]
+    return [handed[0]] + [swap_places(handed[k], k) for k in range(1, len(handed))]
 
 
 def two_terms(value):
@@ -241,49 +265,86 @@
     return high, (value - high.astype(jnp.float32)).astype(jnp.bfloat16)
 
 
+def assemble_kernel(place_ref, *refs):
+    pieces, out = refs[:-1], refs[-1]
+    near = run_size()
+    number = 0
+    for chunk in range(0, len(pieces), near):
+        share = pieces[chunk].shape[0]
+        step = math.gcd(share, HEAD_DIM)
+        for place in range(near):
+            for row in range(0, share, step):
+                value = pieces[chunk + place][row : row + step, :]
+                for other in range(1, near):
+                    piece = pieces[chunk + (place ^ other)]
+                    value = jnp.where(place_ref[0] == other, piece[row : row + step, :], value)
+                head, within = divmod(number, HEAD_DIM)
+                for term, part in enumerate(two_terms(value)):
+                    first = (2 * head + term) * HEAD_DIM + within
+                    out[first : first + step, :] = part
+                number += step
+
+
+def run_size():
+    return math.gcd(lax.axis_size("seq"), 4)
+
+
+def assemble_states(pieces):
+    _, _, place, _ = run_of_blocks()
+    rows = sum(piece.shape[0] for piece in pieces)
+    whole = pl.BlockSpec(memory_space=pltpu.VMEM)
+    return pl.pallas_call(
+        assemble_kernel,
+        out_shape=jax.ShapeDtypeStruct((2 * rows, HEAD_DIM), jnp.bfloat16),
+        in_specs=[pl.BlockSpec(memory_space=pltpu.SMEM)] + [whole] * len(pieces),
+        out_specs=whole,
+        cost_estimate=pl.CostEstimate(
+            flops=8 * rows * HEAD_DIM, bytes_accessed=8 * rows * HEAD_DIM, transcendentals=0
+        ),
+        name="assemble_states",
+    )(jnp.reshape(place, (1,)), *pieces)
+
+
 def attend_kernel(
-    land_ref, seg_col_ref, seg_row_ref, mask_ref, gain_ref, arrived_ref, keys_ref, values_ref,
-    states_ref, *refs,
+    order_ref, causal_ref, carried_ref, gain_ref, arrived_ref, keys_ref, values_ref, states_ref, *refs
 ):
-    out_ref, order, causal, carried = refs[-4:]
-    tok_rows = order.shape[0]
-
-    @pl.when(pl.program_id(0) == 0)
-    def _():
-        rows = lax.broadcasted_iota(jnp.int32, order.shape, 0)
-        order[...] = jnp.where(land_ref[...] == rows, 1.0, 0.0).astype(order.dtype)
-        later = lax.broadcasted_iota(jnp.int32, causal.shape, 0)
-        earlier = lax.broadcasted_iota(jnp.int32, causal.shape, 1)
-        open_pair = (earlier <= later) & (seg_col_ref[...] == seg_row_ref[...])
-        causal[...] = jnp.where(open_pair, 1.0, 0.0).astype(causal.dtype)
-        carried[...] = jnp.broadcast_to(
-            jnp.where(mask_ref[...] != 0, 1.0, 0.0).astype(carried.dtype), carried.shape
-        )
+    out_ref = refs[-1]
+    tok_rows = order_ref.shape[0]
+    half = tok_rows // 2
 
     def product(left, right):
         return jnp.dot(left, right, preferred_element_type=jnp.float32)
 
-    ones = jnp.full((HEAD_DIM, HEAD_DIM), 1.0, jnp.bfloat16)
-    query = product(order[...], arrived_ref[...]).astype(keys_ref.dtype)
-    half = tok_rows // 2
-    for part in range(query.shape[1] // HEAD_DIM):
-        columns = slice(part * HEAD_DIM, (part + 1) * HEAD_DIM)
-        state_high, state_low = two_terms(states_ref[columns, :])
-        for rows, reach in ((slice(0, half), half), (slice(half, tok_rows), tok_rows)):
-            queries = query[rows, columns]
-            scores = lax.dot_general(
-                queries,
-                keys_ref[:reach, columns],
-                (((1,), (1,)), ((), ())),
-                preferred_element_type=jnp.float32,
+    ones = jnp.full((2 * HEAD_DIM, HEAD_DIM), 1.0, jnp.bfloat16)
+    query = product(order_ref[...], arrived_ref[...]).astype(keys_ref.dtype)
+    heads = query.shape[1] // HEAD_DIM
+    together = math.gcd(heads, 2)
+    for group in range(0, heads, together):
+        tiles = []
+        for part in range(group, group + together):
+            columns = slice(part * HEAD_DIM, (part + 1) * HEAD_DIM)
+            for rows, reach in ((slice(0, half), half), (slice(half, tok_rows), tok_rows)):
+                scores = lax.dot_general(
+                    query[rows, columns],
+                    keys_ref[:reach, columns],
+                    (((1,), (1,)), ((), ())),
+                    preferred_element_type=jnp.float32,
+                )
+                weights = scores.astype(keys_ref.dtype) * causal_ref[rows, :reach]
+                tiles.append((part, columns, rows, reach, weights))
+        raws = []
+        for part, columns, rows, reach, weights in tiles:
+            carrying = query[rows, columns] * carried_ref[rows, :]
+            states = states_ref[2 * part * HEAD_DIM : 2 * (part + 1) * HEAD_DIM, :]
+            raws.append(
+                product(
+                    jnp.concatenate([weights, carrying, carrying], axis=1),
+                    jnp.concatenate([values_ref[:reach, columns], states], axis=0),
+                )
             )
-            weights = scores.astype(keys_ref.dtype) * causal[rows, :reach]
-            carrying = queries * carried[rows, :]
-            raw_out = product(weights, values_ref[:reach, columns]) + (
-                product(carrying, state_high) + product(carrying, state_low)
-            )
-            square_high, square_low = two_terms(raw_out * raw_out)
-            mean = (product(square_high, ones) + product(square_low, ones)) * (1.0 / HEAD_DIM)
+        for (part, columns, rows, reach, weights), raw_out in zip(tiles, raws):
+            square = jnp.concatenate(two_terms(raw_out * raw_out), axis=1)
+            mean = product(square, ones) * (1.0 / HEAD_DIM)
             out_ref[rows, columns] = (
                 raw_out * lax.rsqrt(mean + norm_eps) * gain_ref[:, columns]
             ).astype(out_ref.dtype)
@@ -299,27 +360,19 @@
         attend_kernel,
         out_shape=jax.ShapeDtypeStruct((tok_rows, mine), jnp.bfloat16),
         grid=(columns // width,),
-        in_specs=[
-            pl.BlockSpec((1, slots), lambda j: (0, 0)),
-            pl.BlockSpec((tok_rows, 1), lambda j: (0, 0)),
-            pl.BlockSpec((1, tok_rows), lambda j: (0, 0)),
-            pl.BlockSpec((tok_rows, 1), lambda j: (0, 0)),
+        in_specs=[pl.BlockSpec(table.shape, lambda j: (0, 0)) for table in tables]
+        + [
             pl.BlockSpec((1, width), lambda j: (0, first + j)),
             pl.BlockSpec((slots, width), lambda j: (0, j)),
             column_spec,
             column_spec,
-            pl.BlockSpec((width, HEAD_DIM), lambda j: (first + j, 0)),
+            pl.BlockSpec((2 * width, HEAD_DIM), lambda j: (first + j, 0)),
         ]
         + [pl.BlockSpec(memory_space=pl.ANY) for _ in filled],
         out_specs=column_spec,
-        scratch_shapes=[
-            pltpu.VMEM((tok_rows, slots), jnp.bfloat16),
-            pltpu.VMEM((tok_rows, tok_rows), jnp.bfloat16),
-            pltpu.VMEM((tok_rows, HEAD_DIM), jnp.bfloat16),
-        ],
-        input_output_aliases={9: 0} if filled else {},
-        cost_estimate=pl.CostEstimate(
-            flops=ATTEND_WEIGHT * 2 * tok_rows * columns * (slots + 2 * tok_rows + 4 * HEAD_DIM),
+        input_output_aliases={8: 0} if filled else {},
+        cost_estimate=pl.CostEstimate(
+            flops=ATTEND_WEIGHT * tok_rows * columns * (slots + 2 * tok_rows + 4 * HEAD_DIM),
             bytes_accessed=2 * columns * (slots + 4 * tok_rows),
             transcendentals=0,
         ),
@@ -400,31 +453,34 @@
     arrived_next = to_owners(outgoing)
     within, across = carry_tables(last_segment)
     sums = carry_within(block_update(arrived, tail_slots), within)
-    filled = unpack_keys_values(arrived, land_row, tok_rows, 0, columns, ())
+    tables = block_tables(land_row, segment, carried_mask)
+    filled = unpack_keys_values(arrived, tables[0], 0, columns, ())
     incoming = swap_heads(qkv, QUERY, 1, 0, columns)
-    incoming, sums, filled, tables = lax.optimization_barrier(
-        (incoming, sums, filled, (tail_slots, within, across, segment, carried_mask))
-    )
-    tail_slots, within, across, segment, carried_mask = tables
+    incoming, sums, filled, tables, small = lax.optimization_barrier(
+        (incoming, sums, filled, tables, (tail_slots, within, across))
+    )
+    tail_slots, within, across = small
     part = max(2, head_share // 2) * HEAD_DIM
     outgoing, outgoing_next = (
         pack_chunk(qkv, incoming, rows, QUERY, 1, start, size, start)
         for start, size in ((0, part), (part, columns - part))
     )
-    outgoing, pieces = lax.optimization_barrier((outgoing, pass_totals(sums)))
+    outgoing, outgoing_next, pieces = lax.optimization_barrier(
+        (outgoing, outgoing_next, pass_totals(sums))
+    )
     query = to_owners(outgoing)
-    sums = carry_within(block_update(arrived_next, tail_slots), within)
+    shares, pieces = lax.optimization_barrier((block_update(arrived_next, tail_slots), pieces))
     states = hand_back(pieces, across)
-    keys, values = unpack_keys_values(arrived_next, land_row, tok_rows, first, columns, filled)
-    outgoing_next, sums, states, keys, values = lax.optimization_barrier(
-        (outgoing_next, sums, states, keys, values)
+    sums = carry_within(shares, within)
+    filled = unpack_keys_values(arrived_next, tables[0], first, columns, filled)
+    outgoing_next, sums, states, filled = lax.optimization_barrier(
+        (outgoing_next, sums, states, filled)
     )
     pieces = pass_totals(sums)
     query_next = to_owners(outgoing_next)
-    states = jnp.concatenate(states + hand_back(pieces, across), axis=0)
-    tables = (land_row, segment[:, None], segment[None, :], carried_mask)
-    out = attend(query, keys, values, states, tables, gain, 0, ())
-    return attend(query_next, keys, values, states, tables, gain, part, (out,))
+    states = assemble_states(states + hand_back(pieces, across))
+    out = attend(query, *filled, states, tables, gain, 0, ())
+    return attend(query_next, *filled, states, tables, gain, part, (out,))
 
 
 def solution(mesh):

time: 264 us -> 252 us (0.955)
  local copies, waits for them, and re-layouts: 20.9 us -> 11.7 us
  waiting for transfers between devices: 118 us -> 113 us
    pallas_call x2 -> x4, Pallas kernels: 7.09 us -> 14 us  [the longest x2 9.11 us: block_update(): pl.pallas_call(update_kernel, out_shape=(jax.ShapeDtypeStruct((width, HEA...]
    pallas_call x2, Pallas kernels: 18.4 us -> 14.2 us  [attend(): pl.pallas_call(attend_kernel, out_shape=jax.ShapeDtypeStruct((tok_rows, m...]
    dynamic_slice x2 -> x0, local copies, waits for them, and re-layouts: 3.55 us -> none  [carry_within(): mine = lax.dynamic_slice_in_dim(update, (place ^ k) * share, share, axis=0)]
    ppermute x12, waiting for transfers between devices: 26.2 us -> 22.8 us  [swap_places(): return lax.ppermute(value, 'seq', [(i, i ^ k) for i in range(seq_count)])]
    unnamed x47 -> x52, local copies, waits for them, and re-layouts: 9.6 us -> 6.29 us
  transfers between devices with their start and end apart: 23 -> 23, of which waited for: 12 -> 12; matrix products, arithmetic and copies ran while one was open for 10% -> 6% of each run, Pallas kernels for 20% -> 22%
where the time goes in v7:
time: 252 us; the launch traced here: 250 us
  waiting for transfers between devices  113 us (45%)
  Pallas kernels  63 us (25%)
  starting transfers between devices  50.3 us (20%)
  local copies, waits for them, and re-layouts  11.7 us (5%)
  other arithmetic  11.2 us (4%)
    ppermute x4, waiting for transfers between devices, pass_totals(): lax.ppermute(sums[near], 'seq', [(i, i + step) for i in range(seq_count -...  59.2 us
    ppermute x3, waiting for transfers between devices, swap_heads(): return lax.ppermute(outgoing, 'head', [(0, 1), (1, 0)])  28.5 us
    all_to_all x4, starting transfers between devices, to_owners(): lax.all_to_all(outgoing, 'seq', split_axis=0, concat_axis=0, tiled=True)  27.9 us
    ppermute x12, waiting for transfers between devices, swap_places(): return lax.ppermute(value, 'seq', [(i, i ^ k) for i in range(seq_count)])  22.8 us
    pallas_call x4, Pallas kernels, pack_rows(): pl.pallas_call(pack_kernel, out_shape=jax.ShapeDtypeStruct((slots, planes...  17.4 us
    pallas_call x2, Pallas kernels, attend(): pl.pallas_call(attend_kernel, out_shape=jax.ShapeDtypeStruct((tok_rows, m...  14.2 us
    ppermute x4, starting transfers between devices, pass_totals(): lax.ppermute(sums[near], 'seq', [(i, i + step) for i in range(seq_count -...  10.4 us
    pallas_call x2, Pallas kernels, unpack_keys_values(): pl.pallas_call(unpack_kernel, out_shape=(packed, packed), grid=(blocks,),...  9.19 us
  transfers between devices with their start and end apart: 23, of which 12 were waited for; matrix products, arithmetic and copies ran while one was open for 6% of the time, Pallas kernels for 22%

profile of v7, /device:TPU:11, one launch (start us, length us, event | category | flops | bytes accessed | tf_op | source)
XLA Modules:
  0.0 249.9 jit_solution(10667421965628796988)
XLA Ops:
  0.0 1.3 slice_select_fusion.2
  1.3 1.3 collective-permute-start.1
  2.6 2.0 slice_select_fusion
  4.9 0.9 sub.105.refs_0_
  6.7 7.4 %collective-permute-done.1.refs_3_ = bf16[2,256,512]{2,1,0:T(8,128)(2,1)S(1)} collective-permute-done((bf16[2,256,512]{2,1,0:T(8,128)(2,1)S(1)}, bf16[2,256,512]{2,1,0:T(8,128)(2,1)S(1)}, u32[]{:S(2)}, u32[]{:S(2)}) %collective-permute-start.1) | collective-permute-done | bytes 524320 | tf_op jit(solution)/shard_map/ppermute | solution.py:392
  14.9 3.4 %pack_rows.4 = bf16[640,1024]{1,0:T(8,128)(2,1)} custom-call(s32[1]{0:T(128)} %bitcast.8.place_ref, s32[640,1]{1,0:T(8,128)} %sub.105.refs_0_, s32[640,1]{1,0:T(8,128)} %sub.106.refs_1_, bf16[3,256,4096]{2,1,0:T(8,128)(2,1)} %refs_2_.7, bf16[2,256,512]{2,1,0:T(8,128)(2,1)} %copy-done.25), custom_call_target="tpu_custom_call" | custom-call | flops 13421772800 | bytes 2359296 | tf_op jit(solution)/shard_map/pack_rows/pallas_call | solution.py:49
  18.3 8.6 %all-to-all-start = ((bf16[16,40,1024]{2,1,0:T(8,128)(2,1)}), bf16[16,40,1024]{2,1,0:T(8,128)(2,1)S(1)}, u32[]{:S(2)}, u32[]{:S(2)}) async-start(bf16[16,40,1024]{2,1,0:T(8,128)(2,1)} %bitcast.35), calls=%async_computation | async-start | bytes 2621440 | tf_op jit(solution)/shard_map/all_to_all | solution.py:419
  26.9 21.1 %collective-permute-done.7.refs_3_ = bf16[2,256,1536]{2,1,0:T(8,128)(2,1)} collective-permute-done((bf16[2,256,1536]{2,1,0:T(8,128)(2,1)S(1)}, bf16[2,256,1536]{2,1,0:T(8,128)(2,1)}, u32[]{:S(2)}, u32[]{:S(2)}) %collective-permute-start.7) | collective-permute-done | bytes 1572896 | tf_op jit(solution)/shard_map/ppermute | solution.py:392
  47.9 7.2 %pack_rows.7 = bf16[640,3072]{1,0:T(8,128)(2,1)} custom-call(s32[1]{0:T(128)} %bitcast.8.place_ref, s32[640,1]{1,0:T(8,128)} %sub.105.refs_0_, s32[640,1]{1,0:T(8,128)} %sub.106.refs_1_, bf16[3,256,4096]{2,1,0:T(8,128)(2,1)} %refs_2_.7, bf16[2,256,1536]{2,1,0:T(8,128)(2,1)} %collective-permute-done.7.refs_3_), custom_call_target="tpu_custom_call" | custom-call | flops 40265318400 | bytes 7077888 | tf_op jit(solution)/shard_map/pack_rows/pallas_call | solution.py:49
  55.2 2.3 all-to-all-done
  57.4 1.1 copy-done
  58.5 5.2 %all-to-all-start.1 = ((bf16[16,40,3072]{2,1,0:T(8,128)(2,1)}), bf16[16,40,3072]{2,1,0:T(8,128)(2,1)}, u32[]{:S(2)}, u32[]{:S(2)}) async-start(bf16[16,40,3072]{2,1,0:T(8,128)(2,1)} %bitcast.31), calls=%async_computation.1 | async-start | bytes 7864320 | tf_op jit(solution)/shard_map/all_to_all | solution.py:419
  63.7 1.7 slice_select_fusion.1
  65.3 1.3 collective-permute-start
  73.6 0.9 fusion.tail_ref
  75.3 4.1 %block_update.2 = (f32[128,128]{1,0:T(8,128)}, f32[128,128]{1,0:T(8,128)}, f32[128,128]{1,0:T(8,128)}, f32[128,128]{1,0:T(8,128)}) custom-call(s32[1]{0:T(128)} %bitcast.6.place_ref, s32[640,1]{1,0:T(8,128)} %fusion.tail_ref, bf16[640,1024]{1,0:T(8,128)(2,1)} %bitcast.27, bf16[640,1024]{1,0:T(8,128)(2,1)} %bitcast.28), custom_call_target="tpu_custom_call" | custom-call | flops 83886080 | bytes 1572864 | tf_op jit(solution)/shard_map/block_update/pallas_call | solution.py:96
  80.4 1.4 collective-permute-start.4
  82.6 2.4 block_tables.1
  84.9 3.3 %unpack_keys_values.2 = (bf16[512,2048]{1,0:T(8,128)(2,1)}, bf16[512,2048]{1,0:T(8,128)(2,1)}) custom-call(bf16[512,640]{1,0:T(8,128)(2,1)} %get-tuple-element.96.order_ref, bf16[640,1024]{1,0:T(8,128)(2,1)} %bitcast.29, bf16[640,1024]{1,0:T(8,128)(2,1)} %bitcast.30), custom_call_target="tpu_custom_call" | custom-call | flops 671088640 | bytes 2359296 | tf_op jit(solution)/shard_map/unpack_keys_values/pallas_call | solution.py:166
  88.3 1.0 collective-permute-done.3.refs_2_
  89.3 1.4 collective-permute-done.4.refs_3_
  91.3 1.7 sum_pieces.4
  93.0 1.9 collective-permute-start.5
  94.9 2.1 collective-permute-start.6
  97.0 3.4 %pack_rows.6 = bf16[640,1024]{1,0:T(8,128)(2,1)} custom-call(s32[1]{0:T(128)} %bitcast.8.place_ref, s32[640,1]{1,0:T(8,128)} %sub.105.refs_0_, s32[640,1]{1,0:T(8,128)} %sub.106.refs_1_, bf16[3,256,4096]{2,1,0:T(8,128)(2,1)} %refs_2_.7, bf16[1,256,2048]{2,1,0:T(8,128)(2,1)} %copy-done.24), custom_call_target="tpu_custom_call" | custom-call | flops 13421772800 | bytes 2359296 | tf_op jit(solution)/shard_map/pack_rows/pallas_call | solution.py:49
  100.4 3.4 %pack_rows.5 = bf16[640,1024]{1,0:T(8,128)(2,1)} custom-call(s32[1]{0:T(128)} %bitcast.8.place_ref, s32[640,1]{1,0:T(8,128)} %sub.105.refs_0_, s32[640,1]{1,0:T(8,128)} %sub.106.refs_1_, bf16[3,256,4096]{2,1,0:T(8,128)(2,1)} %refs_2_.7, bf16[1,256,2048]{2,1,0:T(8,128)(2,1)} %copy-done.24), custom_call_target="tpu_custom_call" | custom-call | flops 13421772800 | bytes 2359296 | tf_op jit(solution)/shard_map/pack_rows/pallas_call | solution.py:49
  103.8 47.3 %collective-permute-done.5.refs_4_ = f32[128,128]{1,0:T(8,128)S(1)} collective-permute-done((f32[128,128]{1,0:T(8,128)}, f32[128,128]{1,0:T(8,128)S(1)}, u32[]{:S(2)}, u32[]{:S(2)}) %collective-permute-start.5) | collective-permute-done | bytes 65568 | tf_op jit(solution)/shard_map/ppermute | solution.py:253
  151.1 1.4 collective-permute-done.6.refs_5_
  152.5 7.4 %all-to-all-start.3 = ((bf16[16,40,1024]{2,1,0:T(8,128)(2,1)}), bf16[16,40,1024]{2,1,0:T(8,128)(2,1)S(1)}, u32[]{:S(2)}, u32[]{:S(2)}) async-start(bf16[16,40,1024]{2,1,0:T(8,128)(2,1)} %bitcast.33), calls=%async_computation.3 | async-start | bytes 2621440 | tf_op jit(solution)/shard_map/all_to_all | solution.py:419
  160.0 5.0 %block_update.3 = (f32[384,128]{1,0:T(8,128)}, f32[384,128]{1,0:T(8,128)}, f32[384,128]{1,0:T(8,128)}, f32[384,128]{1,0:T(8,128)}) custom-call(s32[1]{0:T(128)} %bitcast.6.place_ref, s32[640,1]{1,0:T(8,128)} %fusion.tail_ref, bf16[640,3072]{1,0:T(8,128)(2,1)} %bitcast.16.keys_ref.values_ref, bf16[640,3072]{1,0:T(8,128)(2,1)} %bitcast.16.keys_ref.values_ref), custom_call_target="tpu_custom_call" | custom-call | flops 251658240 | bytes 4718592 | tf_op jit(solution)/shard_map/block_update/pallas_call | solution.py:96
  165.7 1.2 collective-permute-start.9
  168.0 1.7 sum_pieces.6
  170.7 5.2 %collective-permute-done.10.refs_3_ = f32[384,128]{1,0:T(8,128)S(1)} collective-permute-done((f32[384,128]{1,0:T(8,128)}, f32[384,128]{1,0:T(8,128)S(1)}, u32[]{:S(2)}, u32[]{:S(2)}) %collective-permute-start.10) | collective-permute-done | bytes 196640 | tf_op jit(solution)/shard_map/ppermute | solution.py:223
  175.9 5.9 %unpack_keys_values.3 = (bf16[512,2048]{1,0:T(8,128)(2,1)}, bf16[512,2048]{1,0:T(8,128)(2,1)}) custom-call(bf16[512,640]{1,0:T(8,128)(2,1)} %get-tuple-element.96.order_ref, bf16[640,3072]{1,0:T(8,128)(2,1)} %bitcast.16.keys_ref.values_ref, bf16[640,3072]{1,0:T(8,128)(2,1)} %bitcast.16.keys_ref.values_ref, ...), custom_call_target="tpu_custom_call", output_to_operand_aliasing={{0}: (3, {}), {1}: (4, {})} | custom-call | flops 2013265920 | bytes 7077888 | tf_op jit(solution)/shard_map/unpack_keys_values/pallas_call | solution.py:166
  183.1 2.4 sum_pieces.5
  186.1 4.1 %collective-permute-start.14 = (f32[384,128]{1,0:T(8,128)}, f32[384,128]{1,0:T(8,128)S(1)}, u32[]{:S(2)}, u32[]{:S(2)}) collective-permute-start(f32[384,128]{1,0:T(8,128)} %get-tuple-element.153), channel_id=1, source_target_pairs={{0,8},{2,10},{4,12},{6,14},{8,16},{10,18},{12,20},{14,22},{16,24},... | collective-permute-start | bytes 589832 | tf_op jit(solution)/shard_map/ppermute | solution.py:253
  190.2 2.3 collective-permute-start.15
  192.5 6.7 %all-to-all-start.2 = ((bf16[16,40,1024]{2,1,0:T(8,128)(2,1)}), bf16[16,40,1024]{2,1,0:T(8,128)(2,1)S(1)}, u32[]{:S(2)}, u32[]{:S(2)}) async-start(bf16[16,40,1024]{2,1,0:T(8,128)(2,1)} %bitcast.17), calls=%async_computation.2 | async-start | bytes 2621440 | tf_op jit(solution)/shard_map/all_to_all | solution.py:419
  199.3 10.5 %collective-permute-done.15.refs_5_ = f32[384,128]{1,0:T(8,128)S(1)} collective-permute-done((f32[384,128]{1,0:T(8,128)}, f32[384,128]{1,0:T(8,128)S(1)}, u32[]{:S(2)}, u32[]{:S(2)}) %collective-permute-start.15) | collective-permute-done | bytes 196640 | tf_op jit(solution)/shard_map/ppermute | solution.py:253
  210.5 2.4 sum_pieces.7
  212.9 2.2 collective-permute-start.16
  215.1 1.7 collective-permute-start.18
  216.8 8.6 %collective-permute-done.17.refs_6_ = f32[384,128]{1,0:T(8,128)S(1)} collective-permute-done((f32[384,128]{1,0:T(8,128)}, f32[384,128]{1,0:T(8,128)S(1)}, u32[]{:S(2)}, u32[]{:S(2)}) %collective-permute-start.17) | collective-permute-done | bytes 196640 | tf_op jit(solution)/shard_map/ppermute | solution.py:223
  225.4 6.0 %collective-permute-done.18.refs_7_ = f32[384,128]{1,0:T(8,128)S(1)} collective-permute-done((f32[384,128]{1,0:T(8,128)}, f32[384,128]{1,0:T(8,128)S(1)}, u32[]{:S(2)}, u32[]{:S(2)}) %collective-permute-start.18) | collective-permute-done | bytes 196640 | tf_op jit(solution)/shard_map/ppermute | solution.py:223
  232.1 2.5 %assemble_states.1.states_ref = bf16[4096,128]{1,0:T(8,128)(2,1)} custom-call(s32[1]{0:T(128)} %bitcast.6.place_ref, f32[128,128]{1,0:T(8,128)} %get-tuple-element.145.refs_0_, f32[128,128]{1,0:T(8,128)} %copy-done.13, f32[128,128]{1,0:T(8,128)} %copy-done.14, f32[128,128]{1,0:T(8,128)} %copy-done.15, f32[384,128]{1,0:T(8,128)} %get-tuple-element.154.refs_4_, ...), custom_call_target="tpu_custom_call" | custom-call | flops 2097152 | bytes 2097152 | tf_op jit(solution)/shard_map/assemble_states/pallas_call | solution.py:296
  234.6 7.1 %attend.2.refs_0_ = bf16[512,2048]{1,0:T(8,128)(2,1)} custom-call(bf16[512,640]{1,0:T(8,128)(2,1)} %get-tuple-element.96.order_ref, bf16[512,512]{1,0:T(8,128)(2,1)} %get-tuple-element.97.causal_ref, bf16[512,128]{1,0:T(8,128)(2,1)} %get-tuple-element.98.carried_ref, f32[1,2048]{1,0:T(1,128)} %bitcast.39, bf16[640,1024]{1,0:T(8,128)(2,1)} %bitcast.32, ...), custom_call_target="tpu_custom_call" | custom-call | flops 22817013760 | bytes 5505024 | tf_op jit(solution)/shard_map/attend/pallas_call | solution.py:359
  241.7 1.1 copy-done.3
  242.8 7.1 %attend.3 = bf16[512,2048]{1,0:T(8,128)(2,1)} custom-call(bf16[512,640]{1,0:T(8,128)(2,1)} %get-tuple-element.96.order_ref, bf16[512,512]{1,0:T(8,128)(2,1)} %get-tuple-element.97.causal_ref, bf16[512,128]{1,0:T(8,128)(2,1)} %get-tuple-element.98.carried_ref, f32[1,2048]{1,0:T(1,128)} %bitcast.40, ...), custom_call_target="tpu_custom_call", output_to_operand_aliasing={{}: (8, {})} | custom-call | flops 22817013760 | bytes 5505024 | tf_op jit(solution)/shard_map/attend/pallas_call | solution.py:359
  (109 shorter events, 17.5 us)
Async XLA Ops:
  1.3 3.7 %copy-start.22 = (s32[1,16,40]{2,1,0:T(8,128)S(1)}, s32[1,16,40]{2,1,0:T(8,128)}, u32[]{:S(2)}) copy-start(s32[1,16,40]{2,1,0:T(8,128)} %param.6) | copy-start | bytes 7684
  1.3 12.9 %collective-permute-start.1 = (bf16[2,256,512]{2,1,0:T(8,128)(2,1)S(1)}, bf16[2,256,512]{2,1,0:T(8,128)(2,1)S(1)}, u32[]{:S(2)}, u32[]{:S(2)}) collective-permute-start(bf16[2,256,512]{2,1,0:T(8,128)(2,1)S(1)} %slice_select_fusion.2), channel_id=1, source_target_pairs={{0,1},{1,0},{2,3},{3,2},{4,5},{5,4},{6,7},{7,6},{8,9},{9,8},{10,11... | collective-permute-start | bytes 1572872 | tf_op jit(solution)/shard_map/ppermute | solution.py:392
  4.6 43.3 %collective-permute-start.7 = (bf16[2,256,1536]{2,1,0:T(8,128)(2,1)S(1)}, bf16[2,256,1536]{2,1,0:T(8,128)(2,1)}, u32[]{:S(2)}, u32[]{:S(2)}) collective-permute-start(bf16[2,256,1536]{2,1,0:T(8,128)(2,1)S(1)} %slice_select_fusion), channel_id=1, source_target_pairs={{0,1},{1,0},{2,3},{3,2},{4,5},{5,4},{6,7},{7,6},{8,9},{9,8},{10,11... | collective-permute-start | bytes 4718600 | tf_op jit(solution)/shard_map/ppermute | solution.py:392
  14.1 0.8 copy-start.25
  18.3 39.1 %all-to-all-start = ((bf16[16,40,1024]{2,1,0:T(8,128)(2,1)}), bf16[16,40,1024]{2,1,0:T(8,128)(2,1)S(1)}, u32[]{:S(2)}, u32[]{:S(2)}) async-start(bf16[16,40,1024]{2,1,0:T(8,128)(2,1)} %bitcast.35), calls=%async_computation | async-start | bytes 2621440 | tf_op jit(solution)/shard_map/all_to_all | solution.py:419
  57.4 1.1 copy-start
  58.5 94.0 %all-to-all-start.1 = ((bf16[16,40,3072]{2,1,0:T(8,128)(2,1)}), bf16[16,40,3072]{2,1,0:T(8,128)(2,1)}, u32[]{:S(2)}, u32[]{:S(2)}) async-start(bf16[16,40,3072]{2,1,0:T(8,128)(2,1)} %bitcast.31), calls=%async_computation.1 | async-start | bytes 7864320 | tf_op jit(solution)/shard_map/all_to_all | solution.py:419
  63.6 3.0 %copy-start.23 = (s32[4]{0:T(128)S(1)}, s32[4]{0:T(128)}, u32[]{:S(2)}) copy-start(s32[4]{0:T(128)} %param.8) | copy-start | bytes 52
  63.7 8.1 %copy-start.12 = (s32[1,16,40]{2,1,0:T(8,128)S(1)}, s32[1,16,40]{2,1,0:T(8,128)}, u32[]{:S(2)}) copy-start(s32[1,16,40]{2,1,0:T(8,128)} %param.7) | copy-start | bytes 7684
  65.3 27.7 %collective-permute-start = (bf16[1,256,2048]{2,1,0:T(8,128)(2,1)S(1)}, bf16[1,256,2048]{2,1,0:T(8,128)(2,1)S(1)}, u32[]{:S(2)}, u32[]{:S(2)}) collective-permute-start(bf16[1,256,2048]{2,1,0:T(8,128)(2,1)S(1)} %slice_select_fusion.1), channel_id=1, source_target_pairs={{0,1},{1,0},{2,3},{3,2},{4,5},{5,4},{6,7},{7,6},{8,9},{9,8},{10,11... | collective-permute-start | bytes 3145736 | tf_op jit(solution)/shard_map/ppermute | solution.py:392
  71.7 7.7 %copy-start.21 = (s32[512]{0:T(512)}, s32[512]{0:T(512)S(1)}, u32[]{:S(2)}) copy-start(s32[512]{0:T(512)S(1)} %broadcast_add_fusion.1) | copy-start | bytes 6148
  72.2 10.4 %copy-start.1 = (s32[512,1]{1,0:T(8,128)}, s32[512,1]{1,0:T(8,128)S(1)}, u32[]{:S(2)}) copy-start(s32[512,1]{1,0:T(8,128)S(1)} %copy.39.seg_col_ref) | copy-start | bytes 6148
  79.4 8.9 %collective-permute-start.2 = (f32[128,128]{1,0:T(8,128)}, f32[128,128]{1,0:T(8,128)S(1)}, u32[]{:S(2)}, u32[]{:S(2)}) collective-permute-start(f32[128,128]{1,0:T(8,128)} %get-tuple-element.83), channel_id=1, source_target_pairs={{0,2},{2,0},{4,6},{6,4},{8,10},{10,8},{12,14},{14,12},{16,18},{18,... | collective-permute-start | bytes 196616 | tf_op jit(solution)/shard_map/ppermute | solution.py:223
  80.1 9.2 %collective-permute-start.3 = (f32[128,128]{1,0:T(8,128)}, f32[128,128]{1,0:T(8,128)S(1)}, u32[]{:S(2)}, u32[]{:S(2)}) collective-permute-start(f32[128,128]{1,0:T(8,128)} %get-tuple-element.84), channel_id=1, source_target_pairs={{0,4},{2,6},{4,0},{6,2},{8,12},{10,14},{12,8},{14,10},{16,20},{18,... | collective-permute-start | bytes 196616 | tf_op jit(solution)/shard_map/ppermute | solution.py:223
  80.4 10.3 %collective-permute-start.4 = (f32[128,128]{1,0:T(8,128)}, f32[128,128]{1,0:T(8,128)S(1)}, u32[]{:S(2)}, u32[]{:S(2)}) collective-permute-start(f32[128,128]{1,0:T(8,128)} %get-tuple-element.85), channel_id=1, source_target_pairs={{0,6},{2,4},{4,2},{6,0},{8,14},{10,12},{12,10},{14,8},{16,22},{18,... | collective-permute-start | bytes 196616 | tf_op jit(solution)/shard_map/ppermute | solution.py:223
  88.3 2.4 copy-start.18
  89.3 1.4 copy-start.19
  93.0 4.0 %copy-start.24 = (bf16[1,256,2048]{2,1,0:T(8,128)(2,1)}, bf16[1,256,2048]{2,1,0:T(8,128)(2,1)S(1)}, u32[]{:S(2)}) copy-start(bf16[1,256,2048]{2,1,0:T(8,128)(2,1)S(1)} %collective-permute-done.refs_3_) | copy-start | bytes 3145732
  93.0 58.1 %collective-permute-start.5 = (f32[128,128]{1,0:T(8,128)}, f32[128,128]{1,0:T(8,128)S(1)}, u32[]{:S(2)}, u32[]{:S(2)}) collective-permute-start(f32[128,128]{1,0:T(8,128)} %get-tuple-element.104), channel_id=1, source_target_pairs={{0,8},{2,10},{4,12},{6,14},{8,16},{10,18},{12,20},{14,22},{16,24},... | collective-permute-start | bytes 196616 | tf_op jit(solution)/shard_map/ppermute | solution.py:253
  94.9 57.6 %collective-permute-start.6 = (f32[128,128]{1,0:T(8,128)}, f32[128,128]{1,0:T(8,128)S(1)}, u32[]{:S(2)}, u32[]{:S(2)}) collective-permute-start(f32[128,128]{1,0:T(8,128)} %get-tuple-element.104), channel_id=1, source_target_pairs={{0,16},{2,18},{4,20},{6,22},{8,24},{10,26},{12,28},{14,30},{1,17},... | collective-permute-start | bytes 196616 | tf_op jit(solution)/shard_map/ppermute | solution.py:253
  151.1 13.8 %copy-start.16 = (f32[128,128]{1,0:T(8,128)}, f32[128,128]{1,0:T(8,128)S(1)}, u32[]{:S(2)}) copy-start(f32[128,128]{1,0:T(8,128)S(1)} %collective-permute-done.5.refs_4_) | copy-start | bytes 196612
  152.5 12.4 %copy-start.17 = (f32[128,128]{1,0:T(8,128)}, f32[128,128]{1,0:T(8,128)S(1)}, u32[]{:S(2)}) copy-start(f32[128,128]{1,0:T(8,128)S(1)} %collective-permute-done.6.refs_5_) | copy-start | bytes 196612
  152.5 40.0 %all-to-all-start.3 = ((bf16[16,40,1024]{2,1,0:T(8,128)(2,1)}), bf16[16,40,1024]{2,1,0:T(8,128)(2,1)S(1)}, u32[]{:S(2)}, u32[]{:S(2)}) async-start(bf16[16,40,1024]{2,1,0:T(8,128)(2,1)} %bitcast.33), calls=%async_computation.3 | async-start | bytes 2621440 | tf_op jit(solution)/shard_map/all_to_all | solution.py:419
  164.9 11.0 %collective-permute-start.10 = (f32[384,128]{1,0:T(8,128)}, f32[384,128]{1,0:T(8,128)S(1)}, u32[]{:S(2)}, u32[]{:S(2)}) collective-permute-start(f32[384,128]{1,0:T(8,128)} %get-tuple-element.121), channel_id=1, source_target_pairs={{0,6},{2,4},{4,2},{6,0},{8,14},{10,12},{12,10},{14,8},{16,22},{18,... | collective-permute-start | bytes 589832 | tf_op jit(solution)/shard_map/ppermute | solution.py:223
  165.5 16.2 %collective-permute-start.8 = (f32[384,128]{1,0:T(8,128)}, f32[384,128]{1,0:T(8,128)S(1)}, u32[]{:S(2)}, u32[]{:S(2)}) collective-permute-start(f32[384,128]{1,0:T(8,128)} %get-tuple-element.119), channel_id=1, source_target_pairs={{0,2},{2,0},{4,6},{6,4},{8,10},{10,8},{12,14},{14,12},{16,18},{18,... | collective-permute-start | bytes 589832 | tf_op jit(solution)/shard_map/ppermute | solution.py:223
  165.7 16.1 %collective-permute-start.9 = (f32[384,128]{1,0:T(8,128)}, f32[384,128]{1,0:T(8,128)S(1)}, u32[]{:S(2)}, u32[]{:S(2)}) collective-permute-start(f32[384,128]{1,0:T(8,128)} %get-tuple-element.120), channel_id=1, source_target_pairs={{0,4},{2,6},{4,0},{6,2},{8,12},{10,14},{12,8},{14,10},{16,20},{18,... | collective-permute-start | bytes 589832 | tf_op jit(solution)/shard_map/ppermute | solution.py:223
  169.8 15.7 %collective-permute-start.11 = (f32[128,128]{1,0:T(8,128)}, f32[128,128]{1,0:T(8,128)S(1)}, u32[]{:S(2)}, u32[]{:S(2)}) collective-permute-start(f32[128,128]{1,0:T(8,128)} %get-tuple-element.135), channel_id=1, source_target_pairs={{0,2},{2,0},{4,6},{6,4},{8,10},{10,8},{12,14},{14,12},{16,18},{18,... | collective-permute-start | bytes 196616 | tf_op jit(solution)/shard_map/ppermute | solution.py:223
  170.4 15.1 %collective-permute-start.12 = (f32[128,128]{1,0:T(8,128)}, f32[128,128]{1,0:T(8,128)S(1)}, u32[]{:S(2)}, u32[]{:S(2)}) collective-permute-start(f32[128,128]{1,0:T(8,128)} %get-tuple-element.136), channel_id=1, source_target_pairs={{0,4},{2,6},{4,0},{6,2},{8,12},{10,14},{12,8},{14,10},{16,20},{18,... | collective-permute-start | bytes 196616 | tf_op jit(solution)/shard_map/ppermute | solution.py:223
  175.9 5.9 %copy-start.9 = (f32[384,128]{1,0:T(8,128)}, f32[384,128]{1,0:T(8,128)S(1)}, u32[]{:S(2)}) copy-start(f32[384,128]{1,0:T(8,128)S(1)} %collective-permute-done.10.refs_3_) | copy-start | bytes 589828
  175.9 10.2 %collective-permute-start.13 = (f32[128,128]{1,0:T(8,128)}, f32[128,128]{1,0:T(8,128)S(1)}, u32[]{:S(2)}, u32[]{:S(2)}) collective-permute-start(f32[128,128]{1,0:T(8,128)} %get-tuple-element.137), channel_id=1, source_target_pairs={{0,6},{2,4},{4,2},{6,0},{8,14},{10,12},{12,10},{14,8},{16,22},{18,... | collective-permute-start | bytes 196616 | tf_op jit(solution)/shard_map/ppermute | solution.py:223
  181.8 0.7 copy-start.10
  182.4 0.7 copy-start.11
  185.5 45.9 %copy-start.13 = (f32[128,128]{1,0:T(8,128)}, f32[128,128]{1,0:T(8,128)S(1)}, u32[]{:S(2)}) copy-start(f32[128,128]{1,0:T(8,128)S(1)} %collective-permute-done.11.refs_1_) | copy-start | bytes 196612
  185.6 45.9 %copy-start.14 = (f32[128,128]{1,0:T(8,128)}, f32[128,128]{1,0:T(8,128)S(1)}, u32[]{:S(2)}) copy-start(f32[128,128]{1,0:T(8,128)S(1)} %collective-permute-done.12.refs_2_) | copy-start | bytes 196612
  186.1 45.3 %copy-start.15 = (f32[128,128]{1,0:T(8,128)}, f32[128,128]{1,0:T(8,128)S(1)}, u32[]{:S(2)}) copy-start(f32[128,128]{1,0:T(8,128)S(1)} %collective-permute-done.13.refs_3_) | copy-start | bytes 196612
  186.1 13.1 %collective-permute-start.14 = (f32[384,128]{1,0:T(8,128)}, f32[384,128]{1,0:T(8,128)S(1)}, u32[]{:S(2)}, u32[]{:S(2)}) collective-permute-start(f32[384,128]{1,0:T(8,128)} %get-tuple-element.153), channel_id=1, source_target_pairs={{0,8},{2,10},{4,12},{6,14},{8,16},{10,18},{12,20},{14,22},{16,24},... | collective-permute-start | bytes 589832 | tf_op jit(solution)/shard_map/ppermute | solution.py:253
  190.2 19.6 %collective-permute-start.15 = (f32[384,128]{1,0:T(8,128)}, f32[384,128]{1,0:T(8,128)S(1)}, u32[]{:S(2)}, u32[]{:S(2)}) collective-permute-start(f32[384,128]{1,0:T(8,128)} %get-tuple-element.153), channel_id=1, source_target_pairs={{0,16},{2,18},{4,20},{6,22},{8,24},{10,26},{12,28},{14,30},{1,17},... | collective-permute-start | bytes 589832 | tf_op jit(solution)/shard_map/ppermute | solution.py:253
  192.5 42.1 %copy-start.2 = (bf16[16,40,1024]{2,1,0:T(8,128)(2,1)}, bf16[16,40,1024]{2,1,0:T(8,128)(2,1)S(1)}, u32[]{:S(2)}) copy-start(bf16[16,40,1024]{2,1,0:T(8,128)(2,1)S(1)} %all-to-all-done.3) | copy-start | bytes 3932164
  192.5 49.2 %all-to-all-start.2 = ((bf16[16,40,1024]{2,1,0:T(8,128)(2,1)}), bf16[16,40,1024]{2,1,0:T(8,128)(2,1)S(1)}, u32[]{:S(2)}, u32[]{:S(2)}) async-start(bf16[16,40,1024]{2,1,0:T(8,128)(2,1)} %bitcast.17), calls=%async_computation.2 | async-start | bytes 2621440 | tf_op jit(solution)/shard_map/all_to_all | solution.py:419
  199.3 10.5 %copy-start.4 = (f32[384,128]{1,0:T(8,128)}, f32[384,128]{1,0:T(8,128)S(1)}, u32[]{:S(2)}) copy-start(f32[384,128]{1,0:T(8,128)S(1)} %collective-permute-done.14.refs_4_) | copy-start | bytes 589828
  209.8 0.7 copy-start.5
  212.9 3.9 %collective-permute-start.16 = (f32[384,128]{1,0:T(8,128)}, f32[384,128]{1,0:T(8,128)S(1)}, u32[]{:S(2)}, u32[]{:S(2)}) collective-permute-start(f32[384,128]{1,0:T(8,128)} %get-tuple-element.155), channel_id=1, source_target_pairs={{0,2},{2,0},{4,6},{6,4},{8,10},{10,8},{12,14},{14,12},{16,18},{18,... | collective-permute-start | bytes 589832 | tf_op jit(solution)/shard_map/ppermute | solution.py:223
  215.1 10.3 %collective-permute-start.17 = (f32[384,128]{1,0:T(8,128)}, f32[384,128]{1,0:T(8,128)S(1)}, u32[]{:S(2)}, u32[]{:S(2)}) collective-permute-start(f32[384,128]{1,0:T(8,128)} %get-tuple-element.156), channel_id=1, source_target_pairs={{0,4},{2,6},{4,0},{6,2},{8,12},{10,14},{12,8},{14,10},{16,20},{18,... | collective-permute-start | bytes 589832 | tf_op jit(solution)/shard_map/ppermute | solution.py:223
  215.1 16.3 %collective-permute-start.18 = (f32[384,128]{1,0:T(8,128)}, f32[384,128]{1,0:T(8,128)S(1)}, u32[]{:S(2)}, u32[]{:S(2)}) collective-permute-start(f32[384,128]{1,0:T(8,128)} %get-tuple-element.157), channel_id=1, source_target_pairs={{0,6},{2,4},{4,2},{6,0},{8,14},{10,12},{12,10},{14,8},{16,22},{18,... | collective-permute-start | bytes 589832 | tf_op jit(solution)/shard_map/ppermute | solution.py:223
  216.8 14.7 %copy-start.6 = (f32[384,128]{1,0:T(8,128)}, f32[384,128]{1,0:T(8,128)S(1)}, u32[]{:S(2)}) copy-start(f32[384,128]{1,0:T(8,128)S(1)} %collective-permute-done.16.refs_5_) | copy-start | bytes 589828
  225.4 6.0 %copy-start.7 = (f32[384,128]{1,0:T(8,128)}, f32[384,128]{1,0:T(8,128)S(1)}, u32[]{:S(2)}) copy-start(f32[384,128]{1,0:T(8,128)S(1)} %collective-permute-done.17.refs_6_) | copy-start | bytes 589828
  231.4 0.7 copy-start.8
  241.7 1.1 copy-start.3
  (1 other events, 0.6 us)

commit v8 on v7

--- a/solution.py
+++ b/solution.py
@@ -14,7 +14,8 @@
 QUERY, KEYS, VALUES = 0, 1, 2
 
 PACK_WEIGHT = 20
-ATTEND_WEIGHT = 20
+FINISH_WEIGHT = 1
+ATTEND_WEIGHT = 143
 
 
 def pack_kernel(place_ref, *refs):
@@ -67,16 +68,14 @@
 
 
 def update_kernel(place_ref, tail_ref, keys_ref, values_ref, *outs):
-    tail = tail_ref[...] != 0
     for number, out in enumerate(outs):
 
         @pl.when(pl.program_id(0) == number)
         def _():
             for part in range(keys_ref.shape[1] // HEAD_DIM):
                 columns = slice(part * HEAD_DIM, (part + 1) * HEAD_DIM)
-                keys = keys_ref[:, columns]
                 out[columns, :] = lax.dot_general(
-                    jnp.where(tail, keys, jnp.zeros_like(keys)),
+                    keys_ref[:, columns] * tail_ref[...],
                     values_ref[:, columns],
                     (((0,), (0,)), ((), ())),
                     preferred_element_type=jnp.float32,
@@ -100,7 +99,7 @@
             num_scalar_prefetch=1,
             grid=(blocks,),
             in_specs=[
-                pl.BlockSpec((slots, 1), lambda j, place_ref: (0, 0)),
+                pl.BlockSpec((slots, HEAD_DIM), lambda j, place_ref: (0, 0)),
                 column_spec(0),
                 column_spec(blocks),
             ],
@@ -305,15 +304,16 @@
     )(jnp.reshape(place, (1,)), *pieces)
 
 
+def product(left, right):
+    return jnp.dot(left, right, preferred_element_type=jnp.float32)
+
+
 def attend_kernel(
     order_ref, causal_ref, carried_ref, gain_ref, arrived_ref, keys_ref, values_ref, states_ref, *refs
 ):
     out_ref = refs[-1]
     tok_rows = order_ref.shape[0]
     half = tok_rows // 2
-
-    def product(left, right):
-        return jnp.dot(left, right, preferred_element_type=jnp.float32)
 
     ones = jnp.full((2 * HEAD_DIM, HEAD_DIM), 1.0, jnp.bfloat16)
     query = product(order_ref[...], arrived_ref[...]).astype(keys_ref.dtype)
@@ -372,12 +372,101 @@
         out_specs=column_spec,
         input_output_aliases={8: 0} if filled else {},
         cost_estimate=pl.CostEstimate(
-            flops=ATTEND_WEIGHT * tok_rows * columns * (slots + 2 * tok_rows + 4 * HEAD_DIM),
+            flops=ATTEND_WEIGHT * tok_rows * columns * (slots + 2 * tok_rows + 4 * HEAD_DIM) // 5,
             bytes_accessed=2 * columns * (slots + 4 * tok_rows),
             transcendentals=0,
         ),
         name="attend",
     )(*tables, gain, arrived, keys, values, states, *filled)
+
+
+def local_kernel(order_ref, causal_ref, carried_ref, arrived_ref, keys_ref, values_ref, *refs):
+    query_out, local_out = refs[-2:]
+    tok_rows = order_ref.shape[0]
+    half = tok_rows // 2
+    query = product(order_ref[...], arrived_ref[...]).astype(keys_ref.dtype)
+    heads = query.shape[1] // HEAD_DIM
+    together = math.gcd(heads, 2)
+    for group in range(0, heads, together):
+        tiles = []
+        for part in range(group, group + together):
+            columns = slice(part * HEAD_DIM, (part + 1) * HEAD_DIM)
+            query_out[:, columns] = query[:, columns] * carried_ref[...]
+            for rows, reach in ((slice(0, half), half), (slice(half, tok_rows), tok_rows)):
+                scores = lax.dot_general(
+                    query[rows, columns],
+                    keys_ref[:reach, columns],
+                    (((1,), (1,)), ((), ())),
+                    preferred_element_type=jnp.float32,
+                )
+                weights = scores.astype(keys_ref.dtype) * causal_ref[rows, :reach]
+                tiles.append((columns, rows, reach, weights))
+        for columns, rows, reach, weights in tiles:
+            local_out[rows, columns] = product(weights, values_ref[:reach, columns])
+
+
+def attend_locally(arrived, keys, values, tables):
+    slots, columns = arrived.shape
+    tok_rows = keys.shape[0]
+    width = math.gcd(columns, 4 * HEAD_DIM)
+    column_spec = pl.BlockSpec((tok_rows, width), lambda j: (0, j))
+    return pl.pallas_call(
+        local_kernel,
+        out_shape=tuple(
+            jax.ShapeDtypeStruct((tok_rows, columns), dtype) for dtype in (jnp.bfloat16, jnp.float32)
+        ),
+        grid=(columns // width,),
+        in_specs=[pl.BlockSpec(table.shape, lambda j: (0, 0)) for table in tables]
+        + [pl.BlockSpec((slots, width), lambda j: (0, j)), column_spec, column_spec],
+        out_specs=(column_spec, column_spec),
+        cost_estimate=pl.CostEstimate(
+            flops=ATTEND_WEIGHT * tok_rows * columns * (slots + 2 * tok_rows) // 5,
+            bytes_accessed=2 * columns * (slots + 5 * tok_rows),
+            transcendentals=0,
+        ),
+        name="attend_locally",
+    )(*tables, arrived, keys, values)
+
+
+def finish_kernel(gain_ref, query_ref, local_ref, states_ref, out_ref):
+    ones = jnp.full((2 * HEAD_DIM, HEAD_DIM), 1.0, jnp.bfloat16)
+    raws = []
+    for part in range(out_ref.shape[1] // HEAD_DIM):
+        columns = slice(part * HEAD_DIM, (part + 1) * HEAD_DIM)
+        query = query_ref[:, columns]
+        states = states_ref[2 * part * HEAD_DIM : 2 * (part + 1) * HEAD_DIM, :]
+        carried_term = product(jnp.concatenate([query, query], axis=1), states)
+        raws.append((columns, local_ref[:, columns] + carried_term))
+    for columns, raw_out in raws:
+        square = jnp.concatenate(two_terms(raw_out * raw_out), axis=1)
+        mean = product(square, ones) * (1.0 / HEAD_DIM)
+        out_ref[:, columns] = (raw_out * lax.rsqrt(mean + norm_eps) * gain_ref[:, columns]).astype(
+            out_ref.dtype
+        )
+
+
+def finish(query, local_term, states, gain):
+    tok_rows, columns = query.shape
+    width = math.gcd(columns, 4 * HEAD_DIM)
+    column_spec = pl.BlockSpec((tok_rows, width), lambda j: (0, j))
+    return pl.pallas_call(
+        finish_kernel,
+        out_shape=jax.ShapeDtypeStruct((tok_rows, gain.shape[1]), jnp.bfloat16),
+        grid=(columns // width,),
+        in_specs=[
+            pl.BlockSpec((1, width), lambda j: (0, j)),
+            column_spec,
+            column_spec,
+            pl.BlockSpec((2 * width, HEAD_DIM), lambda j: (j, 0)),
+        ],
+        out_specs=column_spec,
+        cost_estimate=pl.CostEstimate(
+            flops=FINISH_WEIGHT * 8 * tok_rows * columns * HEAD_DIM,
+            bytes_accessed=8 * columns * tok_rows,
+            transcendentals=0,
+        ),
+        name="finish",
+    )(gain, query, local_term, states)
 
 
 def swap_heads(qkv, plane_start, planes, start, columns):
@@ -438,7 +527,7 @@
     landing = first_row + land_row.reshape(-1, 1)
     landing_segment = jnp.sum((req_starts[None, :] <= landing).astype(jnp.int32), axis=1, keepdims=True) - 1
     in_tail = (land_row.reshape(-1, 1) >= 0) & (landing_segment == last_segment[block])
-    tail_slots = in_tail.astype(jnp.int32)
+    tail_slots = jnp.broadcast_to(in_tail.astype(jnp.bfloat16), (land_row.shape[1], HEAD_DIM))
     gain = norm_gain.reshape(1, -1)
 
     rows = send_rows[0]
@@ -478,8 +567,10 @@
     )
     pieces = pass_totals(sums)
     query_next = to_owners(outgoing_next)
-    states = assemble_states(states + hand_back(pieces, across))
-    out = attend(query, *filled, states, tables, gain, 0, ())
+    states += hand_back(pieces, across)
+    local = attend_locally(query, *filled, tables)
+    states = assemble_states(states)
+    out = finish(*local, states, gain)
     return attend(query_next, *filled, states, tables, gain, part, (out,))
 
 

time: 252 us -> 248 us (0.984)
  waiting for transfers between devices: 113 us -> 108 us
    pallas_call x0 -> x2, Pallas kernels: none -> 9.68 us  [the longest x1 5.92 us: attend_locally(): pl.pallas_call(local_kernel, out_shape=tuple((jax.ShapeDtypeStruct((tok_r...]
    pallas_call x2 -> x1, Pallas kernels: 14.2 us -> 7.1 us  [attend(): pl.pallas_call(attend_kernel, out_shape=jax.ShapeDtypeStruct((tok_rows, m...]
    ppermute x12, waiting for transfers between devices: 22.8 us -> 17.4 us  [swap_places(): return lax.ppermute(value, 'seq', [(i, i ^ k) for i in range(seq_count)])]
  transfers between devices with their start and end apart: 23 -> 23, of which waited for: 12 -> 12; matrix products, arithmetic and copies ran while one was open for 6% -> 6% of each run, Pallas kernels for 22% -> 23%
where the time goes in v8:
time: 248 us; the launch traced here: 247 us
  waiting for transfers between devices  108 us (44%)
  Pallas kernels  64.7 us (26%)
  starting transfers between devices  50.7 us (20%)
  local copies, waits for them, and re-layouts  12.5 us (5%)
  other arithmetic  10.2 us (4%)
    ppermute x4, waiting for transfers between devices, pass_totals(): lax.ppermute(sums[near], 'seq', [(i, i + step) for i in range(seq_count -...  59.4 us
    ppermute x3, waiting for transfers between devices, swap_heads(): return lax.ppermute(outgoing, 'head', [(0, 1), (1, 0)])  28.5 us
    all_to_all x4, starting transfers between devices, to_owners(): lax.all_to_all(outgoing, 'seq', split_axis=0, concat_axis=0, tiled=True)  27.9 us
    ppermute x12, waiting for transfers between devices, swap_places(): return lax.ppermute(value, 'seq', [(i, i ^ k) for i in range(seq_count)])  17.4 us
    pallas_call x4, Pallas kernels, pack_rows(): pl.pallas_call(pack_kernel, out_shape=jax.ShapeDtypeStruct((slots, planes...  17.4 us
    ppermute x4, starting transfers between devices, pass_totals(): lax.ppermute(sums[near], 'seq', [(i, i + step) for i in range(seq_count -...  10.9 us
    pallas_call x2, Pallas kernels, unpack_keys_values(): pl.pallas_call(unpack_kernel, out_shape=(packed, packed), grid=(blocks,),...  9.14 us
    ppermute x12, starting transfers between devices, swap_places(): return lax.ppermute(value, 'seq', [(i, i ^ k) for i in range(seq_count)])  9.03 us
  transfers between devices with their start and end apart: 23, of which 12 were waited for; matrix products, arithmetic and copies ran while one was open for 6% of the time, Pallas kernels for 23%

profile of v8, /device:TPU:11, one launch (start us, length us, event | category | flops | bytes accessed | tf_op | source)
XLA Modules:
  0.0 246.6 jit_solution(15680527542702954992)
XLA Ops:
  0.0 1.3 slice_select_fusion.2
  1.3 1.3 collective-permute-start.1
  2.6 2.0 slice_select_fusion
  4.9 0.9 sub.105.refs_0_
  6.7 7.4 %collective-permute-done.1.refs_3_ = bf16[2,256,512]{2,1,0:T(8,128)(2,1)S(1)} collective-permute-done((bf16[2,256,512]{2,1,0:T(8,128)(2,1)S(1)}, bf16[2,256,512]{2,1,0:T(8,128)(2,1)S(1)}, u32[]{:S(2)}, u32[]{:S(2)}) %collective-permute-start.1) | collective-permute-done | bytes 524320 | tf_op jit(solution)/shard_map/ppermute | solution.py:481
  14.9 3.4 %pack_rows.4 = bf16[640,1024]{1,0:T(8,128)(2,1)} custom-call(s32[1]{0:T(128)} %bitcast.8.place_ref, s32[640,1]{1,0:T(8,128)} %sub.105.refs_0_, s32[640,1]{1,0:T(8,128)} %sub.106.refs_1_, bf16[3,256,4096]{2,1,0:T(8,128)(2,1)} %refs_2_.7, bf16[2,256,512]{2,1,0:T(8,128)(2,1)} %copy-done.25), custom_call_target="tpu_custom_call" | custom-call | flops 13421772800 | bytes 2359296 | tf_op jit(solution)/shard_map/pack_rows/pallas_call | solution.py:50
  18.3 8.6 %all-to-all-start = ((bf16[16,40,1024]{2,1,0:T(8,128)(2,1)}), bf16[16,40,1024]{2,1,0:T(8,128)(2,1)S(1)}, u32[]{:S(2)}, u32[]{:S(2)}) async-start(bf16[16,40,1024]{2,1,0:T(8,128)(2,1)} %bitcast.35), calls=%async_computation | async-start | bytes 2621440 | tf_op jit(solution)/shard_map/all_to_all | solution.py:508
  26.9 21.1 %collective-permute-done.7.refs_3_ = bf16[2,256,1536]{2,1,0:T(8,128)(2,1)} collective-permute-done((bf16[2,256,1536]{2,1,0:T(8,128)(2,1)S(1)}, bf16[2,256,1536]{2,1,0:T(8,128)(2,1)}, u32[]{:S(2)}, u32[]{:S(2)}) %collective-permute-start.7) | collective-permute-done | bytes 1572896 | tf_op jit(solution)/shard_map/ppermute | solution.py:481
  47.9 7.2 %pack_rows.7 = bf16[640,3072]{1,0:T(8,128)(2,1)} custom-call(s32[1]{0:T(128)} %bitcast.8.place_ref, s32[640,1]{1,0:T(8,128)} %sub.105.refs_0_, s32[640,1]{1,0:T(8,128)} %sub.106.refs_1_, bf16[3,256,4096]{2,1,0:T(8,128)(2,1)} %refs_2_.7, bf16[2,256,1536]{2,1,0:T(8,128)(2,1)} %collective-permute-done.7.refs_3_), custom_call_target="tpu_custom_call" | custom-call | flops 40265318400 | bytes 7077888 | tf_op jit(solution)/shard_map/pack_rows/pallas_call | solution.py:50
  55.2 2.2 all-to-all-done
  57.4 1.1 copy-done
  58.5 5.2 %all-to-all-start.1 = ((bf16[16,40,3072]{2,1,0:T(8,128)(2,1)}), bf16[16,40,3072]{2,1,0:T(8,128)(2,1)}, u32[]{:S(2)}, u32[]{:S(2)}) async-start(bf16[16,40,3072]{2,1,0:T(8,128)(2,1)} %bitcast.31), calls=%async_computation.1 | async-start | bytes 7864320 | tf_op jit(solution)/shard_map/all_to_all | solution.py:508
  63.7 1.7 slice_select_fusion.1
  65.4 1.3 collective-permute-start
  75.1 3.7 %block_update.2 = (f32[128,128]{1,0:T(8,128)}, f32[128,128]{1,0:T(8,128)}, f32[128,128]{1,0:T(8,128)}, f32[128,128]{1,0:T(8,128)}) custom-call(s32[1]{0:T(128)} %bitcast.6.place_ref, bf16[640,128]{1,0:T(8,128)(2,1)} %broadcast_in_dim.2.tail_ref, bf16[640,1024]{1,0:T(8,128)(2,1)} %bitcast.27, bf16[640,1024]{1,0:T(8,128)(2,1)} %bitcast.28), custom_call_target="tpu_custom_call" | custom-call | flops 83886080 | bytes 1572864 | tf_op jit(solution)/shard_map/block_update/pallas_call | solution.py:95
  79.7 1.4 collective-permute-start.4
  81.9 2.4 block_tables.1
  84.2 3.3 %unpack_keys_values.2 = (bf16[512,2048]{1,0:T(8,128)(2,1)}, bf16[512,2048]{1,0:T(8,128)(2,1)}) custom-call(bf16[512,640]{1,0:T(8,128)(2,1)} %get-tuple-element.98.order_ref, bf16[640,1024]{1,0:T(8,128)(2,1)} %bitcast.29, bf16[640,1024]{1,0:T(8,128)(2,1)} %bitcast.30), custom_call_target="tpu_custom_call" | custom-call | flops 671088640 | bytes 2359296 | tf_op jit(solution)/shard_map/unpack_keys_values/pallas_call | solution.py:165
  87.5 0.9 collective-permute-done.3.refs_2_
  88.4 2.0 collective-permute-done.4.refs_3_
  91.0 1.7 sum_pieces.4
  92.8 2.0 collective-permute-start.5
  94.8 2.3 collective-permute-start.6
  97.1 3.4 %pack_rows.6 = bf16[640,1024]{1,0:T(8,128)(2,1)} custom-call(s32[1]{0:T(128)} %bitcast.8.place_ref, s32[640,1]{1,0:T(8,128)} %sub.105.refs_0_, s32[640,1]{1,0:T(8,128)} %sub.106.refs_1_, bf16[3,256,4096]{2,1,0:T(8,128)(2,1)} %refs_2_.7, bf16[1,256,2048]{2,1,0:T(8,128)(2,1)} %copy-done.24), custom_call_target="tpu_custom_call" | custom-call | flops 13421772800 | bytes 2359296 | tf_op jit(solution)/shard_map/pack_rows/pallas_call | solution.py:50
  100.5 3.4 %pack_rows.5 = bf16[640,1024]{1,0:T(8,128)(2,1)} custom-call(s32[1]{0:T(128)} %bitcast.8.place_ref, s32[640,1]{1,0:T(8,128)} %sub.105.refs_0_, s32[640,1]{1,0:T(8,128)} %sub.106.refs_1_, bf16[3,256,4096]{2,1,0:T(8,128)(2,1)} %refs_2_.7, bf16[1,256,2048]{2,1,0:T(8,128)(2,1)} %copy-done.24), custom_call_target="tpu_custom_call" | custom-call | flops 13421772800 | bytes 2359296 | tf_op jit(solution)/shard_map/pack_rows/pallas_call | solution.py:50
  103.9 47.3 %collective-permute-done.5.refs_4_ = f32[128,128]{1,0:T(8,128)S(1)} collective-permute-done((f32[128,128]{1,0:T(8,128)}, f32[128,128]{1,0:T(8,128)S(1)}, u32[]{:S(2)}, u32[]{:S(2)}) %collective-permute-start.5) | collective-permute-done | bytes 65568 | tf_op jit(solution)/shard_map/ppermute | solution.py:252
  151.1 1.4 collective-permute-done.6.refs_5_
  152.5 7.4 %all-to-all-start.3 = ((bf16[16,40,1024]{2,1,0:T(8,128)(2,1)}), bf16[16,40,1024]{2,1,0:T(8,128)(2,1)S(1)}, u32[]{:S(2)}, u32[]{:S(2)}) async-start(bf16[16,40,1024]{2,1,0:T(8,128)(2,1)} %bitcast.33), calls=%async_computation.3 | async-start | bytes 2621440 | tf_op jit(solution)/shard_map/all_to_all | solution.py:508
  160.0 4.5 %block_update.3 = (f32[384,128]{1,0:T(8,128)}, f32[384,128]{1,0:T(8,128)}, f32[384,128]{1,0:T(8,128)}, f32[384,128]{1,0:T(8,128)}) custom-call(s32[1]{0:T(128)} %bitcast.6.place_ref, bf16[640,128]{1,0:T(8,128)(2,1)} %broadcast_in_dim.2.tail_ref, bf16[640,3072]{1,0:T(8,128)(2,1)} %bitcast.16.keys_ref.values_ref, bf16[640,3072]{1,0:T(8,128)(2,1)} %bitcast.16.keys_ref.values_ref), custom_call_target="tpu_custom_call" | custom-call | flops 251658240 | bytes 4718592 | tf_op jit(solution)/shard_map/block_update/pallas_call | solution.py:95
  165.3 1.2 collective-permute-start.9
  167.6 1.7 sum_pieces.6
  170.3 5.2 %collective-permute-done.10.refs_3_ = f32[384,128]{1,0:T(8,128)S(1)} collective-permute-done((f32[384,128]{1,0:T(8,128)}, f32[384,128]{1,0:T(8,128)S(1)}, u32[]{:S(2)}, u32[]{:S(2)}) %collective-permute-start.10) | collective-permute-done | bytes 196640 | tf_op jit(solution)/shard_map/ppermute | solution.py:222
  175.6 5.9 %unpack_keys_values.3 = (bf16[512,2048]{1,0:T(8,128)(2,1)}, bf16[512,2048]{1,0:T(8,128)(2,1)}) custom-call(bf16[512,640]{1,0:T(8,128)(2,1)} %get-tuple-element.98.order_ref, bf16[640,3072]{1,0:T(8,128)(2,1)} %bitcast.16.keys_ref.values_ref, bf16[640,3072]{1,0:T(8,128)(2,1)} %bitcast.16.keys_ref.values_ref, ...), custom_call_target="tpu_custom_call", output_to_operand_aliasing={{0}: (3, {}), {1}: (4, {})} | custom-call | flops 2013265920 | bytes 7077888 | tf_op jit(solution)/shard_map/unpack_keys_values/pallas_call | solution.py:165
  182.8 2.4 sum_pieces.5
  185.7 4.5 %collective-permute-start.14 = (f32[384,128]{1,0:T(8,128)}, f32[384,128]{1,0:T(8,128)S(1)}, u32[]{:S(2)}, u32[]{:S(2)}) collective-permute-start(f32[384,128]{1,0:T(8,128)} %get-tuple-element.155), channel_id=1, source_target_pairs={{0,8},{2,10},{4,12},{6,14},{8,16},{10,18},{12,20},{14,22},{16,24},... | collective-permute-start | bytes 589832 | tf_op jit(solution)/shard_map/ppermute | solution.py:252
  190.3 2.1 collective-permute-start.15
  192.4 6.7 %all-to-all-start.2 = ((bf16[16,40,1024]{2,1,0:T(8,128)(2,1)}), bf16[16,40,1024]{2,1,0:T(8,128)(2,1)S(1)}, u32[]{:S(2)}, u32[]{:S(2)}) async-start(bf16[16,40,1024]{2,1,0:T(8,128)(2,1)} %bitcast.17), calls=%async_computation.2 | async-start | bytes 2621440 | tf_op jit(solution)/shard_map/all_to_all | solution.py:508
  199.1 10.7 %collective-permute-done.15.refs_5_ = f32[384,128]{1,0:T(8,128)S(1)} collective-permute-done((f32[384,128]{1,0:T(8,128)}, f32[384,128]{1,0:T(8,128)S(1)}, u32[]{:S(2)}, u32[]{:S(2)}) %collective-permute-start.15) | collective-permute-done | bytes 196640 | tf_op jit(solution)/shard_map/ppermute | solution.py:252
  210.5 2.5 %sum_pieces.7 = (f32[384,128]{1,0:T(8,128)}, f32[384,128]{1,0:T(8,128)}, f32[384,128]{1,0:T(8,128)}, f32[384,128]{1,0:T(8,128)}) custom-call(s32[4,6]{1,0:T(4,128)} %convert_element_type.48.take_ref, f32[384,128]{1,0:T(8,128)} %get-tuple-element.151.refs_0_, f32[384,128]{1,0:T(8,128)} %get-tuple-element.152.refs_1_, f32[384,128]{1,0:T(8,128)} %get-tuple-element.153.refs_2_, ...), custom_call_target="tpu_custom_call" | custom-call | flops 1179648 | bytes 1966080 | tf_op jit(solution)/shard_map/sum_pieces/pallas_call | solution.py:200
  212.9 2.2 collective-permute-start.16
  215.1 1.7 collective-permute-start.18
  216.8 5.9 %attend_locally.1 = (bf16[512,1024]{1,0:T(8,128)(2,1)}, f32[512,1024]{1,0:T(8,128)}) custom-call(bf16[512,640]{1,0:T(8,128)(2,1)} %get-tuple-element.98.order_ref, bf16[512,512]{1,0:T(8,128)(2,1)} %get-tuple-element.99.causal_ref, bf16[512,128]{1,0:T(8,128)(2,1)} %get-tuple-element.100.carried_ref, bf16[640,1024]{1,0:T(8,128)(2,1)} %bitcast.32, ...), custom_call_target="tpu_custom_call" | custom-call | flops 24951074816 | bytes 6553600 | tf_op jit(solution)/shard_map/attend_locally/pallas_call | solution.py:413
  222.8 2.8 %collective-permute-done.17.refs_6_ = f32[384,128]{1,0:T(8,128)S(1)} collective-permute-done((f32[384,128]{1,0:T(8,128)}, f32[384,128]{1,0:T(8,128)S(1)}, u32[]{:S(2)}, u32[]{:S(2)}) %collective-permute-start.17) | collective-permute-done | bytes 196640 | tf_op jit(solution)/shard_map/ppermute | solution.py:222
  225.6 6.0 %collective-permute-done.18.refs_7_ = f32[384,128]{1,0:T(8,128)S(1)} collective-permute-done((f32[384,128]{1,0:T(8,128)}, f32[384,128]{1,0:T(8,128)S(1)}, u32[]{:S(2)}, u32[]{:S(2)}) %collective-permute-start.18) | collective-permute-done | bytes 196640 | tf_op jit(solution)/shard_map/ppermute | solution.py:222
  232.2 2.5 %assemble_states.1.states_ref = bf16[4096,128]{1,0:T(8,128)(2,1)} custom-call(s32[1]{0:T(128)} %bitcast.6.place_ref, f32[128,128]{1,0:T(8,128)} %get-tuple-element.147.refs_0_, f32[128,128]{1,0:T(8,128)} %copy-done.13, f32[128,128]{1,0:T(8,128)} %copy-done.14, f32[128,128]{1,0:T(8,128)} %copy-done.15, f32[384,128]{1,0:T(8,128)} %get-tuple-element.156.refs_4_, ...), custom_call_target="tpu_custom_call" | custom-call | flops 2097152 | bytes 2097152 | tf_op jit(solution)/shard_map/assemble_states/pallas_call | solution.py:295
  234.7 3.8 %finish.1.refs_0_ = bf16[512,2048]{1,0:T(8,128)(2,1)} custom-call(f32[1,2048]{1,0:T(1,128)} %bitcast.38, bf16[512,1024]{1,0:T(8,128)(2,1)} %get-tuple-element.161.query_ref, f32[512,1024]{1,0:T(8,128)} %get-tuple-element.162.local_ref, bf16[4096,128]{1,0:T(8,128)(2,1)} %assemble_states.1.states_ref), custom_call_target="tpu_custom_call" | custom-call | flops 536870912 | bytes 4194304 | tf_op jit(solution)/shard_map/finish/pallas_call | solution.py:452
  238.4 1.1 copy-done.3
  239.5 7.1 %attend.1 = bf16[512,2048]{1,0:T(8,128)(2,1)} custom-call(bf16[512,640]{1,0:T(8,128)(2,1)} %get-tuple-element.98.order_ref, bf16[512,512]{1,0:T(8,128)(2,1)} %get-tuple-element.99.causal_ref, bf16[512,128]{1,0:T(8,128)(2,1)} %get-tuple-element.100.carried_ref, f32[1,2048]{1,0:T(1,128)} %bitcast.39, ...), custom_call_target="tpu_custom_call", output_to_operand_aliasing={{}: (8, {})} | custom-call | flops 32628330496 | bytes 5505024 | tf_op jit(solution)/shard_map/attend/pallas_call | solution.py:359
  (110 shorter events, 18.1 us)
Async XLA Ops:
  1.3 3.7 %copy-start.22 = (s32[1,16,40]{2,1,0:T(8,128)S(1)}, s32[1,16,40]{2,1,0:T(8,128)}, u32[]{:S(2)}) copy-start(s32[1,16,40]{2,1,0:T(8,128)} %param.6) | copy-start | bytes 7684
  1.3 12.9 %collective-permute-start.1 = (bf16[2,256,512]{2,1,0:T(8,128)(2,1)S(1)}, bf16[2,256,512]{2,1,0:T(8,128)(2,1)S(1)}, u32[]{:S(2)}, u32[]{:S(2)}) collective-permute-start(bf16[2,256,512]{2,1,0:T(8,128)(2,1)S(1)} %slice_select_fusion.2), channel_id=1, source_target_pairs={{0,1},{1,0},{2,3},{3,2},{4,5},{5,4},{6,7},{7,6},{8,9},{9,8},{10,11... | collective-permute-start | bytes 1572872 | tf_op jit(solution)/shard_map/ppermute | solution.py:481
  4.6 43.3 %collective-permute-start.7 = (bf16[2,256,1536]{2,1,0:T(8,128)(2,1)S(1)}, bf16[2,256,1536]{2,1,0:T(8,128)(2,1)}, u32[]{:S(2)}, u32[]{:S(2)}) collective-permute-start(bf16[2,256,1536]{2,1,0:T(8,128)(2,1)S(1)} %slice_select_fusion), channel_id=1, source_target_pairs={{0,1},{1,0},{2,3},{3,2},{4,5},{5,4},{6,7},{7,6},{8,9},{9,8},{10,11... | collective-permute-start | bytes 4718600 | tf_op jit(solution)/shard_map/ppermute | solution.py:481
  14.1 0.8 copy-start.25
  18.3 39.1 %all-to-all-start = ((bf16[16,40,1024]{2,1,0:T(8,128)(2,1)}), bf16[16,40,1024]{2,1,0:T(8,128)(2,1)S(1)}, u32[]{:S(2)}, u32[]{:S(2)}) async-start(bf16[16,40,1024]{2,1,0:T(8,128)(2,1)} %bitcast.35), calls=%async_computation | async-start | bytes 2621440 | tf_op jit(solution)/shard_map/all_to_all | solution.py:508
  57.4 1.1 copy-start
  58.5 94.1 %all-to-all-start.1 = ((bf16[16,40,3072]{2,1,0:T(8,128)(2,1)}), bf16[16,40,3072]{2,1,0:T(8,128)(2,1)}, u32[]{:S(2)}, u32[]{:S(2)}) async-start(bf16[16,40,3072]{2,1,0:T(8,128)(2,1)} %bitcast.31), calls=%async_computation.1 | async-start | bytes 7864320 | tf_op jit(solution)/shard_map/all_to_all | solution.py:508
  63.7 3.0 %copy-start.23 = (s32[4]{0:T(128)S(1)}, s32[4]{0:T(128)}, u32[]{:S(2)}) copy-start(s32[4]{0:T(128)} %param.8) | copy-start | bytes 52
  63.7 3.2 %copy-start.12 = (s32[1,16,40]{2,1,0:T(8,128)S(1)}, s32[1,16,40]{2,1,0:T(8,128)}, u32[]{:S(2)}) copy-start(s32[1,16,40]{2,1,0:T(8,128)} %param.7) | copy-start | bytes 7684
  65.4 27.4 %collective-permute-start = (bf16[1,256,2048]{2,1,0:T(8,128)(2,1)S(1)}, bf16[1,256,2048]{2,1,0:T(8,128)(2,1)S(1)}, u32[]{:S(2)}, u32[]{:S(2)}) collective-permute-start(bf16[1,256,2048]{2,1,0:T(8,128)(2,1)S(1)} %slice_select_fusion.1), channel_id=1, source_target_pairs={{0,1},{1,0},{2,3},{3,2},{4,5},{5,4},{6,7},{7,6},{8,9},{9,8},{10,11... | collective-permute-start | bytes 3145736 | tf_op jit(solution)/shard_map/ppermute | solution.py:481
  69.9 11.9 %copy-start.21 = (s32[512]{0:T(512)}, s32[512]{0:T(512)S(1)}, u32[]{:S(2)}) copy-start(s32[512]{0:T(512)S(1)} %broadcast_add_fusion.1) | copy-start | bytes 6148
  70.1 11.8 %copy-start.1 = (s32[512,1]{1,0:T(8,128)}, s32[512,1]{1,0:T(8,128)S(1)}, u32[]{:S(2)}) copy-start(s32[512,1]{1,0:T(8,128)S(1)} %copy.33.seg_col_ref) | copy-start | bytes 6148
  78.8 8.7 %collective-permute-start.2 = (f32[128,128]{1,0:T(8,128)}, f32[128,128]{1,0:T(8,128)S(1)}, u32[]{:S(2)}, u32[]{:S(2)}) collective-permute-start(f32[128,128]{1,0:T(8,128)} %get-tuple-element.85), channel_id=1, source_target_pairs={{0,2},{2,0},{4,6},{6,4},{8,10},{10,8},{12,14},{14,12},{16,18},{18,... | collective-permute-start | bytes 196616 | tf_op jit(solution)/shard_map/ppermute | solution.py:222
  79.4 9.0 %collective-permute-start.3 = (f32[128,128]{1,0:T(8,128)}, f32[128,128]{1,0:T(8,128)S(1)}, u32[]{:S(2)}, u32[]{:S(2)}) collective-permute-start(f32[128,128]{1,0:T(8,128)} %get-tuple-element.86), channel_id=1, source_target_pairs={{0,4},{2,6},{4,0},{6,2},{8,12},{10,14},{12,8},{14,10},{16,20},{18,... | collective-permute-start | bytes 196616 | tf_op jit(solution)/shard_map/ppermute | solution.py:222
  79.7 10.7 %collective-permute-start.4 = (f32[128,128]{1,0:T(8,128)}, f32[128,128]{1,0:T(8,128)S(1)}, u32[]{:S(2)}, u32[]{:S(2)}) collective-permute-start(f32[128,128]{1,0:T(8,128)} %get-tuple-element.87), channel_id=1, source_target_pairs={{0,6},{2,4},{4,2},{6,0},{8,14},{10,12},{12,10},{14,8},{16,22},{18,... | collective-permute-start | bytes 196616 | tf_op jit(solution)/shard_map/ppermute | solution.py:222
  87.5 2.9 %copy-start.18 = (f32[128,128]{1,0:T(8,128)}, f32[128,128]{1,0:T(8,128)S(1)}, u32[]{:S(2)}) copy-start(f32[128,128]{1,0:T(8,128)S(1)} %collective-permute-done.2.refs_1_) | copy-start | bytes 196612
  88.4 2.0 copy-start.19
  92.7 4.3 %copy-start.24 = (bf16[1,256,2048]{2,1,0:T(8,128)(2,1)}, bf16[1,256,2048]{2,1,0:T(8,128)(2,1)S(1)}, u32[]{:S(2)}) copy-start(bf16[1,256,2048]{2,1,0:T(8,128)(2,1)S(1)} %collective-permute-done.refs_3_) | copy-start | bytes 3145732
  92.8 58.4 %collective-permute-start.5 = (f32[128,128]{1,0:T(8,128)}, f32[128,128]{1,0:T(8,128)S(1)}, u32[]{:S(2)}, u32[]{:S(2)}) collective-permute-start(f32[128,128]{1,0:T(8,128)} %get-tuple-element.106), channel_id=1, source_target_pairs={{0,8},{2,10},{4,12},{6,14},{8,16},{10,18},{12,20},{14,22},{16,24},... | collective-permute-start | bytes 196616 | tf_op jit(solution)/shard_map/ppermute | solution.py:252
  94.8 57.8 %collective-permute-start.6 = (f32[128,128]{1,0:T(8,128)}, f32[128,128]{1,0:T(8,128)S(1)}, u32[]{:S(2)}, u32[]{:S(2)}) collective-permute-start(f32[128,128]{1,0:T(8,128)} %get-tuple-element.106), channel_id=1, source_target_pairs={{0,16},{2,18},{4,20},{6,22},{8,24},{10,26},{12,28},{14,30},{1,17},... | collective-permute-start | bytes 196616 | tf_op jit(solution)/shard_map/ppermute | solution.py:252
  151.1 13.4 %copy-start.16 = (f32[128,128]{1,0:T(8,128)}, f32[128,128]{1,0:T(8,128)S(1)}, u32[]{:S(2)}) copy-start(f32[128,128]{1,0:T(8,128)S(1)} %collective-permute-done.5.refs_4_) | copy-start | bytes 196612
  152.5 12.0 %copy-start.17 = (f32[128,128]{1,0:T(8,128)}, f32[128,128]{1,0:T(8,128)S(1)}, u32[]{:S(2)}) copy-start(f32[128,128]{1,0:T(8,128)S(1)} %collective-permute-done.6.refs_5_) | copy-start | bytes 196612
  152.5 39.8 %all-to-all-start.3 = ((bf16[16,40,1024]{2,1,0:T(8,128)(2,1)}), bf16[16,40,1024]{2,1,0:T(8,128)(2,1)S(1)}, u32[]{:S(2)}, u32[]{:S(2)}) async-start(bf16[16,40,1024]{2,1,0:T(8,128)(2,1)} %bitcast.33), calls=%async_computation.3 | async-start | bytes 2621440 | tf_op jit(solution)/shard_map/all_to_all | solution.py:508
  164.5 11.0 %collective-permute-start.10 = (f32[384,128]{1,0:T(8,128)}, f32[384,128]{1,0:T(8,128)S(1)}, u32[]{:S(2)}, u32[]{:S(2)}) collective-permute-start(f32[384,128]{1,0:T(8,128)} %get-tuple-element.123), channel_id=1, source_target_pairs={{0,6},{2,4},{4,2},{6,0},{8,14},{10,12},{12,10},{14,8},{16,22},{18,... | collective-permute-start | bytes 589832 | tf_op jit(solution)/shard_map/ppermute | solution.py:222
  165.1 16.3 %collective-permute-start.8 = (f32[384,128]{1,0:T(8,128)}, f32[384,128]{1,0:T(8,128)S(1)}, u32[]{:S(2)}, u32[]{:S(2)}) collective-permute-start(f32[384,128]{1,0:T(8,128)} %get-tuple-element.121), channel_id=1, source_target_pairs={{0,2},{2,0},{4,6},{6,4},{8,10},{10,8},{12,14},{14,12},{16,18},{18,... | collective-permute-start | bytes 589832 | tf_op jit(solution)/shard_map/ppermute | solution.py:222
  165.3 16.2 %collective-permute-start.9 = (f32[384,128]{1,0:T(8,128)}, f32[384,128]{1,0:T(8,128)S(1)}, u32[]{:S(2)}, u32[]{:S(2)}) collective-permute-start(f32[384,128]{1,0:T(8,128)} %get-tuple-element.122), channel_id=1, source_target_pairs={{0,4},{2,6},{4,0},{6,2},{8,12},{10,14},{12,8},{14,10},{16,20},{18,... | collective-permute-start | bytes 589832 | tf_op jit(solution)/shard_map/ppermute | solution.py:222
  169.4 15.8 %collective-permute-start.11 = (f32[128,128]{1,0:T(8,128)}, f32[128,128]{1,0:T(8,128)S(1)}, u32[]{:S(2)}, u32[]{:S(2)}) collective-permute-start(f32[128,128]{1,0:T(8,128)} %get-tuple-element.137), channel_id=1, source_target_pairs={{0,2},{2,0},{4,6},{6,4},{8,10},{10,8},{12,14},{14,12},{16,18},{18,... | collective-permute-start | bytes 196616 | tf_op jit(solution)/shard_map/ppermute | solution.py:222
  170.0 15.2 %collective-permute-start.12 = (f32[128,128]{1,0:T(8,128)}, f32[128,128]{1,0:T(8,128)S(1)}, u32[]{:S(2)}, u32[]{:S(2)}) collective-permute-start(f32[128,128]{1,0:T(8,128)} %get-tuple-element.138), channel_id=1, source_target_pairs={{0,4},{2,6},{4,0},{6,2},{8,12},{10,14},{12,8},{14,10},{16,20},{18,... | collective-permute-start | bytes 196616 | tf_op jit(solution)/shard_map/ppermute | solution.py:222
  175.5 5.9 %copy-start.9 = (f32[384,128]{1,0:T(8,128)}, f32[384,128]{1,0:T(8,128)S(1)}, u32[]{:S(2)}) copy-start(f32[384,128]{1,0:T(8,128)S(1)} %collective-permute-done.10.refs_3_) | copy-start | bytes 589828
  175.5 10.2 %collective-permute-start.13 = (f32[128,128]{1,0:T(8,128)}, f32[128,128]{1,0:T(8,128)S(1)}, u32[]{:S(2)}, u32[]{:S(2)}) collective-permute-start(f32[128,128]{1,0:T(8,128)} %get-tuple-element.139), channel_id=1, source_target_pairs={{0,6},{2,4},{4,2},{6,0},{8,14},{10,12},{12,10},{14,8},{16,22},{18,... | collective-permute-start | bytes 196616 | tf_op jit(solution)/shard_map/ppermute | solution.py:222
  181.4 0.7 copy-start.10
  182.1 0.7 copy-start.11
  185.2 37.6 %copy-start.13 = (f32[128,128]{1,0:T(8,128)}, f32[128,128]{1,0:T(8,128)S(1)}, u32[]{:S(2)}) copy-start(f32[128,128]{1,0:T(8,128)S(1)} %collective-permute-done.11.refs_1_) | copy-start | bytes 196612
  185.2 37.6 %copy-start.14 = (f32[128,128]{1,0:T(8,128)}, f32[128,128]{1,0:T(8,128)S(1)}, u32[]{:S(2)}) copy-start(f32[128,128]{1,0:T(8,128)S(1)} %collective-permute-done.12.refs_2_) | copy-start | bytes 196612
  185.7 37.0 %copy-start.15 = (f32[128,128]{1,0:T(8,128)}, f32[128,128]{1,0:T(8,128)S(1)}, u32[]{:S(2)}) copy-start(f32[128,128]{1,0:T(8,128)S(1)} %collective-permute-done.13.refs_3_) | copy-start | bytes 196612
  185.7 13.4 %collective-permute-start.14 = (f32[384,128]{1,0:T(8,128)}, f32[384,128]{1,0:T(8,128)S(1)}, u32[]{:S(2)}, u32[]{:S(2)}) collective-permute-start(f32[384,128]{1,0:T(8,128)} %get-tuple-element.155), channel_id=1, source_target_pairs={{0,8},{2,10},{4,12},{6,14},{8,16},{10,18},{12,20},{14,22},{16,24},... | collective-permute-start | bytes 589832 | tf_op jit(solution)/shard_map/ppermute | solution.py:252
  190.3 19.5 %collective-permute-start.15 = (f32[384,128]{1,0:T(8,128)}, f32[384,128]{1,0:T(8,128)S(1)}, u32[]{:S(2)}, u32[]{:S(2)}) collective-permute-start(f32[384,128]{1,0:T(8,128)} %get-tuple-element.155), channel_id=1, source_target_pairs={{0,16},{2,18},{4,20},{6,22},{8,24},{10,26},{12,28},{14,30},{1,17},... | collective-permute-start | bytes 589832 | tf_op jit(solution)/shard_map/ppermute | solution.py:252
  192.4 24.5 %copy-start.2 = (bf16[16,40,1024]{2,1,0:T(8,128)(2,1)}, bf16[16,40,1024]{2,1,0:T(8,128)(2,1)S(1)}, u32[]{:S(2)}) copy-start(bf16[16,40,1024]{2,1,0:T(8,128)(2,1)S(1)} %all-to-all-done.3) | copy-start | bytes 3932164
  192.4 46.1 %all-to-all-start.2 = ((bf16[16,40,1024]{2,1,0:T(8,128)(2,1)}), bf16[16,40,1024]{2,1,0:T(8,128)(2,1)S(1)}, u32[]{:S(2)}, u32[]{:S(2)}) async-start(bf16[16,40,1024]{2,1,0:T(8,128)(2,1)} %bitcast.17), calls=%async_computation.2 | async-start | bytes 2621440 | tf_op jit(solution)/shard_map/all_to_all | solution.py:508
  199.1 10.7 %copy-start.5 = (f32[384,128]{1,0:T(8,128)}, f32[384,128]{1,0:T(8,128)S(1)}, u32[]{:S(2)}) copy-start(f32[384,128]{1,0:T(8,128)S(1)} %collective-permute-done.14.refs_4_) | copy-start | bytes 589828
  209.8 0.7 copy-start.7
  212.9 9.8 %collective-permute-start.16 = (f32[384,128]{1,0:T(8,128)}, f32[384,128]{1,0:T(8,128)S(1)}, u32[]{:S(2)}, u32[]{:S(2)}) collective-permute-start(f32[384,128]{1,0:T(8,128)} %get-tuple-element.157), channel_id=1, source_target_pairs={{0,2},{2,0},{4,6},{6,4},{8,10},{10,8},{12,14},{14,12},{16,18},{18,... | collective-permute-start | bytes 589832 | tf_op jit(solution)/shard_map/ppermute | solution.py:222
  215.1 10.4 %collective-permute-start.17 = (f32[384,128]{1,0:T(8,128)}, f32[384,128]{1,0:T(8,128)S(1)}, u32[]{:S(2)}, u32[]{:S(2)}) collective-permute-start(f32[384,128]{1,0:T(8,128)} %get-tuple-element.158), channel_id=1, source_target_pairs={{0,4},{2,6},{4,0},{6,2},{8,12},{10,14},{12,8},{14,10},{16,20},{18,... | collective-permute-start | bytes 589832 | tf_op jit(solution)/shard_map/ppermute | solution.py:222
  215.1 16.4 %collective-permute-start.18 = (f32[384,128]{1,0:T(8,128)}, f32[384,128]{1,0:T(8,128)S(1)}, u32[]{:S(2)}, u32[]{:S(2)}) collective-permute-start(f32[384,128]{1,0:T(8,128)} %get-tuple-element.159), channel_id=1, source_target_pairs={{0,6},{2,4},{4,2},{6,0},{8,14},{10,12},{12,10},{14,8},{16,22},{18,... | collective-permute-start | bytes 589832 | tf_op jit(solution)/shard_map/ppermute | solution.py:222
  222.8 8.8 %copy-start.4 = (f32[384,128]{1,0:T(8,128)}, f32[384,128]{1,0:T(8,128)S(1)}, u32[]{:S(2)}) copy-start(f32[384,128]{1,0:T(8,128)S(1)} %collective-permute-done.16.refs_5_) | copy-start | bytes 589828
  225.6 6.0 %copy-start.6 = (f32[384,128]{1,0:T(8,128)}, f32[384,128]{1,0:T(8,128)S(1)}, u32[]{:S(2)}) copy-start(f32[384,128]{1,0:T(8,128)S(1)} %collective-permute-done.17.refs_6_) | copy-start | bytes 589828
  231.5 0.7 copy-start.8
  238.4 1.1 copy-start.3
  (1 other events, 0.6 us)

commit v9 on v8

--- a/solution.py
+++ b/solution.py
@@ -15,7 +15,7 @@
 
 PACK_WEIGHT = 20
 FINISH_WEIGHT = 1
-ATTEND_WEIGHT = 143
+ATTEND_WEIGHT = 145
 
 
 def pack_kernel(place_ref, *refs):
@@ -561,11 +561,11 @@
     shares, pieces = lax.optimization_barrier((block_update(arrived_next, tail_slots), pieces))
     states = hand_back(pieces, across)
     sums = carry_within(shares, within)
+    outgoing_next, sums, states, arrived_next = lax.optimization_barrier(
+        (outgoing_next, sums, states, arrived_next)
+    )
+    pieces = pass_totals(sums)
     filled = unpack_keys_values(arrived_next, tables[0], first, columns, filled)
-    outgoing_next, sums, states, filled = lax.optimization_barrier(
-        (outgoing_next, sums, states, filled)
-    )
-    pieces = pass_totals(sums)
     query_next = to_owners(outgoing_next)
     states += hand_back(pieces, across)
     local = attend_locally(query, *filled, tables)

time: 248 us -> 247 us (level)
  waiting for transfers between devices: 108 us -> 102 us
  starting transfers between devices: 50.7 us -> 55.2 us
    ppermute x4, waiting for transfers between devices: 59.4 us -> 48 us  [pass_totals(): lax.ppermute(sums[near], 'seq', [(i, i + step) for i in range(seq_count -...]
    ppermute x12, waiting for transfers between devices: 17.4 us -> 23.3 us  [swap_places(): return lax.ppermute(value, 'seq', [(i, i ^ k) for i in range(seq_count)])]
    ppermute x12, starting transfers between devices: 9.03 us -> 14.8 us  [swap_places(): return lax.ppermute(value, 'seq', [(i, i ^ k) for i in range(seq_count)])]
  transfers between devices with their start and end apart: 23 -> 23, of which waited for: 12 -> 11; matrix products, arithmetic and copies ran while one was open for 6% -> 6% of each run, Pallas kernels for 23% -> 23%
where the time goes in v9:
time: 247 us; the launch traced here: 246 us
  waiting for transfers between devices  102 us (41%)
  Pallas kernels  64.6 us (26%)
  starting transfers between devices  55.2 us (22%)
  local copies, waits for them, and re-layouts  12.5 us (5%)
  other arithmetic  10.2 us (4%)
    ppermute x4, waiting for transfers between devices, pass_totals(): lax.ppermute(sums[near], 'seq', [(i, i + step) for i in range(seq_count -...  48 us
    ppermute x3, waiting for transfers between devices, swap_heads(): return lax.ppermute(outgoing, 'head', [(0, 1), (1, 0)])  28.5 us
    all_to_all x4, starting transfers between devices, to_owners(): lax.all_to_all(outgoing, 'seq', split_axis=0, concat_axis=0, tiled=True)  27.7 us
    ppermute x12, waiting for transfers between devices, swap_places(): return lax.ppermute(value, 'seq', [(i, i ^ k) for i in range(seq_count)])  23.3 us
    pallas_call x4, Pallas kernels, pack_rows(): pl.pallas_call(pack_kernel, out_shape=jax.ShapeDtypeStruct((slots, planes...  17.4 us
    ppermute x12, starting transfers between devices, swap_places(): return lax.ppermute(value, 'seq', [(i, i ^ k) for i in range(seq_count)])  14.8 us
    ppermute x4, starting transfers between devices, pass_totals(): lax.ppermute(sums[near], 'seq', [(i, i + step) for i in range(seq_count -...  9.81 us
    pallas_call x2, Pallas kernels, unpack_keys_values(): pl.pallas_call(unpack_kernel, out_shape=(packed, packed), grid=(blocks,),...  9.08 us
  transfers between devices with their start and end apart: 23, of which 11 were waited for; matrix products, arithmetic and copies ran while one was open for 6% of the time, Pallas kernels for 23%

profile of v9, /device:TPU:11, one launch (start us, length us, event | category | flops | bytes accessed | tf_op | source)
XLA Modules:
  0.0 245.6 jit_solution(14948746884410322362)
XLA Ops:
  0.0 1.3 slice_select_fusion.2
  1.3 1.3 collective-permute-start.1
  2.6 2.0 slice_select_fusion
  6.7 7.4 %collective-permute-done.1.refs_3_ = bf16[2,256,512]{2,1,0:T(8,128)(2,1)S(1)} collective-permute-done((bf16[2,256,512]{2,1,0:T(8,128)(2,1)S(1)}, bf16[2,256,512]{2,1,0:T(8,128)(2,1)S(1)}, u32[]{:S(2)}, u32[]{:S(2)}) %collective-permute-start.1) | collective-permute-done | bytes 524320 | tf_op jit(solution)/shard_map/ppermute | solution.py:481
  14.9 3.4 %pack_rows.4 = bf16[640,1024]{1,0:T(8,128)(2,1)} custom-call(s32[1]{0:T(128)} %bitcast.8.place_ref, s32[640,1]{1,0:T(8,128)} %sub.105.refs_0_, s32[640,1]{1,0:T(8,128)} %sub.106.refs_1_, bf16[3,256,4096]{2,1,0:T(8,128)(2,1)} %refs_2_.7, bf16[2,256,512]{2,1,0:T(8,128)(2,1)} %copy-done.25), custom_call_target="tpu_custom_call" | custom-call | flops 13421772800 | bytes 2359296 | tf_op jit(solution)/shard_map/pack_rows/pallas_call | solution.py:50
  18.3 8.6 %all-to-all-start = ((bf16[16,40,1024]{2,1,0:T(8,128)(2,1)}), bf16[16,40,1024]{2,1,0:T(8,128)(2,1)S(1)}, u32[]{:S(2)}, u32[]{:S(2)}) async-start(bf16[16,40,1024]{2,1,0:T(8,128)(2,1)} %bitcast.35), calls=%async_computation | async-start | bytes 2621440 | tf_op jit(solution)/shard_map/all_to_all | solution.py:508
  26.9 21.1 %collective-permute-done.7.refs_3_ = bf16[2,256,1536]{2,1,0:T(8,128)(2,1)} collective-permute-done((bf16[2,256,1536]{2,1,0:T(8,128)(2,1)S(1)}, bf16[2,256,1536]{2,1,0:T(8,128)(2,1)}, u32[]{:S(2)}, u32[]{:S(2)}) %collective-permute-start.7) | collective-permute-done | bytes 1572896 | tf_op jit(solution)/shard_map/ppermute | solution.py:481
  47.9 7.2 %pack_rows.7 = bf16[640,3072]{1,0:T(8,128)(2,1)} custom-call(s32[1]{0:T(128)} %bitcast.8.place_ref, s32[640,1]{1,0:T(8,128)} %sub.105.refs_0_, s32[640,1]{1,0:T(8,128)} %sub.106.refs_1_, bf16[3,256,4096]{2,1,0:T(8,128)(2,1)} %refs_2_.7, bf16[2,256,1536]{2,1,0:T(8,128)(2,1)} %collective-permute-done.7.refs_3_), custom_call_target="tpu_custom_call" | custom-call | flops 40265318400 | bytes 7077888 | tf_op jit(solution)/shard_map/pack_rows/pallas_call | solution.py:50
  55.2 2.2 all-to-all-done
  57.4 1.1 copy-done
  58.5 5.2 %all-to-all-start.1 = ((bf16[16,40,3072]{2,1,0:T(8,128)(2,1)}), bf16[16,40,3072]{2,1,0:T(8,128)(2,1)}, u32[]{:S(2)}, u32[]{:S(2)}) async-start(bf16[16,40,3072]{2,1,0:T(8,128)(2,1)} %bitcast.31), calls=%async_computation.1 | async-start | bytes 7864320 | tf_op jit(solution)/shard_map/all_to_all | solution.py:508
  63.7 1.7 slice_select_fusion.1
  65.4 1.3 collective-permute-start
  75.1 3.7 %block_update.2 = (f32[128,128]{1,0:T(8,128)}, f32[128,128]{1,0:T(8,128)}, f32[128,128]{1,0:T(8,128)}, f32[128,128]{1,0:T(8,128)}) custom-call(s32[1]{0:T(128)} %bitcast.6.place_ref, bf16[640,128]{1,0:T(8,128)(2,1)} %broadcast_in_dim.2.tail_ref, bf16[640,1024]{1,0:T(8,128)(2,1)} %bitcast.27, bf16[640,1024]{1,0:T(8,128)(2,1)} %bitcast.28), custom_call_target="tpu_custom_call" | custom-call | flops 83886080 | bytes 1572864 | tf_op jit(solution)/shard_map/block_update/pallas_call | solution.py:95
  79.7 1.4 collective-permute-start.4
  81.9 2.4 block_tables.1
  84.3 3.3 %unpack_keys_values.2 = (bf16[512,2048]{1,0:T(8,128)(2,1)}, bf16[512,2048]{1,0:T(8,128)(2,1)}) custom-call(bf16[512,640]{1,0:T(8,128)(2,1)} %get-tuple-element.97.order_ref, bf16[640,1024]{1,0:T(8,128)(2,1)} %bitcast.29, bf16[640,1024]{1,0:T(8,128)(2,1)} %bitcast.30), custom_call_target="tpu_custom_call" | custom-call | flops 671088640 | bytes 2359296 | tf_op jit(solution)/shard_map/unpack_keys_values/pallas_call | solution.py:165
  87.5 1.0 collective-permute-done.3.refs_2_
  88.5 1.9 collective-permute-done.4.refs_3_
  91.1 1.7 sum_pieces.4
  92.8 3.0 %collective-permute-start.6 = (f32[128,128]{1,0:T(8,128)}, f32[128,128]{1,0:T(8,128)S(1)}, u32[]{:S(2)}, u32[]{:S(2)}) collective-permute-start(f32[128,128]{1,0:T(8,128)} %get-tuple-element.105), channel_id=1, source_target_pairs={{0,16},{2,18},{4,20},{6,22},{8,24},{10,26},{12,28},{14,30},{1,17},... | collective-permute-start | bytes 196616 | tf_op jit(solution)/shard_map/ppermute | solution.py:252
  95.8 1.9 collective-permute-start.5
  97.7 3.4 %pack_rows.6 = bf16[640,1024]{1,0:T(8,128)(2,1)} custom-call(s32[1]{0:T(128)} %bitcast.8.place_ref, s32[640,1]{1,0:T(8,128)} %sub.105.refs_0_, s32[640,1]{1,0:T(8,128)} %sub.106.refs_1_, bf16[3,256,4096]{2,1,0:T(8,128)(2,1)} %refs_2_.7, bf16[1,256,2048]{2,1,0:T(8,128)(2,1)} %copy-done.24), custom_call_target="tpu_custom_call" | custom-call | flops 13421772800 | bytes 2359296 | tf_op jit(solution)/shard_map/pack_rows/pallas_call | solution.py:50
  101.1 3.4 %pack_rows.5 = bf16[640,1024]{1,0:T(8,128)(2,1)} custom-call(s32[1]{0:T(128)} %bitcast.8.place_ref, s32[640,1]{1,0:T(8,128)} %sub.105.refs_0_, s32[640,1]{1,0:T(8,128)} %sub.106.refs_1_, bf16[3,256,4096]{2,1,0:T(8,128)(2,1)} %refs_2_.7, bf16[1,256,2048]{2,1,0:T(8,128)(2,1)} %copy-done.24), custom_call_target="tpu_custom_call" | custom-call | flops 13421772800 | bytes 2359296 | tf_op jit(solution)/shard_map/pack_rows/pallas_call | solution.py:50
  104.5 46.6 %collective-permute-done.6.refs_5_ = f32[128,128]{1,0:T(8,128)S(1)} collective-permute-done((f32[128,128]{1,0:T(8,128)}, f32[128,128]{1,0:T(8,128)S(1)}, u32[]{:S(2)}, u32[]{:S(2)}) %collective-permute-start.6) | collective-permute-done | bytes 65568 | tf_op jit(solution)/shard_map/ppermute | solution.py:252
  151.1 1.4 collective-permute-done.5.refs_4_
  152.5 6.5 %all-to-all-start.3 = ((bf16[16,40,1024]{2,1,0:T(8,128)(2,1)}), bf16[16,40,1024]{2,1,0:T(8,128)(2,1)S(1)}, u32[]{:S(2)}, u32[]{:S(2)}) async-start(bf16[16,40,1024]{2,1,0:T(8,128)(2,1)} %bitcast.33), calls=%async_computation.3 | async-start | bytes 2621440 | tf_op jit(solution)/shard_map/all_to_all | solution.py:508
  159.1 4.5 %block_update.3 = (f32[384,128]{1,0:T(8,128)}, f32[384,128]{1,0:T(8,128)}, f32[384,128]{1,0:T(8,128)}, f32[384,128]{1,0:T(8,128)}) custom-call(s32[1]{0:T(128)} %bitcast.6.place_ref, bf16[640,128]{1,0:T(8,128)(2,1)} %broadcast_in_dim.2.tail_ref, bf16[640,3072]{1,0:T(8,128)(2,1)} %bitcast.16.keys_ref.values_ref, bf16[640,3072]{1,0:T(8,128)(2,1)} %bitcast.16.keys_ref.values_ref), custom_call_target="tpu_custom_call" | custom-call | flops 251658240 | bytes 4718592 | tf_op jit(solution)/shard_map/block_update/pallas_call | solution.py:95
  164.3 1.5 collective-permute-start.10
  166.4 1.7 sum_pieces.6
  168.5 1.8 collective-permute-start.13
  170.9 1.4 collective-permute-done.9.refs_2_
  172.4 10.2 %collective-permute-done.10.refs_3_ = f32[384,128]{1,0:T(8,128)S(1)} collective-permute-done((f32[384,128]{1,0:T(8,128)}, f32[384,128]{1,0:T(8,128)S(1)}, u32[]{:S(2)}, u32[]{:S(2)}) %collective-permute-start.10) | collective-permute-done | bytes 196640 | tf_op jit(solution)/shard_map/ppermute | solution.py:222
  183.2 2.4 sum_pieces.5
  185.7 2.8 %collective-permute-start.15 = (f32[384,128]{1,0:T(8,128)}, f32[384,128]{1,0:T(8,128)S(1)}, u32[]{:S(2)}, u32[]{:S(2)}) collective-permute-start(f32[384,128]{1,0:T(8,128)} %get-tuple-element.153), channel_id=1, source_target_pairs={{0,16},{2,18},{4,20},{6,22},{8,24},{10,26},{12,28},{14,30},{1,17},... | collective-permute-start | bytes 589832 | tf_op jit(solution)/shard_map/ppermute | solution.py:252
  188.5 2.1 collective-permute-start.14
  190.7 7.4 %all-to-all-start.2 = ((bf16[16,40,1024]{2,1,0:T(8,128)(2,1)}), bf16[16,40,1024]{2,1,0:T(8,128)(2,1)S(1)}, u32[]{:S(2)}, u32[]{:S(2)}) async-start(bf16[16,40,1024]{2,1,0:T(8,128)(2,1)} %bitcast.17), calls=%async_computation.2 | async-start | bytes 2621440 | tf_op jit(solution)/shard_map/all_to_all | solution.py:508
  198.1 5.8 %unpack_keys_values.3 = (bf16[512,2048]{1,0:T(8,128)(2,1)}, bf16[512,2048]{1,0:T(8,128)(2,1)}) custom-call(bf16[512,640]{1,0:T(8,128)(2,1)} %get-tuple-element.97.order_ref, bf16[640,3072]{1,0:T(8,128)(2,1)} %bitcast.16.keys_ref.values_ref, bf16[640,3072]{1,0:T(8,128)(2,1)} %bitcast.16.keys_ref.values_ref, ...), custom_call_target="tpu_custom_call", output_to_operand_aliasing={{0}: (3, {}), {1}: (4, {})} | custom-call | flops 2013265920 | bytes 7077888 | tf_op jit(solution)/shard_map/unpack_keys_values/pallas_call | solution.py:165
  205.2 2.5 %sum_pieces.7 = (f32[384,128]{1,0:T(8,128)}, f32[384,128]{1,0:T(8,128)}, f32[384,128]{1,0:T(8,128)}, f32[384,128]{1,0:T(8,128)}) custom-call(s32[4,6]{1,0:T(4,128)} %convert_element_type.48.take_ref, f32[384,128]{1,0:T(8,128)} %get-tuple-element.149.refs_0_, f32[384,128]{1,0:T(8,128)} %get-tuple-element.150.refs_1_, f32[384,128]{1,0:T(8,128)} %get-tuple-element.151.refs_2_, ...), custom_call_target="tpu_custom_call" | custom-call | flops 1179648 | bytes 1966080 | tf_op jit(solution)/shard_map/sum_pieces/pallas_call | solution.py:200
  207.7 6.4 %collective-permute-start.16 = (f32[384,128]{1,0:T(8,128)}, f32[384,128]{1,0:T(8,128)S(1)}, u32[]{:S(2)}, u32[]{:S(2)}) collective-permute-start(f32[384,128]{1,0:T(8,128)} %get-tuple-element.155), channel_id=1, source_target_pairs={{0,2},{2,0},{4,6},{6,4},{8,10},{10,8},{12,14},{14,12},{16,18},{18,... | collective-permute-start | bytes 589832 | tf_op jit(solution)/shard_map/ppermute | solution.py:222
  214.2 1.7 collective-permute-start.18
  215.8 5.9 %attend_locally.1 = (bf16[512,1024]{1,0:T(8,128)(2,1)}, f32[512,1024]{1,0:T(8,128)}) custom-call(bf16[512,640]{1,0:T(8,128)(2,1)} %get-tuple-element.97.order_ref, bf16[512,512]{1,0:T(8,128)(2,1)} %get-tuple-element.98.causal_ref, bf16[512,128]{1,0:T(8,128)(2,1)} %get-tuple-element.99.carried_ref, bf16[640,1024]{1,0:T(8,128)(2,1)} %bitcast.32, ...), custom_call_target="tpu_custom_call" | custom-call | flops 25300041728 | bytes 6553600 | tf_op jit(solution)/shard_map/attend_locally/pallas_call | solution.py:413
  221.7 2.8 %collective-permute-done.17.refs_6_ = f32[384,128]{1,0:T(8,128)S(1)} collective-permute-done((f32[384,128]{1,0:T(8,128)}, f32[384,128]{1,0:T(8,128)S(1)}, u32[]{:S(2)}, u32[]{:S(2)}) %collective-permute-start.17) | collective-permute-done | bytes 196640 | tf_op jit(solution)/shard_map/ppermute | solution.py:222
  224.5 6.0 %collective-permute-done.18.refs_7_ = f32[384,128]{1,0:T(8,128)S(1)} collective-permute-done((f32[384,128]{1,0:T(8,128)}, f32[384,128]{1,0:T(8,128)S(1)}, u32[]{:S(2)}, u32[]{:S(2)}) %collective-permute-start.18) | collective-permute-done | bytes 196640 | tf_op jit(solution)/shard_map/ppermute | solution.py:222
  231.2 2.5 %assemble_states.1.states_ref = bf16[4096,128]{1,0:T(8,128)(2,1)} custom-call(s32[1]{0:T(128)} %bitcast.6.place_ref, f32[128,128]{1,0:T(8,128)} %get-tuple-element.145.refs_0_, f32[128,128]{1,0:T(8,128)} %copy-done.13, f32[128,128]{1,0:T(8,128)} %copy-done.14, f32[128,128]{1,0:T(8,128)} %copy-done.15, f32[384,128]{1,0:T(8,128)} %get-tuple-element.154.refs_4_, ...), custom_call_target="tpu_custom_call" | custom-call | flops 2097152 | bytes 2097152 | tf_op jit(solution)/shard_map/assemble_states/pallas_call | solution.py:295
  233.7 3.8 %finish.1.refs_0_ = bf16[512,2048]{1,0:T(8,128)(2,1)} custom-call(f32[1,2048]{1,0:T(1,128)} %bitcast.38, bf16[512,1024]{1,0:T(8,128)(2,1)} %get-tuple-element.159.query_ref, f32[512,1024]{1,0:T(8,128)} %get-tuple-element.160.local_ref, bf16[4096,128]{1,0:T(8,128)(2,1)} %assemble_states.1.states_ref), custom_call_target="tpu_custom_call" | custom-call | flops 536870912 | bytes 4194304 | tf_op jit(solution)/shard_map/finish/pallas_call | solution.py:452
  237.4 1.1 copy-done.3
  238.5 7.1 %attend.1 = bf16[512,2048]{1,0:T(8,128)(2,1)} custom-call(bf16[512,640]{1,0:T(8,128)(2,1)} %get-tuple-element.97.order_ref, bf16[512,512]{1,0:T(8,128)(2,1)} %get-tuple-element.98.causal_ref, bf16[512,128]{1,0:T(8,128)(2,1)} %get-tuple-element.99.carried_ref, f32[1,2048]{1,0:T(1,128)} %bitcast.39, ...), custom_call_target="tpu_custom_call", output_to_operand_aliasing={{}: (8, {})} | custom-call | flops 33084669952 | bytes 5505024 | tf_op jit(solution)/shard_map/attend/pallas_call | solution.py:359
  (110 shorter events, 17.9 us)
Async XLA Ops:
  1.3 3.7 %copy-start.22 = (s32[1,16,40]{2,1,0:T(8,128)S(1)}, s32[1,16,40]{2,1,0:T(8,128)}, u32[]{:S(2)}) copy-start(s32[1,16,40]{2,1,0:T(8,128)} %param.6) | copy-start | bytes 7684
  1.3 12.9 %collective-permute-start.1 = (bf16[2,256,512]{2,1,0:T(8,128)(2,1)S(1)}, bf16[2,256,512]{2,1,0:T(8,128)(2,1)S(1)}, u32[]{:S(2)}, u32[]{:S(2)}) collective-permute-start(bf16[2,256,512]{2,1,0:T(8,128)(2,1)S(1)} %slice_select_fusion.2), channel_id=1, source_target_pairs={{0,1},{1,0},{2,3},{3,2},{4,5},{5,4},{6,7},{7,6},{8,9},{9,8},{10,11... | collective-permute-start | bytes 1572872 | tf_op jit(solution)/shard_map/ppermute | solution.py:481
  4.6 43.3 %collective-permute-start.7 = (bf16[2,256,1536]{2,1,0:T(8,128)(2,1)S(1)}, bf16[2,256,1536]{2,1,0:T(8,128)(2,1)}, u32[]{:S(2)}, u32[]{:S(2)}) collective-permute-start(bf16[2,256,1536]{2,1,0:T(8,128)(2,1)S(1)} %slice_select_fusion), channel_id=1, source_target_pairs={{0,1},{1,0},{2,3},{3,2},{4,5},{5,4},{6,7},{7,6},{8,9},{9,8},{10,11... | collective-permute-start | bytes 4718600 | tf_op jit(solution)/shard_map/ppermute | solution.py:481
  14.1 0.8 copy-start.25
  18.3 39.1 %all-to-all-start = ((bf16[16,40,1024]{2,1,0:T(8,128)(2,1)}), bf16[16,40,1024]{2,1,0:T(8,128)(2,1)S(1)}, u32[]{:S(2)}, u32[]{:S(2)}) async-start(bf16[16,40,1024]{2,1,0:T(8,128)(2,1)} %bitcast.35), calls=%async_computation | async-start | bytes 2621440 | tf_op jit(solution)/shard_map/all_to_all | solution.py:508
  57.4 1.1 copy-start
  58.5 94.1 %all-to-all-start.1 = ((bf16[16,40,3072]{2,1,0:T(8,128)(2,1)}), bf16[16,40,3072]{2,1,0:T(8,128)(2,1)}, u32[]{:S(2)}, u32[]{:S(2)}) async-start(bf16[16,40,3072]{2,1,0:T(8,128)(2,1)} %bitcast.31), calls=%async_computation.1 | async-start | bytes 7864320 | tf_op jit(solution)/shard_map/all_to_all | solution.py:508
  63.7 3.0 %copy-start.23 = (s32[4]{0:T(128)S(1)}, s32[4]{0:T(128)}, u32[]{:S(2)}) copy-start(s32[4]{0:T(128)} %param.8) | copy-start | bytes 52
  63.7 4.5 %copy-start.12 = (s32[1,16,40]{2,1,0:T(8,128)S(1)}, s32[1,16,40]{2,1,0:T(8,128)}, u32[]{:S(2)}) copy-start(s32[1,16,40]{2,1,0:T(8,128)} %param.7) | copy-start | bytes 7684
  65.4 27.4 %collective-permute-start = (bf16[1,256,2048]{2,1,0:T(8,128)(2,1)S(1)}, bf16[1,256,2048]{2,1,0:T(8,128)(2,1)S(1)}, u32[]{:S(2)}, u32[]{:S(2)}) collective-permute-start(bf16[1,256,2048]{2,1,0:T(8,128)(2,1)S(1)} %slice_select_fusion.1), channel_id=1, source_target_pairs={{0,1},{1,0},{2,3},{3,2},{4,5},{5,4},{6,7},{7,6},{8,9},{9,8},{10,11... | collective-permute-start | bytes 3145736 | tf_op jit(solution)/shard_map/ppermute | solution.py:481
  70.6 11.3 %copy-start.21 = (s32[512]{0:T(512)}, s32[512]{0:T(512)S(1)}, u32[]{:S(2)}) copy-start(s32[512]{0:T(512)S(1)} %broadcast_add_fusion.1) | copy-start | bytes 6148
  70.7 11.2 %copy-start.1 = (s32[512,1]{1,0:T(8,128)}, s32[512,1]{1,0:T(8,128)S(1)}, u32[]{:S(2)}) copy-start(s32[512,1]{1,0:T(8,128)S(1)} %copy.33.seg_col_ref) | copy-start | bytes 6148
  78.8 8.7 %collective-permute-start.2 = (f32[128,128]{1,0:T(8,128)}, f32[128,128]{1,0:T(8,128)S(1)}, u32[]{:S(2)}, u32[]{:S(2)}) collective-permute-start(f32[128,128]{1,0:T(8,128)} %get-tuple-element.84), channel_id=1, source_target_pairs={{0,2},{2,0},{4,6},{6,4},{8,10},{10,8},{12,14},{14,12},{16,18},{18,... | collective-permute-start | bytes 196616 | tf_op jit(solution)/shard_map/ppermute | solution.py:222
  79.5 9.1 %collective-permute-start.3 = (f32[128,128]{1,0:T(8,128)}, f32[128,128]{1,0:T(8,128)S(1)}, u32[]{:S(2)}, u32[]{:S(2)}) collective-permute-start(f32[128,128]{1,0:T(8,128)} %get-tuple-element.85), channel_id=1, source_target_pairs={{0,4},{2,6},{4,0},{6,2},{8,12},{10,14},{12,8},{14,10},{16,20},{18,... | collective-permute-start | bytes 196616 | tf_op jit(solution)/shard_map/ppermute | solution.py:222
  79.7 10.7 %collective-permute-start.4 = (f32[128,128]{1,0:T(8,128)}, f32[128,128]{1,0:T(8,128)S(1)}, u32[]{:S(2)}, u32[]{:S(2)}) collective-permute-start(f32[128,128]{1,0:T(8,128)} %get-tuple-element.86), channel_id=1, source_target_pairs={{0,6},{2,4},{4,2},{6,0},{8,14},{10,12},{12,10},{14,8},{16,22},{18,... | collective-permute-start | bytes 196616 | tf_op jit(solution)/shard_map/ppermute | solution.py:222
  87.5 2.9 %copy-start.18 = (f32[128,128]{1,0:T(8,128)}, f32[128,128]{1,0:T(8,128)S(1)}, u32[]{:S(2)}) copy-start(f32[128,128]{1,0:T(8,128)S(1)} %collective-permute-done.2.refs_1_) | copy-start | bytes 196612
  88.5 1.9 copy-start.19
  92.8 4.9 %copy-start.24 = (bf16[1,256,2048]{2,1,0:T(8,128)(2,1)}, bf16[1,256,2048]{2,1,0:T(8,128)(2,1)S(1)}, u32[]{:S(2)}) copy-start(bf16[1,256,2048]{2,1,0:T(8,128)(2,1)S(1)} %collective-permute-done.refs_3_) | copy-start | bytes 3145732
  92.8 58.4 %collective-permute-start.6 = (f32[128,128]{1,0:T(8,128)}, f32[128,128]{1,0:T(8,128)S(1)}, u32[]{:S(2)}, u32[]{:S(2)}) collective-permute-start(f32[128,128]{1,0:T(8,128)} %get-tuple-element.105), channel_id=1, source_target_pairs={{0,16},{2,18},{4,20},{6,22},{8,24},{10,26},{12,28},{14,30},{1,17},... | collective-permute-start | bytes 196616 | tf_op jit(solution)/shard_map/ppermute | solution.py:252
  95.8 56.8 %collective-permute-start.5 = (f32[128,128]{1,0:T(8,128)}, f32[128,128]{1,0:T(8,128)S(1)}, u32[]{:S(2)}, u32[]{:S(2)}) collective-permute-start(f32[128,128]{1,0:T(8,128)} %get-tuple-element.105), channel_id=1, source_target_pairs={{0,8},{2,10},{4,12},{6,14},{8,16},{10,18},{12,20},{14,22},{16,24},... | collective-permute-start | bytes 196616 | tf_op jit(solution)/shard_map/ppermute | solution.py:252
  151.1 12.5 %copy-start.16 = (f32[128,128]{1,0:T(8,128)}, f32[128,128]{1,0:T(8,128)S(1)}, u32[]{:S(2)}) copy-start(f32[128,128]{1,0:T(8,128)S(1)} %collective-permute-done.6.refs_5_) | copy-start | bytes 196612
  152.5 11.1 %copy-start.17 = (f32[128,128]{1,0:T(8,128)}, f32[128,128]{1,0:T(8,128)S(1)}, u32[]{:S(2)}) copy-start(f32[128,128]{1,0:T(8,128)S(1)} %collective-permute-done.5.refs_4_) | copy-start | bytes 196612
  152.5 38.1 %all-to-all-start.3 = ((bf16[16,40,1024]{2,1,0:T(8,128)(2,1)}), bf16[16,40,1024]{2,1,0:T(8,128)(2,1)S(1)}, u32[]{:S(2)}, u32[]{:S(2)}) async-start(bf16[16,40,1024]{2,1,0:T(8,128)(2,1)} %bitcast.33), calls=%async_computation.3 | async-start | bytes 2621440 | tf_op jit(solution)/shard_map/all_to_all | solution.py:508
  163.6 4.9 %collective-permute-start.8 = (f32[384,128]{1,0:T(8,128)}, f32[384,128]{1,0:T(8,128)S(1)}, u32[]{:S(2)}, u32[]{:S(2)}) collective-permute-start(f32[384,128]{1,0:T(8,128)} %get-tuple-element.120), channel_id=1, source_target_pairs={{0,2},{2,0},{4,6},{6,4},{8,10},{10,8},{12,14},{14,12},{16,18},{18,... | collective-permute-start | bytes 589832 | tf_op jit(solution)/shard_map/ppermute | solution.py:222
  164.0 8.3 %collective-permute-start.9 = (f32[384,128]{1,0:T(8,128)}, f32[384,128]{1,0:T(8,128)S(1)}, u32[]{:S(2)}, u32[]{:S(2)}) collective-permute-start(f32[384,128]{1,0:T(8,128)} %get-tuple-element.121), channel_id=1, source_target_pairs={{0,4},{2,6},{4,0},{6,2},{8,12},{10,14},{12,8},{14,10},{16,20},{18,... | collective-permute-start | bytes 589832 | tf_op jit(solution)/shard_map/ppermute | solution.py:222
  164.3 18.2 %collective-permute-start.10 = (f32[384,128]{1,0:T(8,128)}, f32[384,128]{1,0:T(8,128)S(1)}, u32[]{:S(2)}, u32[]{:S(2)}) collective-permute-start(f32[384,128]{1,0:T(8,128)} %get-tuple-element.122), channel_id=1, source_target_pairs={{0,6},{2,4},{4,2},{6,0},{8,14},{10,12},{12,10},{14,8},{16,22},{18,... | collective-permute-start | bytes 589832 | tf_op jit(solution)/shard_map/ppermute | solution.py:222
  168.2 17.5 %collective-permute-start.11 = (f32[128,128]{1,0:T(8,128)}, f32[128,128]{1,0:T(8,128)S(1)}, u32[]{:S(2)}, u32[]{:S(2)}) collective-permute-start(f32[128,128]{1,0:T(8,128)} %get-tuple-element.136), channel_id=1, source_target_pairs={{0,2},{2,0},{4,6},{6,4},{8,10},{10,8},{12,14},{14,12},{16,18},{18,... | collective-permute-start | bytes 196616 | tf_op jit(solution)/shard_map/ppermute | solution.py:222
  168.2 17.4 %collective-permute-start.12 = (f32[128,128]{1,0:T(8,128)}, f32[128,128]{1,0:T(8,128)S(1)}, u32[]{:S(2)}, u32[]{:S(2)}) collective-permute-start(f32[128,128]{1,0:T(8,128)} %get-tuple-element.137), channel_id=1, source_target_pairs={{0,4},{2,6},{4,0},{6,2},{8,12},{10,14},{12,8},{14,10},{16,20},{18,... | collective-permute-start | bytes 196616 | tf_op jit(solution)/shard_map/ppermute | solution.py:222
  168.5 14.0 %copy-start.9 = (f32[384,128]{1,0:T(8,128)}, f32[384,128]{1,0:T(8,128)S(1)}, u32[]{:S(2)}) copy-start(f32[384,128]{1,0:T(8,128)S(1)} %collective-permute-done.8.refs_1_) | copy-start | bytes 589828
  168.5 17.2 %collective-permute-start.13 = (f32[128,128]{1,0:T(8,128)}, f32[128,128]{1,0:T(8,128)S(1)}, u32[]{:S(2)}, u32[]{:S(2)}) collective-permute-start(f32[128,128]{1,0:T(8,128)} %get-tuple-element.138), channel_id=1, source_target_pairs={{0,6},{2,4},{4,2},{6,0},{8,14},{10,12},{12,10},{14,8},{16,22},{18,... | collective-permute-start | bytes 196616 | tf_op jit(solution)/shard_map/ppermute | solution.py:222
  172.4 10.2 %copy-start.10 = (f32[384,128]{1,0:T(8,128)}, f32[384,128]{1,0:T(8,128)S(1)}, u32[]{:S(2)}) copy-start(f32[384,128]{1,0:T(8,128)S(1)} %collective-permute-done.9.refs_2_) | copy-start | bytes 589828
  182.6 0.7 copy-start.11
  185.7 18.2 %copy-start.13 = (f32[128,128]{1,0:T(8,128)}, f32[128,128]{1,0:T(8,128)S(1)}, u32[]{:S(2)}) copy-start(f32[128,128]{1,0:T(8,128)S(1)} %collective-permute-done.11.refs_1_) | copy-start | bytes 196612
  185.7 18.2 %copy-start.14 = (f32[128,128]{1,0:T(8,128)}, f32[128,128]{1,0:T(8,128)S(1)}, u32[]{:S(2)}) copy-start(f32[128,128]{1,0:T(8,128)S(1)} %collective-permute-done.12.refs_2_) | copy-start | bytes 196612
  185.7 18.2 %copy-start.15 = (f32[128,128]{1,0:T(8,128)}, f32[128,128]{1,0:T(8,128)S(1)}, u32[]{:S(2)}) copy-start(f32[128,128]{1,0:T(8,128)S(1)} %collective-permute-done.13.refs_3_) | copy-start | bytes 196612
  185.7 18.2 %collective-permute-start.15 = (f32[384,128]{1,0:T(8,128)}, f32[384,128]{1,0:T(8,128)S(1)}, u32[]{:S(2)}, u32[]{:S(2)}) collective-permute-start(f32[384,128]{1,0:T(8,128)} %get-tuple-element.153), channel_id=1, source_target_pairs={{0,16},{2,18},{4,20},{6,22},{8,24},{10,26},{12,28},{14,30},{1,17},... | collective-permute-start | bytes 589832 | tf_op jit(solution)/shard_map/ppermute | solution.py:252
  188.5 15.4 %collective-permute-start.14 = (f32[384,128]{1,0:T(8,128)}, f32[384,128]{1,0:T(8,128)S(1)}, u32[]{:S(2)}, u32[]{:S(2)}) collective-permute-start(f32[384,128]{1,0:T(8,128)} %get-tuple-element.153), channel_id=1, source_target_pairs={{0,8},{2,10},{4,12},{6,14},{8,16},{10,18},{12,20},{14,22},{16,24},... | collective-permute-start | bytes 589832 | tf_op jit(solution)/shard_map/ppermute | solution.py:252
  190.6 13.2 %copy-start.2 = (bf16[16,40,1024]{2,1,0:T(8,128)(2,1)}, bf16[16,40,1024]{2,1,0:T(8,128)(2,1)S(1)}, u32[]{:S(2)}) copy-start(bf16[16,40,1024]{2,1,0:T(8,128)(2,1)S(1)} %all-to-all-done.3) | copy-start | bytes 3932164
  190.7 46.8 %all-to-all-start.2 = ((bf16[16,40,1024]{2,1,0:T(8,128)(2,1)}), bf16[16,40,1024]{2,1,0:T(8,128)(2,1)S(1)}, u32[]{:S(2)}, u32[]{:S(2)}) async-start(bf16[16,40,1024]{2,1,0:T(8,128)(2,1)} %bitcast.17), calls=%async_computation.2 | async-start | bytes 2621440 | tf_op jit(solution)/shard_map/all_to_all | solution.py:508
  203.9 0.7 copy-start.4
  204.6 0.7 copy-start.5
  207.7 14.0 %collective-permute-start.16 = (f32[384,128]{1,0:T(8,128)}, f32[384,128]{1,0:T(8,128)S(1)}, u32[]{:S(2)}, u32[]{:S(2)}) collective-permute-start(f32[384,128]{1,0:T(8,128)} %get-tuple-element.155), channel_id=1, source_target_pairs={{0,2},{2,0},{4,6},{6,4},{8,10},{10,8},{12,14},{14,12},{16,18},{18,... | collective-permute-start | bytes 589832 | tf_op jit(solution)/shard_map/ppermute | solution.py:222
  214.2 10.4 %collective-permute-start.17 = (f32[384,128]{1,0:T(8,128)}, f32[384,128]{1,0:T(8,128)S(1)}, u32[]{:S(2)}, u32[]{:S(2)}) collective-permute-start(f32[384,128]{1,0:T(8,128)} %get-tuple-element.156), channel_id=1, source_target_pairs={{0,4},{2,6},{4,0},{6,2},{8,12},{10,14},{12,8},{14,10},{16,20},{18,... | collective-permute-start | bytes 589832 | tf_op jit(solution)/shard_map/ppermute | solution.py:222
  214.2 16.3 %collective-permute-start.18 = (f32[384,128]{1,0:T(8,128)}, f32[384,128]{1,0:T(8,128)S(1)}, u32[]{:S(2)}, u32[]{:S(2)}) collective-permute-start(f32[384,128]{1,0:T(8,128)} %get-tuple-element.157), channel_id=1, source_target_pairs={{0,6},{2,4},{4,2},{6,0},{8,14},{10,12},{12,10},{14,8},{16,22},{18,... | collective-permute-start | bytes 589832 | tf_op jit(solution)/shard_map/ppermute | solution.py:222
  221.7 8.8 %copy-start.6 = (f32[384,128]{1,0:T(8,128)}, f32[384,128]{1,0:T(8,128)S(1)}, u32[]{:S(2)}) copy-start(f32[384,128]{1,0:T(8,128)S(1)} %collective-permute-done.16.refs_5_) | copy-start | bytes 589828
  224.5 6.0 %copy-start.7 = (f32[384,128]{1,0:T(8,128)}, f32[384,128]{1,0:T(8,128)S(1)}, u32[]{:S(2)}) copy-start(f32[384,128]{1,0:T(8,128)S(1)} %collective-permute-done.17.refs_6_) | copy-start | bytes 589828
  230.5 0.7 copy-start.8
  237.4 1.1 copy-start.3
  (1 other events, 0.6 us)

commit v10 on v9

--- a/solution.py
+++ b/solution.py
@@ -189,17 +189,19 @@
     for number, out in enumerate(outs):
         total = jnp.zeros(out.shape, jnp.float32)
         for piece in range(count):
-            total = total + jnp.where(take_ref[number, piece] != 0, pieces[piece][...], 0.0)
-        out[...] = total
-
-
-def sum_pieces(take, pieces):
+            value = pieces[piece][...].astype(jnp.float32)
+            total = total + jnp.where(take_ref[number, piece] != 0, value, 0.0)
+        out[...] = total.astype(out.dtype)
+
+
+def sum_pieces(take, pieces, last=jnp.float32):
     rows = pieces[0].shape[0]
     count = take.shape[0]
     whole = pl.BlockSpec(memory_space=pltpu.VMEM)
     return pl.pallas_call(
         sum_kernel,
-        out_shape=(jax.ShapeDtypeStruct((rows, HEAD_DIM), jnp.float32),) * count,
+        out_shape=(jax.ShapeDtypeStruct((rows, HEAD_DIM), jnp.float32),) * (count - 1)
+        + (jax.ShapeDtypeStruct((rows, HEAD_DIM), last),),
         in_specs=[pl.BlockSpec(memory_space=pltpu.SMEM)] + [whole] * len(pieces),
         out_specs=(whole,) * count,
         cost_estimate=pl.CostEstimate(
@@ -238,8 +240,9 @@
     return within, jnp.concatenate([own, across], axis=1)
 
 
-def carry_within(shares, within):
-    return sum_pieces(within, [shares[0]] + [swap_places(shares[k], k) for k in range(1, len(shares))])
+def carry_within(shares, within, total_type):
+    pieces = [shares[0]] + [swap_places(shares[k], k) for k in range(1, len(shares))]
+    return sum_pieces(within, pieces, total_type)
 
 
 def pass_totals(sums):
@@ -541,7 +544,7 @@
     )
     arrived_next = to_owners(outgoing)
     within, across = carry_tables(last_segment)
-    sums = carry_within(block_update(arrived, tail_slots), within)
+    sums = carry_within(block_update(arrived, tail_slots), within, jnp.float32)
     tables = block_tables(land_row, segment, carried_mask)
     filled = unpack_keys_values(arrived, tables[0], 0, columns, ())
     incoming = swap_heads(qkv, QUERY, 1, 0, columns)
@@ -560,7 +563,7 @@
     query = to_owners(outgoing)
     shares, pieces = lax.optimization_barrier((block_update(arrived_next, tail_slots), pieces))
     states = hand_back(pieces, across)
-    sums = carry_within(shares, within)
+    sums = carry_within(shares, within, jnp.bfloat16)
     outgoing_next, sums, states, arrived_next = lax.optimization_barrier(
         (outgoing_next, sums, states, arrived_next)
     )

time: 247 us -> 241 us (0.976)
  starting transfers between devices: 55.2 us -> 49.3 us
    ppermute x12, starting transfers between devices: 14.8 us -> 8.85 us  [swap_places(): return lax.ppermute(value, 'seq', [(i, i ^ k) for i in range(seq_count)])]
  transfers between devices with their start and end apart: 23 -> 23, of which waited for: 11 -> 11; matrix products, arithmetic and copies ran while one was open for 6% -> 6% of each run, Pallas kernels for 23% -> 24%
where the time goes in v10:
time: 241 us; the launch traced here: 239 us
  waiting for transfers between devices  102 us (42%)
  Pallas kernels  64.4 us (27%)
  starting transfers between devices  49.3 us (20%)
  local copies, waits for them, and re-layouts  12.4 us (5%)
  other arithmetic  10.2 us (4%)
    ppermute x4, waiting for transfers between devices, pass_totals(): lax.ppermute(sums[near], 'seq', [(i, i + step) for i in range(seq_count -...  48 us
    ppermute x3, waiting for transfers between devices, swap_heads(): return lax.ppermute(outgoing, 'head', [(0, 1), (1, 0)])  28.5 us
    all_to_all x4, starting transfers between devices, to_owners(): lax.all_to_all(outgoing, 'seq', split_axis=0, concat_axis=0, tiled=True)  27.7 us
    ppermute x12, waiting for transfers between devices, swap_places(): return lax.ppermute(value, 'seq', [(i, i ^ k) for i in range(seq_count)])  23.2 us
    pallas_call x4, Pallas kernels, pack_rows(): pl.pallas_call(pack_kernel, out_shape=jax.ShapeDtypeStruct((slots, planes...  17.4 us
    ppermute x4, starting transfers between devices, pass_totals(): lax.ppermute(sums[near], 'seq', [(i, i + step) for i in range(seq_count -...  9.86 us
    pallas_call x2, Pallas kernels, unpack_keys_values(): pl.pallas_call(unpack_kernel, out_shape=(packed, packed), grid=(blocks,),...  9.08 us
    ppermute x12, starting transfers between devices, swap_places(): return lax.ppermute(value, 'seq', [(i, i ^ k) for i in range(seq_count)])  8.85 us
  transfers between devices with their start and end apart: 23, of which 11 were waited for; matrix products, arithmetic and copies ran while one was open for 6% of the time, Pallas kernels for 24%

profile of v10, /device:TPU:11, one launch (start us, length us, event | category | flops | bytes accessed | tf_op | source)
XLA Modules:
  0.0 239.3 jit_solution(17220825633330090864)
XLA Ops:
  0.0 1.3 slice_select_fusion.2
  1.3 1.3 collective-permute-start.1
  2.6 2.0 slice_select_fusion
  4.9 0.9 sub.106.refs_1_
  5.8 0.9 sub.105.refs_0_
  6.7 7.4 %collective-permute-done.1.refs_3_ = bf16[2,256,512]{2,1,0:T(8,128)(2,1)S(1)} collective-permute-done((bf16[2,256,512]{2,1,0:T(8,128)(2,1)S(1)}, bf16[2,256,512]{2,1,0:T(8,128)(2,1)S(1)}, u32[]{:S(2)}, u32[]{:S(2)}) %collective-permute-start.1) | collective-permute-done | bytes 524320 | tf_op jit(solution)/shard_map/ppermute | solution.py:484
  14.9 3.4 %pack_rows.4 = bf16[640,1024]{1,0:T(8,128)(2,1)} custom-call(s32[1]{0:T(128)} %bitcast.8.place_ref, s32[640,1]{1,0:T(8,128)} %sub.105.refs_0_, s32[640,1]{1,0:T(8,128)} %sub.106.refs_1_, bf16[3,256,4096]{2,1,0:T(8,128)(2,1)} %refs_2_.7, bf16[2,256,512]{2,1,0:T(8,128)(2,1)} %copy-done.25), custom_call_target="tpu_custom_call" | custom-call | flops 13421772800 | bytes 2359296 | tf_op jit(solution)/shard_map/pack_rows/pallas_call | solution.py:50
  18.3 8.6 %all-to-all-start = ((bf16[16,40,1024]{2,1,0:T(8,128)(2,1)}), bf16[16,40,1024]{2,1,0:T(8,128)(2,1)S(1)}, u32[]{:S(2)}, u32[]{:S(2)}) async-start(bf16[16,40,1024]{2,1,0:T(8,128)(2,1)} %bitcast.35), calls=%async_computation | async-start | bytes 2621440 | tf_op jit(solution)/shard_map/all_to_all | solution.py:511
  26.9 21.1 %collective-permute-done.7.refs_3_ = bf16[2,256,1536]{2,1,0:T(8,128)(2,1)} collective-permute-done((bf16[2,256,1536]{2,1,0:T(8,128)(2,1)S(1)}, bf16[2,256,1536]{2,1,0:T(8,128)(2,1)}, u32[]{:S(2)}, u32[]{:S(2)}) %collective-permute-start.7) | collective-permute-done | bytes 1572896 | tf_op jit(solution)/shard_map/ppermute | solution.py:484
  47.9 7.2 %pack_rows.7 = bf16[640,3072]{1,0:T(8,128)(2,1)} custom-call(s32[1]{0:T(128)} %bitcast.8.place_ref, s32[640,1]{1,0:T(8,128)} %sub.105.refs_0_, s32[640,1]{1,0:T(8,128)} %sub.106.refs_1_, bf16[3,256,4096]{2,1,0:T(8,128)(2,1)} %refs_2_.7, bf16[2,256,1536]{2,1,0:T(8,128)(2,1)} %collective-permute-done.7.refs_3_), custom_call_target="tpu_custom_call" | custom-call | flops 40265318400 | bytes 7077888 | tf_op jit(solution)/shard_map/pack_rows/pallas_call | solution.py:50
  55.2 2.2 all-to-all-done
  57.4 1.1 copy-done
  58.5 5.2 %all-to-all-start.1 = ((bf16[16,40,3072]{2,1,0:T(8,128)(2,1)}), bf16[16,40,3072]{2,1,0:T(8,128)(2,1)}, u32[]{:S(2)}, u32[]{:S(2)}) async-start(bf16[16,40,3072]{2,1,0:T(8,128)(2,1)} %bitcast.31), calls=%async_computation.1 | async-start | bytes 7864320 | tf_op jit(solution)/shard_map/all_to_all | solution.py:511
  63.7 1.7 slice_select_fusion.1
  65.4 1.3 collective-permute-start
  75.1 3.7 %block_update.2 = (f32[128,128]{1,0:T(8,128)}, f32[128,128]{1,0:T(8,128)}, f32[128,128]{1,0:T(8,128)}, f32[128,128]{1,0:T(8,128)}) custom-call(s32[1]{0:T(128)} %bitcast.6.place_ref, bf16[640,128]{1,0:T(8,128)(2,1)} %broadcast_in_dim.2.tail_ref, bf16[640,1024]{1,0:T(8,128)(2,1)} %bitcast.27, bf16[640,1024]{1,0:T(8,128)(2,1)} %bitcast.28), custom_call_target="tpu_custom_call" | custom-call | flops 83886080 | bytes 1572864 | tf_op jit(solution)/shard_map/block_update/pallas_call | solution.py:95
  79.7 1.4 collective-permute-start.4
  81.9 2.4 block_tables.1
  84.3 3.3 %unpack_keys_values.2 = (bf16[512,2048]{1,0:T(8,128)(2,1)}, bf16[512,2048]{1,0:T(8,128)(2,1)}) custom-call(bf16[512,640]{1,0:T(8,128)(2,1)} %get-tuple-element.97.order_ref, bf16[640,1024]{1,0:T(8,128)(2,1)} %bitcast.29, bf16[640,1024]{1,0:T(8,128)(2,1)} %bitcast.30), custom_call_target="tpu_custom_call" | custom-call | flops 671088640 | bytes 2359296 | tf_op jit(solution)/shard_map/unpack_keys_values/pallas_call | solution.py:165
  87.5 1.0 collective-permute-done.3.refs_2_
  88.5 1.9 collective-permute-done.4.refs_3_
  91.1 1.7 sum_pieces.4
  92.8 3.0 %collective-permute-start.6 = (f32[128,128]{1,0:T(8,128)}, f32[128,128]{1,0:T(8,128)S(1)}, u32[]{:S(2)}, u32[]{:S(2)}) collective-permute-start(f32[128,128]{1,0:T(8,128)} %get-tuple-element.105), channel_id=1, source_target_pairs={{0,16},{2,18},{4,20},{6,22},{8,24},{10,26},{12,28},{14,30},{1,17},... | collective-permute-start | bytes 196616 | tf_op jit(solution)/shard_map/ppermute | solution.py:255
  95.8 1.9 collective-permute-start.5
  97.7 3.4 %pack_rows.6 = bf16[640,1024]{1,0:T(8,128)(2,1)} custom-call(s32[1]{0:T(128)} %bitcast.8.place_ref, s32[640,1]{1,0:T(8,128)} %sub.105.refs_0_, s32[640,1]{1,0:T(8,128)} %sub.106.refs_1_, bf16[3,256,4096]{2,1,0:T(8,128)(2,1)} %refs_2_.7, bf16[1,256,2048]{2,1,0:T(8,128)(2,1)} %copy-done.24), custom_call_target="tpu_custom_call" | custom-call | flops 13421772800 | bytes 2359296 | tf_op jit(solution)/shard_map/pack_rows/pallas_call | solution.py:50
  101.1 3.4 %pack_rows.5 = bf16[640,1024]{1,0:T(8,128)(2,1)} custom-call(s32[1]{0:T(128)} %bitcast.8.place_ref, s32[640,1]{1,0:T(8,128)} %sub.105.refs_0_, s32[640,1]{1,0:T(8,128)} %sub.106.refs_1_, bf16[3,256,4096]{2,1,0:T(8,128)(2,1)} %refs_2_.7, bf16[1,256,2048]{2,1,0:T(8,128)(2,1)} %copy-done.24), custom_call_target="tpu_custom_call" | custom-call | flops 13421772800 | bytes 2359296 | tf_op jit(solution)/shard_map/pack_rows/pallas_call | solution.py:50
  104.5 46.6 %collective-permute-done.6.refs_5_ = f32[128,128]{1,0:T(8,128)S(1)} collective-permute-done((f32[128,128]{1,0:T(8,128)}, f32[128,128]{1,0:T(8,128)S(1)}, u32[]{:S(2)}, u32[]{:S(2)}) %collective-permute-start.6) | collective-permute-done | bytes 65568 | tf_op jit(solution)/shard_map/ppermute | solution.py:255
  151.1 1.4 collective-permute-done.5.refs_4_
  152.5 6.5 %all-to-all-start.3 = ((bf16[16,40,1024]{2,1,0:T(8,128)(2,1)}), bf16[16,40,1024]{2,1,0:T(8,128)(2,1)S(1)}, u32[]{:S(2)}, u32[]{:S(2)}) async-start(bf16[16,40,1024]{2,1,0:T(8,128)(2,1)} %bitcast.33), calls=%async_computation.3 | async-start | bytes 2621440 | tf_op jit(solution)/shard_map/all_to_all | solution.py:511
  159.1 4.5 %block_update.3 = (f32[384,128]{1,0:T(8,128)}, f32[384,128]{1,0:T(8,128)}, f32[384,128]{1,0:T(8,128)}, f32[384,128]{1,0:T(8,128)}) custom-call(s32[1]{0:T(128)} %bitcast.6.place_ref, bf16[640,128]{1,0:T(8,128)(2,1)} %broadcast_in_dim.2.tail_ref, bf16[640,3072]{1,0:T(8,128)(2,1)} %bitcast.16.keys_ref.values_ref, bf16[640,3072]{1,0:T(8,128)(2,1)} %bitcast.16.keys_ref.values_ref), custom_call_target="tpu_custom_call" | custom-call | flops 251658240 | bytes 4718592 | tf_op jit(solution)/shard_map/block_update/pallas_call | solution.py:95
  164.3 1.5 collective-permute-start.10
  166.4 1.7 sum_pieces.6
  168.5 1.8 collective-permute-start.13
  170.9 1.4 collective-permute-done.9.refs_2_
  172.4 10.2 %collective-permute-done.10.refs_3_ = f32[384,128]{1,0:T(8,128)S(1)} collective-permute-done((f32[384,128]{1,0:T(8,128)}, f32[384,128]{1,0:T(8,128)S(1)}, u32[]{:S(2)}, u32[]{:S(2)}) %collective-permute-start.10) | collective-permute-done | bytes 196640 | tf_op jit(solution)/shard_map/ppermute | solution.py:224
  183.2 2.4 sum_pieces.5
  185.6 2.8 %collective-permute-start.15 = (bf16[384,128]{1,0:T(8,128)(2,1)}, bf16[384,128]{1,0:T(8,128)(2,1)S(1)}, u32[]{:S(2)}, u32[]{:S(2)}) collective-permute-start(bf16[384,128]{1,0:T(8,128)(2,1)} %get-tuple-element.153), channel_id=1, source_target_pairs={{0,16},{2,18},{4,20},{6,22},{8,24},{10,26},{12,28},{14,30},{1,17},... | collective-permute-start | bytes 294920 | tf_op jit(solution)/shard_map/ppermute | solution.py:255
  188.5 2.1 collective-permute-start.14
  190.7 7.4 %all-to-all-start.2 = ((bf16[16,40,1024]{2,1,0:T(8,128)(2,1)}), bf16[16,40,1024]{2,1,0:T(8,128)(2,1)S(1)}, u32[]{:S(2)}, u32[]{:S(2)}) async-start(bf16[16,40,1024]{2,1,0:T(8,128)(2,1)} %bitcast.17), calls=%async_computation.2 | async-start | bytes 2621440 | tf_op jit(solution)/shard_map/all_to_all | solution.py:511
  198.0 5.8 %unpack_keys_values.3 = (bf16[512,2048]{1,0:T(8,128)(2,1)}, bf16[512,2048]{1,0:T(8,128)(2,1)}) custom-call(bf16[512,640]{1,0:T(8,128)(2,1)} %get-tuple-element.97.order_ref, bf16[640,3072]{1,0:T(8,128)(2,1)} %bitcast.16.keys_ref.values_ref, bf16[640,3072]{1,0:T(8,128)(2,1)} %bitcast.16.keys_ref.values_ref, ...), custom_call_target="tpu_custom_call", output_to_operand_aliasing={{0}: (3, {}), {1}: (4, {})} | custom-call | flops 2013265920 | bytes 7077888 | tf_op jit(solution)/shard_map/unpack_keys_values/pallas_call | solution.py:165
  205.1 2.3 sum_pieces.7
  208.1 1.5 collective-permute-start.18
  209.6 5.9 %attend_locally.1 = (bf16[512,1024]{1,0:T(8,128)(2,1)}, f32[512,1024]{1,0:T(8,128)}) custom-call(bf16[512,640]{1,0:T(8,128)(2,1)} %get-tuple-element.97.order_ref, bf16[512,512]{1,0:T(8,128)(2,1)} %get-tuple-element.98.causal_ref, bf16[512,128]{1,0:T(8,128)(2,1)} %get-tuple-element.99.carried_ref, bf16[640,1024]{1,0:T(8,128)(2,1)} %bitcast.32, ...), custom_call_target="tpu_custom_call" | custom-call | flops 25300041728 | bytes 6553600 | tf_op jit(solution)/shard_map/attend_locally/pallas_call | solution.py:416
  216.4 7.8 %collective-permute-done.18.refs_7_ = f32[384,128]{1,0:T(8,128)S(1)} collective-permute-done((f32[384,128]{1,0:T(8,128)}, f32[384,128]{1,0:T(8,128)S(1)}, u32[]{:S(2)}, u32[]{:S(2)}) %collective-permute-start.18) | collective-permute-done | bytes 196640 | tf_op jit(solution)/shard_map/ppermute | solution.py:224
  224.8 2.5 %assemble_states.1.states_ref = bf16[4096,128]{1,0:T(8,128)(2,1)} custom-call(s32[1]{0:T(128)} %bitcast.6.place_ref, f32[128,128]{1,0:T(8,128)} %get-tuple-element.145.refs_0_, f32[128,128]{1,0:T(8,128)} %copy-done.13, f32[128,128]{1,0:T(8,128)} %copy-done.14, f32[128,128]{1,0:T(8,128)} %copy-done.15, f32[384,128]{1,0:T(8,128)} %get-tuple-element.154.refs_4_, ...), custom_call_target="tpu_custom_call" | custom-call | flops 2097152 | bytes 2097152 | tf_op jit(solution)/shard_map/assemble_states/pallas_call | solution.py:298
  227.3 3.8 %finish.1.refs_0_ = bf16[512,2048]{1,0:T(8,128)(2,1)} custom-call(f32[1,2048]{1,0:T(1,128)} %bitcast.38, bf16[512,1024]{1,0:T(8,128)(2,1)} %get-tuple-element.159.query_ref, f32[512,1024]{1,0:T(8,128)} %get-tuple-element.160.local_ref, bf16[4096,128]{1,0:T(8,128)(2,1)} %assemble_states.1.states_ref), custom_call_target="tpu_custom_call" | custom-call | flops 536870912 | bytes 4194304 | tf_op jit(solution)/shard_map/finish/pallas_call | solution.py:455
  231.1 1.1 copy-done.3
  232.2 7.1 %attend.1 = bf16[512,2048]{1,0:T(8,128)(2,1)} custom-call(bf16[512,640]{1,0:T(8,128)(2,1)} %get-tuple-element.97.order_ref, bf16[512,512]{1,0:T(8,128)(2,1)} %get-tuple-element.98.causal_ref, bf16[512,128]{1,0:T(8,128)(2,1)} %get-tuple-element.99.carried_ref, f32[1,2048]{1,0:T(1,128)} %bitcast.39, ...), custom_call_target="tpu_custom_call", output_to_operand_aliasing={{}: (8, {})} | custom-call | flops 33084669952 | bytes 5505024 | tf_op jit(solution)/shard_map/attend/pallas_call | solution.py:362
  (110 shorter events, 17.5 us)
Async XLA Ops:
  1.3 3.7 %copy-start.22 = (s32[1,16,40]{2,1,0:T(8,128)S(1)}, s32[1,16,40]{2,1,0:T(8,128)}, u32[]{:S(2)}) copy-start(s32[1,16,40]{2,1,0:T(8,128)} %param.6) | copy-start | bytes 7684
  1.3 12.9 %collective-permute-start.1 = (bf16[2,256,512]{2,1,0:T(8,128)(2,1)S(1)}, bf16[2,256,512]{2,1,0:T(8,128)(2,1)S(1)}, u32[]{:S(2)}, u32[]{:S(2)}) collective-permute-start(bf16[2,256,512]{2,1,0:T(8,128)(2,1)S(1)} %slice_select_fusion.2), channel_id=1, source_target_pairs={{0,1},{1,0},{2,3},{3,2},{4,5},{5,4},{6,7},{7,6},{8,9},{9,8},{10,11... | collective-permute-start | bytes 1572872 | tf_op jit(solution)/shard_map/ppermute | solution.py:484
  4.6 43.3 %collective-permute-start.7 = (bf16[2,256,1536]{2,1,0:T(8,128)(2,1)S(1)}, bf16[2,256,1536]{2,1,0:T(8,128)(2,1)}, u32[]{:S(2)}, u32[]{:S(2)}) collective-permute-start(bf16[2,256,1536]{2,1,0:T(8,128)(2,1)S(1)} %slice_select_fusion), channel_id=1, source_target_pairs={{0,1},{1,0},{2,3},{3,2},{4,5},{5,4},{6,7},{7,6},{8,9},{9,8},{10,11... | collective-permute-start | bytes 4718600 | tf_op jit(solution)/shard_map/ppermute | solution.py:484
  14.1 0.8 copy-start.25
  18.3 39.1 %all-to-all-start = ((bf16[16,40,1024]{2,1,0:T(8,128)(2,1)}), bf16[16,40,1024]{2,1,0:T(8,128)(2,1)S(1)}, u32[]{:S(2)}, u32[]{:S(2)}) async-start(bf16[16,40,1024]{2,1,0:T(8,128)(2,1)} %bitcast.35), calls=%async_computation | async-start | bytes 2621440 | tf_op jit(solution)/shard_map/all_to_all | solution.py:511
  57.4 1.1 copy-start
  58.5 94.1 %all-to-all-start.1 = ((bf16[16,40,3072]{2,1,0:T(8,128)(2,1)}), bf16[16,40,3072]{2,1,0:T(8,128)(2,1)}, u32[]{:S(2)}, u32[]{:S(2)}) async-start(bf16[16,40,3072]{2,1,0:T(8,128)(2,1)} %bitcast.31), calls=%async_computation.1 | async-start | bytes 7864320 | tf_op jit(solution)/shard_map/all_to_all | solution.py:511
  63.7 3.0 %copy-start.23 = (s32[4]{0:T(128)S(1)}, s32[4]{0:T(128)}, u32[]{:S(2)}) copy-start(s32[4]{0:T(128)} %param.8) | copy-start | bytes 52
  63.7 4.5 %copy-start.12 = (s32[1,16,40]{2,1,0:T(8,128)S(1)}, s32[1,16,40]{2,1,0:T(8,128)}, u32[]{:S(2)}) copy-start(s32[1,16,40]{2,1,0:T(8,128)} %param.7) | copy-start | bytes 7684
  65.4 27.4 %collective-permute-start = (bf16[1,256,2048]{2,1,0:T(8,128)(2,1)S(1)}, bf16[1,256,2048]{2,1,0:T(8,128)(2,1)S(1)}, u32[]{:S(2)}, u32[]{:S(2)}) collective-permute-start(bf16[1,256,2048]{2,1,0:T(8,128)(2,1)S(1)} %slice_select_fusion.1), channel_id=1, source_target_pairs={{0,1},{1,0},{2,3},{3,2},{4,5},{5,4},{6,7},{7,6},{8,9},{9,8},{10,11... | collective-permute-start | bytes 3145736 | tf_op jit(solution)/shard_map/ppermute | solution.py:484
  70.6 11.3 %copy-start.21 = (s32[512]{0:T(512)}, s32[512]{0:T(512)S(1)}, u32[]{:S(2)}) copy-start(s32[512]{0:T(512)S(1)} %broadcast_add_fusion.1) | copy-start | bytes 6148
  70.7 11.2 %copy-start.1 = (s32[512,1]{1,0:T(8,128)}, s32[512,1]{1,0:T(8,128)S(1)}, u32[]{:S(2)}) copy-start(s32[512,1]{1,0:T(8,128)S(1)} %copy.33.seg_col_ref) | copy-start | bytes 6148
  78.8 8.7 %collective-permute-start.2 = (f32[128,128]{1,0:T(8,128)}, f32[128,128]{1,0:T(8,128)S(1)}, u32[]{:S(2)}, u32[]{:S(2)}) collective-permute-start(f32[128,128]{1,0:T(8,128)} %get-tuple-element.84), channel_id=1, source_target_pairs={{0,2},{2,0},{4,6},{6,4},{8,10},{10,8},{12,14},{14,12},{16,18},{18,... | collective-permute-start | bytes 196616 | tf_op jit(solution)/shard_map/ppermute | solution.py:224
  79.5 9.1 %collective-permute-start.3 = (f32[128,128]{1,0:T(8,128)}, f32[128,128]{1,0:T(8,128)S(1)}, u32[]{:S(2)}, u32[]{:S(2)}) collective-permute-start(f32[128,128]{1,0:T(8,128)} %get-tuple-element.85), channel_id=1, source_target_pairs={{0,4},{2,6},{4,0},{6,2},{8,12},{10,14},{12,8},{14,10},{16,20},{18,... | collective-permute-start | bytes 196616 | tf_op jit(solution)/shard_map/ppermute | solution.py:224
  79.7 10.7 %collective-permute-start.4 = (f32[128,128]{1,0:T(8,128)}, f32[128,128]{1,0:T(8,128)S(1)}, u32[]{:S(2)}, u32[]{:S(2)}) collective-permute-start(f32[128,128]{1,0:T(8,128)} %get-tuple-element.86), channel_id=1, source_target_pairs={{0,6},{2,4},{4,2},{6,0},{8,14},{10,12},{12,10},{14,8},{16,22},{18,... | collective-permute-start | bytes 196616 | tf_op jit(solution)/shard_map/ppermute | solution.py:224
  87.5 2.9 %copy-start.18 = (f32[128,128]{1,0:T(8,128)}, f32[128,128]{1,0:T(8,128)S(1)}, u32[]{:S(2)}) copy-start(f32[128,128]{1,0:T(8,128)S(1)} %collective-permute-done.2.refs_1_) | copy-start | bytes 196612
  88.5 1.9 copy-start.19
  92.8 4.9 %copy-start.24 = (bf16[1,256,2048]{2,1,0:T(8,128)(2,1)}, bf16[1,256,2048]{2,1,0:T(8,128)(2,1)S(1)}, u32[]{:S(2)}) copy-start(bf16[1,256,2048]{2,1,0:T(8,128)(2,1)S(1)} %collective-permute-done.refs_3_) | copy-start | bytes 3145732
  92.8 58.4 %collective-permute-start.6 = (f32[128,128]{1,0:T(8,128)}, f32[128,128]{1,0:T(8,128)S(1)}, u32[]{:S(2)}, u32[]{:S(2)}) collective-permute-start(f32[128,128]{1,0:T(8,128)} %get-tuple-element.105), channel_id=1, source_target_pairs={{0,16},{2,18},{4,20},{6,22},{8,24},{10,26},{12,28},{14,30},{1,17},... | collective-permute-start | bytes 196616 | tf_op jit(solution)/shard_map/ppermute | solution.py:255
  95.8 56.8 %collective-permute-start.5 = (f32[128,128]{1,0:T(8,128)}, f32[128,128]{1,0:T(8,128)S(1)}, u32[]{:S(2)}, u32[]{:S(2)}) collective-permute-start(f32[128,128]{1,0:T(8,128)} %get-tuple-element.105), channel_id=1, source_target_pairs={{0,8},{2,10},{4,12},{6,14},{8,16},{10,18},{12,20},{14,22},{16,24},... | collective-permute-start | bytes 196616 | tf_op jit(solution)/shard_map/ppermute | solution.py:255
  151.1 12.5 %copy-start.16 = (f32[128,128]{1,0:T(8,128)}, f32[128,128]{1,0:T(8,128)S(1)}, u32[]{:S(2)}) copy-start(f32[128,128]{1,0:T(8,128)S(1)} %collective-permute-done.6.refs_5_) | copy-start | bytes 196612
  152.5 11.1 %copy-start.17 = (f32[128,128]{1,0:T(8,128)}, f32[128,128]{1,0:T(8,128)S(1)}, u32[]{:S(2)}) copy-start(f32[128,128]{1,0:T(8,128)S(1)} %collective-permute-done.5.refs_4_) | copy-start | bytes 196612
  152.5 38.1 %all-to-all-start.3 = ((bf16[16,40,1024]{2,1,0:T(8,128)(2,1)}), bf16[16,40,1024]{2,1,0:T(8,128)(2,1)S(1)}, u32[]{:S(2)}, u32[]{:S(2)}) async-start(bf16[16,40,1024]{2,1,0:T(8,128)(2,1)} %bitcast.33), calls=%async_computation.3 | async-start | bytes 2621440 | tf_op jit(solution)/shard_map/all_to_all | solution.py:511
  163.6 4.9 %collective-permute-start.8 = (f32[384,128]{1,0:T(8,128)}, f32[384,128]{1,0:T(8,128)S(1)}, u32[]{:S(2)}, u32[]{:S(2)}) collective-permute-start(f32[384,128]{1,0:T(8,128)} %get-tuple-element.120), channel_id=1, source_target_pairs={{0,2},{2,0},{4,6},{6,4},{8,10},{10,8},{12,14},{14,12},{16,18},{18,... | collective-permute-start | bytes 589832 | tf_op jit(solution)/shard_map/ppermute | solution.py:224
  164.0 8.3 %collective-permute-start.9 = (f32[384,128]{1,0:T(8,128)}, f32[384,128]{1,0:T(8,128)S(1)}, u32[]{:S(2)}, u32[]{:S(2)}) collective-permute-start(f32[384,128]{1,0:T(8,128)} %get-tuple-element.121), channel_id=1, source_target_pairs={{0,4},{2,6},{4,0},{6,2},{8,12},{10,14},{12,8},{14,10},{16,20},{18,... | collective-permute-start | bytes 589832 | tf_op jit(solution)/shard_map/ppermute | solution.py:224
  164.3 18.2 %collective-permute-start.10 = (f32[384,128]{1,0:T(8,128)}, f32[384,128]{1,0:T(8,128)S(1)}, u32[]{:S(2)}, u32[]{:S(2)}) collective-permute-start(f32[384,128]{1,0:T(8,128)} %get-tuple-element.122), channel_id=1, source_target_pairs={{0,6},{2,4},{4,2},{6,0},{8,14},{10,12},{12,10},{14,8},{16,22},{18,... | collective-permute-start | bytes 589832 | tf_op jit(solution)/shard_map/ppermute | solution.py:224
  168.2 17.4 %collective-permute-start.11 = (f32[128,128]{1,0:T(8,128)}, f32[128,128]{1,0:T(8,128)S(1)}, u32[]{:S(2)}, u32[]{:S(2)}) collective-permute-start(f32[128,128]{1,0:T(8,128)} %get-tuple-element.136), channel_id=1, source_target_pairs={{0,2},{2,0},{4,6},{6,4},{8,10},{10,8},{12,14},{14,12},{16,18},{18,... | collective-permute-start | bytes 196616 | tf_op jit(solution)/shard_map/ppermute | solution.py:224
  168.2 17.4 %collective-permute-start.12 = (f32[128,128]{1,0:T(8,128)}, f32[128,128]{1,0:T(8,128)S(1)}, u32[]{:S(2)}, u32[]{:S(2)}) collective-permute-start(f32[128,128]{1,0:T(8,128)} %get-tuple-element.137), channel_id=1, source_target_pairs={{0,4},{2,6},{4,0},{6,2},{8,12},{10,14},{12,8},{14,10},{16,20},{18,... | collective-permute-start | bytes 196616 | tf_op jit(solution)/shard_map/ppermute | solution.py:224
  168.5 14.0 %copy-start.7 = (f32[384,128]{1,0:T(8,128)}, f32[384,128]{1,0:T(8,128)S(1)}, u32[]{:S(2)}) copy-start(f32[384,128]{1,0:T(8,128)S(1)} %collective-permute-done.8.refs_1_) | copy-start | bytes 589828
  168.5 17.1 %collective-permute-start.13 = (f32[128,128]{1,0:T(8,128)}, f32[128,128]{1,0:T(8,128)S(1)}, u32[]{:S(2)}, u32[]{:S(2)}) collective-permute-start(f32[128,128]{1,0:T(8,128)} %get-tuple-element.138), channel_id=1, source_target_pairs={{0,6},{2,4},{4,2},{6,0},{8,14},{10,12},{12,10},{14,8},{16,22},{18,... | collective-permute-start | bytes 196616 | tf_op jit(solution)/shard_map/ppermute | solution.py:224
  172.4 10.2 %copy-start.8 = (f32[384,128]{1,0:T(8,128)}, f32[384,128]{1,0:T(8,128)S(1)}, u32[]{:S(2)}) copy-start(f32[384,128]{1,0:T(8,128)S(1)} %collective-permute-done.9.refs_2_) | copy-start | bytes 589828
  182.6 0.7 copy-start.9
  185.6 18.2 %copy-start.13 = (f32[128,128]{1,0:T(8,128)}, f32[128,128]{1,0:T(8,128)S(1)}, u32[]{:S(2)}) copy-start(f32[128,128]{1,0:T(8,128)S(1)} %collective-permute-done.11.refs_1_) | copy-start | bytes 196612
  185.6 18.2 %copy-start.14 = (f32[128,128]{1,0:T(8,128)}, f32[128,128]{1,0:T(8,128)S(1)}, u32[]{:S(2)}) copy-start(f32[128,128]{1,0:T(8,128)S(1)} %collective-permute-done.12.refs_2_) | copy-start | bytes 196612
  185.6 18.2 %copy-start.15 = (f32[128,128]{1,0:T(8,128)}, f32[128,128]{1,0:T(8,128)S(1)}, u32[]{:S(2)}) copy-start(f32[128,128]{1,0:T(8,128)S(1)} %collective-permute-done.13.refs_3_) | copy-start | bytes 196612
  185.6 18.2 %collective-permute-start.15 = (bf16[384,128]{1,0:T(8,128)(2,1)}, bf16[384,128]{1,0:T(8,128)(2,1)S(1)}, u32[]{:S(2)}, u32[]{:S(2)}) collective-permute-start(bf16[384,128]{1,0:T(8,128)(2,1)} %get-tuple-element.153), channel_id=1, source_target_pairs={{0,16},{2,18},{4,20},{6,22},{8,24},{10,26},{12,28},{14,30},{1,17},... | collective-permute-start | bytes 294920 | tf_op jit(solution)/shard_map/ppermute | solution.py:255
  188.5 15.4 %collective-permute-start.14 = (bf16[384,128]{1,0:T(8,128)(2,1)}, bf16[384,128]{1,0:T(8,128)(2,1)S(1)}, u32[]{:S(2)}, u32[]{:S(2)}) collective-permute-start(bf16[384,128]{1,0:T(8,128)(2,1)} %get-tuple-element.153), channel_id=1, source_target_pairs={{0,8},{2,10},{4,12},{6,14},{8,16},{10,18},{12,20},{14,22},{16,24},... | collective-permute-start | bytes 294920 | tf_op jit(solution)/shard_map/ppermute | solution.py:255
  190.6 13.2 %copy-start.2 = (bf16[16,40,1024]{2,1,0:T(8,128)(2,1)}, bf16[16,40,1024]{2,1,0:T(8,128)(2,1)S(1)}, u32[]{:S(2)}) copy-start(bf16[16,40,1024]{2,1,0:T(8,128)(2,1)S(1)} %all-to-all-done.3) | copy-start | bytes 3932164
  190.7 40.4 %all-to-all-start.2 = ((bf16[16,40,1024]{2,1,0:T(8,128)(2,1)}), bf16[16,40,1024]{2,1,0:T(8,128)(2,1)S(1)}, u32[]{:S(2)}, u32[]{:S(2)}) async-start(bf16[16,40,1024]{2,1,0:T(8,128)(2,1)} %bitcast.17), calls=%async_computation.2 | async-start | bytes 2621440 | tf_op jit(solution)/shard_map/all_to_all | solution.py:511
  203.9 0.6 copy-start.10
  204.5 0.6 copy-start.11
  207.5 8.1 %collective-permute-start.16 = (f32[384,128]{1,0:T(8,128)}, f32[384,128]{1,0:T(8,128)S(1)}, u32[]{:S(2)}, u32[]{:S(2)}) collective-permute-start(f32[384,128]{1,0:T(8,128)} %get-tuple-element.155), channel_id=1, source_target_pairs={{0,2},{2,0},{4,6},{6,4},{8,10},{10,8},{12,14},{14,12},{16,18},{18,... | collective-permute-start | bytes 589832 | tf_op jit(solution)/shard_map/ppermute | solution.py:224
  207.8 8.6 %collective-permute-start.17 = (f32[384,128]{1,0:T(8,128)}, f32[384,128]{1,0:T(8,128)S(1)}, u32[]{:S(2)}, u32[]{:S(2)}) collective-permute-start(f32[384,128]{1,0:T(8,128)} %get-tuple-element.156), channel_id=1, source_target_pairs={{0,4},{2,6},{4,0},{6,2},{8,12},{10,14},{12,8},{14,10},{16,20},{18,... | collective-permute-start | bytes 589832 | tf_op jit(solution)/shard_map/ppermute | solution.py:224
  208.1 16.0 %collective-permute-start.18 = (f32[384,128]{1,0:T(8,128)}, f32[384,128]{1,0:T(8,128)S(1)}, u32[]{:S(2)}, u32[]{:S(2)}) collective-permute-start(f32[384,128]{1,0:T(8,128)} %get-tuple-element.157), channel_id=1, source_target_pairs={{0,6},{2,4},{4,2},{6,0},{8,14},{10,12},{12,10},{14,8},{16,22},{18,... | collective-permute-start | bytes 589832 | tf_op jit(solution)/shard_map/ppermute | solution.py:224
  215.5 8.6 %copy-start.4 = (f32[384,128]{1,0:T(8,128)}, f32[384,128]{1,0:T(8,128)S(1)}, u32[]{:S(2)}) copy-start(f32[384,128]{1,0:T(8,128)S(1)} %collective-permute-done.16.refs_5_) | copy-start | bytes 589828
  216.4 7.8 %copy-start.5 = (f32[384,128]{1,0:T(8,128)}, f32[384,128]{1,0:T(8,128)S(1)}, u32[]{:S(2)}) copy-start(f32[384,128]{1,0:T(8,128)S(1)} %collective-permute-done.17.refs_6_) | copy-start | bytes 589828
  224.2 0.7 copy-start.6
  231.1 1.1 copy-start.3
  (1 other events, 0.6 us)

commit v11 on v10

--- a/solution.py
+++ b/solution.py
@@ -544,7 +544,7 @@
     )
     arrived_next = to_owners(outgoing)
     within, across = carry_tables(last_segment)
-    sums = carry_within(block_update(arrived, tail_slots), within, jnp.float32)
+    sums = carry_within(block_update(arrived, tail_slots), within, jnp.bfloat16)
     tables = block_tables(land_row, segment, carried_mask)
     filled = unpack_keys_values(arrived, tables[0], 0, columns, ())
     incoming = swap_heads(qkv, QUERY, 1, 0, columns)

time: 241 us -> 240 us (level)
  transfers between devices with their start and end apart: 23 -> 23, of which waited for: 11 -> 12; matrix products, arithmetic and copies ran while one was open for 6% -> 6% of each run, Pallas kernels for 24% -> 24%
where the time goes in v11:
time: 240 us; the launch traced here: 238 us
  waiting for transfers between devices  100 us (42%)
  Pallas kernels  64.4 us (27%)
  starting transfers between devices  49.7 us (21%)
  local copies, waits for them, and re-layouts  12.4 us (5%)
  other arithmetic  10.2 us (4%)
    ppermute x4, waiting for transfers between devices, pass_totals(): lax.ppermute(sums[near], 'seq', [(i, i + step) for i in range(seq_count -...  45.9 us
    ppermute x3, waiting for transfers between devices, swap_heads(): return lax.ppermute(outgoing, 'head', [(0, 1), (1, 0)])  28.5 us
    all_to_all x4, starting transfers between devices, to_owners(): lax.all_to_all(outgoing, 'seq', split_axis=0, concat_axis=0, tiled=True)  28.1 us
    ppermute x12, waiting for transfers between devices, swap_places(): return lax.ppermute(value, 'seq', [(i, i ^ k) for i in range(seq_count)])  23.2 us
    pallas_call x4, Pallas kernels, pack_rows(): pl.pallas_call(pack_kernel, out_shape=jax.ShapeDtypeStruct((slots, planes...  17.4 us
    ppermute x4, starting transfers between devices, pass_totals(): lax.ppermute(sums[near], 'seq', [(i, i + step) for i in range(seq_count -...  9.86 us
    pallas_call x2, Pallas kernels, unpack_keys_values(): pl.pallas_call(unpack_kernel, out_shape=(packed, packed), grid=(blocks,),...  9.08 us
    ppermute x12, starting transfers between devices, swap_places(): return lax.ppermute(value, 'seq', [(i, i ^ k) for i in range(seq_count)])  8.83 us
  transfers between devices with their start and end apart: 23, of which 12 were waited for; matrix products, arithmetic and copies ran while one was open for 6% of the time, Pallas kernels for 24%

profile of v11, /device:TPU:11, one launch (start us, length us, event | category | flops | bytes accessed | tf_op | source)
XLA Modules:
  0.0 237.8 jit_solution(12878828884994852867)
XLA Ops:
  0.0 1.3 slice_select_fusion.2
  1.3 1.3 collective-permute-start.1
  2.6 2.0 slice_select_fusion
  4.9 0.9 sub.106.refs_1_
  5.8 0.9 sub.105.refs_0_
  6.7 7.4 %collective-permute-done.1.refs_3_ = bf16[2,256,512]{2,1,0:T(8,128)(2,1)S(1)} collective-permute-done((bf16[2,256,512]{2,1,0:T(8,128)(2,1)S(1)}, bf16[2,256,512]{2,1,0:T(8,128)(2,1)S(1)}, u32[]{:S(2)}, u32[]{:S(2)}) %collective-permute-start.1) | collective-permute-done | bytes 524320 | tf_op jit(solution)/shard_map/ppermute | solution.py:484
  14.9 3.4 %pack_rows.4 = bf16[640,1024]{1,0:T(8,128)(2,1)} custom-call(s32[1]{0:T(128)} %bitcast.8.place_ref, s32[640,1]{1,0:T(8,128)} %sub.105.refs_0_, s32[640,1]{1,0:T(8,128)} %sub.106.refs_1_, bf16[3,256,4096]{2,1,0:T(8,128)(2,1)} %refs_2_.7, bf16[2,256,512]{2,1,0:T(8,128)(2,1)} %copy-done.25), custom_call_target="tpu_custom_call" | custom-call | flops 13421772800 | bytes 2359296 | tf_op jit(solution)/shard_map/pack_rows/pallas_call | solution.py:50
  18.3 8.6 %all-to-all-start = ((bf16[16,40,1024]{2,1,0:T(8,128)(2,1)}), bf16[16,40,1024]{2,1,0:T(8,128)(2,1)S(1)}, u32[]{:S(2)}, u32[]{:S(2)}) async-start(bf16[16,40,1024]{2,1,0:T(8,128)(2,1)} %bitcast.35), calls=%async_computation | async-start | bytes 2621440 | tf_op jit(solution)/shard_map/all_to_all | solution.py:511
  26.9 21.1 %collective-permute-done.7.refs_3_ = bf16[2,256,1536]{2,1,0:T(8,128)(2,1)} collective-permute-done((bf16[2,256,1536]{2,1,0:T(8,128)(2,1)S(1)}, bf16[2,256,1536]{2,1,0:T(8,128)(2,1)}, u32[]{:S(2)}, u32[]{:S(2)}) %collective-permute-start.7) | collective-permute-done | bytes 1572896 | tf_op jit(solution)/shard_map/ppermute | solution.py:484
  47.9 7.2 %pack_rows.7 = bf16[640,3072]{1,0:T(8,128)(2,1)} custom-call(s32[1]{0:T(128)} %bitcast.8.place_ref, s32[640,1]{1,0:T(8,128)} %sub.105.refs_0_, s32[640,1]{1,0:T(8,128)} %sub.106.refs_1_, bf16[3,256,4096]{2,1,0:T(8,128)(2,1)} %refs_2_.7, bf16[2,256,1536]{2,1,0:T(8,128)(2,1)} %collective-permute-done.7.refs_3_), custom_call_target="tpu_custom_call" | custom-call | flops 40265318400 | bytes 7077888 | tf_op jit(solution)/shard_map/pack_rows/pallas_call | solution.py:50
  55.2 2.2 all-to-all-done
  57.4 1.1 copy-done
  58.5 5.2 %all-to-all-start.1 = ((bf16[16,40,3072]{2,1,0:T(8,128)(2,1)}), bf16[16,40,3072]{2,1,0:T(8,128)(2,1)}, u32[]{:S(2)}, u32[]{:S(2)}) async-start(bf16[16,40,3072]{2,1,0:T(8,128)(2,1)} %bitcast.31), calls=%async_computation.1 | async-start | bytes 7864320 | tf_op jit(solution)/shard_map/all_to_all | solution.py:511
  63.7 1.7 slice_select_fusion.1
  65.4 1.3 collective-permute-start
  75.1 3.7 %block_update.2 = (f32[128,128]{1,0:T(8,128)}, f32[128,128]{1,0:T(8,128)}, f32[128,128]{1,0:T(8,128)}, f32[128,128]{1,0:T(8,128)}) custom-call(s32[1]{0:T(128)} %bitcast.6.place_ref, bf16[640,128]{1,0:T(8,128)(2,1)} %broadcast_in_dim.2.tail_ref, bf16[640,1024]{1,0:T(8,128)(2,1)} %bitcast.27, bf16[640,1024]{1,0:T(8,128)(2,1)} %bitcast.28), custom_call_target="tpu_custom_call" | custom-call | flops 83886080 | bytes 1572864 | tf_op jit(solution)/shard_map/block_update/pallas_call | solution.py:95
  79.7 1.4 collective-permute-start.4
  81.9 2.4 block_tables.1
  84.3 3.3 %unpack_keys_values.2 = (bf16[512,2048]{1,0:T(8,128)(2,1)}, bf16[512,2048]{1,0:T(8,128)(2,1)}) custom-call(bf16[512,640]{1,0:T(8,128)(2,1)} %get-tuple-element.97.order_ref, bf16[640,1024]{1,0:T(8,128)(2,1)} %bitcast.29, bf16[640,1024]{1,0:T(8,128)(2,1)} %bitcast.30), custom_call_target="tpu_custom_call" | custom-call | flops 671088640 | bytes 2359296 | tf_op jit(solution)/shard_map/unpack_keys_values/pallas_call | solution.py:165
  87.5 1.0 collective-permute-done.3.refs_2_
  88.5 1.9 collective-permute-done.4.refs_3_
  91.1 1.7 sum_pieces.4
  92.8 3.0 %collective-permute-start.6 = (bf16[128,128]{1,0:T(8,128)(2,1)}, bf16[128,128]{1,0:T(8,128)(2,1)S(1)}, u32[]{:S(2)}, u32[]{:S(2)}) collective-permute-start(bf16[128,128]{1,0:T(8,128)(2,1)} %get-tuple-element.105), channel_id=1, source_target_pairs={{0,16},{2,18},{4,20},{6,22},{8,24},{10,26},{12,28},{14,30},{1,17},... | collective-permute-start | bytes 98312 | tf_op jit(solution)/shard_map/ppermute | solution.py:255
  95.7 1.9 collective-permute-start.5
  97.7 3.4 %pack_rows.6 = bf16[640,1024]{1,0:T(8,128)(2,1)} custom-call(s32[1]{0:T(128)} %bitcast.8.place_ref, s32[640,1]{1,0:T(8,128)} %sub.105.refs_0_, s32[640,1]{1,0:T(8,128)} %sub.106.refs_1_, bf16[3,256,4096]{2,1,0:T(8,128)(2,1)} %refs_2_.7, bf16[1,256,2048]{2,1,0:T(8,128)(2,1)} %copy-done.24), custom_call_target="tpu_custom_call" | custom-call | flops 13421772800 | bytes 2359296 | tf_op jit(solution)/shard_map/pack_rows/pallas_call | solution.py:50
  101.1 3.4 %pack_rows.5 = bf16[640,1024]{1,0:T(8,128)(2,1)} custom-call(s32[1]{0:T(128)} %bitcast.8.place_ref, s32[640,1]{1,0:T(8,128)} %sub.105.refs_0_, s32[640,1]{1,0:T(8,128)} %sub.106.refs_1_, bf16[3,256,4096]{2,1,0:T(8,128)(2,1)} %refs_2_.7, bf16[1,256,2048]{2,1,0:T(8,128)(2,1)} %copy-done.24), custom_call_target="tpu_custom_call" | custom-call | flops 13421772800 | bytes 2359296 | tf_op jit(solution)/shard_map/pack_rows/pallas_call | solution.py:50
  104.5 45.2 %collective-permute-done.6.refs_5_ = bf16[128,128]{1,0:T(8,128)(2,1)S(1)} collective-permute-done((bf16[128,128]{1,0:T(8,128)(2,1)}, bf16[128,128]{1,0:T(8,128)(2,1)S(1)}, u32[]{:S(2)}, u32[]{:S(2)}) %collective-permute-start.6) | collective-permute-done | bytes 32800 | tf_op jit(solution)/shard_map/ppermute | solution.py:255
  150.6 7.0 %all-to-all-start.3 = ((bf16[16,40,1024]{2,1,0:T(8,128)(2,1)}), bf16[16,40,1024]{2,1,0:T(8,128)(2,1)S(1)}, u32[]{:S(2)}, u32[]{:S(2)}) async-start(bf16[16,40,1024]{2,1,0:T(8,128)(2,1)} %bitcast.33), calls=%async_computation.3 | async-start | bytes 2621440 | tf_op jit(solution)/shard_map/all_to_all | solution.py:511
  157.5 4.5 %block_update.3 = (f32[384,128]{1,0:T(8,128)}, f32[384,128]{1,0:T(8,128)}, f32[384,128]{1,0:T(8,128)}, f32[384,128]{1,0:T(8,128)}) custom-call(s32[1]{0:T(128)} %bitcast.6.place_ref, bf16[640,128]{1,0:T(8,128)(2,1)} %broadcast_in_dim.2.tail_ref, bf16[640,3072]{1,0:T(8,128)(2,1)} %bitcast.16.keys_ref.values_ref, bf16[640,3072]{1,0:T(8,128)(2,1)} %bitcast.16.keys_ref.values_ref), custom_call_target="tpu_custom_call" | custom-call | flops 251658240 | bytes 4718592 | tf_op jit(solution)/shard_map/block_update/pallas_call | solution.py:95
  162.8 1.5 collective-permute-start.10
  164.9 1.7 sum_pieces.6
  166.9 1.8 collective-permute-start.13
  169.3 1.5 collective-permute-done.9.refs_2_
  170.8 10.2 %collective-permute-done.10.refs_3_ = f32[384,128]{1,0:T(8,128)S(1)} collective-permute-done((f32[384,128]{1,0:T(8,128)}, f32[384,128]{1,0:T(8,128)S(1)}, u32[]{:S(2)}, u32[]{:S(2)}) %collective-permute-start.10) | collective-permute-done | bytes 196640 | tf_op jit(solution)/shard_map/ppermute | solution.py:224
  181.7 2.4 sum_pieces.5
  184.1 2.8 %collective-permute-start.15 = (bf16[384,128]{1,0:T(8,128)(2,1)}, bf16[384,128]{1,0:T(8,128)(2,1)S(1)}, u32[]{:S(2)}, u32[]{:S(2)}) collective-permute-start(bf16[384,128]{1,0:T(8,128)(2,1)} %get-tuple-element.153), channel_id=1, source_target_pairs={{0,16},{2,18},{4,20},{6,22},{8,24},{10,26},{12,28},{14,30},{1,17},... | collective-permute-start | bytes 294920 | tf_op jit(solution)/shard_map/ppermute | solution.py:255
  186.9 2.1 collective-permute-start.14
  189.1 7.4 %all-to-all-start.2 = ((bf16[16,40,1024]{2,1,0:T(8,128)(2,1)}), bf16[16,40,1024]{2,1,0:T(8,128)(2,1)S(1)}, u32[]{:S(2)}, u32[]{:S(2)}) async-start(bf16[16,40,1024]{2,1,0:T(8,128)(2,1)} %bitcast.17), calls=%async_computation.2 | async-start | bytes 2621440 | tf_op jit(solution)/shard_map/all_to_all | solution.py:511
  196.5 5.8 %unpack_keys_values.3 = (bf16[512,2048]{1,0:T(8,128)(2,1)}, bf16[512,2048]{1,0:T(8,128)(2,1)}) custom-call(bf16[512,640]{1,0:T(8,128)(2,1)} %get-tuple-element.97.order_ref, bf16[640,3072]{1,0:T(8,128)(2,1)} %bitcast.16.keys_ref.values_ref, bf16[640,3072]{1,0:T(8,128)(2,1)} %bitcast.16.keys_ref.values_ref, ...), custom_call_target="tpu_custom_call", output_to_operand_aliasing={{0}: (3, {}), {1}: (4, {})} | custom-call | flops 2013265920 | bytes 7077888 | tf_op jit(solution)/shard_map/unpack_keys_values/pallas_call | solution.py:165
  203.6 2.3 sum_pieces.7
  206.6 1.5 collective-permute-start.18
  208.1 5.9 %attend_locally.1 = (bf16[512,1024]{1,0:T(8,128)(2,1)}, f32[512,1024]{1,0:T(8,128)}) custom-call(bf16[512,640]{1,0:T(8,128)(2,1)} %get-tuple-element.97.order_ref, bf16[512,512]{1,0:T(8,128)(2,1)} %get-tuple-element.98.causal_ref, bf16[512,128]{1,0:T(8,128)(2,1)} %get-tuple-element.99.carried_ref, bf16[640,1024]{1,0:T(8,128)(2,1)} %bitcast.32, ...), custom_call_target="tpu_custom_call" | custom-call | flops 25300041728 | bytes 6553600 | tf_op jit(solution)/shard_map/attend_locally/pallas_call | solution.py:416
  214.0 0.8 collective-permute-done.17.refs_6_
  214.9 7.8 %collective-permute-done.18.refs_7_ = f32[384,128]{1,0:T(8,128)S(1)} collective-permute-done((f32[384,128]{1,0:T(8,128)}, f32[384,128]{1,0:T(8,128)S(1)}, u32[]{:S(2)}, u32[]{:S(2)}) %collective-permute-start.18) | collective-permute-done | bytes 196640 | tf_op jit(solution)/shard_map/ppermute | solution.py:224
  223.3 2.5 %assemble_states.1.states_ref = bf16[4096,128]{1,0:T(8,128)(2,1)} custom-call(s32[1]{0:T(128)} %bitcast.6.place_ref, f32[128,128]{1,0:T(8,128)} %get-tuple-element.145.refs_0_, f32[128,128]{1,0:T(8,128)} %copy-done.13, f32[128,128]{1,0:T(8,128)} %copy-done.14, f32[128,128]{1,0:T(8,128)} %copy-done.15, f32[384,128]{1,0:T(8,128)} %get-tuple-element.154.refs_4_, ...), custom_call_target="tpu_custom_call" | custom-call | flops 2097152 | bytes 2097152 | tf_op jit(solution)/shard_map/assemble_states/pallas_call | solution.py:298
  225.8 3.8 %finish.1.refs_0_ = bf16[512,2048]{1,0:T(8,128)(2,1)} custom-call(f32[1,2048]{1,0:T(1,128)} %bitcast.38, bf16[512,1024]{1,0:T(8,128)(2,1)} %get-tuple-element.159.query_ref, f32[512,1024]{1,0:T(8,128)} %get-tuple-element.160.local_ref, bf16[4096,128]{1,0:T(8,128)(2,1)} %assemble_states.1.states_ref), custom_call_target="tpu_custom_call" | custom-call | flops 536870912 | bytes 4194304 | tf_op jit(solution)/shard_map/finish/pallas_call | solution.py:455
  229.6 1.1 copy-done.3
  230.7 7.1 %attend.1 = bf16[512,2048]{1,0:T(8,128)(2,1)} custom-call(bf16[512,640]{1,0:T(8,128)(2,1)} %get-tuple-element.97.order_ref, bf16[512,512]{1,0:T(8,128)(2,1)} %get-tuple-element.98.causal_ref, bf16[512,128]{1,0:T(8,128)(2,1)} %get-tuple-element.99.carried_ref, f32[1,2048]{1,0:T(1,128)} %bitcast.39, ...), custom_call_target="tpu_custom_call", output_to_operand_aliasing={{}: (8, {})} | custom-call | flops 33084669952 | bytes 5505024 | tf_op jit(solution)/shard_map/attend/pallas_call | solution.py:362
  (110 shorter events, 17.5 us)
Async XLA Ops:
  1.3 3.7 %copy-start.22 = (s32[1,16,40]{2,1,0:T(8,128)S(1)}, s32[1,16,40]{2,1,0:T(8,128)}, u32[]{:S(2)}) copy-start(s32[1,16,40]{2,1,0:T(8,128)} %param.6) | copy-start | bytes 7684
  1.3 12.9 %collective-permute-start.1 = (bf16[2,256,512]{2,1,0:T(8,128)(2,1)S(1)}, bf16[2,256,512]{2,1,0:T(8,128)(2,1)S(1)}, u32[]{:S(2)}, u32[]{:S(2)}) collective-permute-start(bf16[2,256,512]{2,1,0:T(8,128)(2,1)S(1)} %slice_select_fusion.2), channel_id=1, source_target_pairs={{0,1},{1,0},{2,3},{3,2},{4,5},{5,4},{6,7},{7,6},{8,9},{9,8},{10,11... | collective-permute-start | bytes 1572872 | tf_op jit(solution)/shard_map/ppermute | solution.py:484
  4.6 43.3 %collective-permute-start.7 = (bf16[2,256,1536]{2,1,0:T(8,128)(2,1)S(1)}, bf16[2,256,1536]{2,1,0:T(8,128)(2,1)}, u32[]{:S(2)}, u32[]{:S(2)}) collective-permute-start(bf16[2,256,1536]{2,1,0:T(8,128)(2,1)S(1)} %slice_select_fusion), channel_id=1, source_target_pairs={{0,1},{1,0},{2,3},{3,2},{4,5},{5,4},{6,7},{7,6},{8,9},{9,8},{10,11... | collective-permute-start | bytes 4718600 | tf_op jit(solution)/shard_map/ppermute | solution.py:484
  14.1 0.8 copy-start.25
  18.3 39.1 %all-to-all-start = ((bf16[16,40,1024]{2,1,0:T(8,128)(2,1)}), bf16[16,40,1024]{2,1,0:T(8,128)(2,1)S(1)}, u32[]{:S(2)}, u32[]{:S(2)}) async-start(bf16[16,40,1024]{2,1,0:T(8,128)(2,1)} %bitcast.35), calls=%async_computation | async-start | bytes 2621440 | tf_op jit(solution)/shard_map/all_to_all | solution.py:511
  57.4 1.1 copy-start
  58.5 92.1 %all-to-all-start.1 = ((bf16[16,40,3072]{2,1,0:T(8,128)(2,1)}), bf16[16,40,3072]{2,1,0:T(8,128)(2,1)}, u32[]{:S(2)}, u32[]{:S(2)}) async-start(bf16[16,40,3072]{2,1,0:T(8,128)(2,1)} %bitcast.31), calls=%async_computation.1 | async-start | bytes 7864320 | tf_op jit(solution)/shard_map/all_to_all | solution.py:511
  63.7 3.0 %copy-start.23 = (s32[4]{0:T(128)S(1)}, s32[4]{0:T(128)}, u32[]{:S(2)}) copy-start(s32[4]{0:T(128)} %param.8) | copy-start | bytes 52
  63.7 4.5 %copy-start.12 = (s32[1,16,40]{2,1,0:T(8,128)S(1)}, s32[1,16,40]{2,1,0:T(8,128)}, u32[]{:S(2)}) copy-start(s32[1,16,40]{2,1,0:T(8,128)} %param.7) | copy-start | bytes 7684
  65.4 27.4 %collective-permute-start = (bf16[1,256,2048]{2,1,0:T(8,128)(2,1)S(1)}, bf16[1,256,2048]{2,1,0:T(8,128)(2,1)S(1)}, u32[]{:S(2)}, u32[]{:S(2)}) collective-permute-start(bf16[1,256,2048]{2,1,0:T(8,128)(2,1)S(1)} %slice_select_fusion.1), channel_id=1, source_target_pairs={{0,1},{1,0},{2,3},{3,2},{4,5},{5,4},{6,7},{7,6},{8,9},{9,8},{10,11... | collective-permute-start | bytes 3145736 | tf_op jit(solution)/shard_map/ppermute | solution.py:484
  70.6 11.3 %copy-start.21 = (s32[512]{0:T(512)}, s32[512]{0:T(512)S(1)}, u32[]{:S(2)}) copy-start(s32[512]{0:T(512)S(1)} %broadcast_add_fusion.1) | copy-start | bytes 6148
  70.7 11.2 %copy-start.1 = (s32[512,1]{1,0:T(8,128)}, s32[512,1]{1,0:T(8,128)S(1)}, u32[]{:S(2)}) copy-start(s32[512,1]{1,0:T(8,128)S(1)} %copy.33.seg_col_ref) | copy-start | bytes 6148
  78.8 8.7 %collective-permute-start.2 = (f32[128,128]{1,0:T(8,128)}, f32[128,128]{1,0:T(8,128)S(1)}, u32[]{:S(2)}, u32[]{:S(2)}) collective-permute-start(f32[128,128]{1,0:T(8,128)} %get-tuple-element.84), channel_id=1, source_target_pairs={{0,2},{2,0},{4,6},{6,4},{8,10},{10,8},{12,14},{14,12},{16,18},{18,... | collective-permute-start | bytes 196616 | tf_op jit(solution)/shard_map/ppermute | solution.py:224
  79.5 9.1 %collective-permute-start.3 = (f32[128,128]{1,0:T(8,128)}, f32[128,128]{1,0:T(8,128)S(1)}, u32[]{:S(2)}, u32[]{:S(2)}) collective-permute-start(f32[128,128]{1,0:T(8,128)} %get-tuple-element.85), channel_id=1, source_target_pairs={{0,4},{2,6},{4,0},{6,2},{8,12},{10,14},{12,8},{14,10},{16,20},{18,... | collective-permute-start | bytes 196616 | tf_op jit(solution)/shard_map/ppermute | solution.py:224
  79.7 10.7 %collective-permute-start.4 = (f32[128,128]{1,0:T(8,128)}, f32[128,128]{1,0:T(8,128)S(1)}, u32[]{:S(2)}, u32[]{:S(2)}) collective-permute-start(f32[128,128]{1,0:T(8,128)} %get-tuple-element.86), channel_id=1, source_target_pairs={{0,6},{2,4},{4,2},{6,0},{8,14},{10,12},{12,10},{14,8},{16,22},{18,... | collective-permute-start | bytes 196616 | tf_op jit(solution)/shard_map/ppermute | solution.py:224
  87.5 2.9 %copy-start.16 = (f32[128,128]{1,0:T(8,128)}, f32[128,128]{1,0:T(8,128)S(1)}, u32[]{:S(2)}) copy-start(f32[128,128]{1,0:T(8,128)S(1)} %collective-permute-done.2.refs_1_) | copy-start | bytes 196612
  88.5 1.9 copy-start.17
  92.8 4.9 %copy-start.24 = (bf16[1,256,2048]{2,1,0:T(8,128)(2,1)}, bf16[1,256,2048]{2,1,0:T(8,128)(2,1)S(1)}, u32[]{:S(2)}) copy-start(bf16[1,256,2048]{2,1,0:T(8,128)(2,1)S(1)} %collective-permute-done.refs_3_) | copy-start | bytes 3145732
  92.8 57.0 %collective-permute-start.6 = (bf16[128,128]{1,0:T(8,128)(2,1)}, bf16[128,128]{1,0:T(8,128)(2,1)S(1)}, u32[]{:S(2)}, u32[]{:S(2)}) collective-permute-start(bf16[128,128]{1,0:T(8,128)(2,1)} %get-tuple-element.105), channel_id=1, source_target_pairs={{0,16},{2,18},{4,20},{6,22},{8,24},{10,26},{12,28},{14,30},{1,17},... | collective-permute-start | bytes 98312 | tf_op jit(solution)/shard_map/ppermute | solution.py:255
  95.7 54.7 %collective-permute-start.5 = (bf16[128,128]{1,0:T(8,128)(2,1)}, bf16[128,128]{1,0:T(8,128)(2,1)S(1)}, u32[]{:S(2)}, u32[]{:S(2)}) collective-permute-start(bf16[128,128]{1,0:T(8,128)(2,1)} %get-tuple-element.105), channel_id=1, source_target_pairs={{0,8},{2,10},{4,12},{6,14},{8,16},{10,18},{12,20},{14,22},{16,24},... | collective-permute-start | bytes 98312 | tf_op jit(solution)/shard_map/ppermute | solution.py:255
  149.7 12.3 %copy-start.19 = (bf16[128,128]{1,0:T(8,128)(2,1)}, bf16[128,128]{1,0:T(8,128)(2,1)S(1)}, u32[]{:S(2)}) copy-start(bf16[128,128]{1,0:T(8,128)(2,1)S(1)} %collective-permute-done.6.refs_5_) | copy-start | bytes 98308
  150.4 11.6 %copy-start.20 = (bf16[128,128]{1,0:T(8,128)(2,1)}, bf16[128,128]{1,0:T(8,128)(2,1)S(1)}, u32[]{:S(2)}) copy-start(bf16[128,128]{1,0:T(8,128)(2,1)S(1)} %collective-permute-done.5.refs_4_) | copy-start | bytes 98308
  150.6 38.5 %all-to-all-start.3 = ((bf16[16,40,1024]{2,1,0:T(8,128)(2,1)}), bf16[16,40,1024]{2,1,0:T(8,128)(2,1)S(1)}, u32[]{:S(2)}, u32[]{:S(2)}) async-start(bf16[16,40,1024]{2,1,0:T(8,128)(2,1)} %bitcast.33), calls=%async_computation.3 | async-start | bytes 2621440 | tf_op jit(solution)/shard_map/all_to_all | solution.py:511
  162.1 4.8 %collective-permute-start.8 = (f32[384,128]{1,0:T(8,128)}, f32[384,128]{1,0:T(8,128)S(1)}, u32[]{:S(2)}, u32[]{:S(2)}) collective-permute-start(f32[384,128]{1,0:T(8,128)} %get-tuple-element.120), channel_id=1, source_target_pairs={{0,2},{2,0},{4,6},{6,4},{8,10},{10,8},{12,14},{14,12},{16,18},{18,... | collective-permute-start | bytes 589832 | tf_op jit(solution)/shard_map/ppermute | solution.py:224
  162.5 8.3 %collective-permute-start.9 = (f32[384,128]{1,0:T(8,128)}, f32[384,128]{1,0:T(8,128)S(1)}, u32[]{:S(2)}, u32[]{:S(2)}) collective-permute-start(f32[384,128]{1,0:T(8,128)} %get-tuple-element.121), channel_id=1, source_target_pairs={{0,4},{2,6},{4,0},{6,2},{8,12},{10,14},{12,8},{14,10},{16,20},{18,... | collective-permute-start | bytes 589832 | tf_op jit(solution)/shard_map/ppermute | solution.py:224
  162.8 18.2 %collective-permute-start.10 = (f32[384,128]{1,0:T(8,128)}, f32[384,128]{1,0:T(8,128)S(1)}, u32[]{:S(2)}, u32[]{:S(2)}) collective-permute-start(f32[384,128]{1,0:T(8,128)} %get-tuple-element.122), channel_id=1, source_target_pairs={{0,6},{2,4},{4,2},{6,0},{8,14},{10,12},{12,10},{14,8},{16,22},{18,... | collective-permute-start | bytes 589832 | tf_op jit(solution)/shard_map/ppermute | solution.py:224
  166.6 17.5 %collective-permute-start.11 = (f32[128,128]{1,0:T(8,128)}, f32[128,128]{1,0:T(8,128)S(1)}, u32[]{:S(2)}, u32[]{:S(2)}) collective-permute-start(f32[128,128]{1,0:T(8,128)} %get-tuple-element.136), channel_id=1, source_target_pairs={{0,2},{2,0},{4,6},{6,4},{8,10},{10,8},{12,14},{14,12},{16,18},{18,... | collective-permute-start | bytes 196616 | tf_op jit(solution)/shard_map/ppermute | solution.py:224
  166.6 17.4 %collective-permute-start.12 = (f32[128,128]{1,0:T(8,128)}, f32[128,128]{1,0:T(8,128)S(1)}, u32[]{:S(2)}, u32[]{:S(2)}) collective-permute-start(f32[128,128]{1,0:T(8,128)} %get-tuple-element.137), channel_id=1, source_target_pairs={{0,4},{2,6},{4,0},{6,2},{8,12},{10,14},{12,8},{14,10},{16,20},{18,... | collective-permute-start | bytes 196616 | tf_op jit(solution)/shard_map/ppermute | solution.py:224
  166.9 14.1 %copy-start.7 = (f32[384,128]{1,0:T(8,128)}, f32[384,128]{1,0:T(8,128)S(1)}, u32[]{:S(2)}) copy-start(f32[384,128]{1,0:T(8,128)S(1)} %collective-permute-done.8.refs_1_) | copy-start | bytes 589828
  166.9 17.2 %collective-permute-start.13 = (f32[128,128]{1,0:T(8,128)}, f32[128,128]{1,0:T(8,128)S(1)}, u32[]{:S(2)}, u32[]{:S(2)}) collective-permute-start(f32[128,128]{1,0:T(8,128)} %get-tuple-element.138), channel_id=1, source_target_pairs={{0,6},{2,4},{4,2},{6,0},{8,14},{10,12},{12,10},{14,8},{16,22},{18,... | collective-permute-start | bytes 196616 | tf_op jit(solution)/shard_map/ppermute | solution.py:224
  170.8 10.2 %copy-start.8 = (f32[384,128]{1,0:T(8,128)}, f32[384,128]{1,0:T(8,128)S(1)}, u32[]{:S(2)}) copy-start(f32[384,128]{1,0:T(8,128)S(1)} %collective-permute-done.9.refs_2_) | copy-start | bytes 589828
  181.0 0.7 copy-start.9
  184.1 18.2 %copy-start.13 = (f32[128,128]{1,0:T(8,128)}, f32[128,128]{1,0:T(8,128)S(1)}, u32[]{:S(2)}) copy-start(f32[128,128]{1,0:T(8,128)S(1)} %collective-permute-done.11.refs_1_) | copy-start | bytes 196612
  184.1 18.2 %copy-start.14 = (f32[128,128]{1,0:T(8,128)}, f32[128,128]{1,0:T(8,128)S(1)}, u32[]{:S(2)}) copy-start(f32[128,128]{1,0:T(8,128)S(1)} %collective-permute-done.12.refs_2_) | copy-start | bytes 196612
  184.1 18.2 %copy-start.15 = (f32[128,128]{1,0:T(8,128)}, f32[128,128]{1,0:T(8,128)S(1)}, u32[]{:S(2)}) copy-start(f32[128,128]{1,0:T(8,128)S(1)} %collective-permute-done.13.refs_3_) | copy-start | bytes 196612
  184.1 18.2 %collective-permute-start.15 = (bf16[384,128]{1,0:T(8,128)(2,1)}, bf16[384,128]{1,0:T(8,128)(2,1)S(1)}, u32[]{:S(2)}, u32[]{:S(2)}) collective-permute-start(bf16[384,128]{1,0:T(8,128)(2,1)} %get-tuple-element.153), channel_id=1, source_target_pairs={{0,16},{2,18},{4,20},{6,22},{8,24},{10,26},{12,28},{14,30},{1,17},... | collective-permute-start | bytes 294920 | tf_op jit(solution)/shard_map/ppermute | solution.py:255
  186.9 15.4 %collective-permute-start.14 = (bf16[384,128]{1,0:T(8,128)(2,1)}, bf16[384,128]{1,0:T(8,128)(2,1)S(1)}, u32[]{:S(2)}, u32[]{:S(2)}) collective-permute-start(bf16[384,128]{1,0:T(8,128)(2,1)} %get-tuple-element.153), channel_id=1, source_target_pairs={{0,8},{2,10},{4,12},{6,14},{8,16},{10,18},{12,20},{14,22},{16,24},... | collective-permute-start | bytes 294920 | tf_op jit(solution)/shard_map/ppermute | solution.py:255
  189.1 13.2 %copy-start.2 = (bf16[16,40,1024]{2,1,0:T(8,128)(2,1)}, bf16[16,40,1024]{2,1,0:T(8,128)(2,1)S(1)}, u32[]{:S(2)}) copy-start(bf16[16,40,1024]{2,1,0:T(8,128)(2,1)S(1)} %all-to-all-done.3) | copy-start | bytes 3932164
  189.1 40.4 %all-to-all-start.2 = ((bf16[16,40,1024]{2,1,0:T(8,128)(2,1)}), bf16[16,40,1024]{2,1,0:T(8,128)(2,1)S(1)}, u32[]{:S(2)}, u32[]{:S(2)}) async-start(bf16[16,40,1024]{2,1,0:T(8,128)(2,1)} %bitcast.17), calls=%async_computation.2 | async-start | bytes 2621440 | tf_op jit(solution)/shard_map/all_to_all | solution.py:511
  202.3 0.6 copy-start.10
  203.0 0.6 copy-start.11
  205.9 8.1 %collective-permute-start.16 = (f32[384,128]{1,0:T(8,128)}, f32[384,128]{1,0:T(8,128)S(1)}, u32[]{:S(2)}, u32[]{:S(2)}) collective-permute-start(f32[384,128]{1,0:T(8,128)} %get-tuple-element.155), channel_id=1, source_target_pairs={{0,2},{2,0},{4,6},{6,4},{8,10},{10,8},{12,14},{14,12},{16,18},{18,... | collective-permute-start | bytes 589832 | tf_op jit(solution)/shard_map/ppermute | solution.py:224
  206.3 8.6 %collective-permute-start.17 = (f32[384,128]{1,0:T(8,128)}, f32[384,128]{1,0:T(8,128)S(1)}, u32[]{:S(2)}, u32[]{:S(2)}) collective-permute-start(f32[384,128]{1,0:T(8,128)} %get-tuple-element.156), channel_id=1, source_target_pairs={{0,4},{2,6},{4,0},{6,2},{8,12},{10,14},{12,8},{14,10},{16,20},{18,... | collective-permute-start | bytes 589832 | tf_op jit(solution)/shard_map/ppermute | solution.py:224
  206.6 16.0 %collective-permute-start.18 = (f32[384,128]{1,0:T(8,128)}, f32[384,128]{1,0:T(8,128)S(1)}, u32[]{:S(2)}, u32[]{:S(2)}) collective-permute-start(f32[384,128]{1,0:T(8,128)} %get-tuple-element.157), channel_id=1, source_target_pairs={{0,6},{2,4},{4,2},{6,0},{8,14},{10,12},{12,10},{14,8},{16,22},{18,... | collective-permute-start | bytes 589832 | tf_op jit(solution)/shard_map/ppermute | solution.py:224
  214.0 8.6 %copy-start.4 = (f32[384,128]{1,0:T(8,128)}, f32[384,128]{1,0:T(8,128)S(1)}, u32[]{:S(2)}) copy-start(f32[384,128]{1,0:T(8,128)S(1)} %collective-permute-done.16.refs_5_) | copy-start | bytes 589828
  214.9 7.8 %copy-start.5 = (f32[384,128]{1,0:T(8,128)}, f32[384,128]{1,0:T(8,128)S(1)}, u32[]{:S(2)}) copy-start(f32[384,128]{1,0:T(8,128)S(1)} %collective-permute-done.17.refs_6_) | copy-start | bytes 589828
  222.6 0.7 copy-start.6
  229.5 1.1 copy-start.3
  (1 other events, 0.6 us)

commit v12 on v11

--- a/solution.py
+++ b/solution.py
@@ -18,17 +18,29 @@
 ATTEND_WEIGHT = 145
 
 
+def pick_kernel(*refs):
+    half = len(refs) // 2
+    for pick, onehot in zip(refs[:half], refs[half:]):
+        rows = lax.broadcasted_iota(jnp.int32, onehot.shape, 1)
+        onehot[...] = jnp.where(pick[...] == rows, 1.0, 0.0).astype(onehot.dtype)
+
+
+def pick_matrices(send_rows, rows):
+    head_count, place = lax.axis_size("head"), lax.axis_index("head")
+    slots = send_rows.reshape(-1, 1)
+    picks, length = (slots,), head_count * rows
+    if head_count == 2:
+        picks, length = (slots - place * rows, slots - (1 - place) * rows), rows
+    return pl.pallas_call(
+        pick_kernel,
+        out_shape=(jax.ShapeDtypeStruct((slots.shape[0], length), jnp.bfloat16),) * len(picks),
+        name="pick_matrices",
+    )(*picks)
+
+
 def pack_kernel(place_ref, *refs):
-    count = (len(refs) - 1) // 3
-    picks, sources = refs[:count], refs[count : 2 * count]
-    out_ref, chosen = refs[2 * count], refs[2 * count + 1 :]
-
-    @pl.when((pl.program_id(0) == 0) & (pl.program_id(1) == 0))
-    def _():
-        for pick, onehot in zip(picks, chosen):
-            rows = lax.broadcasted_iota(jnp.int32, onehot.shape, 1)
-            onehot[...] = jnp.where(pick[...] == rows, 1.0, 0.0).astype(onehot.dtype)
-
+    count = (len(refs) - 1) // 2
+    chosen, sources, out_ref = refs[:count], refs[count : 2 * count], refs[-1]
     total = None
     for source, onehot in zip(sources, chosen):
         part = jnp.dot(onehot[...], source[0], preferred_element_type=jnp.float32)
@@ -53,10 +65,9 @@
         grid_spec=pltpu.PrefetchScalarGridSpec(
             num_scalar_prefetch=1,
             grid=(planes, blocks),
-            in_specs=[pl.BlockSpec((slots, 1), lambda p, j, place_ref: (0, 0)) for _ in picks]
+            in_specs=[pl.BlockSpec(pick.shape, lambda p, j, place_ref: (0, 0)) for pick in picks]
             + [source_spec(*source) for source in sources],
             out_specs=pl.BlockSpec((slots, width), lambda p, j, place_ref: (0, p * blocks + j)),
-            scratch_shapes=[pltpu.VMEM((slots, length), jnp.bfloat16) for length in lens],
         ),
         cost_estimate=pl.CostEstimate(
             flops=PACK_WEIGHT * 2 * slots * sum(lens) * planes * columns,
@@ -489,16 +500,13 @@
     return jnp.moveaxis(incoming, 0, 1).reshape(planes, head_count * rows, columns)
 
 
-def pack_chunk(qkv, incoming, send_rows, plane_start, planes, start, columns, offset=0):
+def pack_chunk(qkv, incoming, picks, plane_start, planes, start, columns, offset=0):
     head_count = lax.axis_size("head")
     place = lax.axis_index("head")
-    rows = qkv.shape[1]
     mine = qkv.shape[2] // head_count
-    slots = send_rows.reshape(-1, 1)
     width = math.gcd(math.gcd(columns, start), math.gcd(mine, 512))
-    picks, sources = (slots,), ((incoming, 0, lambda at, width: offset // width),)
+    sources = ((incoming, 0, lambda at, width: offset // width),)
     if head_count == 2:
-        picks = (slots - place * rows, slots - (1 - place) * rows)
         sources = (
             (qkv, plane_start, lambda at, width: at * (mine // width) + start // width),
         ) + sources
@@ -533,7 +541,7 @@
     tail_slots = jnp.broadcast_to(in_tail.astype(jnp.bfloat16), (land_row.shape[1], HEAD_DIM))
     gain = norm_gain.reshape(1, -1)
 
-    rows = send_rows[0]
+    rows = pick_matrices(send_rows[0], qkv.shape[1])
     head_share = columns // HEAD_DIM
     first = max(2, head_share // 4) * HEAD_DIM
     second = columns - first

time: 240 us -> 240 us (level)
  transfers between devices with their start and end apart: 23 -> 23, of which waited for: 12 -> 11; matrix products, arithmetic and copies ran while one was open for 6% -> 6% of each run, Pallas kernels for 24% -> 25%
where the time goes in v12:
time: 240 us; the launch traced here: 237 us
  waiting for transfers between devices  98.6 us (41%)
  Pallas kernels  65.5 us (27%)
  starting transfers between devices  49.9 us (21%)
  local copies, waits for them, and re-layouts  12.4 us (5%)
  other arithmetic  10.1 us (4%)
    ppermute x4, waiting for transfers between devices, pass_totals(): lax.ppermute(sums[near], 'seq', [(i, i + step) for i in range(seq_count -...  46.4 us
    all_to_all x4, starting transfers between devices, to_owners(): lax.all_to_all(outgoing, 'seq', split_axis=0, concat_axis=0, tiled=True)  28.1 us
    ppermute x3, waiting for transfers between devices, swap_heads(): return lax.ppermute(outgoing, 'head', [(0, 1), (1, 0)])  26.7 us
    ppermute x12, waiting for transfers between devices, swap_places(): return lax.ppermute(value, 'seq', [(i, i ^ k) for i in range(seq_count)])  23.1 us
    pallas_call x4, Pallas kernels, pack_rows(): pl.pallas_call(pack_kernel, out_shape=jax.ShapeDtypeStruct((slots, planes...  16.4 us
    ppermute x4, starting transfers between devices, pass_totals(): lax.ppermute(sums[near], 'seq', [(i, i + step) for i in range(seq_count -...  10 us
    pallas_call x2, Pallas kernels, unpack_keys_values(): pl.pallas_call(unpack_kernel, out_shape=(packed, packed), grid=(blocks,),...  9.14 us
    ppermute x12, starting transfers between devices, swap_places(): return lax.ppermute(value, 'seq', [(i, i ^ k) for i in range(seq_count)])  8.85 us
  transfers between devices with their start and end apart: 23, of which 11 were waited for; matrix products, arithmetic and copies ran while one was open for 6% of the time, Pallas kernels for 25%

profile of v12, /device:TPU:11, one launch (start us, length us, event | category | flops | bytes accessed | tf_op | source)
XLA Modules:
  0.0 237.5 jit_solution(10452541696107722066)
XLA Ops:
  0.0 1.3 slice_select_fusion.2
  1.3 1.3 collective-permute-start.1
  2.6 2.0 slice_select_fusion
  4.9 0.9 sub.91.refs_1_
  5.8 0.9 sub.90.refs_0_
  6.7 2.1 pick_matrices.1
  8.8 5.4 %collective-permute-done.1.refs_3_ = bf16[2,256,512]{2,1,0:T(8,128)(2,1)S(1)} collective-permute-done((bf16[2,256,512]{2,1,0:T(8,128)(2,1)S(1)}, bf16[2,256,512]{2,1,0:T(8,128)(2,1)S(1)}, u32[]{:S(2)}, u32[]{:S(2)}) %collective-permute-start.1) | collective-permute-done | bytes 524320 | tf_op jit(solution)/shard_map/ppermute | solution.py:495
  14.9 3.1 %pack_rows.4 = bf16[640,1024]{1,0:T(8,128)(2,1)} custom-call(s32[1]{0:T(128)} %bitcast.8.place_ref, bf16[640,256]{1,0:T(8,128)(2,1)} %get-tuple-element.85.refs_0_, bf16[640,256]{1,0:T(8,128)(2,1)} %get-tuple-element.86.refs_1_, bf16[3,256,4096]{2,1,0:T(8,128)(2,1)} %refs_2_.7, bf16[2,256,512]{2,1,0:T(8,128)(2,1)} %copy-done.25), custom_call_target="tpu_custom_call" | custom-call | flops 13421772800 | bytes 2359296 | tf_op jit(solution)/shard_map/pack_rows/pallas_call | solution.py:62
  18.0 8.6 %all-to-all-start = ((bf16[16,40,1024]{2,1,0:T(8,128)(2,1)}), bf16[16,40,1024]{2,1,0:T(8,128)(2,1)S(1)}, u32[]{:S(2)}, u32[]{:S(2)}) async-start(bf16[16,40,1024]{2,1,0:T(8,128)(2,1)} %bitcast.35), calls=%async_computation | async-start | bytes 2621440 | tf_op jit(solution)/shard_map/all_to_all | solution.py:519
  26.6 21.3 %collective-permute-done.7.refs_3_ = bf16[2,256,1536]{2,1,0:T(8,128)(2,1)} collective-permute-done((bf16[2,256,1536]{2,1,0:T(8,128)(2,1)S(1)}, bf16[2,256,1536]{2,1,0:T(8,128)(2,1)}, u32[]{:S(2)}, u32[]{:S(2)}) %collective-permute-start.7) | collective-permute-done | bytes 1572896 | tf_op jit(solution)/shard_map/ppermute | solution.py:495
  47.9 7.0 %pack_rows.7 = bf16[640,3072]{1,0:T(8,128)(2,1)} custom-call(s32[1]{0:T(128)} %bitcast.8.place_ref, bf16[640,256]{1,0:T(8,128)(2,1)} %get-tuple-element.85.refs_0_, bf16[640,256]{1,0:T(8,128)(2,1)} %get-tuple-element.86.refs_1_, bf16[3,256,4096]{2,1,0:T(8,128)(2,1)} %refs_2_.7, bf16[2,256,1536]{2,1,0:T(8,128)(2,1)} %collective-permute-done.7.refs_3_), custom_call_target="tpu_custom_call" | custom-call | flops 40265318400 | bytes 7077888 | tf_op jit(solution)/shard_map/pack_rows/pallas_call | solution.py:62
  54.9 2.3 all-to-all-done
  57.2 1.1 copy-done
  58.2 5.2 %all-to-all-start.1 = ((bf16[16,40,3072]{2,1,0:T(8,128)(2,1)}), bf16[16,40,3072]{2,1,0:T(8,128)(2,1)}, u32[]{:S(2)}, u32[]{:S(2)}) async-start(bf16[16,40,3072]{2,1,0:T(8,128)(2,1)} %bitcast.31), calls=%async_computation.1 | async-start | bytes 7864320 | tf_op jit(solution)/shard_map/all_to_all | solution.py:519
  63.4 1.7 slice_select_fusion.1
  65.1 1.3 collective-permute-start
  74.7 3.7 %block_update.2 = (f32[128,128]{1,0:T(8,128)}, f32[128,128]{1,0:T(8,128)}, f32[128,128]{1,0:T(8,128)}, f32[128,128]{1,0:T(8,128)}) custom-call(s32[1]{0:T(128)} %bitcast.6.place_ref, bf16[640,128]{1,0:T(8,128)(2,1)} %broadcast_in_dim.2.tail_ref, bf16[640,1024]{1,0:T(8,128)(2,1)} %bitcast.27, bf16[640,1024]{1,0:T(8,128)(2,1)} %bitcast.28), custom_call_target="tpu_custom_call" | custom-call | flops 83886080 | bytes 1572864 | tf_op jit(solution)/shard_map/block_update/pallas_call | solution.py:106
  79.3 1.4 collective-permute-start.4
  81.4 2.4 block_tables.1
  83.8 3.3 %unpack_keys_values.2 = (bf16[512,2048]{1,0:T(8,128)(2,1)}, bf16[512,2048]{1,0:T(8,128)(2,1)}) custom-call(bf16[512,640]{1,0:T(8,128)(2,1)} %get-tuple-element.101.order_ref, bf16[640,1024]{1,0:T(8,128)(2,1)} %bitcast.29, bf16[640,1024]{1,0:T(8,128)(2,1)} %bitcast.30), custom_call_target="tpu_custom_call" | custom-call | flops 671088640 | bytes 2359296 | tf_op jit(solution)/shard_map/unpack_keys_values/pallas_call | solution.py:176
  87.1 2.9 %collective-permute-done.4.refs_3_ = f32[128,128]{1,0:T(8,128)S(1)} collective-permute-done((f32[128,128]{1,0:T(8,128)}, f32[128,128]{1,0:T(8,128)S(1)}, u32[]{:S(2)}, u32[]{:S(2)}) %collective-permute-start.4) | collective-permute-done | bytes 65568 | tf_op jit(solution)/shard_map/ppermute | solution.py:235
  90.6 1.7 sum_pieces.4
  92.3 3.2 %collective-permute-start.6 = (bf16[128,128]{1,0:T(8,128)(2,1)}, bf16[128,128]{1,0:T(8,128)(2,1)S(1)}, u32[]{:S(2)}, u32[]{:S(2)}) collective-permute-start(bf16[128,128]{1,0:T(8,128)(2,1)} %get-tuple-element.109), channel_id=1, source_target_pairs={{0,16},{2,18},{4,20},{6,22},{8,24},{10,26},{12,28},{14,30},{1,17},... | collective-permute-start | bytes 98312 | tf_op jit(solution)/shard_map/ppermute | solution.py:266
  95.5 1.9 collective-permute-start.5
  97.4 3.2 %pack_rows.6 = bf16[640,1024]{1,0:T(8,128)(2,1)} custom-call(s32[1]{0:T(128)} %bitcast.8.place_ref, bf16[640,256]{1,0:T(8,128)(2,1)} %get-tuple-element.85.refs_0_, bf16[640,256]{1,0:T(8,128)(2,1)} %get-tuple-element.86.refs_1_, bf16[3,256,4096]{2,1,0:T(8,128)(2,1)} %refs_2_.7, bf16[1,256,2048]{2,1,0:T(8,128)(2,1)} %copy-done.24), custom_call_target="tpu_custom_call" | custom-call | flops 13421772800 | bytes 2359296 | tf_op jit(solution)/shard_map/pack_rows/pallas_call | solution.py:62
  100.6 3.1 %pack_rows.5 = bf16[640,1024]{1,0:T(8,128)(2,1)} custom-call(s32[1]{0:T(128)} %bitcast.8.place_ref, bf16[640,256]{1,0:T(8,128)(2,1)} %get-tuple-element.85.refs_0_, bf16[640,256]{1,0:T(8,128)(2,1)} %get-tuple-element.86.refs_1_, bf16[3,256,4096]{2,1,0:T(8,128)(2,1)} %refs_2_.7, bf16[1,256,2048]{2,1,0:T(8,128)(2,1)} %copy-done.24), custom_call_target="tpu_custom_call" | custom-call | flops 13421772800 | bytes 2359296 | tf_op jit(solution)/shard_map/pack_rows/pallas_call | solution.py:62
  103.8 45.7 %collective-permute-done.6.refs_5_ = bf16[128,128]{1,0:T(8,128)(2,1)S(1)} collective-permute-done((bf16[128,128]{1,0:T(8,128)(2,1)}, bf16[128,128]{1,0:T(8,128)(2,1)S(1)}, u32[]{:S(2)}, u32[]{:S(2)}) %collective-permute-start.6) | collective-permute-done | bytes 32800 | tf_op jit(solution)/shard_map/ppermute | solution.py:266
  150.3 7.0 %all-to-all-start.3 = ((bf16[16,40,1024]{2,1,0:T(8,128)(2,1)}), bf16[16,40,1024]{2,1,0:T(8,128)(2,1)S(1)}, u32[]{:S(2)}, u32[]{:S(2)}) async-start(bf16[16,40,1024]{2,1,0:T(8,128)(2,1)} %bitcast.33), calls=%async_computation.3 | async-start | bytes 2621440 | tf_op jit(solution)/shard_map/all_to_all | solution.py:519
  157.3 4.5 %block_update.3 = (f32[384,128]{1,0:T(8,128)}, f32[384,128]{1,0:T(8,128)}, f32[384,128]{1,0:T(8,128)}, f32[384,128]{1,0:T(8,128)}) custom-call(s32[1]{0:T(128)} %bitcast.6.place_ref, bf16[640,128]{1,0:T(8,128)(2,1)} %broadcast_in_dim.2.tail_ref, bf16[640,3072]{1,0:T(8,128)(2,1)} %bitcast.16.keys_ref.values_ref, bf16[640,3072]{1,0:T(8,128)(2,1)} %bitcast.16.keys_ref.values_ref), custom_call_target="tpu_custom_call" | custom-call | flops 251658240 | bytes 4718592 | tf_op jit(solution)/shard_map/block_update/pallas_call | solution.py:106
  162.5 1.5 collective-permute-start.10
  164.6 1.7 sum_pieces.6
  166.7 1.8 collective-permute-start.13
  169.1 1.5 collective-permute-done.9.refs_2_
  170.5 10.2 %collective-permute-done.10.refs_3_ = f32[384,128]{1,0:T(8,128)S(1)} collective-permute-done((f32[384,128]{1,0:T(8,128)}, f32[384,128]{1,0:T(8,128)S(1)}, u32[]{:S(2)}, u32[]{:S(2)}) %collective-permute-start.10) | collective-permute-done | bytes 196640 | tf_op jit(solution)/shard_map/ppermute | solution.py:235
  181.4 2.4 sum_pieces.5
  183.9 2.8 %collective-permute-start.15 = (bf16[384,128]{1,0:T(8,128)(2,1)}, bf16[384,128]{1,0:T(8,128)(2,1)S(1)}, u32[]{:S(2)}, u32[]{:S(2)}) collective-permute-start(bf16[384,128]{1,0:T(8,128)(2,1)} %get-tuple-element.157), channel_id=1, source_target_pairs={{0,16},{2,18},{4,20},{6,22},{8,24},{10,26},{12,28},{14,30},{1,17},... | collective-permute-start | bytes 294920 | tf_op jit(solution)/shard_map/ppermute | solution.py:266
  186.7 2.1 collective-permute-start.14
  188.8 7.4 %all-to-all-start.2 = ((bf16[16,40,1024]{2,1,0:T(8,128)(2,1)}), bf16[16,40,1024]{2,1,0:T(8,128)(2,1)S(1)}, u32[]{:S(2)}, u32[]{:S(2)}) async-start(bf16[16,40,1024]{2,1,0:T(8,128)(2,1)} %bitcast.17), calls=%async_computation.2 | async-start | bytes 2621440 | tf_op jit(solution)/shard_map/all_to_all | solution.py:519
  196.2 5.8 %unpack_keys_values.3 = (bf16[512,2048]{1,0:T(8,128)(2,1)}, bf16[512,2048]{1,0:T(8,128)(2,1)}) custom-call(bf16[512,640]{1,0:T(8,128)(2,1)} %get-tuple-element.101.order_ref, bf16[640,3072]{1,0:T(8,128)(2,1)} %bitcast.16.keys_ref.values_ref, bf16[640,3072]{1,0:T(8,128)(2,1)} %bitcast.16.keys_ref.values_ref, ...), custom_call_target="tpu_custom_call", output_to_operand_aliasing={{0}: (3, {}), {1}: (4, {})} | custom-call | flops 2013265920 | bytes 7077888 | tf_op jit(solution)/shard_map/unpack_keys_values/pallas_call | solution.py:176
  203.4 2.3 sum_pieces.7
  206.3 1.5 collective-permute-start.18
  207.8 5.9 %attend_locally.1 = (bf16[512,1024]{1,0:T(8,128)(2,1)}, f32[512,1024]{1,0:T(8,128)}) custom-call(bf16[512,640]{1,0:T(8,128)(2,1)} %get-tuple-element.101.order_ref, bf16[512,512]{1,0:T(8,128)(2,1)} %get-tuple-element.102.causal_ref, bf16[512,128]{1,0:T(8,128)(2,1)} %get-tuple-element.103.carried_ref, bf16[640,1024]{1,0:T(8,128)(2,1)} %bitcast.32, ...), custom_call_target="tpu_custom_call" | custom-call | flops 25300041728 | bytes 6553600 | tf_op jit(solution)/shard_map/attend_locally/pallas_call | solution.py:427
  213.8 0.8 collective-permute-done.17.refs_6_
  214.6 7.8 %collective-permute-done.18.refs_7_ = f32[384,128]{1,0:T(8,128)S(1)} collective-permute-done((f32[384,128]{1,0:T(8,128)}, f32[384,128]{1,0:T(8,128)S(1)}, u32[]{:S(2)}, u32[]{:S(2)}) %collective-permute-start.18) | collective-permute-done | bytes 196640 | tf_op jit(solution)/shard_map/ppermute | solution.py:235
  223.0 2.5 %assemble_states.1.states_ref = bf16[4096,128]{1,0:T(8,128)(2,1)} custom-call(s32[1]{0:T(128)} %bitcast.6.place_ref, f32[128,128]{1,0:T(8,128)} %get-tuple-element.149.refs_0_, f32[128,128]{1,0:T(8,128)} %copy-done.13, f32[128,128]{1,0:T(8,128)} %copy-done.14, f32[128,128]{1,0:T(8,128)} %copy-done.15, f32[384,128]{1,0:T(8,128)} %get-tuple-element.158.refs_4_, ...), custom_call_target="tpu_custom_call" | custom-call | flops 2097152 | bytes 2097152 | tf_op jit(solution)/shard_map/assemble_states/pallas_call | solution.py:309
  225.5 3.8 %finish.1.refs_0_ = bf16[512,2048]{1,0:T(8,128)(2,1)} custom-call(f32[1,2048]{1,0:T(1,128)} %bitcast.38, bf16[512,1024]{1,0:T(8,128)(2,1)} %get-tuple-element.163.query_ref, f32[512,1024]{1,0:T(8,128)} %get-tuple-element.164.local_ref, bf16[4096,128]{1,0:T(8,128)(2,1)} %assemble_states.1.states_ref), custom_call_target="tpu_custom_call" | custom-call | flops 536870912 | bytes 4194304 | tf_op jit(solution)/shard_map/finish/pallas_call | solution.py:466
  229.3 1.1 copy-done.3
  230.4 7.1 %attend.1 = bf16[512,2048]{1,0:T(8,128)(2,1)} custom-call(bf16[512,640]{1,0:T(8,128)(2,1)} %get-tuple-element.101.order_ref, bf16[512,512]{1,0:T(8,128)(2,1)} %get-tuple-element.102.causal_ref, bf16[512,128]{1,0:T(8,128)(2,1)} %get-tuple-element.103.carried_ref, f32[1,2048]{1,0:T(1,128)} %bitcast.39, ...), custom_call_target="tpu_custom_call", output_to_operand_aliasing={{}: (8, {})} | custom-call | flops 33084669952 | bytes 5505024 | tf_op jit(solution)/shard_map/attend/pallas_call | solution.py:373
  (111 shorter events, 17.3 us)
Async XLA Ops:
  1.3 3.7 %copy-start.22 = (s32[1,16,40]{2,1,0:T(8,128)S(1)}, s32[1,16,40]{2,1,0:T(8,128)}, u32[]{:S(2)}) copy-start(s32[1,16,40]{2,1,0:T(8,128)} %param.6) | copy-start | bytes 7684
  1.3 12.9 %collective-permute-start.1 = (bf16[2,256,512]{2,1,0:T(8,128)(2,1)S(1)}, bf16[2,256,512]{2,1,0:T(8,128)(2,1)S(1)}, u32[]{:S(2)}, u32[]{:S(2)}) collective-permute-start(bf16[2,256,512]{2,1,0:T(8,128)(2,1)S(1)} %slice_select_fusion.2), channel_id=1, source_target_pairs={{0,1},{1,0},{2,3},{3,2},{4,5},{5,4},{6,7},{7,6},{8,9},{9,8},{10,11... | collective-permute-start | bytes 1572872 | tf_op jit(solution)/shard_map/ppermute | solution.py:495
  4.6 43.3 %collective-permute-start.7 = (bf16[2,256,1536]{2,1,0:T(8,128)(2,1)S(1)}, bf16[2,256,1536]{2,1,0:T(8,128)(2,1)}, u32[]{:S(2)}, u32[]{:S(2)}) collective-permute-start(bf16[2,256,1536]{2,1,0:T(8,128)(2,1)S(1)} %slice_select_fusion), channel_id=1, source_target_pairs={{0,1},{1,0},{2,3},{3,2},{4,5},{5,4},{6,7},{7,6},{8,9},{9,8},{10,11... | collective-permute-start | bytes 4718600 | tf_op jit(solution)/shard_map/ppermute | solution.py:495
  14.1 0.8 copy-start.25
  18.0 39.1 %all-to-all-start = ((bf16[16,40,1024]{2,1,0:T(8,128)(2,1)}), bf16[16,40,1024]{2,1,0:T(8,128)(2,1)S(1)}, u32[]{:S(2)}, u32[]{:S(2)}) async-start(bf16[16,40,1024]{2,1,0:T(8,128)(2,1)} %bitcast.35), calls=%async_computation | async-start | bytes 2621440 | tf_op jit(solution)/shard_map/all_to_all | solution.py:519
  57.2 1.1 copy-start
  58.2 92.1 %all-to-all-start.1 = ((bf16[16,40,3072]{2,1,0:T(8,128)(2,1)}), bf16[16,40,3072]{2,1,0:T(8,128)(2,1)}, u32[]{:S(2)}, u32[]{:S(2)}) async-start(bf16[16,40,3072]{2,1,0:T(8,128)(2,1)} %bitcast.31), calls=%async_computation.1 | async-start | bytes 7864320 | tf_op jit(solution)/shard_map/all_to_all | solution.py:519
  63.4 3.0 %copy-start.23 = (s32[4]{0:T(128)S(1)}, s32[4]{0:T(128)}, u32[]{:S(2)}) copy-start(s32[4]{0:T(128)} %param.8) | copy-start | bytes 52
  63.4 4.4 %copy-start.12 = (s32[1,16,40]{2,1,0:T(8,128)S(1)}, s32[1,16,40]{2,1,0:T(8,128)}, u32[]{:S(2)}) copy-start(s32[1,16,40]{2,1,0:T(8,128)} %param.7) | copy-start | bytes 7684
  65.1 27.2 %collective-permute-start = (bf16[1,256,2048]{2,1,0:T(8,128)(2,1)S(1)}, bf16[1,256,2048]{2,1,0:T(8,128)(2,1)S(1)}, u32[]{:S(2)}, u32[]{:S(2)}) collective-permute-start(bf16[1,256,2048]{2,1,0:T(8,128)(2,1)S(1)} %slice_select_fusion.1), channel_id=1, source_target_pairs={{0,1},{1,0},{2,3},{3,2},{4,5},{5,4},{6,7},{7,6},{8,9},{9,8},{10,11... | collective-permute-start | bytes 3145736 | tf_op jit(solution)/shard_map/ppermute | solution.py:495
  70.2 11.1 %copy-start.21 = (s32[512]{0:T(512)}, s32[512]{0:T(512)S(1)}, u32[]{:S(2)}) copy-start(s32[512]{0:T(512)S(1)} %broadcast_add_fusion.1) | copy-start | bytes 6148
  70.4 11.0 %copy-start.1 = (s32[512,1]{1,0:T(8,128)}, s32[512,1]{1,0:T(8,128)S(1)}, u32[]{:S(2)}) copy-start(s32[512,1]{1,0:T(8,128)S(1)} %copy.21.seg_col_ref) | copy-start | bytes 6148
  78.3 8.8 %collective-permute-start.2 = (f32[128,128]{1,0:T(8,128)}, f32[128,128]{1,0:T(8,128)S(1)}, u32[]{:S(2)}, u32[]{:S(2)}) collective-permute-start(f32[128,128]{1,0:T(8,128)} %get-tuple-element.88), channel_id=1, source_target_pairs={{0,2},{2,0},{4,6},{6,4},{8,10},{10,8},{12,14},{14,12},{16,18},{18,... | collective-permute-start | bytes 196616 | tf_op jit(solution)/shard_map/ppermute | solution.py:235
  79.0 8.1 %collective-permute-start.3 = (f32[128,128]{1,0:T(8,128)}, f32[128,128]{1,0:T(8,128)S(1)}, u32[]{:S(2)}, u32[]{:S(2)}) collective-permute-start(f32[128,128]{1,0:T(8,128)} %get-tuple-element.89), channel_id=1, source_target_pairs={{0,4},{2,6},{4,0},{6,2},{8,12},{10,14},{12,8},{14,10},{16,20},{18,... | collective-permute-start | bytes 196616 | tf_op jit(solution)/shard_map/ppermute | solution.py:235
  79.3 10.7 %collective-permute-start.4 = (f32[128,128]{1,0:T(8,128)}, f32[128,128]{1,0:T(8,128)S(1)}, u32[]{:S(2)}, u32[]{:S(2)}) collective-permute-start(f32[128,128]{1,0:T(8,128)} %get-tuple-element.90), channel_id=1, source_target_pairs={{0,6},{2,4},{4,2},{6,0},{8,14},{10,12},{12,10},{14,8},{16,22},{18,... | collective-permute-start | bytes 196616 | tf_op jit(solution)/shard_map/ppermute | solution.py:235
  87.1 2.9 %copy-start.16 = (f32[128,128]{1,0:T(8,128)}, f32[128,128]{1,0:T(8,128)S(1)}, u32[]{:S(2)}) copy-start(f32[128,128]{1,0:T(8,128)S(1)} %collective-permute-done.2.refs_1_) | copy-start | bytes 196612
  87.1 2.9 %copy-start.17 = (f32[128,128]{1,0:T(8,128)}, f32[128,128]{1,0:T(8,128)S(1)}, u32[]{:S(2)}) copy-start(f32[128,128]{1,0:T(8,128)S(1)} %collective-permute-done.3.refs_2_) | copy-start | bytes 196612
  92.3 5.1 %copy-start.24 = (bf16[1,256,2048]{2,1,0:T(8,128)(2,1)}, bf16[1,256,2048]{2,1,0:T(8,128)(2,1)S(1)}, u32[]{:S(2)}) copy-start(bf16[1,256,2048]{2,1,0:T(8,128)(2,1)S(1)} %collective-permute-done.refs_3_) | copy-start | bytes 3145732
  92.3 57.2 %collective-permute-start.6 = (bf16[128,128]{1,0:T(8,128)(2,1)}, bf16[128,128]{1,0:T(8,128)(2,1)S(1)}, u32[]{:S(2)}, u32[]{:S(2)}) collective-permute-start(bf16[128,128]{1,0:T(8,128)(2,1)} %get-tuple-element.109), channel_id=1, source_target_pairs={{0,16},{2,18},{4,20},{6,22},{8,24},{10,26},{12,28},{14,30},{1,17},... | collective-permute-start | bytes 98312 | tf_op jit(solution)/shard_map/ppermute | solution.py:266
  95.5 54.7 %collective-permute-start.5 = (bf16[128,128]{1,0:T(8,128)(2,1)}, bf16[128,128]{1,0:T(8,128)(2,1)S(1)}, u32[]{:S(2)}, u32[]{:S(2)}) collective-permute-start(bf16[128,128]{1,0:T(8,128)(2,1)} %get-tuple-element.109), channel_id=1, source_target_pairs={{0,8},{2,10},{4,12},{6,14},{8,16},{10,18},{12,20},{14,22},{16,24},... | collective-permute-start | bytes 98312 | tf_op jit(solution)/shard_map/ppermute | solution.py:266
  149.5 12.3 %copy-start.19 = (bf16[128,128]{1,0:T(8,128)(2,1)}, bf16[128,128]{1,0:T(8,128)(2,1)S(1)}, u32[]{:S(2)}) copy-start(bf16[128,128]{1,0:T(8,128)(2,1)S(1)} %collective-permute-done.6.refs_5_) | copy-start | bytes 98308
  150.2 11.6 %copy-start.20 = (bf16[128,128]{1,0:T(8,128)(2,1)}, bf16[128,128]{1,0:T(8,128)(2,1)S(1)}, u32[]{:S(2)}) copy-start(bf16[128,128]{1,0:T(8,128)(2,1)S(1)} %collective-permute-done.5.refs_4_) | copy-start | bytes 98308
  150.3 38.5 %all-to-all-start.3 = ((bf16[16,40,1024]{2,1,0:T(8,128)(2,1)}), bf16[16,40,1024]{2,1,0:T(8,128)(2,1)S(1)}, u32[]{:S(2)}, u32[]{:S(2)}) async-start(bf16[16,40,1024]{2,1,0:T(8,128)(2,1)} %bitcast.33), calls=%async_computation.3 | async-start | bytes 2621440 | tf_op jit(solution)/shard_map/all_to_all | solution.py:519
  161.8 4.9 %collective-permute-start.8 = (f32[384,128]{1,0:T(8,128)}, f32[384,128]{1,0:T(8,128)S(1)}, u32[]{:S(2)}, u32[]{:S(2)}) collective-permute-start(f32[384,128]{1,0:T(8,128)} %get-tuple-element.124), channel_id=1, source_target_pairs={{0,2},{2,0},{4,6},{6,4},{8,10},{10,8},{12,14},{14,12},{16,18},{18,... | collective-permute-start | bytes 589832 | tf_op jit(solution)/shard_map/ppermute | solution.py:235
  162.2 8.3 %collective-permute-start.9 = (f32[384,128]{1,0:T(8,128)}, f32[384,128]{1,0:T(8,128)S(1)}, u32[]{:S(2)}, u32[]{:S(2)}) collective-permute-start(f32[384,128]{1,0:T(8,128)} %get-tuple-element.125), channel_id=1, source_target_pairs={{0,4},{2,6},{4,0},{6,2},{8,12},{10,14},{12,8},{14,10},{16,20},{18,... | collective-permute-start | bytes 589832 | tf_op jit(solution)/shard_map/ppermute | solution.py:235
  162.5 18.2 %collective-permute-start.10 = (f32[384,128]{1,0:T(8,128)}, f32[384,128]{1,0:T(8,128)S(1)}, u32[]{:S(2)}, u32[]{:S(2)}) collective-permute-start(f32[384,128]{1,0:T(8,128)} %get-tuple-element.126), channel_id=1, source_target_pairs={{0,6},{2,4},{4,2},{6,0},{8,14},{10,12},{12,10},{14,8},{16,22},{18,... | collective-permute-start | bytes 589832 | tf_op jit(solution)/shard_map/ppermute | solution.py:235
  166.3 17.5 %collective-permute-start.11 = (f32[128,128]{1,0:T(8,128)}, f32[128,128]{1,0:T(8,128)S(1)}, u32[]{:S(2)}, u32[]{:S(2)}) collective-permute-start(f32[128,128]{1,0:T(8,128)} %get-tuple-element.140), channel_id=1, source_target_pairs={{0,2},{2,0},{4,6},{6,4},{8,10},{10,8},{12,14},{14,12},{16,18},{18,... | collective-permute-start | bytes 196616 | tf_op jit(solution)/shard_map/ppermute | solution.py:235
  166.4 17.4 %collective-permute-start.12 = (f32[128,128]{1,0:T(8,128)}, f32[128,128]{1,0:T(8,128)S(1)}, u32[]{:S(2)}, u32[]{:S(2)}) collective-permute-start(f32[128,128]{1,0:T(8,128)} %get-tuple-element.141), channel_id=1, source_target_pairs={{0,4},{2,6},{4,0},{6,2},{8,12},{10,14},{12,8},{14,10},{16,20},{18,... | collective-permute-start | bytes 196616 | tf_op jit(solution)/shard_map/ppermute | solution.py:235
  166.7 14.1 %copy-start.7 = (f32[384,128]{1,0:T(8,128)}, f32[384,128]{1,0:T(8,128)S(1)}, u32[]{:S(2)}) copy-start(f32[384,128]{1,0:T(8,128)S(1)} %collective-permute-done.8.refs_1_) | copy-start | bytes 589828
  166.7 17.2 %collective-permute-start.13 = (f32[128,128]{1,0:T(8,128)}, f32[128,128]{1,0:T(8,128)S(1)}, u32[]{:S(2)}, u32[]{:S(2)}) collective-permute-start(f32[128,128]{1,0:T(8,128)} %get-tuple-element.142), channel_id=1, source_target_pairs={{0,6},{2,4},{4,2},{6,0},{8,14},{10,12},{12,10},{14,8},{16,22},{18,... | collective-permute-start | bytes 196616 | tf_op jit(solution)/shard_map/ppermute | solution.py:235
  170.5 10.2 %copy-start.8 = (f32[384,128]{1,0:T(8,128)}, f32[384,128]{1,0:T(8,128)S(1)}, u32[]{:S(2)}) copy-start(f32[384,128]{1,0:T(8,128)S(1)} %collective-permute-done.9.refs_2_) | copy-start | bytes 589828
  180.7 0.7 copy-start.9
  183.8 18.2 %copy-start.13 = (f32[128,128]{1,0:T(8,128)}, f32[128,128]{1,0:T(8,128)S(1)}, u32[]{:S(2)}) copy-start(f32[128,128]{1,0:T(8,128)S(1)} %collective-permute-done.11.refs_1_) | copy-start | bytes 196612
  183.8 18.2 %copy-start.14 = (f32[128,128]{1,0:T(8,128)}, f32[128,128]{1,0:T(8,128)S(1)}, u32[]{:S(2)}) copy-start(f32[128,128]{1,0:T(8,128)S(1)} %collective-permute-done.12.refs_2_) | copy-start | bytes 196612
  183.8 18.2 %copy-start.15 = (f32[128,128]{1,0:T(8,128)}, f32[128,128]{1,0:T(8,128)S(1)}, u32[]{:S(2)}) copy-start(f32[128,128]{1,0:T(8,128)S(1)} %collective-permute-done.13.refs_3_) | copy-start | bytes 196612
  183.9 18.2 %collective-permute-start.15 = (bf16[384,128]{1,0:T(8,128)(2,1)}, bf16[384,128]{1,0:T(8,128)(2,1)S(1)}, u32[]{:S(2)}, u32[]{:S(2)}) collective-permute-start(bf16[384,128]{1,0:T(8,128)(2,1)} %get-tuple-element.157), channel_id=1, source_target_pairs={{0,16},{2,18},{4,20},{6,22},{8,24},{10,26},{12,28},{14,30},{1,17},... | collective-permute-start | bytes 294920 | tf_op jit(solution)/shard_map/ppermute | solution.py:266
  186.7 15.4 %collective-permute-start.14 = (bf16[384,128]{1,0:T(8,128)(2,1)}, bf16[384,128]{1,0:T(8,128)(2,1)S(1)}, u32[]{:S(2)}, u32[]{:S(2)}) collective-permute-start(bf16[384,128]{1,0:T(8,128)(2,1)} %get-tuple-element.157), channel_id=1, source_target_pairs={{0,8},{2,10},{4,12},{6,14},{8,16},{10,18},{12,20},{14,22},{16,24},... | collective-permute-start | bytes 294920 | tf_op jit(solution)/shard_map/ppermute | solution.py:266
  188.8 13.2 %copy-start.2 = (bf16[16,40,1024]{2,1,0:T(8,128)(2,1)}, bf16[16,40,1024]{2,1,0:T(8,128)(2,1)S(1)}, u32[]{:S(2)}) copy-start(bf16[16,40,1024]{2,1,0:T(8,128)(2,1)S(1)} %all-to-all-done.3) | copy-start | bytes 3932164
  188.8 40.4 %all-to-all-start.2 = ((bf16[16,40,1024]{2,1,0:T(8,128)(2,1)}), bf16[16,40,1024]{2,1,0:T(8,128)(2,1)S(1)}, u32[]{:S(2)}, u32[]{:S(2)}) async-start(bf16[16,40,1024]{2,1,0:T(8,128)(2,1)} %bitcast.17), calls=%async_computation.2 | async-start | bytes 2621440 | tf_op jit(solution)/shard_map/all_to_all | solution.py:519
  202.1 0.6 copy-start.10
  202.7 0.6 copy-start.11
  205.7 8.1 %collective-permute-start.16 = (f32[384,128]{1,0:T(8,128)}, f32[384,128]{1,0:T(8,128)S(1)}, u32[]{:S(2)}, u32[]{:S(2)}) collective-permute-start(f32[384,128]{1,0:T(8,128)} %get-tuple-element.159), channel_id=1, source_target_pairs={{0,2},{2,0},{4,6},{6,4},{8,10},{10,8},{12,14},{14,12},{16,18},{18,... | collective-permute-start | bytes 589832 | tf_op jit(solution)/shard_map/ppermute | solution.py:235
  206.0 8.5 %collective-permute-start.17 = (f32[384,128]{1,0:T(8,128)}, f32[384,128]{1,0:T(8,128)S(1)}, u32[]{:S(2)}, u32[]{:S(2)}) collective-permute-start(f32[384,128]{1,0:T(8,128)} %get-tuple-element.160), channel_id=1, source_target_pairs={{0,4},{2,6},{4,0},{6,2},{8,12},{10,14},{12,8},{14,10},{16,20},{18,... | collective-permute-start | bytes 589832 | tf_op jit(solution)/shard_map/ppermute | solution.py:235
  206.3 16.0 %collective-permute-start.18 = (f32[384,128]{1,0:T(8,128)}, f32[384,128]{1,0:T(8,128)S(1)}, u32[]{:S(2)}, u32[]{:S(2)}) collective-permute-start(f32[384,128]{1,0:T(8,128)} %get-tuple-element.161), channel_id=1, source_target_pairs={{0,6},{2,4},{4,2},{6,0},{8,14},{10,12},{12,10},{14,8},{16,22},{18,... | collective-permute-start | bytes 589832 | tf_op jit(solution)/shard_map/ppermute | solution.py:235
  213.8 8.6 %copy-start.4 = (f32[384,128]{1,0:T(8,128)}, f32[384,128]{1,0:T(8,128)S(1)}, u32[]{:S(2)}) copy-start(f32[384,128]{1,0:T(8,128)S(1)} %collective-permute-done.16.refs_5_) | copy-start | bytes 589828
  214.6 7.8 %copy-start.5 = (f32[384,128]{1,0:T(8,128)}, f32[384,128]{1,0:T(8,128)S(1)}, u32[]{:S(2)}) copy-start(f32[384,128]{1,0:T(8,128)S(1)} %collective-permute-done.17.refs_6_) | copy-start | bytes 589828
  222.4 0.7 copy-start.6
  229.3 1.1 copy-start.3
  (1 other events, 0.6 us)
